TPU v7x, 32 devices: a whole 2x2x4 slice. The times are simulated.
32 devices in a mesh: fsdp: 8 (over z, x), tensor: 4 (over y, core).
Axes of the slice: x: 2, y: 2, z: 4, core: 2. Of those that a mesh axis runs over, the one named last changes fastest.
Arguments:
- hidden_in: bfloat16 [4096, 2048], P(('fsdp', 'tensor')), may hold values from -6 to 6
- ln_gain: float32 [2048], replicated, may hold values from 0.5 to 1.5
- ln_bias: float32 [2048], replicated, may hold values from -1.75 to 1.75
- w_qkv: bfloat16 [2048, 3, 2048], P('fsdp', None, 'tensor'), may hold values from -0.125 to 0.125
- b_qkv: float32 [3, 2048], P(None, 'tensor'), may hold values from -1.75 to 1.75
- w_dense: bfloat16 [2048, 2048], P('tensor', 'fsdp'), may hold values from -0.5 to 0.5
- b_dense: float32 [2048], replicated, may hold values from -1.75 to 1.75
- w_fc1: bfloat16 [2048, 8192], P('fsdp', 'tensor'), may hold values from -0.125 to 0.125
- b_fc1: float32 [8192], P('tensor'), may hold values from -1.75 to 1.75
- w_fc2: bfloat16 [8192, 2048], P('tensor', 'fsdp'), may hold values from -0.0625 to 0.0625
- b_fc2: float32 [2048], replicated, may hold values from -1.75 to 1.75
- segment_ids: int32 [8, 512], P('fsdp'), may hold values from 0 to 7, never falling along the last dimension, each value on 1 to 256 neighbouring positions
- out_grad: bfloat16 [4096, 2048], P(('fsdp', 'tensor')), may hold values from -6 to 6
Outputs:
- hidden_out: bfloat16 [4096, 2048], P(('fsdp', 'tensor'))
- input_grad: float32 [4096, 2048], P(('fsdp', 'tensor'))
- ln_gain_grad: float32 [2048], replicated
- ln_bias_grad: float32 [2048], replicated
- w_qkv_grad: float32 [2048, 3, 2048], P('fsdp', None, 'tensor')
- b_qkv_grad: float32 [3, 2048], P(None, 'tensor')
- w_dense_grad: float32 [2048, 2048], P('tensor', 'fsdp')
- b_dense_grad: float32 [2048], replicated
- w_fc1_grad: float32 [2048, 8192], P('fsdp', 'tensor')
- b_fc1_grad: float32 [8192], P('tensor')
- w_fc2_grad: float32 [8192, 2048], P('tensor', 'fsdp')
- b_fc2_grad: float32 [2048], replicated
Inputs may be any that keep to these rules, and one draw needn't show every extreme that they name: `segment_ids`: in each sequence the document numbers never fall; each document has 1 to 256 tokens and one has exactly 256.
All inputs are finite; a program needn't handle non-finite values.
Results may differ from a plain program's by a relative error of at most 0.0093.
Values may be sent and summed in bfloat16 or wider, within the bound.
No kernel may reach another device: no remote copies, remote signals or barrier semaphores. Data moves between devices by JAX's collectives and lax.ppermute only.
A program may use at most 192 MiB of HBM per device.

v0:
```python
import math

import jax
import jax.numpy as jnp
from jax import lax
from jax.sharding import PartitionSpec as P

HEAD_DIM = 64
ROT = 32


EPS = 1e-05


def layer_norm(values, norm_gain, norm_shift):
    centred = values - jnp.mean(values, axis=-1, keepdims=True)
    variance = jnp.mean(centred * centred, axis=-1, keepdims=True)
    return centred * lax.rsqrt(variance + EPS) * norm_gain + norm_shift


def gelu_tanh(values):
    return jax.nn.gelu(values, approximate=True)


def rotary_tables(length):
    positions = jnp.arange(length).astype(jnp.float32)
    inverse = 10000.0 ** (-jnp.arange(0, ROT, 2).astype(jnp.float32) / ROT)
    angles = positions[:, None] * inverse[None, :]
    return (jnp.cos(angles), jnp.sin(angles))


def rotate(values, cosine_rows, sine_rows):
    half_rot = ROT // 2
    first_half = values[..., :half_rot]
    second = values[..., half_rot:ROT]
    others = values[..., ROT:]
    cos_rows = cosine_rows[:, None, :]
    sin_rows = sine_rows[:, None, :]
    return jnp.concatenate(
        [
            first_half * cos_rows - second * sin_rows,
            second * cos_rows + first_half * sin_rows,
            others,
        ],
        axis=-1,
    )


def unrotate(values, cosine_rows, sine_rows):
    half_rot = ROT // 2
    first_half = values[..., :half_rot]
    second = values[..., half_rot:ROT]
    others = values[..., ROT:]
    cos_rows = cosine_rows[:, None, :]
    sin_rows = sine_rows[:, None, :]
    return jnp.concatenate(
        [
            first_half * cos_rows + second * sin_rows,
            second * cos_rows - first_half * sin_rows,
            others,
        ],
        axis=-1,
    )


def contract_rows(left, right):
    return lax.dot_general(
        left, right, (((0,), (0,)), ((), ())), preferred_element_type=jnp.float32
    )


def contract_cols(left, right):
    return lax.dot_general(
        left, right, (((1,), (1,)), ((), ())), preferred_element_type=jnp.float32
    )


def body(
    hidden_in,
    ln_gain,
    ln_bias,
    w_qkv,
    b_qkv,
    w_dense,
    b_dense,
    w_fc1,
    b_fc1,
    w_fc2,
    b_fc2,
    segment_ids,
    out_grad,
):
    hidden = hidden_in.astype(jnp.float32)
    normed = layer_norm(hidden, ln_gain, ln_bias)
    normed_all = lax.all_gather(normed.astype(jnp.bfloat16), "tensor", axis=0, tiled=True)
    seq_len = normed_all.shape[0]
    qkv_weights, up_weights = (
        lax.all_gather(w_qkv, "fsdp", axis=0, tiled=True),
        lax.all_gather(w_fc1, "fsdp", axis=0, tiled=True),
    )
    local_width = b_qkv.shape[1]
    head_count = local_width // HEAD_DIM
    mixed_proj = (
        jnp.einsum("sd,djc->sjc", normed_all, qkv_weights, preferred_element_type=jnp.float32)
        + b_qkv
    )
    before = jnp.dot(normed_all, up_weights, preferred_element_type=jnp.float32) + b_fc1
    cosine_rows, sine_rows = rotary_tables(seq_len)
    split_heads = mixed_proj.reshape(seq_len, 3, head_count, HEAD_DIM)
    queries = rotate(split_heads[:, 0], cosine_rows, sine_rows).astype(jnp.bfloat16)
    key_rows = rotate(split_heads[:, 1], cosine_rows, sine_rows).astype(jnp.bfloat16)
    value_rows = split_heads[:, 2].astype(jnp.bfloat16)
    segments = segment_ids[0]
    block_rows = min(512, seq_len)
    block_count = seq_len // block_rows
    score_scale = 1.0 / math.sqrt(HEAD_DIM)
    col_pos = jnp.arange(seq_len, dtype=jnp.int32)

    def block_scores(offset):
        row_pos = offset + jnp.arange(block_rows, dtype=jnp.int32)
        allowed = (col_pos[None, :] <= row_pos[:, None]) & (segments[:, None] == segments[None, :])
        scores = (
            jnp.einsum("qhd,khd->hqk", queries, key_rows, preferred_element_type=jnp.float32)
            * score_scale
        )
        return (queries, jnp.where(allowed[None], scores, -1e30))

    def forward_block(block_index):
        offset = block_index * block_rows
        query_rows, scores = block_scores(offset)
        highest = jnp.max(scores, axis=-1, keepdims=True)
        shifted = jnp.exp(scores - highest)
        totals = jnp.sum(shifted, axis=-1, keepdims=True)
        attend = (shifted / totals).astype(jnp.bfloat16)
        context = jnp.einsum("hqk,khd->qhd", attend, value_rows, preferred_element_type=jnp.float32)
        return (context, (highest + jnp.log(totals))[..., 0])

    contexts, log_sums = lax.map(forward_block, jnp.arange(block_count, dtype=jnp.int32))
    context_b = contexts.reshape(seq_len, local_width).astype(jnp.bfloat16)
    activated_b = gelu_tanh(before).astype(jnp.bfloat16)
    out_weights, down_weights = (
        lax.all_gather(w_dense, "fsdp", axis=1, tiled=True),
        lax.all_gather(w_fc2, "fsdp", axis=1, tiled=True),
    )
    attn_part = jnp.dot(context_b, out_weights, preferred_element_type=jnp.float32)
    mlp_part = jnp.dot(activated_b, down_weights, preferred_element_type=jnp.float32)
    branch_total = lax.psum_scatter(
        attn_part, "tensor", scatter_dimension=0, tiled=True
    ) + lax.psum_scatter(
        mlp_part.astype(jnp.bfloat16), "tensor", scatter_dimension=0, tiled=True
    ).astype(
        jnp.float32
    )
    hidden_out = (hidden + branch_total + b_dense + b_fc2).astype(jnp.bfloat16)
    grad_all = lax.all_gather(out_grad, "tensor", axis=0, tiled=True)
    dense_grad_local = contract_rows(context_b, grad_all)
    down_grad_local = contract_rows(activated_b, grad_all)
    dense_weight_grad, down_weight_grad = (
        lax.psum_scatter(dense_grad_local, "fsdp", scatter_dimension=1, tiled=True),
        lax.psum_scatter(down_grad_local, "fsdp", scatter_dimension=1, tiled=True),
    )
    context_grad = contract_cols(grad_all, out_weights).astype(jnp.bfloat16)
    activated_grad = contract_cols(grad_all, down_weights)
    gelu_value, gelu_pull = jax.vjp(gelu_tanh, before)
    before_grad = gelu_pull(activated_grad)[0].astype(jnp.bfloat16)
    up_grad_local = contract_rows(normed_all, before_grad)
    context_heads = context_grad.reshape(seq_len, head_count, HEAD_DIM)

    def backward_block(accumulate, block_index):
        key_acc, value_acc = accumulate
        offset = block_index * block_rows
        query_rows, scores = block_scores(offset)
        log_sum = lax.dynamic_index_in_dim(log_sums, block_index, 0, keepdims=False)
        attend = jnp.exp(scores - log_sum[..., None])
        attend_grad = jnp.einsum(
            "qhd,khd->hqk", context_heads, value_rows, preferred_element_type=jnp.float32
        )
        row_inner = jnp.sum(attend * attend_grad, axis=-1, keepdims=True)
        score_grad = (attend * (attend_grad - row_inner)).astype(jnp.bfloat16)
        query_grad = (
            jnp.einsum("hqk,khd->qhd", score_grad, key_rows, preferred_element_type=jnp.float32)
            * score_scale
        )
        key_acc = (
            key_acc
            + jnp.einsum("hqk,qhd->khd", score_grad, query_rows, preferred_element_type=jnp.float32)
            * score_scale
        )
        value_acc = value_acc + jnp.einsum(
            "hqk,qhd->khd",
            attend.astype(jnp.bfloat16),
            context_heads,
            preferred_element_type=jnp.float32,
        )
        return ((key_acc, value_acc), query_grad)

    zero_heads = jnp.zeros((seq_len, head_count, HEAD_DIM), jnp.float32)
    (key_grad, value_grad), query_grads = lax.scan(
        backward_block, (zero_heads, zero_heads), jnp.arange(block_count, dtype=jnp.int32)
    )
    query_grad = query_grads.reshape(seq_len, head_count, HEAD_DIM)
    mixed_grad = jnp.stack(
        [
            unrotate(query_grad, cosine_rows, sine_rows),
            unrotate(key_grad, cosine_rows, sine_rows),
            value_grad,
        ],
        axis=1,
    )
    mixed_grad = mixed_grad.reshape(seq_len, 3, local_width).astype(jnp.bfloat16)
    qkv_grad_local = jnp.einsum(
        "sd,sjc->djc", normed_all, mixed_grad, preferred_element_type=jnp.float32
    )
    attn_back = jnp.einsum(
        "sjc,djc->sd", mixed_grad, qkv_weights, preferred_element_type=jnp.float32
    )
    mlp_back = contract_cols(before_grad, up_weights)
    normed_grad = lax.psum_scatter(
        attn_back, "tensor", scatter_dimension=0, tiled=True
    ) + lax.psum_scatter(
        mlp_back.astype(jnp.bfloat16), "tensor", scatter_dimension=0, tiled=True
    ).astype(
        jnp.float32
    )
    norm_value, norm_pull = jax.vjp(layer_norm, hidden, ln_gain, ln_bias)
    hidden_grad, gain_local, shift_local = norm_pull(normed_grad)
    cotangent = out_grad.astype(jnp.float32)
    input_grad = cotangent + hidden_grad
    gain_grad, shift_grad, out_bias_grad = lax.psum(
        (gain_local, shift_local, jnp.sum(cotangent, axis=0)), ("fsdp", "tensor")
    )
    qkv_bias_grad, up_bias_grad = lax.psum(
        (
            jnp.sum(mixed_grad, axis=0, dtype=jnp.float32),
            jnp.sum(before_grad, axis=0, dtype=jnp.float32),
        ),
        "fsdp",
    )
    qkv_weight_grad, up_weight_grad = (
        lax.psum_scatter(qkv_grad_local, "fsdp", scatter_dimension=0, tiled=True),
        lax.psum_scatter(up_grad_local, "fsdp", scatter_dimension=0, tiled=True),
    )
    return (
        hidden_out,
        input_grad,
        gain_grad,
        shift_grad,
        qkv_weight_grad,
        qkv_bias_grad,
        dense_weight_grad,
        out_bias_grad,
        up_weight_grad,
        up_bias_grad,
        down_weight_grad,
        out_bias_grad,
    )


def solution(mesh):
    in_specs = (
        P(("fsdp", "tensor"), None),
        P(),
        P(),
        P("fsdp", None, "tensor"),
        P(None, "tensor"),
        P("tensor", "fsdp"),
        P(),
        P("fsdp", "tensor"),
        P("tensor"),
        P("tensor", "fsdp"),
        P(),
        P("fsdp", None),
        P(("fsdp", "tensor"), None),
    )
    out_specs = (
        P(("fsdp", "tensor"), None),
        P(("fsdp", "tensor"), None),
        P(),
        P(),
        P("fsdp", None, "tensor"),
        P(None, "tensor"),
        P("tensor", "fsdp"),
        P(),
        P("fsdp", "tensor"),
        P("tensor"),
        P("tensor", "fsdp"),
        P(),
    )
    return jax.shard_map(body, mesh=mesh, in_specs=in_specs, out_specs=out_specs, check_vma=False)
```

profile of v0, /device:TPU:0, one launch (start us, length us, event | category | flops | bytes accessed | tf_op | source)
XLA Modules:
  0.0 1531.2 jit_solution(14621272679159537273)
XLA Ops:
  8.7 1.2 convert_reduce_fusion.2
  9.9 1.3 fusion.35
  12.3 2.3 fusion.33
  14.6 2.3 copy.25
  18.2 0.8 multiply_cosine_fusion
  19.0 0.9 fusion.40
  19.9 15.0 all-gather.17.cloned.1.call-done
  34.9 53.2 %all-gather.11.cloned.1.call-done = bf16[512,2048]{1,0:T(8,128)(2,1)} async-done(((bf16[512,256]{1,0:T(8,128)(2,1)}), bf16[512,2048]{1,0:T(8,128)(2,1)}) %all-gather.11.cloned.1.call-update) | async-done | bytes 2097168 | tf_op jit(solution)/shard_map/all_gather | solution.py:142
  88.1 4.3 convolution_convert_fusion.2
  92.4 18.7 %all-gather.7.cloned.1.call-done = bf16[512,2048]{1,0:T(8,128)(2,1)} async-done(((bf16[128,2048]{1,0:T(8,128)(2,1)}), bf16[512,2048]{1,0:T(8,128)(2,1)}) %all-gather.7.cloned.1.call-update) | async-done | bytes 2097168 | tf_op jit(solution)/shard_map/all_gather | solution.py:95
  111.1 102.4 %all-gather.9.cloned.1.call-done = bf16[2048,3,512]{0,2,1:T(8,128)(2,1)} async-done(((bf16[256,3,512]{0,2,1:T(8,128)(2,1)}), bf16[2048,3,512]{0,2,1:T(8,128)(2,1)}) %all-gather.9.cloned.1.call-update) | async-done | bytes 6291472 | tf_op jit(solution)/shard_map/all_gather | solution.py:98
  213.5 6.4 fusion.17
  221.6 4.7 fusion.53
  226.4 112.2 %all-gather.13.cloned.1.call-done = bf16[2048,2048]{1,0:T(8,128)(2,1)} async-done(((bf16[256,2048]{1,0:T(8,128)(2,1)}), bf16[2048,2048]{1,0:T(8,128)(2,1)}) %all-gather.13.cloned.1.call-update) | async-done | bytes 8388624 | tf_op jit(solution)/shard_map/all_gather | solution.py:99
  338.6 10.5 fusion.55
  349.1 115.0 %all-gather.15.cloned.1.call-done = bf16[2048,2048]{1,0:T(8,128)(2,1)} async-done(((bf16[2048,256]{1,0:T(8,128)(2,1)}), bf16[2048,2048]{1,0:T(8,128)(2,1)}) %all-gather.15.cloned.1.call-update) | async-done | bytes 8388624 | tf_op jit(solution)/shard_map/all_gather | solution.py:143
  464.1 12.8 convert_reduce_fusion
  477.0 1.3 copy-done.41
  478.3 6.0 convolution_convert_fusion
  484.4 4.7 fusion
  489.2 1.4 log_add_fusion
  490.8 3.3 fusion.27
  494.1 2.0 copy.32
  496.2 4.6 multiply_reduce_fusion
  500.8 4.5 multiply_convert_fusion
  506.3 1.4 fusion.24
  507.9 1.0 pad_maximum_fusion.3
  508.9 2.0 copy.30
  511.0 2.1 copy.31
  513.0 8.8 convolution_bitcast_fusion
  522.5 11.8 convolution_convert_fusion.1
  534.4 5.0 fusion.26
  540.2 3.2 fusion.54
  543.6 0.9 copy-done.8
  544.5 4.8 fusion.56
  549.5 8.1 fusion.13
  557.8 14.1 fusion.50
  572.0 12.8 fusion.57
  585.5 35.0 %all-reduce.1 = (f32[3,512]{1,0:T(4,128)}, f32[2048]{0:T(1024)}) all-reduce(f32[3,512]{1,0:T(4,128)S(1)} %convert_reduce_fusion.1, f32[2048]{0:T(1024)S(1)} %copy-done.32), channel_id=1, replica_groups=mesh['fsdp'=8,'tensor'=4] {'fsdp'}, use_global_device_ids=true, to_apply=%region_17.18 | all-reduce | flops 3584 | bytes 28672 | tf_op jit(solution)/shard_map/psum | solution.py:232
  620.5 1.8 fusion.34
  622.3 23.3 %reduce-scatter.9.cloned.1.call-done = f32[128,2048]{1,0:T(8,128)} async-done(((f32[512,2048]{1,0:T(8,128)}), f32[128,2048]{1,0:T(8,128)}) %reduce-scatter.9.cloned.1.call-update) | async-done | bytes 1048592 | tf_op jit(solution)/shard_map/reduce_scatter | solution.py:147
  645.7 3.2 fusion.52
  648.9 1.2 convert_reduce_fusion.3
  650.1 41.6 %all-reduce = (f32[2048]{0:T(1024)}, f32[2048]{0:T(1024)}, f32[2048]{0:T(1024)S(1)}) all-reduce(f32[2048]{0:T(1024)S(1)} %get-tuple-element.58, f32[2048]{0:T(1024)S(1)} %get-tuple-element.60, f32[2048]{0:T(1024)S(1)} %get-tuple-element.91), channel_id=1, replica_groups=mesh['fsdp'=8,'tensor'=4] {'fsdp','tensor'}, use_global_device_ids=true, to_apply=%region_12.13 | all-reduce | flops 6144 | bytes 49152 | tf_op jit(solution)/shard_map/psum | solution.py:229
  691.7 47.7 %reduce-scatter.19.cloned.1.call-done = f32[512,256]{1,0:T(8,128)} async-done(((f32[512,2048]{1,0:T(8,128)}), f32[512,256]{1,0:T(8,128)}) %reduce-scatter.19.cloned.1.call-update) | async-done | bytes 524304 | tf_op jit(solution)/shard_map/reduce_scatter | solution.py:159
  739.4 211.9 %reduce-scatter.17.cloned.1.call-done = f32[256,3,512]{2,0,1:T(8,128)} async-done(((f32[2048,3,512]{2,0,1:T(8,128)}), f32[256,3,512]{2,0,1:T(8,128)}) %reduce-scatter.17.cloned.1.call-update) | async-done | bytes 1572880 | tf_op jit(solution)/shard_map/reduce_scatter | solution.py:240
  951.3 286.5 %reduce-scatter.23.cloned.1.call-done = f32[2048,256]{1,0:T(8,128)} async-done(((f32[2048,2048]{1,0:T(8,128)}), f32[2048,256]{1,0:T(8,128)}) %reduce-scatter.23.cloned.1.call-update) | async-done | bytes 2097168 | tf_op jit(solution)/shard_map/reduce_scatter | solution.py:160
  1237.9 286.0 %reduce-scatter.21.cloned.1.call-done = f32[256,2048]{1,0:T(8,128)} async-done(((f32[2048,2048]{1,0:T(8,128)}), f32[256,2048]{1,0:T(8,128)}) %reduce-scatter.21.cloned.1.call-update) | async-done | bytes 2097168 | tf_op jit(solution)/shard_map/reduce_scatter | solution.py:241
  (129 shorter events, 10.1 us)
Async XLA Ops:
  7.2 11.8 copy-start.31
  7.2 27.7 %all-gather.17.cloned.1.call-start = ((), (), s32[]{:S(2)}) async-start(), calls=%async_computation.15 | async-start | bytes 2621440 | tf_op jit(solution)/shard_map/all_gather | solution.py:155
  7.9 80.2 %all-gather.11.cloned.1.call-start = ((), (), s32[]{:S(2)}) async-start(), calls=%async_computation.10 | async-start | bytes 2359296 | tf_op jit(solution)/shard_map/all_gather | solution.py:142
  8.7 102.4 %all-gather.7.cloned.1.call-start = ((), (), s32[]{:S(2)}) async-start(), calls=%async_computation.8 | async-start | bytes 2621440 | tf_op jit(solution)/shard_map/all_gather | solution.py:95
  9.9 1.9 copy-start.27
  14.6 198.9 %all-gather.9.cloned.1.call-start = ((), (), s32[]{:S(2)}) async-start(), calls=%async_computation.9 | async-start | bytes 7077888 | tf_op jit(solution)/shard_map/all_gather | solution.py:98
  16.9 321.7 %all-gather.13.cloned.1.call-start = ((), (), s32[]{:S(2)}) async-start(), calls=%async_computation.12 | async-start | bytes 9437184 | tf_op jit(solution)/shard_map/all_gather | solution.py:99
  17.5 196.0 %copy-start.39 = (f32[3,512]{1,0:T(4,128)S(1)}, f32[3,512]{1,0:T(4,128)}, u32[]{:S(2)}) copy-start(f32[3,512]{1,0:T(4,128)} %param.17) | copy-start | bytes 18436
  17.5 446.6 %all-gather.15.cloned.1.call-start = ((), (), s32[]{:S(2)}) async-start(), calls=%async_computation.13 | async-start | bytes 9437184 | tf_op jit(solution)/shard_map/all_gather | solution.py:143
  18.1 602.3 %reduce-scatter.15.cloned.1.call-start = ((), (), s32[]{:S(2)}) async-start(), calls=%async_computation.17 | async-start | bytes 2621440 | tf_op jit(solution)/shard_map/reduce_scatter | solution.py:220
  220.0 0.8 copy-start.17
  220.0 0.8 copy-start.19
  220.0 1.7 copy-start.21
  226.4 258.0 %copy-start.23 = (f32[8,512]{1,0:T(8,128)}, f32[8,512]{1,0:T(8,128)S(1)}, u32[]{:S(2)}) copy-start(f32[8,512]{1,0:T(8,128)S(1)} %get-tuple-element.100) | copy-start | bytes 49156
  464.1 14.2 copy-start.38
  477.0 1.3 copy-start.41
  484.3 136.1 %reduce-scatter.13.cloned.1.call-start = ((), (), s32[]{:S(2)}) async-start(), calls=%async_computation.16 | async-start | bytes 5242880 | tf_op jit(solution)/shard_map/reduce_scatter | solution.py:218
  484.4 6.4 copy-start
  489.2 5.0 copy-start.25
  500.8 4.5 copy-start.10
  500.8 4.5 copy-start.14
  500.8 4.5 copy-start.16
  505.4 0.9 copy-start.12
  506.2 1.5 copy-start.18
  506.2 1.5 copy-start.20
  521.9 12.5 copy-start.24
  521.9 12.5 copy-start.26
  521.9 100.4 %reduce-scatter.11.cloned.1.call-start = ((), (), s32[]{:S(2)}) async-start(), calls=%async_computation.14 | async-start | bytes 2621440 | tf_op jit(solution)/shard_map/reduce_scatter | solution.py:149
  534.4 111.3 %reduce-scatter.9.cloned.1.call-start = ((), (), s32[]{:S(2)}) async-start(), calls=%async_computation.11 | async-start | bytes 5242880 | tf_op jit(solution)/shard_map/reduce_scatter | solution.py:147
  534.4 5.8 copy-start.5
  539.4 0.8 copy-start.7
  543.5 1.0 copy-start.8
  543.5 5.9 copy-start.2
  543.5 5.9 copy-start.3
  543.5 5.9 copy-start.4
  543.5 195.9 %reduce-scatter.19.cloned.1.call-start = ((), (), s32[]{:S(2)}) async-start(), calls=%async_computation.19 | async-start | bytes 4718592 | tf_op jit(solution)/shard_map/reduce_scatter | solution.py:159
  549.4 402.0 %reduce-scatter.17.cloned.1.call-start = ((), (), s32[]{:S(2)}) async-start(), calls=%async_computation.18 | async-start | bytes 14155776 | tf_op jit(solution)/shard_map/reduce_scatter | solution.py:240
  557.6 680.2 %reduce-scatter.23.cloned.1.call-start = ((), (), s32[]{:S(2)}) async-start(), calls=%async_computation.21 | async-start | bytes 18874368 | tf_op jit(solution)/shard_map/reduce_scatter | solution.py:160
  571.9 951.9 %reduce-scatter.21.cloned.1.call-start = ((), (), s32[]{:S(2)}) async-start(), calls=%async_computation.20 | async-start | bytes 18874368 | tf_op jit(solution)/shard_map/reduce_scatter | solution.py:241
  584.8 35.7 %copy-start.1 = (bf16[128,2048]{1,0:T(8,128)(2,1)S(1)}, bf16[128,2048]{1,0:T(8,128)(2,1)}, u32[]{:S(2)}) copy-start(bf16[128,2048]{1,0:T(8,128)(2,1)} %param.13) | copy-start | bytes 1572868
  584.8 35.7 %copy-start.22 = (f32[2048]{0:T(1024)S(1)}, f32[2048]{0:T(1024)}, u32[]{:S(2)}) copy-start(f32[2048]{0:T(1024)} %param.14) | copy-start | bytes 24580
  584.8 35.7 %copy-start.28 = (f32[128]{0:T(128)S(1)}, f32[128]{0:T(128)}, u32[]{:S(2)}) copy-start(f32[128]{0:T(128)} %copy-done.27) | copy-start | bytes 1540
  584.8 35.7 %copy-start.35 = (f32[128]{0:T(128)S(1)}, f32[128]{0:T(128)}, u32[]{:S(2)}) copy-start(f32[128]{0:T(128)} %copy-done.34) | copy-start | bytes 1540
  584.8 37.5 %copy-start.37 = (f32[128]{0:T(128)S(1)}, f32[128]{0:T(128)}, u32[]{:S(2)}) copy-start(f32[128]{0:T(128)} %copy-done.36) | copy-start | bytes 1540
  584.8 60.9 %copy-start.29 = (f32[2048]{0:T(1024)S(1)}, f32[2048]{0:T(1024)}, u32[]{:S(2)}) copy-start(f32[2048]{0:T(1024)} %param.23) | copy-start | bytes 24580
  584.8 60.9 %copy-start.30 = (f32[2048]{0:T(1024)S(1)}, f32[2048]{0:T(1024)}, u32[]{:S(2)}) copy-start(f32[2048]{0:T(1024)} %param.19) | copy-start | bytes 24580
  584.8 64.0 %copy-start.6 = (bf16[128,2048]{1,0:T(8,128)(2,1)S(1)}, bf16[128,2048]{1,0:T(8,128)(2,1)}, u32[]{:S(2)}) copy-start(bf16[128,2048]{1,0:T(8,128)(2,1)} %param.25) | copy-start | bytes 1572868
  691.7 832.8 %copy-start.33 = (f32[2048]{0:T(1024)}, f32[2048]{0:T(1024)S(1)}, u32[]{:S(2)}) copy-start(f32[2048]{0:T(1024)S(1)} %get-tuple-element.129) | copy-start | bytes 24580
  (8 other events, 5.2 us)
Sparse Core Ops, SparseCore 0:
  9.6 25.2 all-gather.16
  36.9 51.1 all-gather.10
  90.3 20.7 all-gather.6
  113.5 99.9 all-gather.8
  215.5 123.1 all-gather.12
  340.5 123.5 all-gather.14
  484.5 29.5 reduce-scatter.14
  522.0 42.5 reduce-scatter.12
  567.1 31.4 reduce-scatter.10
  601.1 44.4 reduce-scatter.8
  649.9 89.4 reduce-scatter.18
  743.9 207.4 reduce-scatter.16
  956.2 281.6 reduce-scatter.22
  1242.1 281.7 reduce-scatter.20
where the time goes:
time: 1540 us; the launch traced here: 1530 us
  waiting for transfers between devices  1270 us (82%)
  matrix products  124 us (8%)
  blocking collectives  76.6 us (5%)
  other arithmetic  25 us (2%)
  local copies, waits for them, and re-layouts  15.6 us (1%)
    reduce_scatter x1, waiting for transfers between devices, body(): lax.psum_scatter(down_grad_local, 'fsdp', scatter_dimension=1, tiled=True)  287 us
    reduce_scatter x1, waiting for transfers between devices, body(): lax.psum_scatter(up_grad_local, 'fsdp', scatter_dimension=0, tiled=True)  286 us
    reduce_scatter x1, waiting for transfers between devices, body(): lax.psum_scatter(qkv_grad_local, 'fsdp', scatter_dimension=0, tiled=True)  212 us
    all_gather x1, waiting for transfers between devices, body(): lax.all_gather(w_fc2, 'fsdp', axis=1, tiled=True)  115 us
    all_gather x1, waiting for transfers between devices, body(): lax.all_gather(w_fc1, 'fsdp', axis=0, tiled=True)  112 us
    all_gather x1, waiting for transfers between devices, body(): lax.all_gather(w_qkv, 'fsdp', axis=0, tiled=True)  102 us
    all_gather x1, waiting for transfers between devices, body(): lax.all_gather(w_dense, 'fsdp', axis=1, tiled=True)  53.2 us
    reduce_scatter x1, waiting for transfers between devices, body(): lax.psum_scatter(dense_grad_local, 'fsdp', scatter_dimension=1, tiled=True)  47.7 us
  transfers between devices with their start and end apart: 14, of which 11 were waited for; matrix products, arithmetic and copies ran while one was open for 9% of the time, Pallas kernels for 0%

commit v1 on v0

v1 whole, which is shorter than its diff:
```python
import math

import jax
import jax.numpy as jnp
from jax import lax
from jax.sharding import Mesh
from jax.sharding import PartitionSpec as P

HEAD_DIM = 64
ROT = 32
EPS = 1e-05

BF = jnp.bfloat16
F32 = jnp.float32


def layer_norm(values, norm_gain, norm_shift):
    centred = values - jnp.mean(values, axis=-1, keepdims=True)
    variance = jnp.mean(centred * centred, axis=-1, keepdims=True)
    return centred * lax.rsqrt(variance + EPS) * norm_gain + norm_shift


def gelu_tanh(values):
    return jax.nn.gelu(values, approximate=True)


def rotate(values, cosine, sine):
    half = ROT // 2
    first, second, others = values[..., :half], values[..., half:ROT], values[..., ROT:]
    return jnp.concatenate(
        [first * cosine - second * sine, second * cosine + first * sine, others], axis=-1
    )


def swap_with(values, axis, mask, size):
    return lax.ppermute(values, axis, [(i, i ^ mask) for i in range(size)])


def flip_pairs(values, axis, block):
    count = values.shape[axis] // block
    parts = [lax.slice_in_dim(values, i * block, (i + 1) * block, axis=axis) for i in range(count)]
    return jnp.concatenate([parts[i ^ 1] for i in range(count)], axis=axis)


def dot(left, right, dims):
    return lax.dot_general(left, right, (dims, ((), ())), preferred_element_type=F32)


def make_body(line):
    def body(
        hidden_in, ln_gain, ln_bias, w_qkv, b_qkv, w_dense, b_dense,
        w_fc1, b_fc1, w_fc2, b_fc2, segment_ids, out_grad,
    ):
        z, xb = lax.axis_index("z"), lax.axis_index("x")
        yb, cb = lax.axis_index("y"), lax.axis_index("core")
        tile, width = hidden_in.shape
        block = width // (2 * line)

        def half(values, which, axis):
            size = values.shape[axis] // 2
            return lax.dynamic_slice_in_dim(values, which * size, size, axis)

        def own_order(values, axis):
            return jnp.where(xb == 1, flip_pairs(values, axis, block), values)

        def swap_x(values):
            return swap_with(values, "x", 1, 2)

        def swap_y(values):
            return swap_with(values, "y", 1, 2)

        def swap_c(values):
            return swap_with(values, "core", 1, 2)

        def spread(keep, send, axis):
            both = jnp.concatenate([keep, swap_x(send)], axis=axis)
            return lax.all_gather(both, "z", axis=axis, tiled=True)

        def qkv_half(which):
            piece = half(w_qkv, which, 2)
            return jnp.concatenate([piece[:, j] for j in range(3)], axis=1)

        hidden = hidden_in.astype(F32)
        normed = layer_norm(hidden, ln_gain, ln_bias).astype(BF)

        up_w = spread(half(w_fc1, xb, 1), half(w_fc1, 1 - xb, 1), 0)
        qkv_w = spread(qkv_half(xb), qkv_half(1 - xb), 0)
        dense_w = spread(half(w_dense, xb, 0), half(w_dense, 1 - xb, 0), 1)
        down_w = spread(half(w_fc2, xb, 0), half(w_fc2, 1 - xb, 0), 1)

        def gather_tokens(values):
            mine = own_order(values, 1)
            other = swap_x(flip_pairs(mine, 1, block))
            rows = jnp.stack([mine, other])
            rows = jnp.concatenate([rows, swap_y(rows)], axis=1)
            rows = jnp.concatenate([rows, swap_c(rows)], axis=1)
            return rows.reshape(-1, width)

        def scatter_tokens(partial):
            rows = partial.reshape(2, 4 * tile, width)
            rows = rows[:, : 2 * tile].astype(F32) + swap_c(rows[:, 2 * tile :]).astype(F32)
            rows = rows.astype(BF)
            rows = rows[:, :tile].astype(F32) + swap_y(rows[:, tile:]).astype(F32)
            sent = flip_pairs(rows[1].astype(BF), 1, block)
            return own_order(rows[0] + swap_x(sent).astype(F32), 1)

        normed_all = gather_tokens(normed)
        grad_all = gather_tokens(out_grad)
        seq_len = 4 * tile

        def token_order(values):
            parts = [values[:, i * tile : (i + 1) * tile] for i in range(4)]
            order = [parts[0], parts[2], parts[1], parts[3]]
            order = [jnp.where(yb == 1, order[i ^ 1], order[i]) for i in range(4)]
            order = [jnp.where(cb == 1, order[i ^ 2], order[i]) for i in range(4)]
            return jnp.concatenate(order, axis=1)

        segments = jnp.concatenate([segment_ids, swap_x(segment_ids)], axis=0)
        segments = token_order(segments)
        positions = token_order(jnp.arange(seq_len, dtype=jnp.int32)[None, :])[0]
        inverse = 10000.0 ** (-jnp.arange(0, ROT, 2).astype(F32) / ROT)
        angles = jnp.arange(seq_len).astype(F32)[:, None] * inverse[None, :]
        cosine = token_order(jnp.cos(angles)[None])[0][None, :, None, :]
        sine = token_order(jnp.sin(angles)[None])[0][None, :, None, :]

        up_b = half(b_fc1, xb, 0)
        qkv_b = half(b_qkv, xb, 1).reshape(-1)
        before = dot(normed_all, up_w, ((1,), (0,))) + up_b
        activated = gelu_tanh(before).astype(BF)
        mixed = dot(normed_all, qkv_w, ((1,), (0,))) + qkv_b
        local = qkv_b.shape[0] // 3
        heads = local // HEAD_DIM

        def split(values):
            return values.reshape(2, seq_len, heads, HEAD_DIM)

        queries = rotate(split(mixed[:, :local]), cosine, sine).astype(BF)
        key_rows = rotate(split(mixed[:, local : 2 * local]), cosine, sine).astype(BF)
        value_rows = split(mixed[:, 2 * local :]).astype(BF)
        scale = 1.0 / math.sqrt(HEAD_DIM)
        allowed = (positions[None, None, :] <= positions[None, :, None]) & (
            segments[:, :, None] == segments[:, None, :]
        )

        def ein(spec, left, right):
            return jnp.einsum(spec, left, right, preferred_element_type=F32)

        scores = ein("sqhd,skhd->shqk", queries, key_rows) * scale
        scores = jnp.where(allowed[:, None], scores, -1e30)
        highest = jnp.max(scores, axis=-1, keepdims=True)
        shifted = jnp.exp(scores - highest)
        attend = shifted / jnp.sum(shifted, axis=-1, keepdims=True)
        attend_b = attend.astype(BF)
        context = ein("shqk,skhd->sqhd", attend_b, value_rows)
        context = context.reshape(2 * seq_len, local).astype(BF)

        branch = dot(context, dense_w, ((1,), (0,))) + dot(activated, down_w, ((1,), (0,)))
        branch = scatter_tokens(branch.astype(BF))
        hidden_out = (hidden + branch + b_dense + b_fc2).astype(BF)

        def collect(grad, axis):
            cur, count, bit = grad.astype(BF), line, 1
            while bit < line:
                own = (z // bit) % 2
                count //= 2

                def pick(which, cur=cur, count=count):
                    size = 2 * block
                    return jnp.concatenate(
                        [
                            lax.dynamic_slice_in_dim(cur, (2 * i + which) * size, size, axis)
                            for i in range(count)
                        ],
                        axis=axis,
                    )

                total = pick(own).astype(F32) + swap_with(pick(1 - own), "z", bit, line).astype(F32)
                bit *= 2
                cur = total.astype(BF) if bit < line else total
            keep = lax.slice_in_dim(cur, 0, block, axis=axis)
            back = swap_x(lax.slice_in_dim(cur, block, 2 * block, axis=axis).astype(BF))
            return keep.astype(F32), back.astype(F32)

        def join(keep, back, axis):
            return jnp.where(
                xb == 0,
                jnp.concatenate([keep, back], axis=axis),
                jnp.concatenate([back, keep], axis=axis),
            )

        down_grad = join(*collect(dot(activated, grad_all, ((0,), (0,))), 1), 0)
        dense_grad = join(*collect(dot(context, grad_all, ((0,), (0,))), 1), 0)

        context_grad = dot(grad_all, dense_w, ((1,), (1,))).astype(BF)
        activated_grad = dot(grad_all, down_w, ((1,), (1,)))
        before_grad = jax.vjp(gelu_tanh, before)[1](activated_grad)[0].astype(BF)
        up_grad = join(*collect(dot(normed_all, before_grad, ((0,), (0,))), 0), 1)

        context_heads = split(context_grad)
        attend_grad = ein("sqhd,skhd->shqk", context_heads, value_rows)
        inner = jnp.sum(attend * attend_grad, axis=-1, keepdims=True)
        score_grad = (attend * (attend_grad - inner)).astype(BF)
        query_grad = ein("shqk,skhd->sqhd", score_grad, key_rows) * scale
        key_grad = ein("shqk,sqhd->skhd", score_grad, queries) * scale
        value_grad = ein("shqk,sqhd->skhd", attend_b, context_heads)
        mixed_grad = jnp.concatenate(
            [
                part.reshape(2 * seq_len, local).astype(BF)
                for part in (
                    rotate(query_grad, cosine, -sine),
                    rotate(key_grad, cosine, -sine),
                    value_grad,
                )
            ],
            axis=1,
        )
        keep, back = collect(dot(normed_all, mixed_grad, ((0,), (0,))), 0)
        qkv_grad = join(
            jnp.stack([keep[:, j * local : (j + 1) * local] for j in range(3)], axis=1),
            jnp.stack([back[:, j * local : (j + 1) * local] for j in range(3)], axis=1),
            2,
        )
        normed_part = dot(mixed_grad, qkv_w, ((1,), (1,))) + dot(before_grad, up_w, ((1,), (1,)))
        normed_grad = scatter_tokens(normed_part.astype(BF))
        hidden_grad, gain_local, shift_local = jax.vjp(layer_norm, hidden, ln_gain, ln_bias)[1](
            normed_grad
        )
        cotangent = out_grad.astype(F32)
        input_grad = cotangent + hidden_grad

        def over_line(values):
            bit = 1
            while bit < line:
                values = values + swap_with(values, "z", bit, line)
                bit *= 2
            return values

        bias = over_line(
            jnp.concatenate(
                [
                    jnp.sum(mixed_grad, axis=0, dtype=F32),
                    jnp.sum(before_grad, axis=0, dtype=F32),
                ]
            )
        )
        bias_back = swap_x(bias)
        qkv_bias_grad = join(
            bias[: 3 * local].reshape(3, local), bias_back[: 3 * local].reshape(3, local), 1
        )
        up_bias_grad = join(bias[3 * local :], bias_back[3 * local :], 0)
        total = jnp.concatenate([gain_local, shift_local, jnp.sum(cotangent, axis=0)])
        total = over_line(total)
        for swap in (swap_x, swap_y, swap_c):
            total = total + swap(total)
        gain_grad, shift_grad, out_bias_grad = (
            total[:width], total[width : 2 * width], total[2 * width :]
        )
        return (
            hidden_out, input_grad, gain_grad, shift_grad, qkv_grad, qkv_bias_grad,
            dense_grad, out_bias_grad, up_grad, up_bias_grad, down_grad, out_bias_grad,
        )

    return body


def solution(mesh):
    line = mesh.shape["fsdp"] // 2
    grid = Mesh(mesh.devices.reshape(line, 2, 2, 2), ("z", "x", "y", "core"))
    rows, cols = ("z", "x"), ("y", "core")
    tokens = rows + cols
    in_specs = (
        P(tokens, None), P(), P(), P(rows, None, cols), P(None, cols), P(cols, rows), P(),
        P(rows, cols), P(cols), P(cols, rows), P(), P(rows, None), P(tokens, None),
    )
    out_specs = (
        P(tokens, None), P(tokens, None), P(), P(), P(rows, None, cols), P(None, cols),
        P(cols, rows), P(), P(rows, cols), P(cols), P(cols, rows), P(),
    )
    return jax.shard_map(
        make_body(line), mesh=grid, in_specs=in_specs, out_specs=out_specs, check_vma=False
    )
```

time: 1540 us -> 591 us (0.38)
  waiting for transfers between devices: 1270 us -> 330 us
  blocking collectives: 76.6 us -> 0 us
  local copies, waits for them, and re-layouts: 15.6 us -> 65.8 us
  matrix products: 124 us -> 75.7 us
  starting transfers between devices: 1.2 us -> 39 us
  other arithmetic: 25 us -> 59.8 us
    reduce_scatter x8 -> x0, waiting for transfers between devices: 855 us -> none  [the longest x1 287 us: body(): lax.psum_scatter(down_grad_local, 'fsdp', scatter_dimension=1, tiled=True)]
    all_gather x6 -> x4, waiting for transfers between devices: 417 us -> 0.01 us  [spread(): return lax.all_gather(both, 'z', axis=axis, tiled=True)]
    ppermute x0 -> x37, waiting for transfers between devices: none -> 330 us  [swap_with(): return lax.ppermute(values, axis, [(i, i ^ mask) for i in range(size)])]
    psum x2 -> x0, blocking collectives: 76.6 us -> none  [the longest x1 41.6 us: body(): lax.psum((gain_local, shift_local, jnp.sum(cotangent, axis=0)), ('fsdp',...]
    dot_general x18 -> x17, matrix products: 124 us -> 70.1 us  [the longest x12 60.1 us: dot(): lax.dot_general(left, right, (dims, ((), ())), preferred_element_type=F32)]
    ppermute x0 -> x37, starting transfers between devices: none -> 38.8 us  [swap_with(): return lax.ppermute(values, axis, [(i, i ^ mask) for i in range(size)])]
    concatenate x1 -> x19, other arithmetic: 1.04 us -> 22.8 us  [the longest x2 7.55 us: gather_tokens(): rows = jnp.concatenate([rows, swap_c(rows)], axis=1)]
    unnamed x86 -> x177, local copies, waits for them, and re-layouts: 9.06 us -> 30.3 us
  transfers between devices with their start and end apart: 14 -> 41, of which waited for: 11 -> 19; matrix products, arithmetic and copies ran while one was open for 9% -> 33% of each run, Pallas kernels for 0% -> 0%
where the time goes in v1:
time: 591 us; the launch traced here: 586 us
  waiting for transfers between devices  330 us (56%)
  matrix products  75.7 us (13%)
  local copies, waits for them, and re-layouts  65.8 us (11%)
  other arithmetic  59.8 us (10%)
  starting transfers between devices  39 us (7%)
  between operations  15.8 us (3%)
    ppermute x37, waiting for transfers between devices, swap_with(): return lax.ppermute(values, axis, [(i, i ^ mask) for i in range(size)])  330 us
    dot_general x12, matrix products, dot(): lax.dot_general(left, right, (dims, ((), ())), preferred_element_type=F32)  60.1 us
    ppermute x37, starting transfers between devices, swap_with(): return lax.ppermute(values, axis, [(i, i ^ mask) for i in range(size)])  38.8 us
    unnamed x177, local copies, waits for them, and re-layouts  30.3 us
  transfers between devices with their start and end apart: 41, of which 19 were waited for; matrix products, arithmetic and copies ran while one was open for 33% of the time, Pallas kernels for 0%

profile of v1, /device:TPU:0, one launch (start us, length us, event | category | flops | bytes accessed | tf_op | source)
XLA Modules:
  0.0 586.3 jit_solution(2982052896533093886)
XLA Ops:
  9.4 2.9 collective-permute-start.3
  15.9 8.5 %collective-permute-done.5 = bf16[256,256]{1,0:T(8,128)(2,1)S(1)} collective-permute-done((bf16[256,256]{1,0:T(8,128)(2,1)S(1)}, bf16[256,256]{1,0:T(8,128)(2,1)S(1)}, u32[]{:S(2)}, u32[]{:S(2)}) %collective-permute-start.5) | collective-permute-done | bytes 131104 | tf_op jit(solution)/shard_map/ppermute | solution.py:36
  37.3 20.6 %collective-permute-done.6 = bf16[256,1024]{1,0:T(8,128)(2,1)S(1)} collective-permute-done((bf16[256,1024]{1,0:T(8,128)(2,1)S(1)}, bf16[256,1024]{1,0:T(8,128)(2,1)S(1)}, u32[]{:S(2)}, u32[]{:S(2)}) %collective-permute-start.6) | collective-permute-done | bytes 524320 | tf_op jit(solution)/shard_map/ppermute | solution.py:36
  69.2 2.2 constant_dynamic-slice_fusion.21
  73.1 6.6 %collective-permute-done = bf16[128,2048]{1,0:T(8,128)(2,1)S(1)} collective-permute-done((bf16[128,2048]{1,0:T(8,128)(2,1)}, bf16[128,2048]{1,0:T(8,128)(2,1)S(1)}, u32[]{:S(2)}, u32[]{:S(2)}) %collective-permute-start) | collective-permute-done | bytes 524320 | tf_op jit(solution)/shard_map/ppermute | solution.py:36
  81.3 12.7 %collective-permute-done.12 = bf16[2,128,2048]{2,1,0:T(8,128)(2,1)S(1)} collective-permute-done((bf16[2,128,2048]{2,1,0:T(8,128)(2,1)}, bf16[2,128,2048]{2,1,0:T(8,128)(2,1)S(1)}, u32[]{:S(2)}, u32[]{:S(2)}) %collective-permute-start.12) | collective-permute-done | bytes 1048608 | tf_op jit(solution)/shard_map/ppermute | solution.py:36
  95.6 17.7 %collective-permute-done.1 = bf16[2,128,2048]{2,1,0:T(8,128)(2,1)S(1)} collective-permute-done((bf16[2,128,2048]{2,1,0:T(8,128)(2,1)S(1)}, bf16[2,128,2048]{2,1,0:T(8,128)(2,1)S(1)}, u32[]{:S(2)}, u32[]{:S(2)}) %collective-permute-start.1) | collective-permute-done | bytes 1048608 | tf_op jit(solution)/shard_map/ppermute | solution.py:36
  117.4 2.3 pad_maximum_fusion.9
  119.7 3.8 pad_maximum_fusion.1
  123.5 3.8 convolution_convert_fusion.4
  129.0 3.8 pad_maximum_fusion
  132.8 6.1 %convolution_add_fusion = f32[1024,768]{1,0:T(8,128)S(1)} fusion(bf16[1024,2048]{1,0:T(8,128)(2,1)} %bitcast.127, bf16[2048,768]{1,0:T(8,128)(2,1)} %all-gather.5.cloned.1.call-done, f32[768]{0:T(1024)S(1)} %add.236), kind=kOutput, calls=%fused_computation.50 | convolution fusion | flops 3222011904 | bytes 10488832 | tf_op jit(solution)/shard_map/dot_general | solution.py:46
  141.9 3.2 fusion.63
  145.7 2.1 reshape.274
  147.8 3.1 fusion.64
  152.5 2.2 slice.959
  158.0 2.6 copy.76
  160.6 2.5 copy.77
  166.6 5.6 fusion.66
  172.2 5.0 fusion.28
  180.0 2.3 multiply_convert_fusion
  193.8 4.2 convolution_convert_fusion.2
  200.5 9.6 %collective-permute-done.28 = bf16[256,1024]{1,0:T(8,128)(2,1)} collective-permute-done((bf16[256,1024]{1,0:T(8,128)(2,1)}, bf16[256,1024]{1,0:T(8,128)(2,1)}, u32[]{:S(2)}, u32[]{:S(2)}) %collective-permute-start.28) | collective-permute-done | bytes 524320 | tf_op jit(solution)/shard_map/ppermute | solution.py:36
  212.3 2.9 collective-permute-start.29
  215.2 66.6 %collective-permute-done.29 = bf16[256,512]{1,0:T(8,128)(2,1)} collective-permute-done((bf16[256,512]{1,0:T(8,128)(2,1)S(1)}, bf16[256,512]{1,0:T(8,128)(2,1)}, u32[]{:S(2)}, u32[]{:S(2)}) %collective-permute-start.29) | collective-permute-done | bytes 262176 | tf_op jit(solution)/shard_map/ppermute | solution.py:36
  285.1 3.1 collective-permute-done.30
  289.1 22.2 %collective-permute-done.22 = bf16[1024,768]{1,0:T(8,128)(2,1)} collective-permute-done((bf16[1024,768]{1,0:T(8,128)(2,1)}, bf16[1024,768]{1,0:T(8,128)(2,1)}, u32[]{:S(2)}, u32[]{:S(2)}) %collective-permute-start.22) | collective-permute-done | bytes 1572896 | tf_op jit(solution)/shard_map/ppermute | solution.py:36
  314.0 7.7 %fusion.67 = f32[1024,1024]{1,0:T(8,128)S(1)} fusion(bf16[1024,2048]{1,0:T(8,128)(2,1)} %bitcast.128, bf16[2048,1024]{1,0:T(8,128)(2,1)} %all-gather.9.cloned.1.call-done), kind=kOutput, calls=%fused_computation.307 | convolution fusion | flops 4294967296 | bytes 12582912 | tf_op jit(solution)/shard_map/dot_general | solution.py:46
  321.6 5.4 convolution_convert_fusion
  330.8 2.5 collective-permute-start.34
  333.3 11.7 %convert_reduce_fusion = (f32[1024]{0:T(1024)S(1)}, bf16[1024,1024]{1,0:T(8,128)(2,1)S(1)}) fusion(f32[1024,1024]{1,0:T(8,128)} %copy-done.52, f32[1024]{0:T(1024)S(1)} %dynamic_slice.109, bf16[1024,2048]{1,0:T(8,128)(2,1)} %bitcast.124, bf16[1024,2048]{1,0:T(8,128)(2,1)} %all-gather.11.cloned.1.call-done), kind=kOutput, calls=%fused_computation.21 | convolution fusion | flops 4319083520 | bytes 14688256 | tf_op jit(solution)/shard_map/dot_general | solution.py:46
  345.1 5.1 convolution_convert_fusion.1
  355.6 5.0 fusion.60
  363.4 30.8 %collective-permute-done.25 = f32[1792]{0:T(1024)S(1)} collective-permute-done((f32[1792]{0:T(1024)S(1)}, f32[1792]{0:T(1024)S(1)}, u32[]{:S(2)}, u32[]{:S(2)}) %collective-permute-start.25) | collective-permute-done | bytes 7200 | tf_op jit(solution)/shard_map/ppermute | solution.py:36
  396.1 4.6 fusion.68
  400.7 22.9 %collective-permute-done.26 = f32[1792]{0:T(1024)S(1)} collective-permute-done((f32[1792]{0:T(1024)S(1)}, f32[1792]{0:T(1024)S(1)}, u32[]{:S(2)}, u32[]{:S(2)}) %collective-permute-start.26) | collective-permute-done | bytes 7200 | tf_op jit(solution)/shard_map/ppermute | solution.py:36
  425.5 4.0 add_convert_fusion
  436.0 10.1 %collective-permute-done.24 = bf16[256,768]{1,0:T(8,128)(2,1)S(1)} collective-permute-done((bf16[256,768]{1,0:T(8,128)(2,1)S(1)}, bf16[256,768]{1,0:T(8,128)(2,1)S(1)}, u32[]{:S(2)}, u32[]{:S(2)}) %collective-permute-start.24) | collective-permute-done | bytes 393248 | tf_op jit(solution)/shard_map/ppermute | solution.py:36
  446.2 3.2 add_convert_fusion.2
  449.6 3.4 collective-permute-start.35
  453.0 2.5 add_convert_fusion.5
  457.2 2.8 add_convert_fusion.3
  460.3 2.5 add_convert_fusion.4
  463.5 58.4 %collective-permute-done.35 = bf16[1024,512]{1,0:T(8,128)(2,1)S(1)} collective-permute-done((bf16[1024,512]{1,0:T(8,128)(2,1)S(1)}, bf16[1024,512]{1,0:T(8,128)(2,1)S(1)}, u32[]{:S(2)}, u32[]{:S(2)}) %collective-permute-start.35) | collective-permute-done | bytes 1048608 | tf_op jit(solution)/shard_map/ppermute | solution.py:36
  526.1 22.4 %collective-permute-done.10 = bf16[128,2048]{1,0:T(8,128)(2,1)S(1)} collective-permute-done((bf16[128,2048]{1,0:T(8,128)(2,1)S(1)}, bf16[128,2048]{1,0:T(8,128)(2,1)S(1)}, u32[]{:S(2)}, u32[]{:S(2)}) %collective-permute-start.10) | collective-permute-done | bytes 524320 | tf_op jit(solution)/shard_map/ppermute | solution.py:36
  548.8 8.1 %collective-permute-done.16 = bf16[128,2048]{1,0:T(8,128)(2,1)S(1)} collective-permute-done((bf16[128,2048]{1,0:T(8,128)(2,1)S(1)}, bf16[128,2048]{1,0:T(8,128)(2,1)S(1)}, u32[]{:S(2)}, u32[]{:S(2)}) %collective-permute-start.16) | collective-permute-done | bytes 524320 | tf_op jit(solution)/shard_map/ppermute | solution.py:36
  561.4 2.8 collective-permute-done.17
  564.5 4.4 collective-permute-done.18
  (380 shorter events, 121.8 us)
Async XLA Ops:
  7.2 108.8 %copy-start = (f32[3,512]{1,0:T(4,128)S(1)}, f32[3,512]{1,0:T(4,128)}, u32[]{:S(2)}) copy-start(f32[3,512]{1,0:T(4,128)} %param.17) | copy-start | bytes 18436
  7.2 116.3 %all-gather.7.cloned.1.call-start = ((), (), s32[]{:S(2)}) async-start(), calls=%async_computation.1 | async-start | bytes 1310720 | tf_op jit(solution)/shard_map/all_gather | solution.py:77
  9.4 16.9 %collective-permute-start.3 = (bf16[256,768]{1,0:T(8,128)(2,1)}, bf16[256,768]{1,0:T(8,128)(2,1)}, u32[]{:S(2)}, u32[]{:S(2)}) collective-permute-start(bf16[256,768]{1,0:T(8,128)(2,1)} %pad_maximum_fusion.17), channel_id=1, source_target_pairs={{0,4},{4,0},{1,5},{5,1},{2,6},{6,2},{3,7},{7,3},{8,12},{12,8},{9,1... | collective-permute-start | bytes 1179656 | tf_op jit(solution)/shard_map/ppermute | solution.py:36
  13.3 11.1 %collective-permute-start.5 = (bf16[256,256]{1,0:T(8,128)(2,1)S(1)}, bf16[256,256]{1,0:T(8,128)(2,1)S(1)}, u32[]{:S(2)}, u32[]{:S(2)}) collective-permute-start(bf16[256,256]{1,0:T(8,128)(2,1)S(1)} %get-tuple-element.71), channel_id=1, source_target_pairs={{0,4},{4,0},{1,5},{5,1},{2,6},{6,2},{3,7},{7,3},{8,12},{12,8},{9,1... | collective-permute-start | bytes 393224 | tf_op jit(solution)/shard_map/ppermute | solution.py:36
  25.2 107.6 %all-gather.5.cloned.1.call-start = ((), (), s32[]{:S(2)}) async-start(), calls=%async_computation | async-start | bytes 3932160 | tf_op jit(solution)/shard_map/all_gather | solution.py:77
  28.2 285.8 %all-gather.9.cloned.1.call-start = ((), (), s32[]{:S(2)}) async-start(), calls=%async_computation.2 | async-start | bytes 5242880 | tf_op jit(solution)/shard_map/all_gather | solution.py:77
  33.3 33.3 %collective-permute-start.11 = (bf16[128,2048]{1,0:T(8,128)(2,1)}, bf16[128,2048]{1,0:T(8,128)(2,1)S(1)}, u32[]{:S(2)}, u32[]{:S(2)}) collective-permute-start(bf16[128,2048]{1,0:T(8,128)(2,1)} %constant_dynamic-update-slice_fusion.40), channel_id=1, source_target_pairs={{0,4},{4,0},{1,5},{5,1},{2,6},{6,2},{3,7},{7,3},{8,12},{12,8},{9,1... | collective-permute-start | bytes 1572872 | tf_op jit(solution)/shard_map/ppermute | solution.py:36
  35.2 22.7 %collective-permute-start.6 = (bf16[256,1024]{1,0:T(8,128)(2,1)S(1)}, bf16[256,1024]{1,0:T(8,128)(2,1)S(1)}, u32[]{:S(2)}, u32[]{:S(2)}) collective-permute-start(bf16[256,1024]{1,0:T(8,128)(2,1)S(1)} %get-tuple-element.51), channel_id=1, source_target_pairs={{0,4},{4,0},{1,5},{5,1},{2,6},{6,2},{3,7},{7,3},{8,12},{12,8},{9,1... | collective-permute-start | bytes 1572872 | tf_op jit(solution)/shard_map/ppermute | solution.py:36
  36.0 31.7 %copy-start.41 = (f32[128]{0:T(128)}, f32[128]{0:T(128)S(1)}, u32[]{:S(2)}) copy-start(f32[128]{0:T(128)S(1)} %fusion.53) | copy-start | bytes 1540
  59.0 274.3 %all-gather.11.cloned.1.call-start = ((), (), s32[]{:S(2)}) async-start(), calls=%async_computation.3 | async-start | bytes 5242880 | tf_op jit(solution)/shard_map/all_gather | solution.py:77
  64.6 15.1 %collective-permute-start = (bf16[128,2048]{1,0:T(8,128)(2,1)}, bf16[128,2048]{1,0:T(8,128)(2,1)S(1)}, u32[]{:S(2)}, u32[]{:S(2)}) collective-permute-start(bf16[128,2048]{1,0:T(8,128)(2,1)} %constant_dynamic-update-slice_fusion.8), channel_id=1, source_target_pairs={{0,4},{4,0},{1,5},{5,1},{2,6},{6,2},{3,7},{7,3},{8,12},{12,8},{9,1... | collective-permute-start | bytes 1572872 | tf_op jit(solution)/shard_map/ppermute | solution.py:36
  66.1 50.0 %collective-permute-start.4 = (s32[1,512]{1,0:T(1,128)S(1)}, s32[1,512]{1,0:T(1,128)S(1)}, u32[]{:S(2)}, u32[]{:S(2)}) collective-permute-start(s32[1,512]{1,0:T(1,128)S(1)} %copy-done.45), channel_id=1, source_target_pairs={{0,4},{4,0},{1,5},{5,1},{2,6},{6,2},{3,7},{7,3},{8,12},{12,8},{9,1... | collective-permute-start | bytes 6152 | tf_op jit(solution)/shard_map/ppermute | solution.py:36
  67.7 26.3 %collective-permute-start.12 = (bf16[2,128,2048]{2,1,0:T(8,128)(2,1)}, bf16[2,128,2048]{2,1,0:T(8,128)(2,1)S(1)}, u32[]{:S(2)}, u32[]{:S(2)}) collective-permute-start(bf16[2,128,2048]{2,1,0:T(8,128)(2,1)} %pad_maximum_fusion.10), channel_id=1, source_target_pairs={{0,2},{2,0},{1,3},{3,1},{4,6},{6,4},{5,7},{7,5},{8,10},{10,8},{9,1... | collective-permute-start | bytes 3145736 | tf_op jit(solution)/shard_map/ppermute | solution.py:36
  71.4 46.0 %collective-permute-start.7 = (bf16[1024,256]{1,0:T(8,128)(2,1)}, bf16[1024,256]{1,0:T(8,128)(2,1)}, u32[]{:S(2)}, u32[]{:S(2)}) collective-permute-start(bf16[1024,256]{1,0:T(8,128)(2,1)} %get-tuple-element.53), channel_id=1, source_target_pairs={{0,4},{4,0},{1,5},{5,1},{2,6},{6,2},{3,7},{7,3},{8,12},{12,8},{9,1... | collective-permute-start | bytes 1572872 | tf_op jit(solution)/shard_map/ppermute | solution.py:36
  79.8 33.5 %collective-permute-start.1 = (bf16[2,128,2048]{2,1,0:T(8,128)(2,1)S(1)}, bf16[2,128,2048]{2,1,0:T(8,128)(2,1)S(1)}, u32[]{:S(2)}, u32[]{:S(2)}) collective-permute-start(bf16[2,128,2048]{2,1,0:T(8,128)(2,1)S(1)} %pad_maximum_fusion.7), channel_id=1, source_target_pairs={{0,2},{2,0},{1,3},{3,1},{4,6},{6,4},{5,7},{7,5},{8,10},{10,8},{9,1... | collective-permute-start | bytes 3145736 | tf_op jit(solution)/shard_map/ppermute | solution.py:36
  95.5 24.2 %collective-permute-start.13 = (bf16[2,256,2048]{2,1,0:T(8,128)(2,1)}, bf16[2,256,2048]{2,1,0:T(8,128)(2,1)}, u32[]{:S(2)}, u32[]{:S(2)}) collective-permute-start(bf16[2,256,2048]{2,1,0:T(8,128)(2,1)} %pad_maximum_fusion.3), channel_id=1, source_target_pairs={{0,1},{1,0},{2,3},{3,2},{4,5},{5,4},{6,7},{7,6},{8,9},{9,8},{10,11... | collective-permute-start | bytes 6291464 | tf_op jit(solution)/shard_map/ppermute | solution.py:36
  115.8 13.2 %collective-permute-start.2 = (bf16[2,256,2048]{2,1,0:T(8,128)(2,1)}, bf16[2,256,2048]{2,1,0:T(8,128)(2,1)}, u32[]{:S(2)}, u32[]{:S(2)}) collective-permute-start(bf16[2,256,2048]{2,1,0:T(8,128)(2,1)} %pad_maximum_fusion.2), channel_id=1, source_target_pairs={{0,1},{1,0},{2,3},{3,2},{4,5},{5,4},{6,7},{7,6},{8,9},{9,8},{10,11... | collective-permute-start | bytes 6291464 | tf_op jit(solution)/shard_map/ppermute | solution.py:36
  192.6 17.5 %collective-permute-start.28 = (bf16[256,1024]{1,0:T(8,128)(2,1)}, bf16[256,1024]{1,0:T(8,128)(2,1)}, u32[]{:S(2)}, u32[]{:S(2)}) collective-permute-start(bf16[256,1024]{1,0:T(8,128)(2,1)} %pad_maximum_fusion.16), channel_id=1, source_target_pairs={{0,8},{8,0},{16,24},{24,16},{1,9},{9,1},{17,25},{25,17},{2,10},{10... | collective-permute-start | bytes 1572872 | tf_op jit(solution)/shard_map/ppermute | solution.py:36
  193.8 91.0 %copy-start.22 = (bf16[1024,768]{0,1:T(8,128)(2,1)}, bf16[1024,768]{0,1:T(8,128)(2,1)S(1)}, u32[]{:S(2)}) copy-start(bf16[1024,768]{0,1:T(8,128)(2,1)S(1)} %constant_dynamic-update-slice_fusion.48) | copy-start | bytes 4718596
  199.5 111.7 %collective-permute-start.22 = (bf16[1024,768]{1,0:T(8,128)(2,1)}, bf16[1024,768]{1,0:T(8,128)(2,1)}, u32[]{:S(2)}, u32[]{:S(2)}) collective-permute-start(bf16[1024,768]{1,0:T(8,128)(2,1)} %pad_maximum_fusion.6), channel_id=1, source_target_pairs={{0,8},{8,0},{16,24},{24,16},{1,9},{9,1},{17,25},{25,17},{2,10},{10... | collective-permute-start | bytes 4718600 | tf_op jit(solution)/shard_map/ppermute | solution.py:36
  212.3 69.5 %collective-permute-start.29 = (bf16[256,512]{1,0:T(8,128)(2,1)S(1)}, bf16[256,512]{1,0:T(8,128)(2,1)}, u32[]{:S(2)}, u32[]{:S(2)}) collective-permute-start(bf16[256,512]{1,0:T(8,128)(2,1)S(1)} %constant_dynamic-slice_fusion.10), channel_id=1, source_target_pairs={{0,16},{8,24},{16,0},{24,8},{1,17},{9,25},{17,1},{25,9},{2,18},{10... | collective-permute-start | bytes 786440 | tf_op jit(solution)/shard_map/ppermute | solution.py:36
  283.0 5.2 collective-permute-start.30
  313.2 119.9 %collective-permute-start.23 = (bf16[512,768]{1,0:T(8,128)(2,1)S(1)}, bf16[512,768]{1,0:T(8,128)(2,1)}, u32[]{:S(2)}, u32[]{:S(2)}) collective-permute-start(bf16[512,768]{1,0:T(8,128)(2,1)S(1)} %constant_dynamic-slice_fusion.15), channel_id=1, source_target_pairs={{0,16},{8,24},{16,0},{24,8},{1,17},{9,25},{17,1},{25,9},{2,18},{10... | collective-permute-start | bytes 2359304 | tf_op jit(solution)/shard_map/ppermute | solution.py:36
  330.8 115.4 %collective-permute-start.34 = (bf16[1024,1024]{1,0:T(8,128)(2,1)}, bf16[1024,1024]{1,0:T(8,128)(2,1)}, u32[]{:S(2)}, u32[]{:S(2)}) collective-permute-start(bf16[1024,1024]{1,0:T(8,128)(2,1)} %pad_maximum_fusion.5), channel_id=1, source_target_pairs={{0,8},{8,0},{16,24},{24,16},{1,9},{9,1},{17,25},{25,17},{2,10},{10... | collective-permute-start | bytes 6291464 | tf_op jit(solution)/shard_map/ppermute | solution.py:36
  345.0 49.2 %collective-permute-start.25 = (f32[1792]{0:T(1024)S(1)}, f32[1792]{0:T(1024)S(1)}, u32[]{:S(2)}, u32[]{:S(2)}) collective-permute-start(f32[1792]{0:T(1024)S(1)} %pad_maximum_fusion.20), channel_id=1, source_target_pairs={{0,8},{8,0},{16,24},{24,16},{1,9},{9,1},{17,25},{25,17},{2,10},{10... | collective-permute-start | bytes 21512 | tf_op jit(solution)/shard_map/ppermute | solution.py:36
  353.6 103.5 %collective-permute-start.31 = (bf16[1024,1024]{1,0:T(8,128)(2,1)}, bf16[1024,1024]{1,0:T(8,128)(2,1)}, u32[]{:S(2)}, u32[]{:S(2)}) collective-permute-start(bf16[1024,1024]{1,0:T(8,128)(2,1)} %pad_maximum_fusion.4), channel_id=1, source_target_pairs={{0,8},{8,0},{16,24},{24,16},{1,9},{9,1},{17,25},{25,17},{2,10},{10... | collective-permute-start | bytes 6291464 | tf_op jit(solution)/shard_map/ppermute | solution.py:36
  361.9 38.8 %copy-start.4 = (bf16[1024,2048]{1,0:T(8,128)(2,1)}, bf16[1024,2048]{1,0:T(8,128)(2,1)S(1)}, u32[]{:S(2)}) copy-start(bf16[1024,2048]{1,0:T(8,128)(2,1)S(1)} %add_convert_fusion.1) | copy-start | bytes 12582916
  361.9 34.1 %copy-start.49 = (bf16[2048,1024]{1,0:T(8,128)(2,1)S(1)}, bf16[2048,1024]{1,0:T(8,128)(2,1)}, u32[]{:S(2)}) copy-start(bf16[2048,1024]{1,0:T(8,128)(2,1)} %all-gather.9.cloned.1.call-done) | copy-start | bytes 12582916
  363.4 89.6 %collective-permute-start.8 = (bf16[2,256,2048]{2,1,0:T(8,128)(2,1)}, bf16[2,256,2048]{2,1,0:T(8,128)(2,1)}, u32[]{:S(2)}, u32[]{:S(2)}) collective-permute-start(bf16[2,256,2048]{2,1,0:T(8,128)(2,1)} %slice.633), channel_id=1, source_target_pairs={{0,1},{1,0},{2,3},{3,2},{4,5},{5,4},{6,7},{7,6},{8,9},{9,8},{10,11... | collective-permute-start | bytes 6291464 | tf_op jit(solution)/shard_map/ppermute | solution.py:36
  394.2 29.4 %collective-permute-start.26 = (f32[1792]{0:T(1024)S(1)}, f32[1792]{0:T(1024)S(1)}, u32[]{:S(2)}, u32[]{:S(2)}) collective-permute-start(f32[1792]{0:T(1024)S(1)} %fusion.56), channel_id=1, source_target_pairs={{0,16},{8,24},{16,0},{24,8},{1,17},{9,25},{17,1},{25,9},{2,18},{10... | collective-permute-start | bytes 21512 | tf_op jit(solution)/shard_map/ppermute | solution.py:36
  423.6 9.5 %collective-permute-start.27 = (f32[1792]{0:T(1024)S(1)}, f32[1792]{0:T(1024)S(1)}, u32[]{:S(2)}, u32[]{:S(2)}) collective-permute-start(f32[1792]{0:T(1024)S(1)} %add.281), channel_id=1, source_target_pairs={{0,4},{4,0},{1,5},{5,1},{2,6},{6,2},{3,7},{7,3},{8,12},{12,8},{9,1... | collective-permute-start | bytes 21512 | tf_op jit(solution)/shard_map/ppermute | solution.py:36
  433.1 27.2 %collective-permute-start.14 = (bf16[2,256,2048]{2,1,0:T(8,128)(2,1)}, bf16[2,256,2048]{2,1,0:T(8,128)(2,1)}, u32[]{:S(2)}, u32[]{:S(2)}) collective-permute-start(bf16[2,256,2048]{2,1,0:T(8,128)(2,1)} %slice.669), channel_id=1, source_target_pairs={{0,1},{1,0},{2,3},{3,2},{4,5},{5,4},{6,7},{7,6},{8,9},{9,8},{10,11... | collective-permute-start | bytes 6291464 | tf_op jit(solution)/shard_map/ppermute | solution.py:36
  434.6 11.6 %collective-permute-start.24 = (bf16[256,768]{1,0:T(8,128)(2,1)S(1)}, bf16[256,768]{1,0:T(8,128)(2,1)S(1)}, u32[]{:S(2)}, u32[]{:S(2)}) collective-permute-start(bf16[256,768]{1,0:T(8,128)(2,1)S(1)} %slice.960), channel_id=1, source_target_pairs={{0,4},{4,0},{1,5},{5,1},{2,6},{6,2},{3,7},{7,3},{8,12},{12,8},{9,1... | collective-permute-start | bytes 1179656 | tf_op jit(solution)/shard_map/ppermute | solution.py:36
  449.6 72.4 %collective-permute-start.35 = (bf16[1024,512]{1,0:T(8,128)(2,1)S(1)}, bf16[1024,512]{1,0:T(8,128)(2,1)S(1)}, u32[]{:S(2)}, u32[]{:S(2)}) collective-permute-start(bf16[1024,512]{1,0:T(8,128)(2,1)S(1)} %constant_dynamic-slice_fusion), channel_id=1, source_target_pairs={{0,16},{8,24},{16,0},{24,8},{1,17},{9,25},{17,1},{25,9},{2,18},{10... | collective-permute-start | bytes 3145736 | tf_op jit(solution)/shard_map/ppermute | solution.py:36
  455.6 67.1 %collective-permute-start.9 = (bf16[2,128,2048]{2,1,0:T(8,128)(2,1)S(1)}, bf16[2,128,2048]{2,1,0:T(8,128)(2,1)S(1)}, u32[]{:S(2)}, u32[]{:S(2)}) collective-permute-start(bf16[2,128,2048]{2,1,0:T(8,128)(2,1)S(1)} %slice.635), channel_id=1, source_target_pairs={{0,2},{2,0},{1,3},{3,1},{4,6},{6,4},{5,7},{7,5},{8,10},{10,8},{9,1... | collective-permute-start | bytes 3145736 | tf_op jit(solution)/shard_map/ppermute | solution.py:36
  460.1 100.1 %collective-permute-start.32 = (bf16[512,1024]{1,0:T(8,128)(2,1)S(1)}, bf16[512,1024]{1,0:T(8,128)(2,1)S(1)}, u32[]{:S(2)}, u32[]{:S(2)}) collective-permute-start(bf16[512,1024]{1,0:T(8,128)(2,1)S(1)} %constant_dynamic-slice_fusion.5), channel_id=1, source_target_pairs={{0,16},{8,24},{16,0},{24,8},{1,17},{9,25},{17,1},{25,9},{2,18},{10... | collective-permute-start | bytes 3145736 | tf_op jit(solution)/shard_map/ppermute | solution.py:36
  462.9 62.3 %collective-permute-start.15 = (bf16[2,128,2048]{2,1,0:T(8,128)(2,1)S(1)}, bf16[2,128,2048]{2,1,0:T(8,128)(2,1)S(1)}, u32[]{:S(2)}, u32[]{:S(2)}) collective-permute-start(bf16[2,128,2048]{2,1,0:T(8,128)(2,1)S(1)} %slice.671), channel_id=1, source_target_pairs={{0,2},{2,0},{1,3},{3,1},{4,6},{6,4},{5,7},{7,5},{8,10},{10,8},{9,1... | collective-permute-start | bytes 3145736 | tf_op jit(solution)/shard_map/ppermute | solution.py:36
  522.3 48.5 %copy-start.8 = (f32[1024,512]{1,0:T(8,128)}, f32[1024,512]{1,0:T(8,128)S(1)}, u32[]{:S(2)}) copy-start(f32[1024,512]{1,0:T(8,128)S(1)} %convert_add_fusion) | copy-start | bytes 6291460
  522.4 48.4 %collective-permute-start.36 = (bf16[1024,256]{1,0:T(8,128)(2,1)S(1)}, bf16[1024,256]{1,0:T(8,128)(2,1)S(1)}, u32[]{:S(2)}, u32[]{:S(2)}) collective-permute-start(bf16[1024,256]{1,0:T(8,128)(2,1)S(1)} %slice.957), channel_id=1, source_target_pairs={{0,4},{4,0},{1,5},{5,1},{2,6},{6,2},{3,7},{7,3},{8,12},{12,8},{9,1... | collective-permute-start | bytes 1572872 | tf_op jit(solution)/shard_map/ppermute | solution.py:36
  523.3 25.2 %collective-permute-start.10 = (bf16[128,2048]{1,0:T(8,128)(2,1)S(1)}, bf16[128,2048]{1,0:T(8,128)(2,1)S(1)}, u32[]{:S(2)}, u32[]{:S(2)}) collective-permute-start(bf16[128,2048]{1,0:T(8,128)(2,1)S(1)} %constant_dynamic-update-slice_fusion.16), channel_id=1, source_target_pairs={{0,4},{4,0},{1,5},{5,1},{2,6},{6,2},{3,7},{7,3},{8,12},{12,8},{9,1... | collective-permute-start | bytes 1572872 | tf_op jit(solution)/shard_map/ppermute | solution.py:36
  525.8 31.4 %copy-start.3 = (bf16[128,2048]{1,0:T(8,128)(2,1)S(1)}, bf16[128,2048]{1,0:T(8,128)(2,1)}, u32[]{:S(2)}) copy-start(bf16[128,2048]{1,0:T(8,128)(2,1)} %param.13) | copy-start | bytes 1572868
  525.8 31.1 %collective-permute-start.16 = (bf16[128,2048]{1,0:T(8,128)(2,1)S(1)}, bf16[128,2048]{1,0:T(8,128)(2,1)S(1)}, u32[]{:S(2)}, u32[]{:S(2)}) collective-permute-start(bf16[128,2048]{1,0:T(8,128)(2,1)S(1)} %constant_dynamic-update-slice_fusion.51), channel_id=1, source_target_pairs={{0,4},{4,0},{1,5},{5,1},{2,6},{6,2},{3,7},{7,3},{8,12},{12,8},{9,1... | collective-permute-start | bytes 1572872 | tf_op jit(solution)/shard_map/ppermute | solution.py:36
  560.2 4.0 collective-permute-start.17
  560.7 15.2 %collective-permute-start.33 = (bf16[256,1024]{1,0:T(8,128)(2,1)S(1)}, bf16[256,1024]{1,0:T(8,128)(2,1)S(1)}, u32[]{:S(2)}, u32[]{:S(2)}) collective-permute-start(bf16[256,1024]{1,0:T(8,128)(2,1)S(1)} %slice.958), channel_id=1, source_target_pairs={{0,4},{4,0},{1,5},{5,1},{2,6},{6,2},{3,7},{7,3},{8,12},{12,8},{9,1... | collective-permute-start | bytes 1572872 | tf_op jit(solution)/shard_map/ppermute | solution.py:36
  564.2 4.7 collective-permute-start.18
  568.9 3.8 collective-permute-start.19
  572.8 3.9 collective-permute-start.20
  576.7 1.6 collective-permute-start.21
  (49 other events, 491.2 us)
Sparse Core Ops, SparseCore 0:
  25.3 29.4 all-gather.6
  56.9 62.9 all-gather.4
  121.5 79.4 all-gather.8
  202.4 115.4 all-gather.10

commit v2 on v1

v2 whole, which is shorter than its diff:
```python
import math

import jax
import jax.numpy as jnp
from jax import lax
from jax.experimental import pallas as pl
from jax.experimental.pallas import tpu as pltpu
from jax.sharding import Mesh
from jax.sharding import PartitionSpec as P

HEAD_DIM = 64
ROT = 32
EPS = 1e-05
BLOCK = 128
REACH = 256
SCALE = 1.0 / math.sqrt(HEAD_DIM)

BF = jnp.bfloat16
F32 = jnp.float32


def layer_norm(values, norm_gain, norm_shift):
    centred = values - jnp.mean(values, axis=-1, keepdims=True)
    variance = jnp.mean(centred * centred, axis=-1, keepdims=True)
    return centred * lax.rsqrt(variance + EPS) * norm_gain + norm_shift


def gelu_tanh(values):
    return jax.nn.gelu(values, approximate=True)


def rotary_tables(length, lanes):
    lane = jnp.arange(lanes) % HEAD_DIM
    pair = lane % (ROT // 2)
    angles = jnp.arange(length).astype(F32)[:, None] * (
        10000.0 ** (-(2.0 * pair.astype(F32)) / ROT)
    )
    cosine = jnp.where(lane < ROT, jnp.cos(angles), 1.0)
    sine = jnp.sin(angles)
    first = jnp.where(lane < ROT // 2, -sine, 0.0)
    second = jnp.where((lane >= ROT // 2) & (lane < ROT), sine, 0.0)
    return cosine, first, second


def turn(values, cosine, first, second):
    half, lanes = ROT // 2, values.shape[1]
    return (
        values * cosine
        + pltpu.roll(values, lanes - half, 1) * first
        + pltpu.roll(values, half, 1) * second
    )


def nt(left, right):
    return lax.dot_general(left, right, (((1,), (1,)), ((), ())), preferred_element_type=F32)


def tn(left, right):
    return lax.dot_general(left, right, (((0,), (0,)), ((), ())), preferred_element_type=F32)


def windows(length):
    for start in range(0, length, BLOCK):
        low = max(0, (start - REACH + 1) // BLOCK * BLOCK)
        yield start, low, start + BLOCK


def allowed_mask(row_ref, col_ref, start, low, high):
    size = high - low
    key = low + lax.broadcasted_iota(jnp.int32, (size, BLOCK), 0)
    query = start + lax.broadcasted_iota(jnp.int32, (size, BLOCK), 1)
    same = col_ref[low:high, :] == row_ref[0, :, start : start + BLOCK]
    return same & (key <= query)


def head_lanes(rows, head, lanes):
    lane = lax.broadcasted_iota(jnp.int32, (rows, lanes), 1)
    return lane // HEAD_DIM == head


def attend_kernel(mixed_ref, cos_ref, a_ref, b_ref, row_ref, col_ref, qkv_ref, out_ref, lse_ref):
    length, lanes = out_ref.shape
    tables = cos_ref[...], a_ref[...], b_ref[...]
    query = turn(mixed_ref[:, :lanes], *tables).astype(BF)
    query = (query.astype(F32) * SCALE).astype(BF)
    key = turn(mixed_ref[:, lanes : 2 * lanes], *tables).astype(BF)
    value = mixed_ref[:, 2 * lanes :].astype(BF)
    qkv_ref[:, :lanes] = query
    qkv_ref[:, lanes : 2 * lanes] = key
    qkv_ref[:, 2 * lanes :] = value
    for start, low, high in windows(length):
        mask = allowed_mask(row_ref, col_ref, start, low, high)
        mine = query[start:high]
        out = jnp.zeros((BLOCK, lanes), F32)
        for head in range(lanes // HEAD_DIM):
            own = head_lanes(BLOCK, head, lanes)
            scores = nt(key[low:high], jnp.where(own, mine, jnp.zeros_like(mine)))
            scores = jnp.where(mask, scores, -1e30)
            highest = jnp.max(scores, axis=0, keepdims=True)
            shifted = jnp.exp(scores - highest)
            total = jnp.sum(shifted, axis=0, keepdims=True)
            attend = (shifted / total).astype(BF)
            out = jnp.where(own, tn(attend, value[low:high]), out)
            lse_ref[0, head : head + 1, start:high] = highest + jnp.log(total)
        out_ref[start:high, :] = out.astype(BF)


def attend_grad_kernel(
    qkv_ref, grad_ref, lse_ref, cos_ref, a_ref, b_ref, row_ref, col_ref, out_ref, key_ref, value_ref
):
    length, lanes = grad_ref.shape
    key_ref[...] = jnp.zeros_like(key_ref)
    value_ref[...] = jnp.zeros_like(value_ref)
    for start, low, high in windows(length):
        mask = allowed_mask(row_ref, col_ref, start, low, high)
        query = qkv_ref[start:high, :lanes]
        key = qkv_ref[low:high, lanes : 2 * lanes]
        value = qkv_ref[low:high, 2 * lanes :]
        grad = grad_ref[start:high, :]
        query_grad = jnp.zeros((BLOCK, lanes), F32)
        key_grad = jnp.zeros((high - low, lanes), F32)
        value_grad = jnp.zeros((high - low, lanes), F32)
        for head in range(lanes // HEAD_DIM):
            own = head_lanes(BLOCK, head, lanes)
            own_keys = head_lanes(high - low, head, lanes)
            none = jnp.zeros_like(query)
            scores = nt(key, jnp.where(own, query, none))
            scores = jnp.where(mask, scores, -1e30)
            attend = jnp.exp(scores - lse_ref[0, head : head + 1, start:high])
            attend_grad = nt(value, jnp.where(own, grad, none))
            inner = jnp.sum(attend * attend_grad, axis=0, keepdims=True)
            score_grad = (attend * (attend_grad - inner)).astype(BF)
            query_grad = jnp.where(own, tn(score_grad, key), query_grad)
            key_grad = jnp.where(
                own_keys, jnp.dot(score_grad, query, preferred_element_type=F32), key_grad
            )
            value_grad = jnp.where(
                own_keys,
                jnp.dot(attend.astype(BF), grad, preferred_element_type=F32),
                value_grad,
            )
        back = [ref[start:high, :] for ref in (cos_ref, a_ref, b_ref)]
        query_grad = turn(query_grad * SCALE, back[0], -back[1], -back[2])
        out_ref[start:high, :lanes] = query_grad.astype(BF)
        key_ref[low:high, :] += key_grad
        value_ref[low:high, :] += value_grad
    key_grad = turn(key_ref[...], cos_ref[...], -a_ref[...], -b_ref[...])
    out_ref[:, lanes : 2 * lanes] = key_grad.astype(BF)
    out_ref[:, 2 * lanes :] = value_ref[...].astype(BF)


def attention_specs(length, lanes):
    table = pl.BlockSpec((length, lanes), lambda s: (0, 0))
    return dict(
        table=table,
        wide=pl.BlockSpec((length, 3 * lanes), lambda s: (s, 0)),
        slim=pl.BlockSpec((length, lanes), lambda s: (s, 0)),
        lse=pl.BlockSpec((1, lanes // HEAD_DIM, length), lambda s: (s, 0, 0)),
        row=pl.BlockSpec((1, 1, length), lambda s: (s, 0, 0)),
        col=pl.BlockSpec((length, 1), lambda s: (s, 0)),
    )


def attention(mixed, tables, segments):
    sequences, length = segments.shape
    lanes = mixed.shape[1] // 3
    spec = attention_specs(length, lanes)
    rows = sequences * length
    return pl.pallas_call(
        attend_kernel,
        grid=(sequences,),
        in_specs=[spec["wide"]] + [spec["table"]] * 3 + [spec["row"], spec["col"]],
        out_specs=[spec["wide"], spec["slim"], spec["lse"]],
        out_shape=[
            jax.ShapeDtypeStruct((rows, 3 * lanes), BF),
            jax.ShapeDtypeStruct((rows, lanes), BF),
            jax.ShapeDtypeStruct((sequences, lanes // HEAD_DIM, length), F32),
        ],
        compiler_params=pltpu.CompilerParams(vmem_limit_bytes=32 << 20),
        name="attend",
    )(mixed, *tables, segments[:, None, :], segments.reshape(-1, 1))


def attention_grad(qkv, grad, lse, tables, segments):
    sequences, length = segments.shape
    rows, lanes = grad.shape
    spec = attention_specs(length, lanes)
    return pl.pallas_call(
        attend_grad_kernel,
        grid=(sequences,),
        in_specs=[spec["wide"], spec["slim"], spec["lse"]]
        + [spec["table"]] * 3
        + [spec["row"], spec["col"]],
        out_specs=spec["wide"],
        out_shape=jax.ShapeDtypeStruct((rows, 3 * lanes), BF),
        scratch_shapes=[pltpu.VMEM((length, lanes), F32)] * 2,
        compiler_params=pltpu.CompilerParams(vmem_limit_bytes=32 << 20),
        name="attend_grad",
    )(qkv, grad, lse, *tables, segments[:, None, :], segments.reshape(-1, 1))


def place(order, sources, count, axis, shape):
    arrays = []
    for array, _, _, _ in sources:
        if not any(array is seen for seen in arrays):
            arrays.append(array)
    where = [[array is seen for seen in arrays].index(True) for array, _, _, _ in sources]
    size = shape[axis] // count

    def kernel(order_ref, *refs):
        ins, out = refs[: len(arrays)], refs[-1]
        for i, (_, (rows, cols), slot, entry) in enumerate(sources):
            to = pl.multiple_of((slot * 4 + order_ref[entry]) * size, size)
            if axis == 0:
                out[pl.ds(to, size), :] = ins[where[i]][rows : rows + size, cols : cols + shape[1]]
            else:
                out[:, pl.ds(to, size)] = ins[where[i]][rows : rows + shape[0], cols : cols + size]

    if axis == 1 and size % 128:
        result = jnp.zeros(shape, arrays[0].dtype)
        for array, (rows, cols), slot, entry in sources:
            piece = lax.slice(array, (rows, cols), (rows + shape[0], cols + size))
            to = (slot * 4 + order[entry]) * size
            result = lax.dynamic_update_slice_in_dim(result, piece, to, 1)
        return result

    whole = pl.BlockSpec(memory_space=pltpu.VMEM)
    return pl.pallas_call(
        kernel,
        in_specs=[pl.BlockSpec(memory_space=pltpu.SMEM)] + [whole] * len(arrays),
        out_specs=whole,
        out_shape=jax.ShapeDtypeStruct(shape, arrays[0].dtype),
        compiler_params=pltpu.CompilerParams(vmem_limit_bytes=24 << 20),
        name="place",
    )(order, *arrays)


def swap_with(values, axis, mask, size):
    return lax.ppermute(values, axis, [(i, i ^ mask) for i in range(size)])


def dot(left, right, dims):
    return lax.dot_general(left, right, (dims, ((), ())), preferred_element_type=F32)


def after(values, *earlier):
    return lax.optimization_barrier((values,) + earlier)[0]


def step(*values):
    return lax.optimization_barrier(values)


TEAM = ("l", "x", "y", "core")


def make_body(groups):
    def body(
        hidden_in, ln_gain, ln_bias, w_qkv, b_qkv, w_dense, b_dense,
        w_fc1, b_fc1, w_fc2, b_fc2, segment_ids, out_grad,
    ):
        group, lb, xb = lax.axis_index("h"), lax.axis_index("l"), lax.axis_index("x")
        quad = 2 * lb + xb
        tile, width = hidden_in.shape
        span = width // groups

        def part(values, which, count, axis):
            size = values.shape[axis] // count
            return lax.dynamic_slice_in_dim(values, which * size, size, axis)

        def fixed(values, which, count, axis):
            size = values.shape[axis] // count
            return lax.slice_in_dim(values, which * size, (which + 1) * size, axis=axis)

        def own_order(values, axis):
            bit = 1
            while bit < groups:
                blocks = [fixed(values, j ^ bit, groups, axis) for j in range(groups)]
                flipped = jnp.concatenate(blocks, axis=axis)
                values = jnp.where((group // bit) % 2 == 1, flipped, values)
                bit *= 2
            return values

        def trade(give, own):
            return [own] + [swap_with(give(quad ^ m), ("l", "x"), m, 4) for m in (1, 2, 3)]

        def in_order(parts, axis):
            blocks = [
                jnp.where(
                    lb == 1,
                    jnp.where(xb == 1, parts[j ^ 3], parts[j ^ 2]),
                    jnp.where(xb == 1, parts[j ^ 1], parts[j]),
                )
                for j in range(4)
            ]
            return jnp.concatenate(blocks, axis=axis)

        def swap_h(values):
            return [swap_with(values, "h", k, groups) for k in range(1, groups)]

        def fold_start(rows, axis, name):
            sent = lax.dynamic_index_in_dim(rows, 1 - lax.axis_index(name), axis, keepdims=False)
            return swap_with(sent, name, 1, 2)

        def fold_end(rows, got, axis, name):
            mine = lax.dynamic_index_in_dim(rows, lax.axis_index(name), axis, keepdims=False)
            return mine.astype(F32) + got.astype(F32)

        def halves(rows):
            return rows[..., : width // 2], rows[..., width // 2 :]

        def swap_c(values):
            return swap_with(values, "core", 1, 2)

        def quad_swap(values, m):
            return swap_with(values, ("l", "x"), m, 4)

        seg_len = segment_ids.shape[1]
        in_cols = 3 * w_qkv.shape[2] // 4 + w_fc1.shape[1] // 4
        labels = jnp.pad(segment_ids.astype(BF), ((0, 15), (0, in_cols - seg_len)))

        def take_in(which):
            piece = part(w_qkv, which, 4, 2)
            rows = jnp.concatenate(
                [piece[:, j] for j in range(3)] + [part(w_fc1, which, 4, 1)], axis=1
            )
            return jnp.concatenate([rows, labels], axis=0)

        def take_out(which):
            return jnp.concatenate([part(w_dense, which, 4, 0), part(w_fc2, which, 4, 0)], axis=0)

        def stacked(parts, axis):
            return jnp.concatenate(parts, axis=axis)

        def unstack(values, count, axis):
            return [fixed(values, m, count, axis) for m in range(count)]

        local = w_dense.shape[0] // 4
        qkv_cols = 3 * local

        order = jnp.stack([quad, quad ^ 1, quad ^ 2, quad ^ 3])
        rows_in, cols_out = w_fc1.shape[0], w_fc2.shape[1]

        hidden = hidden_in.astype(F32)
        mine_n = own_order(layer_norm(hidden, ln_gain, ln_bias).astype(BF), 1)
        mine_g = own_order(out_grad, 1)
        in_own = take_in(quad)
        in_first = swap_h(in_own[:rows_in])
        in_1 = quad_swap(take_in(quad ^ 1), 1)
        next_n = swap_with(mine_n, "l", 1, 2)
        in_first, in_1, next_n, in_own = step(in_first, in_1, next_n, in_own)

        def gather_tokens(mine, other):
            rows = lax.all_gather(
                jnp.stack([mine, other]), ("x", "y", "core"), axis=1, tiled=True
            )
            return rows.reshape(-1, width)

        normed_all = gather_tokens(mine_n, next_n)
        in_2, in_3 = (quad_swap(take_in(quad ^ m), m) for m in (2, 3))
        out_own = take_out(quad)
        out_first = swap_h(out_own)
        in_2, in_3, out_first, out_own = step(in_2, in_3, out_first, out_own)
        in_parts = [in_own, in_1, in_2, in_3]

        qkv_rest = swap_h(stacked([p[:rows_in, :qkv_cols] for p in in_parts[1:]], 0))
        out_parts = [out_own] + [quad_swap(take_out(quad ^ m), m) for m in (1, 2, 3)]
        next_g = swap_with(mine_g, "l", 1, 2)
        up_send = stacked([p[:rows_in, qkv_cols:] for p in in_parts[1:]], 0)
        qkv_rest, out_parts, next_g, up_send = step(qkv_rest, out_parts, next_g, up_send)

        def place_in(first_col, cols, rest):
            sources = [(p, (0, first_col), 0, m) for m, p in enumerate(in_parts)]
            for k in range(1, groups):
                sources.append((in_first[k - 1], (0, first_col), k, 0))
                sources += [(rest[k - 1], ((m - 1) * rows_in, 0), k, m) for m in (1, 2, 3)]
            return place(order, sources, 4 * groups, 0, (width, cols))

        def place_out(first_row, rows, rest):
            sources = [(p, (first_row, 0), 0, m) for m, p in enumerate(out_parts)]
            for k in range(1, groups):
                sources.append((out_first[k - 1], (first_row, 0), k, 0))
                sources += [(rest[k - 1], (0, (m - 1) * cols_out), k, m) for m in (1, 2, 3)]
            return place(order, sources, 4 * groups, 1, (rows, width))

        up_rest = swap_h(up_send)
        dense_rest = swap_h(stacked([p[:local] for p in out_parts[1:]], 1))
        qkv_w = place_in(0, qkv_cols, qkv_rest)
        labels_all = [p[rows_in, :seg_len].astype(jnp.int32)[None] for p in in_parts]
        ordered = in_order(labels_all, 0)
        segments = jnp.where(lb == 1, jnp.roll(ordered, 2, axis=0), ordered)
        grad_all = gather_tokens(after(mine_g, normed_all, qkv_w), next_g)
        up_b = part(b_fc1, quad, 4, 0)
        qkv_b = part(b_qkv, quad, 4, 1).reshape(-1)
        mixed = dot(normed_all, qkv_w, ((1,), (0,))) + qkv_b
        tables = rotary_tables(segments.shape[1], local)
        qkv, context, lse = attention(mixed, tables, segments)
        down_send = stacked([p[local:] for p in out_parts[1:]], 1)
        qkv, context, lse, up_rest, dense_rest, down_send = step(
            qkv, context, lse, up_rest, dense_rest, down_send
        )

        def slot(values, k, axis):
            return fixed(values, k, groups, axis)

        down_rest = swap_h(down_send)
        up_w = place_in(qkv_cols, in_cols - qkv_cols, up_rest)
        dense_w = place_out(0, local, dense_rest)
        before = dot(after(normed_all, context), up_w, ((1,), (0,))) + up_b
        activated = gelu_tanh(before).astype(BF)
        acts = stacked([context, activated], 1)
        out_part = dot(acts, grad_all, ((0,), (0,))).astype(BF)
        cuts = [0, out_part.shape[0] * 2 // 5, out_part.shape[0] * 7 // 10, out_part.shape[0]]

        def out_slot(k, i):
            return slot(out_part, k, 1)[cuts[i] : cuts[i + 1]]

        out_send = [[out_slot(k, i) for i in range(3)] for k in range(groups)]
        context_grad = dot(after(grad_all, out_part), dense_w, ((1,), (1,))).astype(BF)
        mixed_grad = attention_grad(qkv, context_grad, lse, tables, segments)
        mixed_grad, down_rest, out_send, before, acts = step(
            mixed_grad, down_rest, out_send, before, acts
        )

        def send_out(i):
            return [swap_with(out_send[k][i], "h", k, groups) for k in range(1, groups)]

        out_a = send_out(0)
        down_w = place_out(local, w_fc2.shape[0] // 4, down_rest)
        branch = dot(acts, stacked([dense_w, down_w], 0), ((1,), (0,)))
        branch = lax.psum_scatter(
            branch.astype(BF).reshape(2, -1, width),
            ("x", "y", "core"),
            scatter_dimension=1,
            tiled=True,
        )
        activated_grad = dot(after(grad_all, mixed_grad), down_w, ((1,), (1,)))
        before_grad = jax.vjp(gelu_tanh, before)[1](activated_grad)[0].astype(BF)
        into = stacked([mixed_grad, before_grad], 1)
        into, out_a = step(into, out_a)
        out_b = send_out(1)
        terms = dot(into, stacked([qkv_w, up_w], 1), ((1,), (1,)))
        unit = (normed_all.astype(F32) - own_order(ln_bias, 0)) / own_order(ln_gain, 0)
        small = [
            own_order(jnp.sum(terms * unit, axis=0), 0),
            own_order(jnp.sum(terms, axis=0), 0),
            jnp.sum(out_grad.astype(F32), axis=0),
        ]
        shape5 = (2, 2, 2, 2, tile, width)
        terms = terms.astype(BF).reshape(shape5)
        team = 4 * (2 * lax.axis_index("y") + lax.axis_index("core"))
        bias = jnp.sum(into, axis=0, dtype=F32)
        size = into.shape[1]
        bias = lax.dynamic_update_slice(jnp.zeros((16 * size,), F32), bias, ((team + quad) * size,))
        total = stacked(small + [bias], 0)
        sent_c = lax.dynamic_index_in_dim(terms, 1 - lax.axis_index("core"), 3, keepdims=False)
        terms, total, into, sent_c, out_b = step(terms, total, into, sent_c, out_b)
        out_c = send_out(2)
        in_part = dot(normed_all, into, ((0,), (0,))).astype(BF)

        def block(k, m):
            start = k * span + (quad ^ m) * (span // 4)
            return lax.dynamic_slice_in_dim(in_part, start, span // 4, 0)

        def add_up(mine, others):
            mine = mine.astype(F32)
            for piece in others:
                mine = mine + piece.astype(F32)
            return mine

        in_send = [[block(k, m) for m in range(4)] for k in range(groups)]
        in_send, out_c = step(in_send, out_c)

        def send_in(m):
            return [swap_with(in_send[k][m], "h", k, groups) for k in range(1, groups)]

        in_a = send_in(1)
        got_c = swap_c(sent_c)
        out_sum = [
            add_up(out_send[0][i], got) for i, got in enumerate((out_a, out_b, out_c))
        ]
        out_sum = stacked(out_sum, 0)
        sent = out_sum.astype(BF)
        out_back = [quad_swap(part(sent, quad ^ m, 4, 1), m) for m in (1, 2, 3)]
        in_a, got_c, out_back = step(in_a, got_c, out_back)

        in_b = send_in(2)
        rows = fold_end(terms, got_c, 3, "core").astype(BF)
        left, right = halves(rows)
        got_l, got_r = fold_start(left, 2, "y"), fold_start(right, 1, "x")
        total = total + swap_c(total)
        out_pieces = [part(out_sum, quad, 4, 1)] + [p.astype(F32) for p in out_back]
        dense_grad = in_order([p[:local] for p in out_pieces], 0)
        down_grad = in_order([p[local:] for p in out_pieces], 0)
        back_1 = add_up(in_send[0][1], in_a).astype(BF)
        in_b, left, right, got_l, got_r, total, back_1, dense_grad, down_grad = step(
            in_b, left, right, got_l, got_r, total, back_1, dense_grad, down_grad
        )

        in_c = send_in(3)
        back_1 = quad_swap(back_1, 1)
        left = fold_end(left, got_l, 2, "y").astype(BF)
        right = fold_end(right, got_r, 1, "x").astype(BF)
        got_l, got_r = fold_start(left, 1, "x"), fold_start(right, 1, "y")
        total = total + swap_with(total, "y", 1, 2)
        back_2 = add_up(in_send[0][2], in_b).astype(BF)
        in_c, left, right, got_l, got_r, total, back_1, back_2 = step(
            in_c, left, right, got_l, got_r, total, back_1, back_2
        )

        in_d = send_in(0)
        back_2 = quad_swap(back_2, 2)
        rows = stacked(
            [fold_end(left, got_l, 1, "x").astype(BF), fold_end(right, got_r, 1, "y").astype(BF)],
            -1,
        )
        got_n = swap_with(rows[1], "l", 1, 2)
        total = total + swap_with(total, "x", 1, 2)
        back_3 = add_up(in_send[0][3], in_c).astype(BF)
        in_d, back_2, back_3, got_n, total = step(in_d, back_2, back_3, got_n, total)

        back_3 = quad_swap(back_3, 3)
        total = total + swap_with(total, "l", 1, 2)
        got_m = swap_with(branch[1], "l", 1, 2)
        normed_grad = own_order(rows[0].astype(F32) + got_n.astype(F32), 1)
        hidden_grad = jax.vjp(lambda v: layer_norm(v, ln_gain, ln_bias), hidden)[1](normed_grad)[0]
        input_grad = out_grad.astype(F32) + hidden_grad
        bit = 1
        while bit < groups:
            total = total + swap_with(total, "h", bit, groups)
            bit *= 2
        branch = own_order(branch[0].astype(F32) + got_m.astype(F32), 1)
        hidden_out = (hidden + branch + b_dense + b_fc2).astype(BF)
        pieces = [add_up(in_send[0][0], in_d)] + [p.astype(F32) for p in (back_1, back_2, back_3)]
        up_grad = in_order([p[:, qkv_cols:] for p in pieces], 1)
        qkv_grad = jnp.stack(
            [in_order([p[:, j * local : (j + 1) * local] for p in pieces], 1) for j in range(3)],
            axis=1,
        )
        gain_grad, shift_grad, out_bias_grad = (
            total[:width], total[width : 2 * width], total[2 * width : 3 * width]
        )
        bias = lax.dynamic_slice(total, (3 * width + team * size,), (4 * size,)).reshape(4, size)
        up_bias_grad = bias[:, qkv_cols:].reshape(-1)
        qkv_bias_grad = jnp.stack(
            [bias[:, j * local : (j + 1) * local].reshape(-1) for j in range(3)]
        )
        return (
            hidden_out, input_grad, gain_grad, shift_grad, qkv_grad, qkv_bias_grad,
            dense_grad, out_bias_grad, up_grad, up_bias_grad, down_grad, out_bias_grad,
        )

    return body


def solution(mesh):
    groups = mesh.shape["fsdp"] // 4
    grid = Mesh(mesh.devices.reshape(groups, 2, 2, 2, 2), ("h", "l", "x", "y", "core"))
    rows, cols = ("h", "l", "x"), ("y", "core")
    tokens = rows + cols
    in_specs = (
        P(tokens, None), P(), P(), P(rows, None, cols), P(None, cols), P(cols, rows), P(),
        P(rows, cols), P(cols), P(cols, rows), P(), P(rows, None), P(tokens, None),
    )
    out_specs = (
        P(tokens, None), P(tokens, None), P(), P(), P(rows, None, cols), P(None, cols),
        P(cols, rows), P(), P(rows, cols), P(cols), P(cols, rows), P(),
    )
    return jax.shard_map(
        make_body(groups), mesh=grid, in_specs=in_specs, out_specs=out_specs, check_vma=False
    )
```

time: 591 us -> 506 us (0.86)
  waiting for transfers between devices: 330 us -> 228 us
  Pallas kernels: 0 us -> 21.6 us
  local copies, waits for them, and re-layouts: 65.8 us -> 47.2 us
  starting transfers between devices: 39 us -> 53.6 us
    ppermute x37 -> x39, waiting for transfers between devices: 330 us -> 227 us  [swap_with(): return lax.ppermute(values, axis, [(i, i ^ mask) for i in range(size)])]
    pallas_call x0 -> x6, Pallas kernels: none -> 21.6 us  [the longest x1 11.5 us: attention_grad(): pl.pallas_call(attend_grad_kernel, grid=(sequences,), in_specs=[spec['wid...]
    unnamed x177 -> x183, local copies, waits for them, and re-layouts: 30.3 us -> 14.2 us
    dot_general x12 -> x8, matrix products: 60.1 us -> 74.7 us  [dot(): lax.dot_general(left, right, (dims, ((), ())), preferred_element_type=F32)]
    ppermute x37 -> x39, starting transfers between devices: 38.8 us -> 53.3 us  [swap_with(): return lax.ppermute(values, axis, [(i, i ^ mask) for i in range(size)])]
    concatenate x19 -> x20, other arithmetic: 22.8 us -> 11.9 us  [the longest x8 6.95 us: stacked(): return jnp.concatenate(parts, axis=axis)]
    dot_general x5 -> x0, matrix products: 9.91 us -> none  [ein(): return jnp.einsum(spec, left, right, preferred_element_type=F32)]
    squeeze x1 -> x7, local copies, waits for them, and re-layouts: 1.3 us -> 7.57 us  [the longest x1 5 us: body(): lax.dynamic_index_in_dim(terms, 1 - lax.axis_index('core'), 3, keepdims=F...]
  transfers between devices with their start and end apart: 41 -> 42, of which waited for: 19 -> 22; matrix products, arithmetic and copies ran while one was open for 33% -> 32% of each run, Pallas kernels for 0% -> 4%
where the time goes in v2:
time: 506 us; the launch traced here: 501 us
  waiting for transfers between devices  228 us (45%)
  matrix products  74.7 us (15%)
  other arithmetic  60.3 us (12%)
  starting transfers between devices  53.6 us (11%)
  local copies, waits for them, and re-layouts  47.2 us (9%)
  Pallas kernels  21.6 us (4%)
  between operations  15.6 us (3%)
    ppermute x39, waiting for transfers between devices, swap_with(): return lax.ppermute(values, axis, [(i, i ^ mask) for i in range(size)])  227 us
    dot_general x8, matrix products, dot(): lax.dot_general(left, right, (dims, ((), ())), preferred_element_type=F32)  74.7 us
    ppermute x39, starting transfers between devices, swap_with(): return lax.ppermute(values, axis, [(i, i ^ mask) for i in range(size)])  53.3 us
    unnamed x183, local copies, waits for them, and re-layouts  14.2 us
    pallas_call x1, Pallas kernels, attention_grad(): pl.pallas_call(attend_grad_kernel, grid=(sequences,), in_specs=[spec['wid...  11.5 us
  transfers between devices with their start and end apart: 42, of which 22 were waited for; matrix products, arithmetic and copies ran while one was open for 32% of the time, Pallas kernels for 4%

profile of v2, /device:TPU:0, one launch (start us, length us, event | category | flops | bytes accessed | tf_op | source)
XLA Modules:
  0.0 500.9 jit_solution(11433512739150229090)
XLA Ops:
  11.5 2.9 collective-permute-start.1
  17.6 2.7 collective-permute-start
  20.3 18.0 %collective-permute-done.refs_4_ = bf16[256,896]{1,0:T(8,128)(2,1)S(1)} collective-permute-done((bf16[256,896]{1,0:T(8,128)(2,1)S(1)}, bf16[256,896]{1,0:T(8,128)(2,1)S(1)}, u32[]{:S(2)}, u32[]{:S(2)}) %collective-permute-start) | collective-permute-done | bytes 458784 | tf_op jit(solution)/shard_map/ppermute | solution.py:239
  40.4 2.7 collective-permute-start.3
  45.5 1.9 collective-permute-start.5
  50.1 19.8 %collective-permute-done.5.refs_4_ = bf16[640,256]{1,0:T(8,128)(2,1)S(1)} collective-permute-done((bf16[640,256]{1,0:T(8,128)(2,1)S(1)}, bf16[640,256]{1,0:T(8,128)(2,1)S(1)}, u32[]{:S(2)}, u32[]{:S(2)}) %collective-permute-start.5) | collective-permute-done | bytes 327712 | tf_op jit(solution)/shard_map/ppermute | solution.py:239
  70.8 2.7 collective-permute-start.6
  78.7 28.6 %collective-permute-done.8.refs_2_ = bf16[640,256]{1,0:T(8,128)(2,1)S(1)} collective-permute-done((bf16[640,256]{1,0:T(8,128)(2,1)S(1)}, bf16[640,256]{1,0:T(8,128)(2,1)S(1)}, u32[]{:S(2)}, u32[]{:S(2)}) %collective-permute-start.8) | collective-permute-done | bytes 327712 | tf_op jit(solution)/shard_map/ppermute | solution.py:239
  107.3 4.4 collective-permute-done.9.refs_3_
  115.5 2.3 pad_maximum_fusion.7
  121.8 1.9 fusion.48
  129.9 2.5 collective-permute-start.11
  134.0 7.0 %convolution_add_fusion.1.mixed_ref = f32[2048,384]{1,0:T(8,128)S(1)} fusion(bf16[2048,2048]{1,0:T(8,128)(2,1)} %bitcast.134, bf16[2048,384]{1,0:T(8,128)(2,1)S(1)} %copy-done.25, f32[384]{0:T(512)S(1)} %copy-done.84), kind=kOutput, calls=%fused_computation.32 | convolution fusion | flops 3222011904 | bytes 13108736 | tf_op jit(solution)/shard_map/dot_general | solution.py:243
  141.1 6.7 %attend.1 = (bf16[2048,384]{1,0:T(8,128)(2,1)S(1)}, bf16[2048,128]{1,0:T(8,128)(2,1)S(1)}, f32[4,2,512]{2,1,0:T(2,128)S(1)}) custom-call(f32[2048,384]{1,0:T(8,128)S(1)} %convolution_add_fusion.1.mixed_ref, f32[512,128]{1,0:T(8,128)S(1)} %copy-done.15, f32[512,128]{1,0:T(8,128)S(1)} %copy-done.13, f32[512,128]{1,0:T(8,128)S(1)} %copy-done.11, ...), custom_call_target="tpu_custom_call" | custom-call | tf_op jit(solution)/shard_map/attend/pallas_call | solution.py:169
  149.0 27.1 %collective-permute-done.12.refs_5_ = bf16[128,768]{1,0:T(8,128)(2,1)S(1)} collective-permute-done((bf16[128,768]{1,0:T(8,128)(2,1)S(1)}, bf16[128,768]{1,0:T(8,128)(2,1)S(1)}, u32[]{:S(2)}, u32[]{:S(2)}) %collective-permute-start.12) | collective-permute-done | bytes 196640 | tf_op jit(solution)/shard_map/ppermute | solution.py:239
  177.0 2.0 copy.32
  183.0 10.8 %fusion.15 = (bf16[2048,512]{0,1:T(8,128)(2,1)S(1)}, f32[2048,512]{0,1:T(8,128)}) fusion(f32[512]{0:T(512)S(1)} %dynamic_slice.144, bf16[2048,2048]{1,0:T(8,128)(2,1)} %bitcast.135, bf16[2048,512]{1,0:T(8,128)(2,1)S(1)} %place.5), kind=kOutput, calls=%fused_computation.22 | convolution fusion | flops 4305453056 | bytes 16779264 | tf_op jit(solution)/shard_map/dot_general | solution.py:243
  196.8 10.2 %convolution_convert_fusion.2 = bf16[640,2048]{1,0:T(8,128)(2,1)S(1)} fusion(bf16[2048,2048]{1,0:T(8,128)(2,1)} %bitcast.137, bf16[2048,512]{0,1:T(8,128)(2,1)} %copy-done.46, bf16[2048,128]{0,1:T(8,128)(2,1)S(1)} %copy-done.45), kind=kOutput, calls=%fused_computation.30 | convolution fusion | flops 5375262720 | bytes 13631488 | tf_op jit(solution)/shard_map/dot_general | solution.py:243
  207.0 2.4 convolution_convert_fusion.3.grad_ref
  209.5 11.5 %attend_grad.1 = bf16[2048,384]{1,0:T(8,128)(2,1)S(1)} custom-call(bf16[2048,384]{1,0:T(8,128)(2,1)S(1)} %copy-done.28, bf16[2048,128]{1,0:T(8,128)(2,1)S(1)} %convolution_convert_fusion.3.grad_ref, f32[4,2,512]{2,1,0:T(2,128)S(1)} %get-tuple-element.118.lse_ref, f32[512,128]{1,0:T(8,128)S(1)} %copy-done.16, f32[512,128]{1,0:T(8,128)S(1)} %copy-done.14, ...), custom_call_target="tpu_custom_call" | custom-call | tf_op jit(solution)/shard_map/attend_grad/pallas_call | solution.py:188
  224.6 2.5 collective-permute-start.15
  227.6 4.5 fusion.78
  232.1 3.8 fusion.7
  237.7 2.3 pad_maximum_fusion
  240.0 20.0 %collective-permute-done.15 = bf16[256,1024]{1,0:T(8,128)(2,1)S(1)} collective-permute-done((bf16[256,1024]{1,0:T(8,128)(2,1)S(1)}, bf16[256,1024]{1,0:T(8,128)(2,1)S(1)}, u32[]{:S(2)}, u32[]{:S(2)}) %collective-permute-start.15) | collective-permute-done | bytes 524320 | tf_op jit(solution)/shard_map/ppermute | solution.py:239
  260.7 15.9 %multiply_reduce_fusion = (f32[2048]{0:T(1024)S(1)}, f32[2048]{0:T(1024)S(1)}, bf16[2048,2048]{1,0:T(8,128)(2,1)}) fusion(f32[2048]{0:T(1024)S(1)} %copy-done.81, f32[2048]{0:T(1024)S(1)} %copy-done.80, bf16[2,1024,2048]{2,1,0:T(8,128)(2,1)} %all-gather.3.cloned.1.call-done, bf16[2048,896]{0,1:T(8,128)(2,1)S(1)} %pad_maximum_fusion, ...), kind=kOutput, calls=%fused_computation | convolution fusion | flops 7552888832 | bytes 24150016 | tf_op jit(solution)/shard_map/dot_general | solution.py:243
  276.6 5.0 copy_bitcast_fusion
  282.6 10.9 %convolution_convert_fusion = bf16[2048,2048]{1,0:T(8,128)(2,1)} fusion(bf16[2048,640]{0,1:T(8,128)(2,1)} %pad_maximum_fusion.1, bf16[512,2048]{1,0:T(8,128)(2,1)S(1)} %copy-done.18, bf16[128,2048]{1,0:T(8,128)(2,1)S(1)} %copy-done.35), kind=kOutput, calls=%fused_computation.3 | convolution fusion | flops 5378146304 | bytes 13631488 | tf_op jit(solution)/shard_map/dot_general | solution.py:243
  294.5 13.1 %convolution_convert_fusion.1 = bf16[2048,896]{1,0:T(8,128)(2,1)S(1)} fusion(bf16[2048,2048]{1,0:T(8,128)(2,1)} %bitcast.136, bf16[2048,896]{0,1:T(8,128)(2,1)} %copy-done.39), kind=kOutput, calls=%fused_computation.29 | convolution fusion | flops 7518027776 | bytes 15728640 | tf_op jit(solution)/shard_map/dot_general | solution.py:243
  309.2 4.8 collective-permute-done.17
  316.1 2.8 collective-permute-start.23
  321.6 11.6 %collective-permute-done.22 = bf16[640,256]{1,0:T(8,128)(2,1)} collective-permute-done((bf16[640,256]{1,0:T(8,128)(2,1)}, bf16[640,256]{1,0:T(8,128)(2,1)}, u32[]{:S(2)}, u32[]{:S(2)}) %collective-permute-start.22) | collective-permute-done | bytes 327712 | tf_op jit(solution)/shard_map/ppermute | solution.py:239
  333.2 9.9 %collective-permute-start.19 = (bf16[256,896]{1,0:T(8,128)(2,1)S(1)}, bf16[256,896]{1,0:T(8,128)(2,1)S(1)}, u32[]{:S(2)}, u32[]{:S(2)}) collective-permute-start(bf16[256,896]{1,0:T(8,128)(2,1)S(1)} %copy-done.58), channel_id=1, source_target_pairs={{0,16},{16,0},{1,17},{17,1},{2,18},{18,2},{3,19},{19,3},{4,20},{20... | collective-permute-start | bytes 1376264 | tf_op jit(solution)/shard_map/ppermute | solution.py:239
  343.0 5.1 %collective-permute-done.24 = bf16[640,256]{1,0:T(8,128)(2,1)} collective-permute-done((bf16[640,256]{1,0:T(8,128)(2,1)}, bf16[640,256]{1,0:T(8,128)(2,1)}, u32[]{:S(2)}, u32[]{:S(2)}) %collective-permute-start.24) | collective-permute-done | bytes 327712 | tf_op jit(solution)/shard_map/ppermute | solution.py:239
  348.1 5.4 %fusion = bf16[2,2,2,128,2048]{4,3,0,2,1:T(8,128)(2,1)S(1)} fusion(bf16[2,2,2,128,2048]{4,3,0,2,1:T(8,128)(2,1)} %collective-permute-done.21, s32[]{:T(128)S(6)} %select_n.635, bf16[2,2,2,2,128,2048]{5,4,3,2,1,0:T(8,128)(2,1)} %bitcast.120), kind=kLoop, calls=%fused_computation.2 | loop fusion | flops 8388608 | bytes 12582916 | tf_op jit(solution)/shard_map/convert_element_type | solution.py:488
  354.3 2.0 collective-permute-start.25
  363.4 27.1 %collective-permute-done.25 = bf16[2,2,128,1024]{3,2,0,1:T(8,128)(2,1)S(1)} collective-permute-done((bf16[2,2,128,1024]{3,2,0,1:T(8,128)(2,1)S(1)}, bf16[2,2,128,1024]{3,2,0,1:T(8,128)(2,1)S(1)}, u32[]{:S(2)}, u32[]{:S(2)}) %collective-permute-start.25) | collective-permute-done | bytes 1048608 | tf_op jit(solution)/shard_map/ppermute | solution.py:239
  398.1 9.4 %collective-permute-done.30 = f32[20480]{0:T(1024)S(1)} collective-permute-done((f32[20480]{0:T(1024)S(1)}, f32[20480]{0:T(1024)S(1)}, u32[]{:S(2)}, u32[]{:S(2)}) %collective-permute-start.30) | collective-permute-done | bytes 81952 | tf_op jit(solution)/shard_map/ppermute | solution.py:239
  408.1 5.9 %collective-permute-done.18 = bf16[256,896]{1,0:T(8,128)(2,1)S(1)} collective-permute-done((bf16[256,896]{1,0:T(8,128)(2,1)S(1)}, bf16[256,896]{1,0:T(8,128)(2,1)S(1)}, u32[]{:S(2)}, u32[]{:S(2)}) %collective-permute-start.18) | collective-permute-done | bytes 458784 | tf_op jit(solution)/shard_map/ppermute | solution.py:239
  415.6 1.9 collective-permute-start.33
  418.4 1.9 add_convert_fusion
  420.3 2.0 convert_element_type.324
  423.2 14.5 %collective-permute-done.32 = bf16[256,896]{1,0:T(8,128)(2,1)S(1)} collective-permute-done((bf16[256,896]{1,0:T(8,128)(2,1)}, bf16[256,896]{1,0:T(8,128)(2,1)S(1)}, u32[]{:S(2)}, u32[]{:S(2)}) %collective-permute-start.32) | collective-permute-done | bytes 458784 | tf_op jit(solution)/shard_map/ppermute | solution.py:239
  437.7 10.4 %collective-permute-done.33 = bf16[256,896]{1,0:T(8,128)(2,1)} collective-permute-done((bf16[256,896]{1,0:T(8,128)(2,1)}, bf16[256,896]{1,0:T(8,128)(2,1)}, u32[]{:S(2)}, u32[]{:S(2)}) %collective-permute-start.33) | collective-permute-done | bytes 458784 | tf_op jit(solution)/shard_map/ppermute | solution.py:239
  451.4 2.9 collective-permute-start.38
  455.6 2.0 convert_element_type.323
  457.6 7.5 %collective-permute-done.37 = f32[20480]{0:T(1024)S(1)} collective-permute-done((f32[20480]{0:T(1024)S(1)}, f32[20480]{0:T(1024)S(1)}, u32[]{:S(2)}, u32[]{:S(2)}) %collective-permute-start.37) | collective-permute-done | bytes 81952 | tf_op jit(solution)/shard_map/ppermute | solution.py:239
  482.3 8.2 %collective-permute-done.14 = bf16[128,2048]{1,0:T(8,128)(2,1)S(1)} collective-permute-done((bf16[128,2048]{1,0:T(8,128)(2,1)S(1)}, bf16[128,2048]{1,0:T(8,128)(2,1)S(1)}, u32[]{:S(2)}, u32[]{:S(2)}) %collective-permute-start.14) | collective-permute-done | bytes 524320 | tf_op jit(solution)/shard_map/ppermute | solution.py:239
  (371 shorter events, 104.0 us)
Async XLA Ops:
  7.2 111.7 %copy-start = (f32[3,512]{1,0:T(4,128)S(1)}, f32[3,512]{1,0:T(4,128)}, u32[]{:S(2)}) copy-start(f32[3,512]{1,0:T(4,128)} %param.17) | copy-start | bytes 18436
  7.2 108.3 %all-gather.3.cloned.1.call-start = ((), (), s32[]{:S(2)}) async-start(), calls=%async_computation.1 | async-start | bytes 9437184 | tf_op jit(solution)/shard_map/all_gather | solution.py:354
  11.5 26.8 %collective-permute-start.1 = (bf16[272,896]{1,0:T(8,128)(2,1)S(1)}, bf16[272,896]{1,0:T(8,128)(2,1)S(1)}, u32[]{:S(2)}, u32[]{:S(2)}) collective-permute-start(bf16[272,896]{1,0:T(8,128)(2,1)S(1)} %get-tuple-element.277), channel_id=1, source_target_pairs={{0,4},{4,0},{8,12},{12,8},{1,5},{5,1},{9,13},{13,9},{2,6},{6,2},{1... | collective-permute-start | bytes 1462280 | tf_op jit(solution)/shard_map/ppermute | solution.py:239
  15.9 23.3 %collective-permute-start.2 = (bf16[128,2048]{1,0:T(8,128)(2,1)S(1)}, bf16[128,2048]{1,0:T(8,128)(2,1)S(1)}, u32[]{:S(2)}, u32[]{:S(2)}) collective-permute-start(bf16[128,2048]{1,0:T(8,128)(2,1)S(1)} %maximum_select_fusion.2), channel_id=1, source_target_pairs={{0,8},{8,0},{1,9},{9,1},{2,10},{10,2},{3,11},{11,3},{4,12},{12,4},... | collective-permute-start | bytes 1572872 | tf_op jit(solution)/shard_map/ppermute | solution.py:239
  17.6 20.7 %collective-permute-start = (bf16[256,896]{1,0:T(8,128)(2,1)S(1)}, bf16[256,896]{1,0:T(8,128)(2,1)S(1)}, u32[]{:S(2)}, u32[]{:S(2)}) collective-permute-start(bf16[256,896]{1,0:T(8,128)(2,1)S(1)} %pad_maximum_fusion.13), channel_id=1, source_target_pairs={{0,16},{16,0},{1,17},{17,1},{2,18},{18,2},{3,19},{19,3},{4,20},{20... | collective-permute-start | bytes 1376264 | tf_op jit(solution)/shard_map/ppermute | solution.py:239
  40.3 156.5 %all-gather.5.cloned.1.call-start = ((), (), s32[]{:S(2)}) async-start(), calls=%async_computation.2 | async-start | bytes 9437184 | tf_op jit(solution)/shard_map/all_gather | solution.py:354
  40.4 29.4 %collective-permute-start.3 = (bf16[272,896]{1,0:T(8,128)(2,1)S(1)}, bf16[272,896]{1,0:T(8,128)(2,1)S(1)}, u32[]{:S(2)}, u32[]{:S(2)}) collective-permute-start(bf16[272,896]{1,0:T(8,128)(2,1)S(1)} %fusion.44), channel_id=1, source_target_pairs={{0,8},{4,12},{8,0},{12,4},{1,9},{5,13},{9,1},{13,5},{2,10},{6,14},... | collective-permute-start | bytes 1462280 | tf_op jit(solution)/shard_map/ppermute | solution.py:239
  43.2 27.5 %collective-permute-start.4 = (bf16[272,896]{1,0:T(8,128)(2,1)}, bf16[272,896]{1,0:T(8,128)(2,1)S(1)}, u32[]{:S(2)}, u32[]{:S(2)}) collective-permute-start(bf16[272,896]{1,0:T(8,128)(2,1)} %get-tuple-element.276), channel_id=1, source_target_pairs={{0,12},{4,8},{8,4},{12,0},{1,13},{5,9},{9,5},{13,1},{2,14},{6,10},... | collective-permute-start | bytes 1462280 | tf_op jit(solution)/shard_map/ppermute | solution.py:239
  45.5 24.3 %collective-permute-start.5 = (bf16[640,256]{1,0:T(8,128)(2,1)S(1)}, bf16[640,256]{1,0:T(8,128)(2,1)S(1)}, u32[]{:S(2)}, u32[]{:S(2)}) collective-permute-start(bf16[640,256]{1,0:T(8,128)(2,1)S(1)} %pad_maximum_fusion.14.refs_0_), channel_id=1, source_target_pairs={{0,16},{16,0},{1,17},{17,1},{2,18},{18,2},{3,19},{19,3},{4,20},{20... | collective-permute-start | bytes 983048 | tf_op jit(solution)/shard_map/ppermute | solution.py:239
  47.5 31.2 %collective-permute-start.7 = (bf16[640,256]{1,0:T(8,128)(2,1)S(1)}, bf16[640,256]{1,0:T(8,128)(2,1)S(1)}, u32[]{:S(2)}, u32[]{:S(2)}) collective-permute-start(bf16[640,256]{1,0:T(8,128)(2,1)S(1)} %pad_maximum_fusion.15), channel_id=1, source_target_pairs={{0,4},{4,0},{8,12},{12,8},{1,5},{5,1},{9,13},{13,9},{2,6},{6,2},{1... | collective-permute-start | bytes 983048 | tf_op jit(solution)/shard_map/ppermute | solution.py:239
  70.7 41.8 %copy-start.22 = (bf16[256,896]{1,0:T(8,128)(2,1)S(1)}, bf16[256,896]{1,0:T(8,128)(2,1)}, u32[]{:S(2)}) copy-start(bf16[256,896]{1,0:T(8,128)(2,1)} %copy-done.21) | copy-start | bytes 1376260
  70.8 40.9 %collective-permute-start.6 = (bf16[768,384]{1,0:T(8,128)(2,1)S(1)}, bf16[768,384]{1,0:T(8,128)(2,1)S(1)}, u32[]{:S(2)}, u32[]{:S(2)}) collective-permute-start(bf16[768,384]{1,0:T(8,128)(2,1)S(1)} %pad_maximum_fusion.10), channel_id=1, source_target_pairs={{0,16},{16,0},{1,17},{17,1},{2,18},{18,2},{3,19},{19,3},{4,20},{20... | collective-permute-start | bytes 1769480 | tf_op jit(solution)/shard_map/ppermute | solution.py:239
  73.6 38.0 %copy-start.47 = (bf16[128,2048]{1,0:T(8,128)(2,1)}, bf16[128,2048]{1,0:T(8,128)(2,1)S(1)}, u32[]{:S(2)}) copy-start(bf16[128,2048]{1,0:T(8,128)(2,1)S(1)} %maximum_select_fusion.3) | copy-start | bytes 1572868
  73.6 38.0 %collective-permute-start.10 = (bf16[128,2048]{1,0:T(8,128)(2,1)S(1)}, bf16[128,2048]{1,0:T(8,128)(2,1)S(1)}, u32[]{:S(2)}, u32[]{:S(2)}) collective-permute-start(bf16[128,2048]{1,0:T(8,128)(2,1)S(1)} %maximum_select_fusion.3), channel_id=1, source_target_pairs={{0,8},{8,0},{1,9},{9,1},{2,10},{10,2},{3,11},{11,3},{4,12},{12,4},... | collective-permute-start | bytes 1572872 | tf_op jit(solution)/shard_map/ppermute | solution.py:239
  74.5 32.8 %collective-permute-start.8 = (bf16[640,256]{1,0:T(8,128)(2,1)S(1)}, bf16[640,256]{1,0:T(8,128)(2,1)S(1)}, u32[]{:S(2)}, u32[]{:S(2)}) collective-permute-start(bf16[640,256]{1,0:T(8,128)(2,1)S(1)} %pad_maximum_fusion.16), channel_id=1, source_target_pairs={{0,8},{4,12},{8,0},{12,4},{1,9},{5,13},{9,1},{13,5},{2,10},{6,14},... | collective-permute-start | bytes 983048 | tf_op jit(solution)/shard_map/ppermute | solution.py:239
  75.9 35.8 %collective-permute-start.9 = (bf16[640,256]{1,0:T(8,128)(2,1)S(1)}, bf16[640,256]{1,0:T(8,128)(2,1)S(1)}, u32[]{:S(2)}, u32[]{:S(2)}) collective-permute-start(bf16[640,256]{1,0:T(8,128)(2,1)S(1)} %pad_maximum_fusion.17), channel_id=1, source_target_pairs={{0,12},{4,8},{8,4},{12,0},{1,13},{5,9},{9,5},{13,1},{2,14},{6,10},... | collective-permute-start | bytes 983048 | tf_op jit(solution)/shard_map/ppermute | solution.py:239
  78.7 45.1 %copy-start.2 = (bf16[640,256]{1,0:T(8,128)(2,1)}, bf16[640,256]{1,0:T(8,128)(2,1)S(1)}, u32[]{:S(2)}) copy-start(bf16[640,256]{1,0:T(8,128)(2,1)S(1)} %collective-permute-done.7.refs_1_) | copy-start | bytes 983044
  117.8 359.8 %reduce-scatter.2.cloned.1.call-start = ((), (), s32[]{:S(2)}) async-start(), calls=%async_computation.3 | async-start | bytes 9437184 | tf_op jit(solution)/shard_map/reduce_scatter | solution.py:431
  129.9 46.2 %collective-permute-start.11 = (bf16[768,512]{1,0:T(8,128)(2,1)}, bf16[768,512]{1,0:T(8,128)(2,1)S(1)}, u32[]{:S(2)}, u32[]{:S(2)}) collective-permute-start(bf16[768,512]{1,0:T(8,128)(2,1)} %pad_maximum_fusion.8), channel_id=1, source_target_pairs={{0,16},{16,0},{1,17},{17,1},{2,18},{18,2},{3,19},{19,3},{4,20},{20... | collective-permute-start | bytes 2359304 | tf_op jit(solution)/shard_map/ppermute | solution.py:239
  132.4 43.7 %collective-permute-start.12 = (bf16[128,768]{1,0:T(8,128)(2,1)S(1)}, bf16[128,768]{1,0:T(8,128)(2,1)S(1)}, u32[]{:S(2)}, u32[]{:S(2)}) collective-permute-start(bf16[128,768]{1,0:T(8,128)(2,1)S(1)} %pad_maximum_fusion.18), channel_id=1, source_target_pairs={{0,16},{16,0},{1,17},{17,1},{2,18},{18,2},{3,19},{19,3},{4,20},{20... | collective-permute-start | bytes 589832 | tf_op jit(solution)/shard_map/ppermute | solution.py:239
  181.9 41.2 %collective-permute-start.13 = (bf16[512,768]{1,0:T(8,128)(2,1)}, bf16[512,768]{1,0:T(8,128)(2,1)}, u32[]{:S(2)}, u32[]{:S(2)}) collective-permute-start(bf16[512,768]{1,0:T(8,128)(2,1)} %pad_maximum_fusion.9), channel_id=1, source_target_pairs={{0,16},{16,0},{1,17},{17,1},{2,18},{18,2},{3,19},{19,3},{4,20},{20... | collective-permute-start | bytes 2359304 | tf_op jit(solution)/shard_map/ppermute | solution.py:239
  224.6 35.5 %collective-permute-start.15 = (bf16[256,1024]{1,0:T(8,128)(2,1)S(1)}, bf16[256,1024]{1,0:T(8,128)(2,1)S(1)}, u32[]{:S(2)}, u32[]{:S(2)}) collective-permute-start(bf16[256,1024]{1,0:T(8,128)(2,1)S(1)} %get-tuple-element.125), channel_id=1, source_target_pairs={{0,16},{16,0},{1,17},{17,1},{2,18},{18,2},{3,19},{19,3},{4,20},{20... | collective-permute-start | bytes 1572872 | tf_op jit(solution)/shard_map/ppermute | solution.py:239
  227.1 55.4 %collective-permute-start.16 = (bf16[192,1024]{1,0:T(8,128)(2,1)}, bf16[192,1024]{1,0:T(8,128)(2,1)S(1)}, u32[]{:S(2)}, u32[]{:S(2)}) collective-permute-start(bf16[192,1024]{1,0:T(8,128)(2,1)} %get-tuple-element.127), channel_id=1, source_target_pairs={{0,16},{16,0},{1,17},{17,1},{2,18},{18,2},{3,19},{19,3},{4,20},{20... | collective-permute-start | bytes 1179656 | tf_op jit(solution)/shard_map/ppermute | solution.py:239
  240.0 36.5 %copy-start.39 = (bf16[2048,896]{0,1:T(8,128)(2,1)}, bf16[2048,896]{0,1:T(8,128)(2,1)S(1)}, u32[]{:S(2)}) copy-start(bf16[2048,896]{0,1:T(8,128)(2,1)S(1)} %pad_maximum_fusion) | copy-start | bytes 11010052
  282.5 65.6 %collective-permute-start.21 = (bf16[2,2,2,128,2048]{4,3,0,2,1:T(8,128)(2,1)}, bf16[2,2,2,128,2048]{4,3,0,2,1:T(8,128)(2,1)}, u32[]{:S(2)}, u32[]{:S(2)}) collective-permute-start(bf16[2,2,2,128,2048]{4,3,0,2,1:T(8,128)(2,1)} %copy_bitcast_fusion), channel_id=1, source_target_pairs={{0,1},{1,0},{2,3},{3,2},{4,5},{5,4},{6,7},{7,6},{8,9},{9,8},{10,11... | collective-permute-start | bytes 12582920 | tf_op jit(solution)/shard_map/ppermute | solution.py:239
  294.4 19.6 %collective-permute-start.17 = (bf16[192,1024]{1,0:T(8,128)(2,1)S(1)}, bf16[192,1024]{1,0:T(8,128)(2,1)S(1)}, u32[]{:S(2)}, u32[]{:S(2)}) collective-permute-start(bf16[192,1024]{1,0:T(8,128)(2,1)S(1)} %copy-done.62), channel_id=1, source_target_pairs={{0,16},{16,0},{1,17},{17,1},{2,18},{18,2},{3,19},{19,3},{4,20},{20... | collective-permute-start | bytes 1179656 | tf_op jit(solution)/shard_map/ppermute | solution.py:239
  314.1 34.1 %collective-permute-start.20 = (bf16[256,896]{1,0:T(8,128)(2,1)}, bf16[256,896]{1,0:T(8,128)(2,1)}, u32[]{:S(2)}, u32[]{:S(2)}) collective-permute-start(bf16[256,896]{1,0:T(8,128)(2,1)} %get-tuple-element.133), channel_id=1, source_target_pairs={{0,16},{16,0},{1,17},{17,1},{2,18},{18,2},{3,19},{19,3},{4,20},{20... | collective-permute-start | bytes 1376264 | tf_op jit(solution)/shard_map/ppermute | solution.py:239
  314.1 4.8 collective-permute-start.27
  315.8 17.4 %collective-permute-start.22 = (bf16[640,256]{1,0:T(8,128)(2,1)}, bf16[640,256]{1,0:T(8,128)(2,1)}, u32[]{:S(2)}, u32[]{:S(2)}) collective-permute-start(bf16[640,256]{1,0:T(8,128)(2,1)} %get-tuple-element.225), channel_id=1, source_target_pairs={{0,4},{4,0},{8,12},{12,8},{1,5},{5,1},{9,13},{13,9},{2,6},{6,2},{1... | collective-permute-start | bytes 983048 | tf_op jit(solution)/shard_map/ppermute | solution.py:239
  316.1 26.9 %collective-permute-start.23 = (bf16[640,256]{1,0:T(8,128)(2,1)}, bf16[640,256]{1,0:T(8,128)(2,1)}, u32[]{:S(2)}, u32[]{:S(2)}) collective-permute-start(bf16[640,256]{1,0:T(8,128)(2,1)} %get-tuple-element.224), channel_id=1, source_target_pairs={{0,8},{4,12},{8,0},{12,4},{1,9},{5,13},{9,1},{13,5},{2,10},{6,14},... | collective-permute-start | bytes 983048 | tf_op jit(solution)/shard_map/ppermute | solution.py:239
  319.5 28.6 %collective-permute-start.24 = (bf16[640,256]{1,0:T(8,128)(2,1)}, bf16[640,256]{1,0:T(8,128)(2,1)}, u32[]{:S(2)}, u32[]{:S(2)}) collective-permute-start(bf16[640,256]{1,0:T(8,128)(2,1)} %get-tuple-element.223), channel_id=1, source_target_pairs={{0,12},{4,8},{8,4},{12,0},{1,13},{5,9},{9,5},{13,1},{2,14},{6,10},... | collective-permute-start | bytes 983048 | tf_op jit(solution)/shard_map/ppermute | solution.py:239
  333.2 30.2 %collective-permute-start.19 = (bf16[256,896]{1,0:T(8,128)(2,1)S(1)}, bf16[256,896]{1,0:T(8,128)(2,1)S(1)}, u32[]{:S(2)}, u32[]{:S(2)}) collective-permute-start(bf16[256,896]{1,0:T(8,128)(2,1)S(1)} %copy-done.58), channel_id=1, source_target_pairs={{0,16},{16,0},{1,17},{17,1},{2,18},{18,2},{3,19},{19,3},{4,20},{20... | collective-permute-start | bytes 1376264 | tf_op jit(solution)/shard_map/ppermute | solution.py:239
  354.3 36.2 %collective-permute-start.25 = (bf16[2,2,128,1024]{3,2,0,1:T(8,128)(2,1)S(1)}, bf16[2,2,128,1024]{3,2,0,1:T(8,128)(2,1)S(1)}, u32[]{:S(2)}, u32[]{:S(2)}) collective-permute-start(bf16[2,2,128,1024]{3,2,0,1:T(8,128)(2,1)S(1)} %dynamic-slice_bitcast_fusion.1), channel_id=1, source_target_pairs={{0,2},{2,0},{1,3},{3,1},{4,6},{6,4},{5,7},{7,5},{8,10},{10,8},{9,1... | collective-permute-start | bytes 3145736 | tf_op jit(solution)/shard_map/ppermute | solution.py:239
  356.4 35.7 %collective-permute-start.26 = (bf16[2,2,128,1024]{3,2,0,1:T(8,128)(2,1)S(1)}, bf16[2,2,128,1024]{3,2,0,1:T(8,128)(2,1)S(1)}, u32[]{:S(2)}, u32[]{:S(2)}) collective-permute-start(bf16[2,2,128,1024]{3,2,0,1:T(8,128)(2,1)S(1)} %dynamic-slice_bitcast_fusion), channel_id=1, source_target_pairs={{0,4},{4,0},{1,5},{5,1},{2,6},{6,2},{3,7},{7,3},{8,12},{12,8},{9,1... | collective-permute-start | bytes 3145736 | tf_op jit(solution)/shard_map/ppermute | solution.py:239
  392.6 22.2 %collective-permute-start.28 = (bf16[2,128,1024]{2,1,0:T(8,128)(2,1)S(1)}, bf16[2,128,1024]{2,1,0:T(8,128)(2,1)S(1)}, u32[]{:S(2)}, u32[]{:S(2)}) collective-permute-start(bf16[2,128,1024]{2,1,0:T(8,128)(2,1)S(1)} %dynamic-slice_bitcast_fusion.3), channel_id=1, source_target_pairs={{0,4},{4,0},{1,5},{5,1},{2,6},{6,2},{3,7},{7,3},{8,12},{12,8},{9,1... | collective-permute-start | bytes 1572872 | tf_op jit(solution)/shard_map/ppermute | solution.py:239
  393.4 21.4 %collective-permute-start.29 = (bf16[2,128,1024]{2,1,0:T(8,128)(2,1)S(1)}, bf16[2,128,1024]{2,1,0:T(8,128)(2,1)S(1)}, u32[]{:S(2)}, u32[]{:S(2)}) collective-permute-start(bf16[2,128,1024]{2,1,0:T(8,128)(2,1)S(1)} %dynamic-slice_bitcast_fusion.2), channel_id=1, source_target_pairs={{0,2},{2,0},{1,3},{3,1},{4,6},{6,4},{5,7},{7,5},{8,10},{10,8},{9,1... | collective-permute-start | bytes 1572872 | tf_op jit(solution)/shard_map/ppermute | solution.py:239
  393.8 20.2 %collective-permute-start.18 = (bf16[256,896]{1,0:T(8,128)(2,1)S(1)}, bf16[256,896]{1,0:T(8,128)(2,1)S(1)}, u32[]{:S(2)}, u32[]{:S(2)}) collective-permute-start(bf16[256,896]{1,0:T(8,128)(2,1)S(1)} %copy-done.57), channel_id=1, source_target_pairs={{0,16},{16,0},{1,17},{17,1},{2,18},{18,2},{3,19},{19,3},{4,20},{20... | collective-permute-start | bytes 1376264 | tf_op jit(solution)/shard_map/ppermute | solution.py:239
  394.2 20.6 %collective-permute-start.31 = (bf16[256,896]{1,0:T(8,128)(2,1)S(1)}, bf16[256,896]{1,0:T(8,128)(2,1)S(1)}, u32[]{:S(2)}, u32[]{:S(2)}) collective-permute-start(bf16[256,896]{1,0:T(8,128)(2,1)S(1)} %add_convert_fusion.2), channel_id=1, source_target_pairs={{0,4},{4,0},{8,12},{12,8},{1,5},{5,1},{9,13},{13,9},{2,6},{6,2},{1... | collective-permute-start | bytes 1376264 | tf_op jit(solution)/shard_map/ppermute | solution.py:239
  395.6 11.9 %collective-permute-start.30 = (f32[20480]{0:T(1024)S(1)}, f32[20480]{0:T(1024)S(1)}, u32[]{:S(2)}, u32[]{:S(2)}) collective-permute-start(f32[20480]{0:T(1024)S(1)} %add.364), channel_id=1, source_target_pairs={{0,2},{2,0},{1,3},{3,1},{4,6},{6,4},{5,7},{7,5},{8,10},{10,8},{9,1... | collective-permute-start | bytes 245768 | tf_op jit(solution)/shard_map/ppermute | solution.py:239
  415.3 32.9 %collective-permute-start.34 = (bf16[128,2048]{1,0:T(8,128)(2,1)S(1)}, bf16[128,2048]{1,0:T(8,128)(2,1)S(1)}, u32[]{:S(2)}, u32[]{:S(2)}) collective-permute-start(bf16[128,2048]{1,0:T(8,128)(2,1)S(1)} %fusion.43), channel_id=1, source_target_pairs={{0,8},{8,0},{1,9},{9,1},{2,10},{10,2},{3,11},{11,3},{4,12},{12,4},... | collective-permute-start | bytes 1572872 | tf_op jit(solution)/shard_map/ppermute | solution.py:239
  415.4 22.4 %collective-permute-start.32 = (bf16[256,896]{1,0:T(8,128)(2,1)}, bf16[256,896]{1,0:T(8,128)(2,1)S(1)}, u32[]{:S(2)}, u32[]{:S(2)}) collective-permute-start(bf16[256,896]{1,0:T(8,128)(2,1)} %get-tuple-element.160), channel_id=1, source_target_pairs={{0,16},{16,0},{1,17},{17,1},{2,18},{18,2},{3,19},{19,3},{4,20},{20... | collective-permute-start | bytes 1376264 | tf_op jit(solution)/shard_map/ppermute | solution.py:239
  415.6 32.6 %collective-permute-start.33 = (bf16[256,896]{1,0:T(8,128)(2,1)}, bf16[256,896]{1,0:T(8,128)(2,1)}, u32[]{:S(2)}, u32[]{:S(2)}) collective-permute-start(bf16[256,896]{1,0:T(8,128)(2,1)} %add_convert_fusion.1), channel_id=1, source_target_pairs={{0,8},{4,12},{8,0},{12,4},{1,9},{5,13},{9,1},{13,5},{2,10},{6,14},... | collective-permute-start | bytes 1376264 | tf_op jit(solution)/shard_map/ppermute | solution.py:239
  417.5 33.1 %copy-start.76 = (f32[128]{0:T(128)S(1)}, f32[128]{0:T(128)}, u32[]{:S(2)}) copy-start(f32[128]{0:T(128)} %copy-done.75) | copy-start | bytes 1540
  417.5 4.9 collective-permute-start.35
  449.0 5.4 %collective-permute-start.36 = (f32[20480]{0:T(1024)S(1)}, f32[20480]{0:T(1024)S(1)}, u32[]{:S(2)}, u32[]{:S(2)}) collective-permute-start(f32[20480]{0:T(1024)S(1)} %add.375), channel_id=1, source_target_pairs={{0,8},{8,0},{1,9},{9,1},{2,10},{10,2},{3,11},{11,3},{4,12},{12,4},... | collective-permute-start | bytes 245768 | tf_op jit(solution)/shard_map/ppermute | solution.py:239
  451.4 20.3 %collective-permute-start.38 = (bf16[256,896]{1,0:T(8,128)(2,1)}, bf16[256,896]{1,0:T(8,128)(2,1)}, u32[]{:S(2)}, u32[]{:S(2)}) collective-permute-start(bf16[256,896]{1,0:T(8,128)(2,1)} %add_convert_fusion), channel_id=1, source_target_pairs={{0,12},{4,8},{8,4},{12,0},{1,13},{5,9},{9,5},{13,1},{2,14},{6,10},... | collective-permute-start | bytes 1376264 | tf_op jit(solution)/shard_map/ppermute | solution.py:239
  454.3 10.7 %collective-permute-start.37 = (f32[20480]{0:T(1024)S(1)}, f32[20480]{0:T(1024)S(1)}, u32[]{:S(2)}, u32[]{:S(2)}) collective-permute-start(f32[20480]{0:T(1024)S(1)} %add.378), channel_id=1, source_target_pairs={{0,16},{16,0},{1,17},{17,1},{2,18},{18,2},{3,19},{19,3},{4,20},{20... | collective-permute-start | bytes 245768 | tf_op jit(solution)/shard_map/ppermute | solution.py:239
  478.7 11.8 %collective-permute-start.14 = (bf16[128,2048]{1,0:T(8,128)(2,1)S(1)}, bf16[128,2048]{1,0:T(8,128)(2,1)S(1)}, u32[]{:S(2)}, u32[]{:S(2)}) collective-permute-start(bf16[128,2048]{1,0:T(8,128)(2,1)S(1)} %slice_bitcast_fusion), channel_id=1, source_target_pairs={{0,8},{8,0},{1,9},{9,1},{2,10},{10,2},{3,11},{11,3},{4,12},{12,4},... | collective-permute-start | bytes 1572872 | tf_op jit(solution)/shard_map/ppermute | solution.py:239
  (83 other events, 777.4 us)
Sparse Core Ops, SparseCore 0:
  40.4 75.0 all-gather.2
  118.0 54.3 all-gather.4
  293.6 98.1 reduce-scatter.1

commit v3 on v2

--- a/solution.py
+++ b/solution.py
@@ -161,9 +161,8 @@
     )
 
 
-def attention(mixed, tables, segments):
+def attention(mixed, lanes, tables, segments):
     sequences, length = segments.shape
-    lanes = mixed.shape[1] // 3
     spec = attention_specs(length, lanes)
     rows = sequences * length
     return pl.pallas_call(
@@ -346,9 +345,9 @@
         mine_g = own_order(out_grad, 1)
         in_own = take_in(quad)
         in_first = swap_h(in_own[:rows_in])
-        in_1 = quad_swap(take_in(quad ^ 1), 1)
+        in_parts = trade(take_in, in_own)
         next_n = swap_with(mine_n, "l", 1, 2)
-        in_first, in_1, next_n, in_own = step(in_first, in_1, next_n, in_own)
+        in_first, in_parts, next_n = step(in_first, in_parts, next_n)
 
         def gather_tokens(mine, other):
             rows = lax.all_gather(
@@ -357,181 +356,174 @@
             return rows.reshape(-1, width)
 
         normed_all = gather_tokens(mine_n, next_n)
-        in_2, in_3 = (quad_swap(take_in(quad ^ m), m) for m in (2, 3))
-        out_own = take_out(quad)
-        out_first = swap_h(out_own)
-        in_2, in_3, out_first, out_own = step(in_2, in_3, out_first, out_own)
-        in_parts = [in_own, in_1, in_2, in_3]
-
-        qkv_rest = swap_h(stacked([p[:rows_in, :qkv_cols] for p in in_parts[1:]], 0))
-        out_parts = [out_own] + [quad_swap(take_out(quad ^ m), m) for m in (1, 2, 3)]
+        in_rest = swap_h(stacked([p[:rows_in] for p in in_parts[1:]], 0))
+        out_parts = trade(take_out, take_out(quad))
         next_g = swap_with(mine_g, "l", 1, 2)
-        up_send = stacked([p[:rows_in, qkv_cols:] for p in in_parts[1:]], 0)
-        qkv_rest, out_parts, next_g, up_send = step(qkv_rest, out_parts, next_g, up_send)
-
-        def place_in(first_col, cols, rest):
-            sources = [(p, (0, first_col), 0, m) for m, p in enumerate(in_parts)]
-            for k in range(1, groups):
-                sources.append((in_first[k - 1], (0, first_col), k, 0))
-                sources += [(rest[k - 1], ((m - 1) * rows_in, 0), k, m) for m in (1, 2, 3)]
-            return place(order, sources, 4 * groups, 0, (width, cols))
-
-        def place_out(first_row, rows, rest):
-            sources = [(p, (first_row, 0), 0, m) for m, p in enumerate(out_parts)]
-            for k in range(1, groups):
-                sources.append((out_first[k - 1], (first_row, 0), k, 0))
-                sources += [(rest[k - 1], (0, (m - 1) * cols_out), k, m) for m in (1, 2, 3)]
-            return place(order, sources, 4 * groups, 1, (rows, width))
-
-        up_rest = swap_h(up_send)
-        dense_rest = swap_h(stacked([p[:local] for p in out_parts[1:]], 1))
-        qkv_w = place_in(0, qkv_cols, qkv_rest)
+        out_stack = stacked(out_parts, 1)
+        in_rest, out_parts, out_stack, next_g = step(in_rest, out_parts, out_stack, next_g)
+
+        out_rest = swap_h(out_stack)
+        in_first, in_parts, in_rest = step(in_first, in_parts, in_rest)
+        sources = [(p, (0, 0), 0, m) for m, p in enumerate(in_parts)]
+        for k in range(1, groups):
+            sources.append((in_first[k - 1], (0, 0), k, 0))
+            sources += [(in_rest[k - 1], ((m - 1) * rows_in, 0), k, m) for m in (1, 2, 3)]
+        in_w = place(order, sources, 4 * groups, 0, (width, in_cols))
         labels_all = [p[rows_in, :seg_len].astype(jnp.int32)[None] for p in in_parts]
         ordered = in_order(labels_all, 0)
         segments = jnp.where(lb == 1, jnp.roll(ordered, 2, axis=0), ordered)
-        grad_all = gather_tokens(after(mine_g, normed_all, qkv_w), next_g)
-        up_b = part(b_fc1, quad, 4, 0)
-        qkv_b = part(b_qkv, quad, 4, 1).reshape(-1)
-        mixed = dot(normed_all, qkv_w, ((1,), (0,))) + qkv_b
+        grad_all = gather_tokens(after(mine_g, normed_all, out_stack), next_g)
+        in_b = stacked([part(b_qkv, quad, 4, 1).reshape(-1), part(b_fc1, quad, 4, 0)], 0)
+        mixed = dot(normed_all, in_w, ((1,), (0,))) + in_b
         tables = rotary_tables(segments.shape[1], local)
-        qkv, context, lse = attention(mixed, tables, segments)
-        down_send = stacked([p[local:] for p in out_parts[1:]], 1)
-        qkv, context, lse, up_rest, dense_rest, down_send = step(
-            qkv, context, lse, up_rest, dense_rest, down_send
-        )
+        qkv, context, lse = attention(mixed, local, tables, segments)
+        before = mixed[:, qkv_cols:]
+        acts = stacked([context, gelu_tanh(before).astype(BF)], 1)
+        qkv, acts, lse, before, out_rest = step(qkv, acts, lse, before, out_rest)
 
         def slot(values, k, axis):
             return fixed(values, k, groups, axis)
 
-        down_rest = swap_h(down_send)
-        up_w = place_in(qkv_cols, in_cols - qkv_cols, up_rest)
-        dense_w = place_out(0, local, dense_rest)
-        before = dot(after(normed_all, context), up_w, ((1,), (0,))) + up_b
-        activated = gelu_tanh(before).astype(BF)
-        acts = stacked([context, activated], 1)
+        out_rows = acts.shape[1]
         out_part = dot(acts, grad_all, ((0,), (0,))).astype(BF)
-        cuts = [0, out_part.shape[0] * 2 // 5, out_part.shape[0] * 7 // 10, out_part.shape[0]]
-
-        def out_slot(k, i):
-            return slot(out_part, k, 1)[cuts[i] : cuts[i + 1]]
-
-        out_send = [[out_slot(k, i) for i in range(3)] for k in range(groups)]
-        context_grad = dot(after(grad_all, out_part), dense_w, ((1,), (1,))).astype(BF)
-        mixed_grad = attention_grad(qkv, context_grad, lse, tables, segments)
-        mixed_grad, down_rest, out_send, before, acts = step(
-            mixed_grad, down_rest, out_send, before, acts
-        )
+        cuts = [out_rows * i // 40 for i in (0, 10, 17, 24, 33, 40)]
+        out_send = [
+            [slot(out_part, k, 1)[cuts[i] : cuts[i + 1]] for i in range(5)] for k in range(groups)
+        ]
+        out_ws = []
+        for low, high in ((0, local), (local, out_rows)):
+            sources = [(p, (low, 0), 0, m) for m, p in enumerate(out_parts)]
+            for k in range(1, groups):
+                sources += [(out_rest[k - 1], (low, m * cols_out), k, m) for m in range(4)]
+            out_ws.append(place(order, sources, 4 * groups, 1, (high - low, width)))
+        out_send, out_ws = step(out_send, out_ws)
 
         def send_out(i):
             return [swap_with(out_send[k][i], "h", k, groups) for k in range(1, groups)]
 
-        out_a = send_out(0)
-        down_w = place_out(local, w_fc2.shape[0] // 4, down_rest)
-        branch = dot(acts, stacked([dense_w, down_w], 0), ((1,), (0,)))
-        branch = lax.psum_scatter(
-            branch.astype(BF).reshape(2, -1, width),
-            ("x", "y", "core"),
-            scatter_dimension=1,
-            tiled=True,
-        )
-        activated_grad = dot(after(grad_all, mixed_grad), down_w, ((1,), (1,)))
+        out_0 = send_out(0)
+        out_ws, qkv, lse = step(out_ws, qkv, lse)
+        context_grad = dot(grad_all, out_ws[0], ((1,), (1,))).astype(BF)
+        mixed_grad = attention_grad(qkv, context_grad, lse, tables, segments)
+        mixed_grad, out_0, out_send = step(mixed_grad, out_0, out_send)
+
+        out_1 = send_out(1)
+        mixed_grad, before = step(mixed_grad, before)
+        activated_grad = dot(after(grad_all, mixed_grad), out_ws[1], ((1,), (1,)))
         before_grad = jax.vjp(gelu_tanh, before)[1](activated_grad)[0].astype(BF)
         into = stacked([mixed_grad, before_grad], 1)
-        into, out_a = step(into, out_a)
-        out_b = send_out(1)
-        terms = dot(into, stacked([qkv_w, up_w], 1), ((1,), (1,)))
+        out_w = stacked(out_ws, 0)
+        into, out_1, out_w, out_send = step(into, out_1, out_w, out_send)
+        out_2 = send_out(2)
+        into, out_w = step(into, out_w)
+        branch = dot(after(acts, into), out_w, ((1,), (0,))).astype(BF)
+        team_sum = lax.psum_scatter(
+            branch.reshape(2, -1, width), ("x", "y", "core"), scatter_dimension=1, tiled=True
+        )
+        into, branch, out_2, out_send = step(into, branch, out_2, out_send)
+        out_3 = send_out(3)
+        into, branch = step(into, branch)
+        in_part = dot(normed_all, into, ((0,), (0,))).astype(BF)
+
+        def block(k, m):
+            start = k * span + (quad ^ m) * (span // 4)
+            return lax.dynamic_slice_in_dim(in_part, start, span // 4, 0)
+
+        def add_up(mine, others):
+            mine = mine.astype(F32)
+            for piece in others:
+                mine = mine + piece.astype(F32)
+            return mine
+
+        in_part, out_3, into, out_send = step(in_part, out_3, into, out_send)
+
+        out_4 = send_out(4)
+        into, in_w = step(into, in_w)
+        terms = dot(into, in_w, ((1,), (1,)))
         unit = (normed_all.astype(F32) - own_order(ln_bias, 0)) / own_order(ln_gain, 0)
+        gain_sum, shift_sum = jnp.sum(terms * unit, axis=0), jnp.sum(terms, axis=0)
+        shape5 = (2, 2, 2, 2, tile, width)
+        terms = terms.astype(BF).reshape(shape5)
+        in_part, terms, gain_sum, shift_sum, out_4 = step(
+            in_part, terms, gain_sum, shift_sum, out_4
+        )
+
+        def send_in(m):
+            return [swap_with(block(k, m), "h", k, groups) for k in range(1, groups)]
+
+        in_1 = send_in(1)
+        got_c = fold_start(terms, 3, "core")
+        out_got = (out_0, out_1, out_2, out_3, out_4)
+        out_sum = stacked([add_up(out_send[0][i], got) for i, got in enumerate(out_got)], 0)
+        sent = out_sum.astype(BF)
+        out_back = [quad_swap(part(sent, quad ^ m, 4, 1), m) for m in (1, 2, 3)]
         small = [
-            own_order(jnp.sum(terms * unit, axis=0), 0),
-            own_order(jnp.sum(terms, axis=0), 0),
+            own_order(gain_sum, 0),
+            own_order(shift_sum, 0),
             jnp.sum(out_grad.astype(F32), axis=0),
         ]
-        shape5 = (2, 2, 2, 2, tile, width)
-        terms = terms.astype(BF).reshape(shape5)
         team = 4 * (2 * lax.axis_index("y") + lax.axis_index("core"))
         bias = jnp.sum(into, axis=0, dtype=F32)
         size = into.shape[1]
         bias = lax.dynamic_update_slice(jnp.zeros((16 * size,), F32), bias, ((team + quad) * size,))
         total = stacked(small + [bias], 0)
-        sent_c = lax.dynamic_index_in_dim(terms, 1 - lax.axis_index("core"), 3, keepdims=False)
-        terms, total, into, sent_c, out_b = step(terms, total, into, sent_c, out_b)
-        out_c = send_out(2)
-        in_part = dot(normed_all, into, ((0,), (0,))).astype(BF)
-
-        def block(k, m):
-            start = k * span + (quad ^ m) * (span // 4)
-            return lax.dynamic_slice_in_dim(in_part, start, span // 4, 0)
-
-        def add_up(mine, others):
-            mine = mine.astype(F32)
-            for piece in others:
-                mine = mine + piece.astype(F32)
-            return mine
-
-        in_send = [[block(k, m) for m in range(4)] for k in range(groups)]
-        in_send, out_c = step(in_send, out_c)
-
-        def send_in(m):
-            return [swap_with(in_send[k][m], "h", k, groups) for k in range(1, groups)]
-
-        in_a = send_in(1)
-        got_c = swap_c(sent_c)
-        out_sum = [
-            add_up(out_send[0][i], got) for i, got in enumerate((out_a, out_b, out_c))
-        ]
-        out_sum = stacked(out_sum, 0)
-        sent = out_sum.astype(BF)
-        out_back = [quad_swap(part(sent, quad ^ m, 4, 1), m) for m in (1, 2, 3)]
-        in_a, got_c, out_back = step(in_a, got_c, out_back)
-
-        in_b = send_in(2)
         rows = fold_end(terms, got_c, 3, "core").astype(BF)
+        in_1, rows, out_back, out_sum, total, in_part = step(
+            in_1, rows, out_back, out_sum, total, in_part
+        )
+
+        in_2 = send_in(2)
         left, right = halves(rows)
         got_l, got_r = fold_start(left, 2, "y"), fold_start(right, 1, "x")
         total = total + swap_c(total)
+        back_1 = add_up(block(0, 1), in_1).astype(BF)
+        left = fold_end(left, got_l, 2, "y").astype(BF)
+        right = fold_end(right, got_r, 1, "x").astype(BF)
         out_pieces = [part(out_sum, quad, 4, 1)] + [p.astype(F32) for p in out_back]
         dense_grad = in_order([p[:local] for p in out_pieces], 0)
         down_grad = in_order([p[local:] for p in out_pieces], 0)
-        back_1 = add_up(in_send[0][1], in_a).astype(BF)
-        in_b, left, right, got_l, got_r, total, back_1, dense_grad, down_grad = step(
-            in_b, left, right, got_l, got_r, total, back_1, dense_grad, down_grad
-        )
-
-        in_c = send_in(3)
+        in_2, left, right, total, dense_grad, down_grad, back_1, in_part = step(
+            in_2, left, right, total, dense_grad, down_grad, back_1, in_part
+        )
+
+        in_3 = send_in(3)
         back_1 = quad_swap(back_1, 1)
-        left = fold_end(left, got_l, 2, "y").astype(BF)
-        right = fold_end(right, got_r, 1, "x").astype(BF)
         got_l, got_r = fold_start(left, 1, "x"), fold_start(right, 1, "y")
         total = total + swap_with(total, "y", 1, 2)
-        back_2 = add_up(in_send[0][2], in_b).astype(BF)
-        in_c, left, right, got_l, got_r, total, back_1, back_2 = step(
-            in_c, left, right, got_l, got_r, total, back_1, back_2
-        )
-
-        in_d = send_in(0)
-        back_2 = quad_swap(back_2, 2)
+        back_2 = add_up(block(0, 2), in_2).astype(BF)
         rows = stacked(
             [fold_end(left, got_l, 1, "x").astype(BF), fold_end(right, got_r, 1, "y").astype(BF)],
             -1,
         )
+        in_3, rows, total, back_1, back_2, in_part = step(
+            in_3, rows, total, back_1, back_2, in_part
+        )
+
+        in_0 = send_in(0)
         got_n = swap_with(rows[1], "l", 1, 2)
+        back_2 = quad_swap(back_2, 2)
         total = total + swap_with(total, "x", 1, 2)
-        back_3 = add_up(in_send[0][3], in_c).astype(BF)
-        in_d, back_2, back_3, got_n, total = step(in_d, back_2, back_3, got_n, total)
+        back_3 = add_up(block(0, 3), in_3).astype(BF)
+        in_0, got_n, back_2, back_3, total, in_part = step(
+            in_0, got_n, back_2, back_3, total, in_part
+        )
 
         back_3 = quad_swap(back_3, 3)
+        got_m = swap_with(team_sum[1], "l", 1, 2)
         total = total + swap_with(total, "l", 1, 2)
-        got_m = swap_with(branch[1], "l", 1, 2)
         normed_grad = own_order(rows[0].astype(F32) + got_n.astype(F32), 1)
         hidden_grad = jax.vjp(lambda v: layer_norm(v, ln_gain, ln_bias), hidden)[1](normed_grad)[0]
         input_grad = out_grad.astype(F32) + hidden_grad
+        own_in = add_up(block(0, 0), in_0)
+        back_3, got_m, total, input_grad, own_in = step(back_3, got_m, total, input_grad, own_in)
+
         bit = 1
         while bit < groups:
             total = total + swap_with(total, "h", bit, groups)
             bit *= 2
-        branch = own_order(branch[0].astype(F32) + got_m.astype(F32), 1)
+        branch = own_order(team_sum[0].astype(F32) + got_m.astype(F32), 1)
         hidden_out = (hidden + branch + b_dense + b_fc2).astype(BF)
-        pieces = [add_up(in_send[0][0], in_d)] + [p.astype(F32) for p in (back_1, back_2, back_3)]
+        pieces = [own_in] + [p.astype(F32) for p in (back_1, back_2, back_3)]
         up_grad = in_order([p[:, qkv_cols:] for p in pieces], 1)
         qkv_grad = jnp.stack(
             [in_order([p[:, j * local : (j + 1) * local] for p in pieces], 1) for j in range(3)],

time: 506 us -> 458 us (0.905)
  waiting for transfers between devices: 228 us -> 202 us
  matrix products: 74.7 us -> 67.3 us
  local copies, waits for them, and re-layouts: 47.2 us -> 39.8 us
    ppermute x39 -> x38, waiting for transfers between devices: 227 us -> 202 us  [swap_with(): return lax.ppermute(values, axis, [(i, i ^ mask) for i in range(size)])]
    unnamed x183 -> x143, local copies, waits for them, and re-layouts: 14.2 us -> 21.8 us
    dot_general x8 -> x7, matrix products: 74.7 us -> 67.3 us  [dot(): lax.dot_general(left, right, (dims, ((), ())), preferred_element_type=F32)]
    slice x14 -> x6, local copies, waits for them, and re-layouts: 7.81 us -> 2.02 us  [the longest x3 1.91 us: body(): slot(out_part, k, 1)[cuts[i]:cuts[i + 1]]]
    ppermute x39 -> x38, starting transfers between devices: 53.3 us -> 52 us  [swap_with(): return lax.ppermute(values, axis, [(i, i ^ mask) for i in range(size)])]
  transfers between devices with their start and end apart: 42 -> 41, of which waited for: 22 -> 22; matrix products, arithmetic and copies ran while one was open for 32% -> 26% of each run, Pallas kernels for 4% -> 5%
where the time goes in v3:
time: 458 us; the launch traced here: 453 us
  waiting for transfers between devices  202 us (44%)
  matrix products  67.3 us (15%)
  other arithmetic  56.2 us (12%)
  starting transfers between devices  52.2 us (11%)
  local copies, waits for them, and re-layouts  39.8 us (9%)
  Pallas kernels  20.7 us (5%)
  between operations  15.3 us (3%)
    ppermute x38, waiting for transfers between devices, swap_with(): return lax.ppermute(values, axis, [(i, i ^ mask) for i in range(size)])  202 us
    dot_general x7, matrix products, dot(): lax.dot_general(left, right, (dims, ((), ())), preferred_element_type=F32)  67.3 us
    ppermute x38, starting transfers between devices, swap_with(): return lax.ppermute(values, axis, [(i, i ^ mask) for i in range(size)])  52 us
    unnamed x143, local copies, waits for them, and re-layouts  21.8 us
    pallas_call x1, Pallas kernels, attention_grad(): pl.pallas_call(attend_grad_kernel, grid=(sequences,), in_specs=[spec['wid...  11.5 us
  transfers between devices with their start and end apart: 41, of which 22 were waited for; matrix products, arithmetic and copies ran while one was open for 26% of the time, Pallas kernels for 5%

profile of v3, /device:TPU:0, one launch (start us, length us, event | category | flops | bytes accessed | tf_op | source)
XLA Modules:
  0.0 453.4 jit_solution(16653044827813914908)
XLA Ops:
  11.7 2.9 collective-permute-start.1
  18.5 2.1 collective-permute-start.4
  20.6 2.7 collective-permute-start
  23.3 35.6 %collective-permute-done.refs_4_ = bf16[256,896]{1,0:T(8,128)(2,1)S(1)} collective-permute-done((bf16[256,896]{1,0:T(8,128)(2,1)S(1)}, bf16[256,896]{1,0:T(8,128)(2,1)S(1)}, u32[]{:S(2)}, u32[]{:S(2)}) %collective-permute-start) | collective-permute-done | bytes 458784 | tf_op jit(solution)/shard_map/ppermute | solution.py:238
  62.0 3.4 collective-permute-start.5
  70.3 32.8 %collective-permute-done.7.refs_2_ = bf16[640,256]{1,0:T(8,128)(2,1)S(1)} collective-permute-done((bf16[640,256]{1,0:T(8,128)(2,1)S(1)}, bf16[640,256]{1,0:T(8,128)(2,1)S(1)}, u32[]{:S(2)}, u32[]{:S(2)}) %collective-permute-start.7) | collective-permute-done | bytes 327712 | tf_op jit(solution)/shard_map/ppermute | solution.py:238
  103.1 15.7 %collective-permute-done.8.refs_3_ = bf16[640,256]{1,0:T(8,128)(2,1)S(1)} collective-permute-done((bf16[640,256]{1,0:T(8,128)(2,1)S(1)}, bf16[640,256]{1,0:T(8,128)(2,1)S(1)}, u32[]{:S(2)}, u32[]{:S(2)}) %collective-permute-start.8) | collective-permute-done | bytes 327712 | tf_op jit(solution)/shard_map/ppermute | solution.py:238
  120.8 2.8 collective-permute-done.5.refs_5_
  124.7 2.3 pad_maximum_fusion.9
  128.2 1.9 fusion.38
  140.6 12.6 %broadcast_add_fusion.mixed_ref = f32[2048,896]{1,0:T(8,128)S(1)} fusion(f32[896]{0:T(1024)S(1)} %pad_maximum_fusion.19, bf16[2048,2048]{1,0:T(8,128)(2,1)} %bitcast.138, bf16[2048,896]{1,0:T(8,128)(2,1)S(1)} %place.3), kind=kOutput, calls=%fused_computation.25 | convolution fusion | flops 7518027776 | bytes 19402240 | tf_op jit(solution)/shard_map/dot_general | solution.py:242
  153.2 7.0 %attend.1 = (bf16[2048,384]{1,0:T(8,128)(2,1)S(1)}, bf16[2048,128]{1,0:T(8,128)(2,1)S(1)}, f32[4,2,512]{2,1,0:T(2,128)S(1)}) custom-call(f32[2048,896]{1,0:T(8,128)S(1)} %broadcast_add_fusion.mixed_ref, f32[512,128]{1,0:T(8,128)S(1)} %copy-done.15, f32[512,128]{1,0:T(8,128)S(1)} %copy-done.13, f32[512,128]{1,0:T(8,128)S(1)} %copy-done.11, ...), custom_call_target="tpu_custom_call" | custom-call | tf_op jit(solution)/shard_map/attend/pallas_call | solution.py:168
  160.3 3.3 fusion.53
  165.3 23.3 %collective-permute-done.10.refs_4_ = bf16[640,1024]{1,0:T(8,128)(2,1)S(1)} collective-permute-done((bf16[640,1024]{1,0:T(8,128)(2,1)}, bf16[640,1024]{1,0:T(8,128)(2,1)S(1)}, u32[]{:S(2)}, u32[]{:S(2)}) %collective-permute-start.10) | collective-permute-done | bytes 1310752 | tf_op jit(solution)/shard_map/ppermute | solution.py:238
  195.1 9.2 %convolution_convert_fusion.2 = bf16[640,2048]{1,0:T(8,128)(2,1)S(1)} fusion(bf16[2048,640]{1,0:T(8,128)(2,1)} %pad_maximum_fusion.1, bf16[2048,2048]{1,0:T(8,128)(2,1)} %bitcast.140), kind=kOutput, calls=%fused_computation.27 | convolution fusion | flops 5370019840 | bytes 13631488 | tf_op jit(solution)/shard_map/dot_general | solution.py:242
  206.4 2.4 convolution_convert_fusion.3.grad_ref
  208.9 11.5 %attend_grad.1 = bf16[2048,384]{1,0:T(8,128)(2,1)S(1)} custom-call(bf16[2048,384]{1,0:T(8,128)(2,1)S(1)} %copy-done.28, bf16[2048,128]{1,0:T(8,128)(2,1)S(1)} %convolution_convert_fusion.3.grad_ref, f32[4,2,512]{2,1,0:T(2,128)S(1)} %get-tuple-element.173.lse_ref, f32[512,128]{1,0:T(8,128)S(1)} %copy-done.16, f32[512,128]{1,0:T(8,128)S(1)} %copy-done.14, ...), custom_call_target="tpu_custom_call" | custom-call | tf_op jit(solution)/shard_map/attend_grad/pallas_call | solution.py:187
  220.7 2.0 collective-permute-done.11
  224.4 7.5 %fusion.7 = bf16[2048,512]{1,0:T(8,128)(2,1)S(1)} fusion(f32[2048,512]{1,0:T(8,128)S(1)} %copy-done.39, bf16[2048,2048]{1,0:T(8,128)(2,1)S(1)} %bitcast.142, bf16[512,2048]{1,0:T(8,128)(2,1)S(1)} %place.5), kind=kOutput, calls=%fused_computation.14 | convolution fusion | flops 4315938816 | bytes 16777216 | tf_op jit(solution)/shard_map/dot_general | solution.py:242
  231.9 2.1 pad_maximum_fusion
  236.0 9.4 %convolution_convert_fusion = bf16[2048,2048]{1,0:T(8,128)(2,1)} fusion(bf16[2048,640]{1,0:T(8,128)(2,1)S(1)} %copy-done.40, bf16[640,2048]{1,0:T(8,128)(2,1)S(1)} %pad_maximum_fusion.2), kind=kOutput, calls=%fused_computation.3 | convolution fusion | flops 5372903424 | bytes 13631488 | tf_op jit(solution)/shard_map/dot_general | solution.py:242
  246.7 1.9 collective-permute-start.14
  248.6 14.5 %convolution_convert_fusion.1 = bf16[2048,896]{1,0:T(8,128)(2,1)} fusion(bf16[2048,2048]{1,0:T(8,128)(2,1)} %bitcast.139, bf16[2048,896]{1,0:T(8,128)(2,1)} %pad_maximum_fusion), kind=kOutput, calls=%fused_computation.26 | convolution fusion | flops 7518027776 | bytes 15728640 | tf_op jit(solution)/shard_map/dot_general | solution.py:242
  264.5 11.7 %fusion.51 = (f32[2048]{0:T(1024)S(1)}, f32[2048]{0:T(1024)S(1)}, bf16[2048,2048]{1,0:T(8,128)(2,1)S(1)}) fusion(f32[2048]{0:T(1024)S(1)} %get-tuple-element.378, f32[2048]{0:T(1024)S(1)} %get-tuple-element.377, bf16[2,1024,2048]{2,1,0:T(8,128)(2,1)} %all-gather.3.cloned.1.call-done, bf16[2048,896]{1,0:T(8,128)(2,1)S(1)} %copy-done.35, ...), kind=kOutput, calls=%fused_computation.232 | convolution fusion | flops 7545548800 | bytes 24150016 | tf_op jit(solution)/shard_map/dot_general | solution.py:242
  276.2 3.3 copy-done.36
  279.5 2.3 copy_bitcast_fusion
  282.0 2.9 convert_reduce_fusion
  292.6 5.5 %fusion = bf16[2,2,2,128,2048]{4,3,0,2,1:T(8,128)(2,1)S(1)} fusion(bf16[2,2,2,128,2048]{4,3,0,2,1:T(8,128)(2,1)} %collective-permute-done.17, s32[]{:T(128)S(6)} %select_n.623, bf16[2,2,2,2,128,2048]{5,4,3,2,1,0:T(8,128)(2,1)} %bitcast.124), kind=kLoop, calls=%fused_computation.2 | loop fusion | flops 8388608 | bytes 12582916 | tf_op jit(solution)/shard_map/convert_element_type | solution.py:470
  298.1 5.7 %collective-permute-done.18 = bf16[640,256]{1,0:T(8,128)(2,1)S(1)} collective-permute-done((bf16[640,256]{1,0:T(8,128)(2,1)S(1)}, bf16[640,256]{1,0:T(8,128)(2,1)S(1)}, u32[]{:S(2)}, u32[]{:S(2)}) %collective-permute-start.18) | collective-permute-done | bytes 327712 | tf_op jit(solution)/shard_map/ppermute | solution.py:238
  303.8 2.7 collective-permute-done.19
  306.5 8.9 %collective-permute-done.20 = bf16[640,256]{1,0:T(8,128)(2,1)S(1)} collective-permute-done((bf16[640,256]{1,0:T(8,128)(2,1)S(1)}, bf16[640,256]{1,0:T(8,128)(2,1)S(1)}, u32[]{:S(2)}, u32[]{:S(2)}) %collective-permute-start.20) | collective-permute-done | bytes 327712 | tf_op jit(solution)/shard_map/ppermute | solution.py:238
  321.4 1.9 add_convert_fusion.2
  326.1 16.3 %collective-permute-done.22 = bf16[2,2,128,1024]{3,2,0,1:T(8,128)(2,1)S(1)} collective-permute-done((bf16[2,2,128,1024]{3,2,0,1:T(8,128)(2,1)S(1)}, bf16[2,2,128,1024]{3,2,0,1:T(8,128)(2,1)S(1)}, u32[]{:S(2)}, u32[]{:S(2)}) %collective-permute-start.22) | collective-permute-done | bytes 1048608 | tf_op jit(solution)/shard_map/ppermute | solution.py:238
  342.8 4.5 collective-permute-done.23
  352.0 4.2 collective-permute-start.25
  357.3 2.0 add_convert_fusion.1
  359.3 5.2 %collective-permute-done.28 = f32[20480]{0:T(1024)S(1)} collective-permute-done((f32[20480]{0:T(1024)S(1)}, f32[20480]{0:T(1024)S(1)}, u32[]{:S(2)}, u32[]{:S(2)}) %collective-permute-start.28) | collective-permute-done | bytes 81952 | tf_op jit(solution)/shard_map/ppermute | solution.py:238
  366.1 9.5 %collective-permute-done.25 = bf16[256,896]{1,0:T(8,128)(2,1)S(1)} collective-permute-done((bf16[256,896]{1,0:T(8,128)(2,1)S(1)}, bf16[256,896]{1,0:T(8,128)(2,1)S(1)}, u32[]{:S(2)}, u32[]{:S(2)}) %collective-permute-start.25) | collective-permute-done | bytes 458784 | tf_op jit(solution)/shard_map/ppermute | solution.py:238
  376.9 1.8 constant_dynamic-slice_fusion
  378.8 3.4 collective-permute-start.30
  382.7 2.0 add_convert_fusion
  388.4 14.1 %collective-permute-done.30 = bf16[256,896]{1,0:T(8,128)(2,1)} collective-permute-done((bf16[256,896]{1,0:T(8,128)(2,1)}, bf16[256,896]{1,0:T(8,128)(2,1)}, u32[]{:S(2)}, u32[]{:S(2)}) %collective-permute-start.30) | collective-permute-done | bytes 458784 | tf_op jit(solution)/shard_map/ppermute | solution.py:238
  402.4 7.0 %collective-permute-done.32 = bf16[256,896]{1,0:T(8,128)(2,1)} collective-permute-done((bf16[256,896]{1,0:T(8,128)(2,1)}, bf16[256,896]{1,0:T(8,128)(2,1)}, u32[]{:S(2)}, u32[]{:S(2)}) %collective-permute-start.32) | collective-permute-done | bytes 458784 | tf_op jit(solution)/shard_map/ppermute | solution.py:238
  414.2 1.9 collective-permute-start.35
  416.0 2.4 convert_add_fusion.4
  420.7 3.7 collective-permute-done.36
  425.4 8.0 %collective-permute-done.35 = bf16[128,2048]{1,0:T(8,128)(2,1)S(1)} collective-permute-done((bf16[128,2048]{1,0:T(8,128)(2,1)S(1)}, bf16[128,2048]{1,0:T(8,128)(2,1)S(1)}, u32[]{:S(2)}, u32[]{:S(2)}) %collective-permute-start.35) | collective-permute-done | bytes 524320 | tf_op jit(solution)/shard_map/ppermute | solution.py:238
  436.0 4.1 collective-permute-start.37
  (323 shorter events, 94.2 us)
Async XLA Ops:
  7.2 121.0 %copy-start = (f32[3,512]{1,0:T(4,128)S(1)}, f32[3,512]{1,0:T(4,128)}, u32[]{:S(2)}) copy-start(f32[3,512]{1,0:T(4,128)} %param.17) | copy-start | bytes 18436
  7.2 117.5 %all-gather.3.cloned.1.call-start = ((), (), s32[]{:S(2)}) async-start(), calls=%async_computation.1 | async-start | bytes 9437184 | tf_op jit(solution)/shard_map/all_gather | solution.py:353
  11.7 120.1 %copy-start.19 = (bf16[272,896]{1,0:T(8,128)(2,1)}, bf16[272,896]{1,0:T(8,128)(2,1)S(1)}, u32[]{:S(2)}) copy-start(bf16[272,896]{1,0:T(8,128)(2,1)S(1)} %get-tuple-element.149.refs_0_) | copy-start | bytes 1462276
  11.7 48.0 %collective-permute-start.1 = (bf16[272,896]{1,0:T(8,128)(2,1)}, bf16[272,896]{1,0:T(8,128)(2,1)S(1)}, u32[]{:S(2)}, u32[]{:S(2)}) collective-permute-start(bf16[272,896]{1,0:T(8,128)(2,1)} %get-tuple-element.373), channel_id=1, source_target_pairs={{0,4},{4,0},{8,12},{12,8},{1,5},{5,1},{9,13},{13,9},{2,6},{6,2},{1... | collective-permute-start | bytes 1462280 | tf_op jit(solution)/shard_map/ppermute | solution.py:238
  15.4 44.2 %collective-permute-start.2 = (bf16[272,896]{1,0:T(8,128)(2,1)}, bf16[272,896]{1,0:T(8,128)(2,1)S(1)}, u32[]{:S(2)}, u32[]{:S(2)}) collective-permute-start(bf16[272,896]{1,0:T(8,128)(2,1)} %fusion.34), channel_id=1, source_target_pairs={{0,8},{4,12},{8,0},{12,4},{1,9},{5,13},{9,1},{13,5},{2,10},{6,14},... | collective-permute-start | bytes 1462280 | tf_op jit(solution)/shard_map/ppermute | solution.py:238
  17.0 42.6 %collective-permute-start.3 = (bf16[272,896]{1,0:T(8,128)(2,1)}, bf16[272,896]{1,0:T(8,128)(2,1)S(1)}, u32[]{:S(2)}, u32[]{:S(2)}) collective-permute-start(bf16[272,896]{1,0:T(8,128)(2,1)} %get-tuple-element.371), channel_id=1, source_target_pairs={{0,12},{4,8},{8,4},{12,0},{1,13},{5,9},{9,5},{13,1},{2,14},{6,10},... | collective-permute-start | bytes 1462280 | tf_op jit(solution)/shard_map/ppermute | solution.py:238
  18.5 41.3 %collective-permute-start.4 = (bf16[128,2048]{1,0:T(8,128)(2,1)S(1)}, bf16[128,2048]{1,0:T(8,128)(2,1)S(1)}, u32[]{:S(2)}, u32[]{:S(2)}) collective-permute-start(bf16[128,2048]{1,0:T(8,128)(2,1)S(1)} %maximum_select_fusion.2), channel_id=1, source_target_pairs={{0,8},{8,0},{1,9},{9,1},{2,10},{10,2},{3,11},{11,3},{4,12},{12,4},... | collective-permute-start | bytes 1572872 | tf_op jit(solution)/shard_map/ppermute | solution.py:238
  20.6 38.2 %collective-permute-start = (bf16[256,896]{1,0:T(8,128)(2,1)S(1)}, bf16[256,896]{1,0:T(8,128)(2,1)S(1)}, u32[]{:S(2)}, u32[]{:S(2)}) collective-permute-start(bf16[256,896]{1,0:T(8,128)(2,1)S(1)} %pad_maximum_fusion.12), channel_id=1, source_target_pairs={{0,16},{16,0},{1,17},{17,1},{2,18},{18,2},{3,19},{19,3},{4,20},{20... | collective-permute-start | bytes 1376264 | tf_op jit(solution)/shard_map/ppermute | solution.py:238
  59.6 72.2 %copy-start.21 = (bf16[272,896]{1,0:T(8,128)(2,1)}, bf16[272,896]{1,0:T(8,128)(2,1)S(1)}, u32[]{:S(2)}) copy-start(bf16[272,896]{1,0:T(8,128)(2,1)S(1)} %collective-permute-done.1.refs_1_) | copy-start | bytes 1462276
  59.6 67.4 %copy-start.23 = (bf16[272,896]{1,0:T(8,128)(2,1)}, bf16[272,896]{1,0:T(8,128)(2,1)S(1)}, u32[]{:S(2)}) copy-start(bf16[272,896]{1,0:T(8,128)(2,1)S(1)} %collective-permute-done.2.refs_2_) | copy-start | bytes 1462276
  59.7 67.4 %copy-start.25 = (bf16[272,896]{1,0:T(8,128)(2,1)}, bf16[272,896]{1,0:T(8,128)(2,1)S(1)}, u32[]{:S(2)}) copy-start(bf16[272,896]{1,0:T(8,128)(2,1)S(1)} %collective-permute-done.3.refs_3_) | copy-start | bytes 1462276
  61.1 134.1 %all-gather.5.cloned.1.call-start = ((), (), s32[]{:S(2)}) async-start(), calls=%async_computation.2 | async-start | bytes 9437184 | tf_op jit(solution)/shard_map/all_gather | solution.py:353
  61.3 9.1 %collective-permute-start.6 = (bf16[640,256]{1,0:T(8,128)(2,1)S(1)}, bf16[640,256]{1,0:T(8,128)(2,1)S(1)}, u32[]{:S(2)}, u32[]{:S(2)}) collective-permute-start(bf16[640,256]{1,0:T(8,128)(2,1)S(1)} %pad_maximum_fusion.14), channel_id=1, source_target_pairs={{0,4},{4,0},{8,12},{12,8},{1,5},{5,1},{9,13},{13,9},{2,6},{6,2},{1... | collective-permute-start | bytes 983048 | tf_op jit(solution)/shard_map/ppermute | solution.py:238
  62.0 61.6 %collective-permute-start.5 = (bf16[768,896]{1,0:T(8,128)(2,1)S(1)}, bf16[768,896]{1,0:T(8,128)(2,1)S(1)}, u32[]{:S(2)}, u32[]{:S(2)}) collective-permute-start(bf16[768,896]{1,0:T(8,128)(2,1)S(1)} %pad_maximum_fusion.6), channel_id=1, source_target_pairs={{0,16},{16,0},{1,17},{17,1},{2,18},{18,2},{3,19},{19,3},{4,20},{20... | collective-permute-start | bytes 4128776 | tf_op jit(solution)/shard_map/ppermute | solution.py:238
  65.5 37.6 %collective-permute-start.7 = (bf16[640,256]{1,0:T(8,128)(2,1)S(1)}, bf16[640,256]{1,0:T(8,128)(2,1)S(1)}, u32[]{:S(2)}, u32[]{:S(2)}) collective-permute-start(bf16[640,256]{1,0:T(8,128)(2,1)S(1)} %pad_maximum_fusion.15), channel_id=1, source_target_pairs={{0,8},{4,12},{8,0},{12,4},{1,9},{5,13},{9,1},{13,5},{2,10},{6,14},... | collective-permute-start | bytes 983048 | tf_op jit(solution)/shard_map/ppermute | solution.py:238
  66.5 53.6 %collective-permute-start.9 = (bf16[128,2048]{1,0:T(8,128)(2,1)S(1)}, bf16[128,2048]{1,0:T(8,128)(2,1)S(1)}, u32[]{:S(2)}, u32[]{:S(2)}) collective-permute-start(bf16[128,2048]{1,0:T(8,128)(2,1)S(1)} %maximum_select_fusion.3), channel_id=1, source_target_pairs={{0,8},{8,0},{1,9},{9,1},{2,10},{10,2},{3,11},{11,3},{4,12},{12,4},... | collective-permute-start | bytes 1572872 | tf_op jit(solution)/shard_map/ppermute | solution.py:238
  67.8 50.9 %collective-permute-start.8 = (bf16[640,256]{1,0:T(8,128)(2,1)S(1)}, bf16[640,256]{1,0:T(8,128)(2,1)S(1)}, u32[]{:S(2)}, u32[]{:S(2)}) collective-permute-start(bf16[640,256]{1,0:T(8,128)(2,1)S(1)} %pad_maximum_fusion.16), channel_id=1, source_target_pairs={{0,12},{4,8},{8,4},{12,0},{1,13},{5,9},{9,5},{13,1},{2,14},{6,10},... | collective-permute-start | bytes 983048 | tf_op jit(solution)/shard_map/ppermute | solution.py:238
  103.1 85.5 %copy-start.6 = (bf16[640,256]{1,0:T(8,128)(2,1)}, bf16[640,256]{1,0:T(8,128)(2,1)S(1)}, u32[]{:S(2)}) copy-start(bf16[640,256]{1,0:T(8,128)(2,1)S(1)} %collective-permute-done.7.refs_2_) | copy-start | bytes 983044
  118.8 69.8 %copy-start.8 = (bf16[640,256]{1,0:T(8,128)(2,1)}, bf16[640,256]{1,0:T(8,128)(2,1)S(1)}, u32[]{:S(2)}) copy-start(bf16[640,256]{1,0:T(8,128)(2,1)S(1)} %collective-permute-done.8.refs_3_) | copy-start | bytes 983044
  127.0 286.0 %reduce-scatter.2.cloned.1.call-start = ((), (), s32[]{:S(2)}) async-start(), calls=%async_computation.3 | async-start | bytes 9437184 | tf_op jit(solution)/shard_map/reduce_scatter | solution.py:420
  130.1 58.4 %collective-permute-start.10 = (bf16[640,1024]{1,0:T(8,128)(2,1)}, bf16[640,1024]{1,0:T(8,128)(2,1)S(1)}, u32[]{:S(2)}, u32[]{:S(2)}) collective-permute-start(bf16[640,1024]{1,0:T(8,128)(2,1)} %pad_maximum_fusion.7), channel_id=1, source_target_pairs={{0,16},{16,0},{1,17},{17,1},{2,18},{18,2},{3,19},{19,3},{4,20},{20... | collective-permute-start | bytes 3932168 | tf_op jit(solution)/shard_map/ppermute | solution.py:238
  206.3 16.4 %collective-permute-start.11 = (bf16[160,1024]{1,0:T(8,128)(2,1)S(1)}, bf16[160,1024]{1,0:T(8,128)(2,1)S(1)}, u32[]{:S(2)}, u32[]{:S(2)}) collective-permute-start(bf16[160,1024]{1,0:T(8,128)(2,1)S(1)} %get-tuple-element.174), channel_id=1, source_target_pairs={{0,16},{16,0},{1,17},{17,1},{2,18},{18,2},{3,19},{19,3},{4,20},{20... | collective-permute-start | bytes 983048 | tf_op jit(solution)/shard_map/ppermute | solution.py:238
  223.4 11.8 %collective-permute-start.12 = (bf16[112,1024]{1,0:T(8,128)(2,1)S(1)}, bf16[112,1024]{1,0:T(8,128)(2,1)S(1)}, u32[]{:S(2)}, u32[]{:S(2)}) collective-permute-start(bf16[112,1024]{1,0:T(8,128)(2,1)S(1)} %get-tuple-element.190), channel_id=1, source_target_pairs={{0,16},{16,0},{1,17},{17,1},{2,18},{18,2},{3,19},{19,3},{4,20},{20... | collective-permute-start | bytes 688136 | tf_op jit(solution)/shard_map/ppermute | solution.py:238
  235.3 11.4 %collective-permute-start.13 = (bf16[112,1024]{1,0:T(8,128)(2,1)}, bf16[112,1024]{1,0:T(8,128)(2,1)S(1)}, u32[]{:S(2)}, u32[]{:S(2)}) collective-permute-start(bf16[112,1024]{1,0:T(8,128)(2,1)} %get-tuple-element.204), channel_id=1, source_target_pairs={{0,16},{16,0},{1,17},{17,1},{2,18},{18,2},{3,19},{19,3},{4,20},{20... | collective-permute-start | bytes 688136 | tf_op jit(solution)/shard_map/ppermute | solution.py:238
  246.7 16.4 %collective-permute-start.14 = (bf16[144,1024]{1,0:T(8,128)(2,1)S(1)}, bf16[144,1024]{1,0:T(8,128)(2,1)S(1)}, u32[]{:S(2)}, u32[]{:S(2)}) collective-permute-start(bf16[144,1024]{1,0:T(8,128)(2,1)S(1)} %copy-done.55), channel_id=1, source_target_pairs={{0,16},{16,0},{1,17},{17,1},{2,18},{18,2},{3,19},{19,3},{4,20},{20... | collective-permute-start | bytes 884744 | tf_op jit(solution)/shard_map/ppermute | solution.py:238
  263.1 13.1 %collective-permute-start.15 = (bf16[112,1024]{1,0:T(8,128)(2,1)S(1)}, bf16[112,1024]{1,0:T(8,128)(2,1)S(1)}, u32[]{:S(2)}, u32[]{:S(2)}) collective-permute-start(bf16[112,1024]{1,0:T(8,128)(2,1)S(1)} %copy-done.57), channel_id=1, source_target_pairs={{0,16},{16,0},{1,17},{17,1},{2,18},{18,2},{3,19},{19,3},{4,20},{20... | collective-permute-start | bytes 688136 | tf_op jit(solution)/shard_map/ppermute | solution.py:238
  281.8 10.8 %collective-permute-start.17 = (bf16[2,2,2,128,2048]{4,3,0,2,1:T(8,128)(2,1)}, bf16[2,2,2,128,2048]{4,3,0,2,1:T(8,128)(2,1)}, u32[]{:S(2)}, u32[]{:S(2)}) collective-permute-start(bf16[2,2,2,128,2048]{4,3,0,2,1:T(8,128)(2,1)} %copy_bitcast_fusion), channel_id=1, source_target_pairs={{0,1},{1,0},{2,3},{3,2},{4,5},{5,4},{6,7},{7,6},{8,9},{9,8},{10,11... | collective-permute-start | bytes 12582920 | tf_op jit(solution)/shard_map/ppermute | solution.py:238
  286.8 28.6 %collective-permute-start.16 = (bf16[256,896]{1,0:T(8,128)(2,1)S(1)}, bf16[256,896]{1,0:T(8,128)(2,1)S(1)}, u32[]{:S(2)}, u32[]{:S(2)}) collective-permute-start(bf16[256,896]{1,0:T(8,128)(2,1)S(1)} %constant_dynamic-slice_fusion.7), channel_id=1, source_target_pairs={{0,16},{16,0},{1,17},{17,1},{2,18},{18,2},{3,19},{19,3},{4,20},{20... | collective-permute-start | bytes 1376264 | tf_op jit(solution)/shard_map/ppermute | solution.py:238
  289.0 14.8 %collective-permute-start.18 = (bf16[640,256]{1,0:T(8,128)(2,1)S(1)}, bf16[640,256]{1,0:T(8,128)(2,1)S(1)}, u32[]{:S(2)}, u32[]{:S(2)}) collective-permute-start(bf16[640,256]{1,0:T(8,128)(2,1)S(1)} %get-tuple-element.321), channel_id=1, source_target_pairs={{0,4},{4,0},{8,12},{12,8},{1,5},{5,1},{9,13},{13,9},{2,6},{6,2},{1... | collective-permute-start | bytes 983048 | tf_op jit(solution)/shard_map/ppermute | solution.py:238
  289.1 17.5 %collective-permute-start.19 = (bf16[640,256]{1,0:T(8,128)(2,1)S(1)}, bf16[640,256]{1,0:T(8,128)(2,1)S(1)}, u32[]{:S(2)}, u32[]{:S(2)}) collective-permute-start(bf16[640,256]{1,0:T(8,128)(2,1)S(1)} %get-tuple-element.320), channel_id=1, source_target_pairs={{0,8},{4,12},{8,0},{12,4},{1,9},{5,13},{9,1},{13,5},{2,10},{6,14},... | collective-permute-start | bytes 983048 | tf_op jit(solution)/shard_map/ppermute | solution.py:238
  290.9 24.6 %collective-permute-start.20 = (bf16[640,256]{1,0:T(8,128)(2,1)S(1)}, bf16[640,256]{1,0:T(8,128)(2,1)S(1)}, u32[]{:S(2)}, u32[]{:S(2)}) collective-permute-start(bf16[640,256]{1,0:T(8,128)(2,1)S(1)} %get-tuple-element.319), channel_id=1, source_target_pairs={{0,12},{4,8},{8,4},{12,0},{1,13},{5,9},{9,5},{13,1},{2,14},{6,10},... | collective-permute-start | bytes 983048 | tf_op jit(solution)/shard_map/ppermute | solution.py:238
  316.5 31.2 %collective-permute-start.21 = (bf16[256,896]{1,0:T(8,128)(2,1)S(1)}, bf16[256,896]{1,0:T(8,128)(2,1)S(1)}, u32[]{:S(2)}, u32[]{:S(2)}) collective-permute-start(bf16[256,896]{1,0:T(8,128)(2,1)S(1)} %constant_dynamic-slice_fusion.2), channel_id=1, source_target_pairs={{0,16},{16,0},{1,17},{17,1},{2,18},{18,2},{3,19},{19,3},{4,20},{20... | collective-permute-start | bytes 1376264 | tf_op jit(solution)/shard_map/ppermute | solution.py:238
  318.2 24.1 %collective-permute-start.22 = (bf16[2,2,128,1024]{3,2,0,1:T(8,128)(2,1)S(1)}, bf16[2,2,128,1024]{3,2,0,1:T(8,128)(2,1)S(1)}, u32[]{:S(2)}, u32[]{:S(2)}) collective-permute-start(bf16[2,2,128,1024]{3,2,0,1:T(8,128)(2,1)S(1)} %dynamic-slice_bitcast_fusion.1), channel_id=1, source_target_pairs={{0,2},{2,0},{1,3},{3,1},{4,6},{6,4},{5,7},{7,5},{8,10},{10,8},{9,1... | collective-permute-start | bytes 3145736 | tf_op jit(solution)/shard_map/ppermute | solution.py:238
  319.8 27.5 %collective-permute-start.23 = (bf16[2,2,128,1024]{3,2,0,1:T(8,128)(2,1)S(1)}, bf16[2,2,128,1024]{3,2,0,1:T(8,128)(2,1)S(1)}, u32[]{:S(2)}, u32[]{:S(2)}) collective-permute-start(bf16[2,2,128,1024]{3,2,0,1:T(8,128)(2,1)S(1)} %dynamic-slice_bitcast_fusion), channel_id=1, source_target_pairs={{0,4},{4,0},{1,5},{5,1},{2,6},{6,2},{3,7},{7,3},{8,12},{12,8},{9,1... | collective-permute-start | bytes 3145736 | tf_op jit(solution)/shard_map/ppermute | solution.py:238
  321.4 4.6 %collective-permute-start.24 = (f32[20480]{0:T(1024)S(1)}, f32[20480]{0:T(1024)S(1)}, u32[]{:S(2)}, u32[]{:S(2)}) collective-permute-start(f32[20480]{0:T(1024)S(1)} %pad_maximum_fusion.17), channel_id=1, source_target_pairs={{0,1},{1,0},{2,3},{3,2},{4,5},{5,4},{6,7},{7,6},{8,9},{9,8},{10,11... | collective-permute-start | bytes 245768 | tf_op jit(solution)/shard_map/ppermute | solution.py:238
  349.3 15.8 %collective-permute-start.27 = (bf16[2,128,1024]{2,1,0:T(8,128)(2,1)}, bf16[2,128,1024]{2,1,0:T(8,128)(2,1)S(1)}, u32[]{:S(2)}, u32[]{:S(2)}) collective-permute-start(bf16[2,128,1024]{2,1,0:T(8,128)(2,1)} %dynamic-slice_bitcast_fusion.2), channel_id=1, source_target_pairs={{0,2},{2,0},{1,3},{3,1},{4,6},{6,4},{5,7},{7,5},{8,10},{10,8},{9,1... | collective-permute-start | bytes 1572872 | tf_op jit(solution)/shard_map/ppermute | solution.py:238
  350.8 14.9 %collective-permute-start.26 = (bf16[2,128,1024]{2,1,0:T(8,128)(2,1)S(1)}, bf16[2,128,1024]{2,1,0:T(8,128)(2,1)S(1)}, u32[]{:S(2)}, u32[]{:S(2)}) collective-permute-start(bf16[2,128,1024]{2,1,0:T(8,128)(2,1)S(1)} %dynamic-slice_bitcast_fusion.3), channel_id=1, source_target_pairs={{0,4},{4,0},{1,5},{5,1},{2,6},{6,2},{3,7},{7,3},{8,12},{12,8},{9,1... | collective-permute-start | bytes 1572872 | tf_op jit(solution)/shard_map/ppermute | solution.py:238
  352.0 23.5 %collective-permute-start.25 = (bf16[256,896]{1,0:T(8,128)(2,1)S(1)}, bf16[256,896]{1,0:T(8,128)(2,1)S(1)}, u32[]{:S(2)}, u32[]{:S(2)}) collective-permute-start(bf16[256,896]{1,0:T(8,128)(2,1)S(1)} %constant_dynamic-slice_fusion.1), channel_id=1, source_target_pairs={{0,16},{16,0},{1,17},{17,1},{2,18},{18,2},{3,19},{19,3},{4,20},{20... | collective-permute-start | bytes 1376264 | tf_op jit(solution)/shard_map/ppermute | solution.py:238
  356.2 8.3 %collective-permute-start.28 = (f32[20480]{0:T(1024)S(1)}, f32[20480]{0:T(1024)S(1)}, u32[]{:S(2)}, u32[]{:S(2)}) collective-permute-start(f32[20480]{0:T(1024)S(1)} %add.350), channel_id=1, source_target_pairs={{0,2},{2,0},{1,3},{3,1},{4,6},{6,4},{5,7},{7,5},{8,10},{10,8},{9,1... | collective-permute-start | bytes 245768 | tf_op jit(solution)/shard_map/ppermute | solution.py:238
  356.7 18.8 %collective-permute-start.29 = (bf16[256,896]{1,0:T(8,128)(2,1)}, bf16[256,896]{1,0:T(8,128)(2,1)S(1)}, u32[]{:S(2)}, u32[]{:S(2)}) collective-permute-start(bf16[256,896]{1,0:T(8,128)(2,1)} %add_convert_fusion.2), channel_id=1, source_target_pairs={{0,4},{4,0},{8,12},{12,8},{1,5},{5,1},{9,13},{13,9},{2,6},{6,2},{1... | collective-permute-start | bytes 1376264 | tf_op jit(solution)/shard_map/ppermute | solution.py:238
  376.4 33.0 %collective-permute-start.31 = (bf16[128,2048]{1,0:T(8,128)(2,1)}, bf16[128,2048]{1,0:T(8,128)(2,1)S(1)}, u32[]{:S(2)}, u32[]{:S(2)}) collective-permute-start(bf16[128,2048]{1,0:T(8,128)(2,1)} %slice_bitcast_fusion.2), channel_id=1, source_target_pairs={{0,8},{8,0},{1,9},{9,1},{2,10},{10,2},{3,11},{11,3},{4,12},{12,4},... | collective-permute-start | bytes 1572872 | tf_op jit(solution)/shard_map/ppermute | solution.py:238
  378.8 23.7 %collective-permute-start.30 = (bf16[256,896]{1,0:T(8,128)(2,1)}, bf16[256,896]{1,0:T(8,128)(2,1)}, u32[]{:S(2)}, u32[]{:S(2)}) collective-permute-start(bf16[256,896]{1,0:T(8,128)(2,1)} %constant_dynamic-slice_fusion), channel_id=1, source_target_pairs={{0,16},{16,0},{1,17},{17,1},{2,18},{18,2},{3,19},{19,3},{4,20},{20... | collective-permute-start | bytes 1376264 | tf_op jit(solution)/shard_map/ppermute | solution.py:238
  382.1 27.3 %collective-permute-start.32 = (bf16[256,896]{1,0:T(8,128)(2,1)}, bf16[256,896]{1,0:T(8,128)(2,1)}, u32[]{:S(2)}, u32[]{:S(2)}) collective-permute-start(bf16[256,896]{1,0:T(8,128)(2,1)} %add_convert_fusion.1), channel_id=1, source_target_pairs={{0,8},{4,12},{8,0},{12,4},{1,9},{5,13},{9,1},{13,5},{2,10},{6,14},... | collective-permute-start | bytes 1376264 | tf_op jit(solution)/shard_map/ppermute | solution.py:238
  382.2 4.7 %collective-permute-start.33 = (f32[20480]{0:T(1024)}, f32[20480]{0:T(1024)S(1)}, u32[]{:S(2)}, u32[]{:S(2)}) collective-permute-start(f32[20480]{0:T(1024)} %add.357), channel_id=1, source_target_pairs={{0,4},{4,0},{1,5},{5,1},{2,6},{6,2},{3,7},{7,3},{8,12},{12,8},{9,1... | collective-permute-start | bytes 245768 | tf_op jit(solution)/shard_map/ppermute | solution.py:238
  409.4 16.0 %collective-permute-start.34 = (bf16[256,896]{1,0:T(8,128)(2,1)}, bf16[256,896]{1,0:T(8,128)(2,1)}, u32[]{:S(2)}, u32[]{:S(2)}) collective-permute-start(bf16[256,896]{1,0:T(8,128)(2,1)} %add_convert_fusion), channel_id=1, source_target_pairs={{0,12},{4,8},{8,4},{12,0},{1,13},{5,9},{9,5},{13,1},{2,14},{6,10},... | collective-permute-start | bytes 1376264 | tf_op jit(solution)/shard_map/ppermute | solution.py:238
  410.7 13.7 %collective-permute-start.36 = (f32[20480]{0:T(1024)}, f32[20480]{0:T(1024)}, u32[]{:S(2)}, u32[]{:S(2)}) collective-permute-start(f32[20480]{0:T(1024)} %add.363), channel_id=1, source_target_pairs={{0,8},{8,0},{1,9},{9,1},{2,10},{10,2},{3,11},{11,3},{4,12},{12,4},... | collective-permute-start | bytes 245768 | tf_op jit(solution)/shard_map/ppermute | solution.py:238
  414.2 19.3 %collective-permute-start.35 = (bf16[128,2048]{1,0:T(8,128)(2,1)S(1)}, bf16[128,2048]{1,0:T(8,128)(2,1)S(1)}, u32[]{:S(2)}, u32[]{:S(2)}) collective-permute-start(bf16[128,2048]{1,0:T(8,128)(2,1)S(1)} %slice_bitcast_fusion), channel_id=1, source_target_pairs={{0,8},{8,0},{1,9},{9,1},{2,10},{10,2},{3,11},{11,3},{4,12},{12,4},... | collective-permute-start | bytes 1572872 | tf_op jit(solution)/shard_map/ppermute | solution.py:238
  436.0 8.1 %collective-permute-start.37 = (f32[20480]{0:T(1024)S(1)}, f32[20480]{0:T(1024)S(1)}, u32[]{:S(2)}, u32[]{:S(2)}) collective-permute-start(f32[20480]{0:T(1024)S(1)} %add.364), channel_id=1, source_target_pairs={{0,16},{16,0},{1,17},{17,1},{2,18},{18,2},{3,19},{19,3},{4,20},{20... | collective-permute-start | bytes 245768 | tf_op jit(solution)/shard_map/ppermute | solution.py:238
  (62 other events, 642.6 us)
Sparse Core Ops, SparseCore 0:
  61.1 56.1 all-gather.2
  127.1 54.8 all-gather.4
  245.6 83.7 reduce-scatter.1

commit v4 on v3

--- a/solution.py
+++ b/solution.py
@@ -386,7 +386,7 @@
 
         out_rows = acts.shape[1]
         out_part = dot(acts, grad_all, ((0,), (0,))).astype(BF)
-        cuts = [out_rows * i // 40 for i in (0, 10, 17, 24, 33, 40)]
+        cuts = [out_rows * i // 40 for i in (0, 7, 17, 24, 32, 40)]
         out_send = [
             [slot(out_part, k, 1)[cuts[i] : cuts[i + 1]] for i in range(5)] for k in range(groups)
         ]
@@ -401,33 +401,53 @@
         def send_out(i):
             return [swap_with(out_send[k][i], "h", k, groups) for k in range(1, groups)]
 
+        def team_sum(values):
+            return lax.psum_scatter(
+                values.reshape(2, -1, width), ("x", "y", "core"), scatter_dimension=1, tiled=True
+            )
+
         out_0 = send_out(0)
+        acts, out_ws = step(acts, out_ws)
+        branch = dot(acts, stacked(out_ws, 0), ((1,), (0,))).astype(BF)
+        branch, out_ws, out_0, out_send = step(branch, out_ws, out_0, out_send)
+        branch_sum = team_sum(branch)
+        out_1 = send_out(1)
         out_ws, qkv, lse = step(out_ws, qkv, lse)
         context_grad = dot(grad_all, out_ws[0], ((1,), (1,))).astype(BF)
         mixed_grad = attention_grad(qkv, context_grad, lse, tables, segments)
-        mixed_grad, out_0, out_send = step(mixed_grad, out_0, out_send)
-
-        out_1 = send_out(1)
+        mixed_grad, out_1, out_send = step(mixed_grad, out_1, out_send)
+
+        out_2 = send_out(2)
         mixed_grad, before = step(mixed_grad, before)
         activated_grad = dot(after(grad_all, mixed_grad), out_ws[1], ((1,), (1,)))
         before_grad = jax.vjp(gelu_tanh, before)[1](activated_grad)[0].astype(BF)
         into = stacked([mixed_grad, before_grad], 1)
-        out_w = stacked(out_ws, 0)
-        into, out_1, out_w, out_send = step(into, out_1, out_w, out_send)
-        out_2 = send_out(2)
-        into, out_w = step(into, out_w)
-        branch = dot(after(acts, into), out_w, ((1,), (0,))).astype(BF)
-        team_sum = lax.psum_scatter(
-            branch.reshape(2, -1, width), ("x", "y", "core"), scatter_dimension=1, tiled=True
-        )
-        into, branch, out_2, out_send = step(into, branch, out_2, out_send)
+        into, out_2, out_send = step(into, out_2, out_send)
         out_3 = send_out(3)
-        into, branch = step(into, branch)
+        into, in_w = step(into, in_w)
+        terms = dot(into, in_w, ((1,), (1,)))
+        unit = (normed_all.astype(F32) - own_order(ln_bias, 0)) / own_order(ln_gain, 0)
+        gain_sum, shift_sum = jnp.sum(terms * unit, axis=0), jnp.sum(terms, axis=0)
+        terms = terms.astype(BF)
+        terms, gain_sum, shift_sum, into, out_3, out_send = step(
+            terms, gain_sum, shift_sum, into, out_3, out_send
+        )
+        terms_sum = team_sum(terms)
+
+        out_4 = send_out(4)
+        into, normed_all = step(into, normed_all)
         in_part = dot(normed_all, into, ((0,), (0,))).astype(BF)
+        in_part, into, out_4 = step(in_part, into, out_4)
 
         def block(k, m):
             start = k * span + (quad ^ m) * (span // 4)
             return lax.dynamic_slice_in_dim(in_part, start, span // 4, 0)
+
+        def blocks(k, *which):
+            return stacked([block(k, m) for m in which], 0)
+
+        def send_in(*which):
+            return [swap_with(blocks(k, *which), "h", k, groups) for k in range(1, groups)]
 
         def add_up(mine, others):
             mine = mine.astype(F32)
@@ -435,28 +455,12 @@
                 mine = mine + piece.astype(F32)
             return mine
 
-        in_part, out_3, into, out_send = step(in_part, out_3, into, out_send)
-
-        out_4 = send_out(4)
-        into, in_w = step(into, in_w)
-        terms = dot(into, in_w, ((1,), (1,)))
-        unit = (normed_all.astype(F32) - own_order(ln_bias, 0)) / own_order(ln_gain, 0)
-        gain_sum, shift_sum = jnp.sum(terms * unit, axis=0), jnp.sum(terms, axis=0)
-        shape5 = (2, 2, 2, 2, tile, width)
-        terms = terms.astype(BF).reshape(shape5)
-        in_part, terms, gain_sum, shift_sum, out_4 = step(
-            in_part, terms, gain_sum, shift_sum, out_4
-        )
-
-        def send_in(m):
-            return [swap_with(block(k, m), "h", k, groups) for k in range(1, groups)]
-
-        in_1 = send_in(1)
-        got_c = fold_start(terms, 3, "core")
+        in_a = send_in(3, 2)
         out_got = (out_0, out_1, out_2, out_3, out_4)
         out_sum = stacked([add_up(out_send[0][i], got) for i, got in enumerate(out_got)], 0)
         sent = out_sum.astype(BF)
         out_back = [quad_swap(part(sent, quad ^ m, 4, 1), m) for m in (1, 2, 3)]
+        got_m = swap_with(branch_sum[1], "l", 1, 2)
         small = [
             own_order(gain_sum, 0),
             own_order(shift_sum, 0),
@@ -467,63 +471,42 @@
         size = into.shape[1]
         bias = lax.dynamic_update_slice(jnp.zeros((16 * size,), F32), bias, ((team + quad) * size,))
         total = stacked(small + [bias], 0)
-        rows = fold_end(terms, got_c, 3, "core").astype(BF)
-        in_1, rows, out_back, out_sum, total, in_part = step(
-            in_1, rows, out_back, out_sum, total, in_part
-        )
-
-        in_2 = send_in(2)
-        left, right = halves(rows)
-        got_l, got_r = fold_start(left, 2, "y"), fold_start(right, 1, "x")
         total = total + swap_c(total)
-        back_1 = add_up(block(0, 1), in_1).astype(BF)
-        left = fold_end(left, got_l, 2, "y").astype(BF)
-        right = fold_end(right, got_r, 1, "x").astype(BF)
+        total = total + swap_with(total, "y", 1, 2)
+        send_b = [blocks(k, 1, 0) for k in range(groups)]
+        keep_a = blocks(0, 3, 2)
+        in_a, out_back, out_sum, total, send_b, keep_a, got_m = step(
+            in_a, out_back, out_sum, total, send_b, keep_a, got_m
+        )
+
+        in_b = [swap_with(send_b[k], "h", k, groups) for k in range(1, groups)]
+        keep_a, in_a = step(keep_a, in_a)
+        sum_a = unstack(add_up(keep_a, in_a).astype(BF), 2, 0)
+        back_3, back_2 = quad_swap(sum_a[0], 3), quad_swap(sum_a[1], 2)
+        total = total + swap_with(total, "x", 1, 2)
+        total = total + swap_with(total, "l", 1, 2)
         out_pieces = [part(out_sum, quad, 4, 1)] + [p.astype(F32) for p in out_back]
         dense_grad = in_order([p[:local] for p in out_pieces], 0)
         down_grad = in_order([p[local:] for p in out_pieces], 0)
-        in_2, left, right, total, dense_grad, down_grad, back_1, in_part = step(
-            in_2, left, right, total, dense_grad, down_grad, back_1, in_part
-        )
-
-        in_3 = send_in(3)
-        back_1 = quad_swap(back_1, 1)
-        got_l, got_r = fold_start(left, 1, "x"), fold_start(right, 1, "y")
-        total = total + swap_with(total, "y", 1, 2)
-        back_2 = add_up(block(0, 2), in_2).astype(BF)
-        rows = stacked(
-            [fold_end(left, got_l, 1, "x").astype(BF), fold_end(right, got_r, 1, "y").astype(BF)],
-            -1,
-        )
-        in_3, rows, total, back_1, back_2, in_part = step(
-            in_3, rows, total, back_1, back_2, in_part
-        )
-
-        in_0 = send_in(0)
-        got_n = swap_with(rows[1], "l", 1, 2)
-        back_2 = quad_swap(back_2, 2)
-        total = total + swap_with(total, "x", 1, 2)
-        back_3 = add_up(block(0, 3), in_3).astype(BF)
-        in_0, got_n, back_2, back_3, total, in_part = step(
-            in_0, got_n, back_2, back_3, total, in_part
-        )
-
-        back_3 = quad_swap(back_3, 3)
-        got_m = swap_with(team_sum[1], "l", 1, 2)
-        total = total + swap_with(total, "l", 1, 2)
-        normed_grad = own_order(rows[0].astype(F32) + got_n.astype(F32), 1)
-        hidden_grad = jax.vjp(lambda v: layer_norm(v, ln_gain, ln_bias), hidden)[1](normed_grad)[0]
-        input_grad = out_grad.astype(F32) + hidden_grad
-        own_in = add_up(block(0, 0), in_0)
-        back_3, got_m, total, input_grad, own_in = step(back_3, got_m, total, input_grad, own_in)
-
+        branch = own_order(branch_sum[0].astype(F32) + got_m.astype(F32), 1)
+        hidden_out = (hidden + branch + b_dense + b_fc2).astype(BF)
+        in_b, back_3, back_2, total, dense_grad, down_grad, terms_sum, send_b, hidden_out = step(
+            in_b, back_3, back_2, total, dense_grad, down_grad, terms_sum, send_b, hidden_out
+        )
+
+        got_n = swap_with(terms_sum[1], "l", 1, 2)
+        send_b, in_b = step(send_b, in_b)
+        sum_b = unstack(add_up(send_b[0], in_b), 2, 0)
+        back_1 = quad_swap(sum_b[0].astype(BF), 1)
         bit = 1
         while bit < groups:
             total = total + swap_with(total, "h", bit, groups)
             bit *= 2
-        branch = own_order(team_sum[0].astype(F32) + got_m.astype(F32), 1)
-        hidden_out = (hidden + branch + b_dense + b_fc2).astype(BF)
-        pieces = [own_in] + [p.astype(F32) for p in (back_1, back_2, back_3)]
+        back_1, got_n, total, sum_b = step(back_1, got_n, total, sum_b)
+        normed_grad = own_order(terms_sum[0].astype(F32) + got_n.astype(F32), 1)
+        hidden_grad = jax.vjp(lambda v: layer_norm(v, ln_gain, ln_bias), hidden)[1](normed_grad)[0]
+        input_grad = out_grad.astype(F32) + hidden_grad
+        pieces = [sum_b[1]] + [p.astype(F32) for p in (back_1, back_2, back_3)]
         up_grad = in_order([p[:, qkv_cols:] for p in pieces], 1)
         qkv_grad = jnp.stack(
             [in_order([p[:, j * local : (j + 1) * local] for p in pieces], 1) for j in range(3)],

time: 458 us -> 429 us (0.937)
  waiting for transfers between devices: 202 us -> 187 us
  starting transfers between devices: 52.2 us -> 40.6 us
  other arithmetic: 56.2 us -> 48.8 us
  matrix products: 67.3 us -> 72.9 us
    ppermute x38 -> x31, waiting for transfers between devices: 202 us -> 187 us  [swap_with(): return lax.ppermute(values, axis, [(i, i ^ mask) for i in range(size)])]
    ppermute x38 -> x31, starting transfers between devices: 52 us -> 40.2 us  [swap_with(): return lax.ppermute(values, axis, [(i, i ^ mask) for i in range(size)])]
    convert_element_type x11 -> x4, other arithmetic: 15.9 us -> 4.68 us  [the longest x3 3.24 us: body(): pieces = [sum_b[1]] + [p.astype(F32) for p in (back_1, back_2, back_3)]]
    dot_general x7, matrix products: 67.3 us -> 72.9 us  [dot(): lax.dot_general(left, right, (dims, ((), ())), preferred_element_type=F32)]
    select_n x7, other arithmetic: 1.48 us -> 6.62 us  [in_order(): jnp.where(lb == 1, jnp.where(xb == 1, parts[j ^ 3], parts[j ^ 2]), jnp.wh...]
    unnamed x143 -> x189, local copies, waits for them, and re-layouts: 21.8 us -> 20.8 us
  transfers between devices with their start and end apart: 41 -> 35, of which waited for: 22 -> 14; matrix products, arithmetic and copies ran while one was open for 26% -> 25% of each run, Pallas kernels for 5% -> 5%
where the time goes in v4:
time: 429 us; the launch traced here: 424 us
  waiting for transfers between devices  187 us (44%)
  matrix products  72.9 us (17%)
  other arithmetic  48.8 us (11%)
  starting transfers between devices  40.6 us (9%)
  local copies, waits for them, and re-layouts  38.4 us (9%)
  Pallas kernels  20.8 us (5%)
  between operations  15.6 us (4%)
    ppermute x31, waiting for transfers between devices, swap_with(): return lax.ppermute(values, axis, [(i, i ^ mask) for i in range(size)])  187 us
    dot_general x7, matrix products, dot(): lax.dot_general(left, right, (dims, ((), ())), preferred_element_type=F32)  72.9 us
    ppermute x31, starting transfers between devices, swap_with(): return lax.ppermute(values, axis, [(i, i ^ mask) for i in range(size)])  40.2 us
    unnamed x189, local copies, waits for them, and re-layouts  20.8 us
    pallas_call x1, Pallas kernels, attention_grad(): pl.pallas_call(attend_grad_kernel, grid=(sequences,), in_specs=[spec['wid...  11.5 us
  transfers between devices with their start and end apart: 35, of which 14 were waited for; matrix products, arithmetic and copies ran while one was open for 25% of the time, Pallas kernels for 5%

profile of v4, /device:TPU:0, one launch (start us, length us, event | category | flops | bytes accessed | tf_op | source)
XLA Modules:
  0.0 424.4 jit_solution(10962872104876574169)
XLA Ops:
  10.5 2.9 collective-permute-start.1
  13.4 1.5 collective-permute-start.3
  17.3 2.0 collective-permute-start.4
  19.4 2.7 collective-permute-start
  22.1 34.6 %collective-permute-done.refs_4_ = bf16[256,896]{1,0:T(8,128)(2,1)S(1)} collective-permute-done((bf16[256,896]{1,0:T(8,128)(2,1)S(1)}, bf16[256,896]{1,0:T(8,128)(2,1)S(1)}, u32[]{:S(2)}, u32[]{:S(2)}) %collective-permute-start) | collective-permute-done | bytes 458784 | tf_op jit(solution)/shard_map/ppermute | solution.py:238
  61.0 1.7 collective-permute-start.6
  63.0 3.3 collective-permute-start.5
  67.3 1.4 collective-permute-start.9
  70.3 33.7 %collective-permute-done.7.refs_2_ = bf16[640,256]{1,0:T(8,128)(2,1)S(1)} collective-permute-done((bf16[640,256]{1,0:T(8,128)(2,1)S(1)}, bf16[640,256]{1,0:T(8,128)(2,1)S(1)}, u32[]{:S(2)}, u32[]{:S(2)}) %collective-permute-start.7) | collective-permute-done | bytes 327712 | tf_op jit(solution)/shard_map/ppermute | solution.py:238
  104.0 15.7 %collective-permute-done.8.refs_3_ = bf16[640,256]{1,0:T(8,128)(2,1)S(1)} collective-permute-done((bf16[640,256]{1,0:T(8,128)(2,1)S(1)}, bf16[640,256]{1,0:T(8,128)(2,1)S(1)}, u32[]{:S(2)}, u32[]{:S(2)}) %collective-permute-start.8) | collective-permute-done | bytes 327712 | tf_op jit(solution)/shard_map/ppermute | solution.py:238
  121.7 2.9 collective-permute-done.5.refs_5_
  125.6 2.3 pad_maximum_fusion.8
  129.1 1.9 fusion.36
  140.3 12.6 %broadcast_add_fusion.mixed_ref = f32[2048,896]{1,0:T(8,128)S(1)} fusion(f32[896]{0:T(1024)S(1)} %pad_maximum_fusion.21, bf16[2048,2048]{1,0:T(8,128)(2,1)} %bitcast.111, bf16[2048,896]{1,0:T(8,128)(2,1)S(1)} %place.3), kind=kOutput, calls=%fused_computation.22 | convolution fusion | flops 7518027776 | bytes 19402240 | tf_op jit(solution)/shard_map/dot_general | solution.py:242
  152.9 7.0 %attend.1 = (bf16[2048,384]{1,0:T(8,128)(2,1)S(1)}, bf16[2048,128]{1,0:T(8,128)(2,1)S(1)}, f32[4,2,512]{2,1,0:T(2,128)S(1)}) custom-call(f32[2048,896]{1,0:T(8,128)S(1)} %broadcast_add_fusion.mixed_ref, f32[512,128]{1,0:T(8,128)S(1)} %copy-done.9, f32[512,128]{1,0:T(8,128)S(1)} %copy-done.7, f32[512,128]{1,0:T(8,128)S(1)} %copy-done.5, ...), custom_call_target="tpu_custom_call" | custom-call | tf_op jit(solution)/shard_map/attend/pallas_call | solution.py:168
  159.9 3.3 fusion.53
  163.2 1.8 pad_maximum_fusion.1
  165.0 23.6 %collective-permute-done.10.refs_4_ = bf16[640,1024]{1,0:T(8,128)(2,1)S(1)} collective-permute-done((bf16[640,1024]{1,0:T(8,128)(2,1)}, bf16[640,1024]{1,0:T(8,128)(2,1)S(1)}, u32[]{:S(2)}, u32[]{:S(2)}) %collective-permute-start.10) | collective-permute-done | bytes 1310752 | tf_op jit(solution)/shard_map/ppermute | solution.py:238
  192.2 8.9 %convolution_convert_fusion.2 = bf16[640,2048]{1,0:T(8,128)(2,1)S(1)} fusion(bf16[2048,640]{1,0:T(8,128)(2,1)} %pad_maximum_fusion.1, bf16[2048,2048]{1,0:T(8,128)(2,1)} %bitcast.115), kind=kOutput, calls=%fused_computation.24 | convolution fusion | flops 5370019840 | bytes 13631488 | tf_op jit(solution)/shard_map/dot_general | solution.py:242
  204.5 9.4 %convolution_convert_fusion = bf16[2048,2048]{1,0:T(8,128)(2,1)} fusion(bf16[2048,640]{1,0:T(8,128)(2,1)S(1)} %copy-done.40, bf16[512,2048]{1,0:T(8,128)(2,1)S(1)} %copy-done.12, bf16[128,2048]{1,0:T(8,128)(2,1)S(1)} %copy-done.26), kind=kOutput, calls=%fused_computation.1 | convolution fusion | flops 5378146304 | bytes 13631488 | tf_op jit(solution)/shard_map/dot_general | solution.py:242
  213.8 1.8 collective-permute-done.11
  216.4 6.5 %convolution_convert_fusion.3.grad_ref = bf16[2048,128]{1,0:T(8,128)(2,1)S(1)} fusion(bf16[2048,2048]{1,0:T(8,128)(2,1)} %bitcast.116, bf16[128,2048]{1,0:T(8,128)(2,1)} %copy-done.25), kind=kOutput, calls=%fused_computation.29 | convolution fusion | flops 1074003968 | bytes 9437184 | tf_op jit(solution)/shard_map/dot_general | solution.py:242
  223.0 11.5 %attend_grad.1 = bf16[2048,384]{1,0:T(8,128)(2,1)S(1)} custom-call(bf16[2048,384]{1,0:T(8,128)(2,1)S(1)} %copy-done.22, bf16[2048,128]{1,0:T(8,128)(2,1)S(1)} %convolution_convert_fusion.3.grad_ref, f32[4,2,512]{2,1,0:T(2,128)S(1)} %get-tuple-element.185.lse_ref, f32[512,128]{1,0:T(8,128)S(1)} %copy-done.10, f32[512,128]{1,0:T(8,128)S(1)} %copy-done.8, ...), custom_call_target="tpu_custom_call" | custom-call | tf_op jit(solution)/shard_map/attend_grad/pallas_call | solution.py:187
  235.3 2.0 collective-permute-start.13
  237.3 11.3 %fusion.6 = bf16[2048,512]{1,0:T(8,128)(2,1)S(1)} fusion(f32[2048,512]{1,0:T(8,128)S(1)} %copy-done.36, bf16[2048,2048]{1,0:T(8,128)(2,1)} %bitcast.117, bf16[512,2048]{1,0:T(8,128)(2,1)S(1)} %copy-done.12), kind=kOutput, calls=%fused_computation.12 | convolution fusion | flops 4315938816 | bytes 16777216 | tf_op jit(solution)/shard_map/dot_general | solution.py:242
  249.8 2.4 copy-done.3
  252.2 11.4 %fusion.51 = (f32[2048]{0:T(1024)S(1)}, f32[2048]{0:T(1024)S(1)}, bf16[2048,2048]{1,0:T(8,128)(2,1)}) fusion(f32[2048]{0:T(1024)S(1)} %get-tuple-element.380, f32[2048]{0:T(1024)S(1)} %get-tuple-element.379, bf16[2,1024,2048]{2,1,0:T(8,128)(2,1)S(1)} %bitcast.114, bf16[2048,896]{1,0:T(8,128)(2,1)S(1)} %pad_maximum_fusion, bf16[2048,896]{1,0:T(8,128)(2,1)S(1)} %copy-done.3), kind=kOutput, calls=%fused_computation.226 | convolution fusion | flops 7545548800 | bytes 24150016 | tf_op jit(solution)/shard_map/dot_general | solution.py:242
  266.8 12.9 %convolution_convert_fusion.1 = bf16[2048,896]{1,0:T(8,128)(2,1)} fusion(bf16[2048,2048]{1,0:T(8,128)(2,1)} %bitcast.112, bf16[2048,896]{1,0:T(8,128)(2,1)S(1)} %copy-done.32), kind=kOutput, calls=%fused_computation.23 | convolution fusion | flops 7518027776 | bytes 15728640 | tf_op jit(solution)/shard_map/dot_general | solution.py:242
  282.5 2.3 convert_element_type.221
  287.1 2.1 collective-permute-start.16
  289.2 1.6 collective-permute-start.21
  292.3 2.1 collective-permute-start.18
  294.4 1.4 collective-permute-start.19
  297.9 3.6 collective-permute-done.17
  301.4 32.1 %collective-permute-done.18 = bf16[640,256]{1,0:T(8,128)(2,1)S(1)} collective-permute-done((bf16[640,256]{1,0:T(8,128)(2,1)S(1)}, bf16[640,256]{1,0:T(8,128)(2,1)S(1)}, u32[]{:S(2)}, u32[]{:S(2)}) %collective-permute-start.18) | collective-permute-done | bytes 327712 | tf_op jit(solution)/shard_map/ppermute | solution.py:238
  333.5 4.7 %collective-permute-done.19 = bf16[640,256]{1,0:T(8,128)(2,1)S(1)} collective-permute-done((bf16[640,256]{1,0:T(8,128)(2,1)S(1)}, bf16[640,256]{1,0:T(8,128)(2,1)S(1)}, u32[]{:S(2)}, u32[]{:S(2)}) %collective-permute-start.19) | collective-permute-done | bytes 327712 | tf_op jit(solution)/shard_map/ppermute | solution.py:238
  338.4 2.5 collective-permute-start.26
  340.8 1.4 add_convert_fusion
  342.5 1.5 collective-permute-start.25
  346.6 1.5 pad_maximum_fusion.2
  349.1 5.5 %collective-permute-start.27 = (f32[20480]{0:T(1024)S(1)}, f32[20480]{0:T(1024)S(1)}, u32[]{:S(2)}, u32[]{:S(2)}) collective-permute-start(f32[20480]{0:T(1024)S(1)} %add.303), channel_id=1, source_target_pairs={{0,8},{8,0},{1,9},{9,1},{2,10},{10,2},{3,11},{11,3},{4,12},{12,4},... | collective-permute-start | bytes 245768 | tf_op jit(solution)/shard_map/ppermute | solution.py:238
  355.4 26.9 %collective-permute-done.27 = f32[20480]{0:T(1024)S(1)} collective-permute-done((f32[20480]{0:T(1024)S(1)}, f32[20480]{0:T(1024)S(1)}, u32[]{:S(2)}, u32[]{:S(2)}) %collective-permute-start.27) | collective-permute-done | bytes 81952 | tf_op jit(solution)/shard_map/ppermute | solution.py:238
  382.3 2.7 collective-permute-done.23
  385.1 2.2 slice_bitcast_fusion.2
  387.8 1.6 convert_add_fusion
  394.2 4.3 %collective-permute-done.30 = f32[20480]{0:T(1024)} collective-permute-done((f32[20480]{0:T(1024)S(1)}, f32[20480]{0:T(1024)}, u32[]{:S(2)}, u32[]{:S(2)}) %collective-permute-start.30) | collective-permute-done | bytes 81952 | tf_op jit(solution)/shard_map/ppermute | solution.py:238
  401.3 1.4 broadcast_select_fusion.3
  415.6 1.5 pad_maximum_fusion.3
  (348 shorter events, 73.2 us)
Async XLA Ops:
  7.2 121.8 %copy-start = (f32[3,512]{1,0:T(4,128)S(1)}, f32[3,512]{1,0:T(4,128)}, u32[]{:S(2)}) copy-start(f32[3,512]{1,0:T(4,128)} %param.17) | copy-start | bytes 18436
  7.2 118.4 %all-gather.3.cloned.1.call-start = ((), (), s32[]{:S(2)}) async-start(), calls=%async_computation.2 | async-start | bytes 9437184 | tf_op jit(solution)/shard_map/all_gather | solution.py:353
  10.5 121.1 %copy-start.13 = (bf16[272,896]{1,0:T(8,128)(2,1)}, bf16[272,896]{1,0:T(8,128)(2,1)S(1)}, u32[]{:S(2)}) copy-start(bf16[272,896]{1,0:T(8,128)(2,1)S(1)} %get-tuple-element.146.refs_0_) | copy-start | bytes 1462276
  10.5 46.9 %collective-permute-start.1 = (bf16[272,896]{1,0:T(8,128)(2,1)}, bf16[272,896]{1,0:T(8,128)(2,1)S(1)}, u32[]{:S(2)}, u32[]{:S(2)}) collective-permute-start(bf16[272,896]{1,0:T(8,128)(2,1)} %get-tuple-element.375), channel_id=1, source_target_pairs={{0,4},{4,0},{8,12},{12,8},{1,5},{5,1},{9,13},{13,9},{2,6},{6,2},{1... | collective-permute-start | bytes 1462280 | tf_op jit(solution)/shard_map/ppermute | solution.py:238
  13.4 44.0 %collective-permute-start.3 = (bf16[272,896]{1,0:T(8,128)(2,1)S(1)}, bf16[272,896]{1,0:T(8,128)(2,1)S(1)}, u32[]{:S(2)}, u32[]{:S(2)}) collective-permute-start(bf16[272,896]{1,0:T(8,128)(2,1)S(1)} %get-tuple-element.373), channel_id=1, source_target_pairs={{0,12},{4,8},{8,4},{12,0},{1,13},{5,9},{9,5},{13,1},{2,14},{6,10},... | collective-permute-start | bytes 1462280 | tf_op jit(solution)/shard_map/ppermute | solution.py:238
  15.8 41.6 %collective-permute-start.2 = (bf16[272,896]{1,0:T(8,128)(2,1)}, bf16[272,896]{1,0:T(8,128)(2,1)S(1)}, u32[]{:S(2)}, u32[]{:S(2)}) collective-permute-start(bf16[272,896]{1,0:T(8,128)(2,1)} %fusion.32), channel_id=1, source_target_pairs={{0,8},{4,12},{8,0},{12,4},{1,9},{5,13},{9,1},{13,5},{2,10},{6,14},... | collective-permute-start | bytes 1462280 | tf_op jit(solution)/shard_map/ppermute | solution.py:238
  16.0 42.7 %copy-start.82 = (f32[128]{0:T(128)}, f32[128]{0:T(128)S(1)}, u32[]{:S(2)}) copy-start(f32[128]{0:T(128)S(1)} %broadcast_multiply_fusion) | copy-start | bytes 1540
  16.3 42.4 %copy-start.88 = (f32[128]{0:T(128)}, f32[128]{0:T(128)S(1)}, u32[]{:S(2)}) copy-start(f32[128]{0:T(128)S(1)} %fusion.22) | copy-start | bytes 1540
  16.4 42.3 %copy-start.86 = (f32[128]{0:T(128)}, f32[128]{0:T(128)S(1)}, u32[]{:S(2)}) copy-start(f32[128]{0:T(128)S(1)} %fusion.48) | copy-start | bytes 1540
  17.3 40.2 %collective-permute-start.4 = (bf16[128,2048]{1,0:T(8,128)(2,1)S(1)}, bf16[128,2048]{1,0:T(8,128)(2,1)S(1)}, u32[]{:S(2)}, u32[]{:S(2)}) collective-permute-start(bf16[128,2048]{1,0:T(8,128)(2,1)S(1)} %maximum_select_fusion.2), channel_id=1, source_target_pairs={{0,8},{8,0},{1,9},{9,1},{2,10},{10,2},{3,11},{11,3},{4,12},{12,4},... | collective-permute-start | bytes 1572872 | tf_op jit(solution)/shard_map/ppermute | solution.py:238
  19.4 37.2 %collective-permute-start = (bf16[256,896]{1,0:T(8,128)(2,1)S(1)}, bf16[256,896]{1,0:T(8,128)(2,1)S(1)}, u32[]{:S(2)}, u32[]{:S(2)}) collective-permute-start(bf16[256,896]{1,0:T(8,128)(2,1)S(1)} %pad_maximum_fusion.14), channel_id=1, source_target_pairs={{0,16},{16,0},{1,17},{17,1},{2,18},{18,2},{3,19},{19,3},{4,20},{20... | collective-permute-start | bytes 1376264 | tf_op jit(solution)/shard_map/ppermute | solution.py:238
  57.4 74.2 %copy-start.15 = (bf16[272,896]{1,0:T(8,128)(2,1)}, bf16[272,896]{1,0:T(8,128)(2,1)S(1)}, u32[]{:S(2)}) copy-start(bf16[272,896]{1,0:T(8,128)(2,1)S(1)} %collective-permute-done.1.refs_1_) | copy-start | bytes 1462276
  58.7 133.5 %all-gather.5.cloned.1.call-start = ((), (), s32[]{:S(2)}) async-start(), calls=%async_computation.3 | async-start | bytes 9437184 | tf_op jit(solution)/shard_map/all_gather | solution.py:353
  61.0 9.2 %collective-permute-start.6 = (bf16[640,256]{1,0:T(8,128)(2,1)S(1)}, bf16[640,256]{1,0:T(8,128)(2,1)S(1)}, u32[]{:S(2)}, u32[]{:S(2)}) collective-permute-start(bf16[640,256]{1,0:T(8,128)(2,1)S(1)} %pad_maximum_fusion.16), channel_id=1, source_target_pairs={{0,4},{4,0},{8,12},{12,8},{1,5},{5,1},{9,13},{13,9},{2,6},{6,2},{1... | collective-permute-start | bytes 983048 | tf_op jit(solution)/shard_map/ppermute | solution.py:238
  63.0 61.5 %collective-permute-start.5 = (bf16[768,896]{1,0:T(8,128)(2,1)S(1)}, bf16[768,896]{1,0:T(8,128)(2,1)S(1)}, u32[]{:S(2)}, u32[]{:S(2)}) collective-permute-start(bf16[768,896]{1,0:T(8,128)(2,1)S(1)} %pad_maximum_fusion.5), channel_id=1, source_target_pairs={{0,16},{16,0},{1,17},{17,1},{2,18},{18,2},{3,19},{19,3},{4,20},{20... | collective-permute-start | bytes 4128776 | tf_op jit(solution)/shard_map/ppermute | solution.py:238
  66.3 37.6 %collective-permute-start.7 = (bf16[640,256]{1,0:T(8,128)(2,1)S(1)}, bf16[640,256]{1,0:T(8,128)(2,1)S(1)}, u32[]{:S(2)}, u32[]{:S(2)}) collective-permute-start(bf16[640,256]{1,0:T(8,128)(2,1)S(1)} %pad_maximum_fusion.17), channel_id=1, source_target_pairs={{0,8},{4,12},{8,0},{12,4},{1,9},{5,13},{9,1},{13,5},{2,10},{6,14},... | collective-permute-start | bytes 983048 | tf_op jit(solution)/shard_map/ppermute | solution.py:238
  67.3 53.6 %copy-start.42 = (bf16[128,2048]{1,0:T(8,128)(2,1)}, bf16[128,2048]{1,0:T(8,128)(2,1)S(1)}, u32[]{:S(2)}) copy-start(bf16[128,2048]{1,0:T(8,128)(2,1)S(1)} %maximum_select_fusion.3) | copy-start | bytes 1572868
  67.3 53.6 %collective-permute-start.9 = (bf16[128,2048]{1,0:T(8,128)(2,1)S(1)}, bf16[128,2048]{1,0:T(8,128)(2,1)S(1)}, u32[]{:S(2)}, u32[]{:S(2)}) collective-permute-start(bf16[128,2048]{1,0:T(8,128)(2,1)S(1)} %maximum_select_fusion.3), channel_id=1, source_target_pairs={{0,8},{8,0},{1,9},{9,1},{2,10},{10,2},{3,11},{11,3},{4,12},{12,4},... | collective-permute-start | bytes 1572872 | tf_op jit(solution)/shard_map/ppermute | solution.py:238
  68.7 50.9 %collective-permute-start.8 = (bf16[640,256]{1,0:T(8,128)(2,1)S(1)}, bf16[640,256]{1,0:T(8,128)(2,1)S(1)}, u32[]{:S(2)}, u32[]{:S(2)}) collective-permute-start(bf16[640,256]{1,0:T(8,128)(2,1)S(1)} %pad_maximum_fusion.18), channel_id=1, source_target_pairs={{0,12},{4,8},{8,4},{12,0},{1,13},{5,9},{9,5},{13,1},{2,14},{6,10},... | collective-permute-start | bytes 983048 | tf_op jit(solution)/shard_map/ppermute | solution.py:238
  127.9 162.9 %reduce-scatter.3.cloned.1.call-start = ((), (), s32[]{:S(2)}) async-start(), calls=%async_computation.4 | async-start | bytes 9437184 | tf_op jit(solution)/shard_map/reduce_scatter | solution.py:405
  131.0 57.7 %collective-permute-start.10 = (bf16[640,1024]{1,0:T(8,128)(2,1)}, bf16[640,1024]{1,0:T(8,128)(2,1)S(1)}, u32[]{:S(2)}, u32[]{:S(2)}) collective-permute-start(bf16[640,1024]{1,0:T(8,128)(2,1)} %pad_maximum_fusion.6), channel_id=1, source_target_pairs={{0,16},{16,0},{1,17},{17,1},{2,18},{18,2},{3,19},{19,3},{4,20},{20... | collective-permute-start | bytes 3932168 | tf_op jit(solution)/shard_map/ppermute | solution.py:238
  163.2 25.4 %copy-start.4 = (bf16[640,256]{1,0:T(8,128)(2,1)S(1)}, bf16[640,256]{1,0:T(8,128)(2,1)}, u32[]{:S(2)}) copy-start(bf16[640,256]{1,0:T(8,128)(2,1)} %pad_maximum_fusion.15.refs_0_) | copy-start | bytes 983044
  203.8 11.8 %collective-permute-start.11 = (bf16[112,1024]{1,0:T(8,128)(2,1)S(1)}, bf16[112,1024]{1,0:T(8,128)(2,1)}, u32[]{:S(2)}, u32[]{:S(2)}) collective-permute-start(bf16[112,1024]{1,0:T(8,128)(2,1)S(1)} %get-tuple-element.169), channel_id=1, source_target_pairs={{0,16},{16,0},{1,17},{17,1},{2,18},{18,2},{3,19},{19,3},{4,20},{20... | collective-permute-start | bytes 688136 | tf_op jit(solution)/shard_map/ppermute | solution.py:238
  215.6 166.7 %reduce-scatter.5.cloned.1.call-start = ((), (), s32[]{:S(2)}) async-start(), calls=%async_computation.5 | async-start | bytes 9437184 | tf_op jit(solution)/shard_map/reduce_scatter | solution.py:405
  215.8 18.8 %collective-permute-start.12 = (bf16[160,1024]{1,0:T(8,128)(2,1)}, bf16[160,1024]{1,0:T(8,128)(2,1)S(1)}, u32[]{:S(2)}, u32[]{:S(2)}) collective-permute-start(bf16[160,1024]{1,0:T(8,128)(2,1)} %get-tuple-element.186), channel_id=1, source_target_pairs={{0,16},{16,0},{1,17},{17,1},{2,18},{18,2},{3,19},{19,3},{4,20},{20... | collective-permute-start | bytes 983048 | tf_op jit(solution)/shard_map/ppermute | solution.py:238
  223.0 14.4 %copy-start.36 = (f32[2048,512]{1,0:T(8,128)S(1)}, f32[2048,512]{1,0:T(8,128)}, u32[]{:S(2)}) copy-start(f32[2048,512]{1,0:T(8,128)} %get-tuple-element.200) | copy-start | bytes 12582916
  223.0 26.8 %slice-start = ((s8[8388608]{0:T(1024)(128)(4,1)}), s8[4194304]{0:T(1024)(128)(4,1)S(1)}, s32[]{:S(2)}) async-start(s8[8388608]{0:T(1024)(128)(4,1)} %bitcast.113), calls=%async_computation.6 | async-start | bytes 8388608
  234.5 15.3 %slice-start.1 = ((s8[8388608]{0:T(1024)(128)(4,1)}), s8[4194304]{0:T(1024)(128)(4,1)S(1)}, s32[]{:S(2)}) async-start(s8[8388608]{0:T(1024)(128)(4,1)} %bitcast.113), calls=%async_computation.7 | async-start | bytes 8388608
  235.3 13.7 %collective-permute-start.13 = (bf16[112,1024]{1,0:T(8,128)(2,1)S(1)}, bf16[112,1024]{1,0:T(8,128)(2,1)S(1)}, u32[]{:S(2)}, u32[]{:S(2)}) collective-permute-start(bf16[112,1024]{1,0:T(8,128)(2,1)S(1)} %copy-done.78), channel_id=1, source_target_pairs={{0,16},{16,0},{1,17},{17,1},{2,18},{18,2},{3,19},{19,3},{4,20},{20... | collective-permute-start | bytes 688136 | tf_op jit(solution)/shard_map/ppermute | solution.py:238
  249.0 14.5 %copy-start.31 = (bf16[2048,896]{1,0:T(8,128)(2,1)}, bf16[2048,896]{1,0:T(8,128)(2,1)S(1)}, u32[]{:S(2)}) copy-start(bf16[2048,896]{1,0:T(8,128)(2,1)S(1)} %pad_maximum_fusion) | copy-start | bytes 11010052
  249.6 13.9 %collective-permute-start.14 = (bf16[128,1024]{1,0:T(8,128)(2,1)S(1)}, bf16[128,1024]{1,0:T(8,128)(2,1)S(1)}, u32[]{:S(2)}, u32[]{:S(2)}) collective-permute-start(bf16[128,1024]{1,0:T(8,128)(2,1)S(1)} %copy-done.77), channel_id=1, source_target_pairs={{0,16},{16,0},{1,17},{17,1},{2,18},{18,2},{3,19},{19,3},{4,20},{20... | collective-permute-start | bytes 786440 | tf_op jit(solution)/shard_map/ppermute | solution.py:238
  264.7 15.1 %collective-permute-start.15 = (bf16[128,1024]{1,0:T(8,128)(2,1)S(1)}, bf16[128,1024]{1,0:T(8,128)(2,1)S(1)}, u32[]{:S(2)}, u32[]{:S(2)}) collective-permute-start(bf16[128,1024]{1,0:T(8,128)(2,1)S(1)} %copy-done.76), channel_id=1, source_target_pairs={{0,16},{16,0},{1,17},{17,1},{2,18},{18,2},{3,19},{19,3},{4,20},{20... | collective-permute-start | bytes 786440 | tf_op jit(solution)/shard_map/ppermute | solution.py:238
  266.8 12.9 %copy-start.51 = (bf16[128,1024]{1,0:T(8,128)(2,1)S(1)}, bf16[128,1024]{1,0:T(8,128)(2,1)}, u32[]{:S(2)}) copy-start(bf16[128,1024]{1,0:T(8,128)(2,1)} %get-tuple-element.230) | copy-start | bytes 786436
  281.5 7.6 %collective-permute-start.20 = (f32[20480]{0:T(1024)S(1)}, f32[20480]{0:T(1024)S(1)}, u32[]{:S(2)}, u32[]{:S(2)}) collective-permute-start(f32[20480]{0:T(1024)S(1)} %pad_maximum_fusion.19), channel_id=1, source_target_pairs={{0,1},{1,0},{2,3},{3,2},{4,5},{5,4},{6,7},{7,6},{8,9},{9,8},{10,11... | collective-permute-start | bytes 245768 | tf_op jit(solution)/shard_map/ppermute | solution.py:238
  287.1 51.1 %collective-permute-start.16 = (bf16[512,896]{1,0:T(8,128)(2,1)}, bf16[512,896]{1,0:T(8,128)(2,1)}, u32[]{:S(2)}, u32[]{:S(2)}) collective-permute-start(bf16[512,896]{1,0:T(8,128)(2,1)} %pad_maximum_fusion.9), channel_id=1, source_target_pairs={{0,16},{16,0},{1,17},{17,1},{2,18},{18,2},{3,19},{19,3},{4,20},{20... | collective-permute-start | bytes 2752520 | tf_op jit(solution)/shard_map/ppermute | solution.py:238
  289.2 5.2 %collective-permute-start.21 = (f32[20480]{0:T(1024)S(1)}, f32[20480]{0:T(1024)S(1)}, u32[]{:S(2)}, u32[]{:S(2)}) collective-permute-start(f32[20480]{0:T(1024)S(1)} %fusion.50), channel_id=1, source_target_pairs={{0,2},{2,0},{1,3},{3,1},{4,6},{6,4},{5,7},{7,5},{8,10},{10,8},{9,1... | collective-permute-start | bytes 245768 | tf_op jit(solution)/shard_map/ppermute | solution.py:238
  292.0 46.2 %collective-permute-start.22 = (bf16[128,2048]{1,0:T(8,128)(2,1)S(1)}, bf16[128,2048]{1,0:T(8,128)(2,1)S(1)}, u32[]{:S(2)}, u32[]{:S(2)}) collective-permute-start(bf16[128,2048]{1,0:T(8,128)(2,1)S(1)} %slice_bitcast_fusion.1), channel_id=1, source_target_pairs={{0,8},{8,0},{1,9},{9,1},{2,10},{10,2},{3,11},{11,3},{4,12},{12,4},... | collective-permute-start | bytes 1572872 | tf_op jit(solution)/shard_map/ppermute | solution.py:238
  292.2 9.2 %collective-permute-start.17 = (bf16[640,256]{1,0:T(8,128)(2,1)S(1)}, bf16[640,256]{1,0:T(8,128)(2,1)S(1)}, u32[]{:S(2)}, u32[]{:S(2)}) collective-permute-start(bf16[640,256]{1,0:T(8,128)(2,1)S(1)} %get-tuple-element.321), channel_id=1, source_target_pairs={{0,4},{4,0},{8,12},{12,8},{1,5},{5,1},{9,13},{13,9},{2,6},{6,2},{1... | collective-permute-start | bytes 983048 | tf_op jit(solution)/shard_map/ppermute | solution.py:238
  292.3 41.2 %collective-permute-start.18 = (bf16[640,256]{1,0:T(8,128)(2,1)S(1)}, bf16[640,256]{1,0:T(8,128)(2,1)S(1)}, u32[]{:S(2)}, u32[]{:S(2)}) collective-permute-start(bf16[640,256]{1,0:T(8,128)(2,1)S(1)} %get-tuple-element.320), channel_id=1, source_target_pairs={{0,8},{4,12},{8,0},{12,4},{1,9},{5,13},{9,1},{13,5},{2,10},{6,14},... | collective-permute-start | bytes 983048 | tf_op jit(solution)/shard_map/ppermute | solution.py:238
  294.4 43.8 %collective-permute-start.19 = (bf16[640,256]{1,0:T(8,128)(2,1)S(1)}, bf16[640,256]{1,0:T(8,128)(2,1)S(1)}, u32[]{:S(2)}, u32[]{:S(2)}) collective-permute-start(bf16[640,256]{1,0:T(8,128)(2,1)S(1)} %get-tuple-element.319), channel_id=1, source_target_pairs={{0,12},{4,8},{8,4},{12,0},{1,13},{5,9},{9,5},{13,1},{2,14},{6,10},... | collective-permute-start | bytes 983048 | tf_op jit(solution)/shard_map/ppermute | solution.py:238
  338.4 10.7 %collective-permute-start.26 = (f32[20480]{0:T(1024)S(1)}, f32[20480]{0:T(1024)S(1)}, u32[]{:S(2)}, u32[]{:S(2)}) collective-permute-start(f32[20480]{0:T(1024)S(1)} %add.294), channel_id=1, source_target_pairs={{0,4},{4,0},{1,5},{5,1},{2,6},{6,2},{3,7},{7,3},{8,12},{12,8},{9,1... | collective-permute-start | bytes 245768 | tf_op jit(solution)/shard_map/ppermute | solution.py:238
  342.4 39.9 %collective-permute-start.24 = (bf16[256,896]{1,0:T(8,128)(2,1)S(1)}, bf16[256,896]{1,0:T(8,128)(2,1)S(1)}, u32[]{:S(2)}, u32[]{:S(2)}) collective-permute-start(bf16[256,896]{1,0:T(8,128)(2,1)S(1)} %get-tuple-element.335), channel_id=1, source_target_pairs={{0,12},{4,8},{8,4},{12,0},{1,13},{5,9},{9,5},{13,1},{2,14},{6,10},... | collective-permute-start | bytes 1376264 | tf_op jit(solution)/shard_map/ppermute | solution.py:238
  342.5 39.9 %collective-permute-start.25 = (bf16[256,896]{1,0:T(8,128)(2,1)S(1)}, bf16[256,896]{1,0:T(8,128)(2,1)}, u32[]{:S(2)}, u32[]{:S(2)}) collective-permute-start(bf16[256,896]{1,0:T(8,128)(2,1)S(1)} %get-tuple-element.334), channel_id=1, source_target_pairs={{0,8},{4,12},{8,0},{12,4},{1,9},{5,13},{9,1},{13,5},{2,10},{6,14},... | collective-permute-start | bytes 1376264 | tf_op jit(solution)/shard_map/ppermute | solution.py:238
  344.0 41.1 %collective-permute-start.23 = (bf16[512,896]{1,0:T(8,128)(2,1)}, bf16[512,896]{1,0:T(8,128)(2,1)S(1)}, u32[]{:S(2)}, u32[]{:S(2)}) collective-permute-start(bf16[512,896]{1,0:T(8,128)(2,1)} %pad_maximum_fusion.11), channel_id=1, source_target_pairs={{0,16},{16,0},{1,17},{17,1},{2,18},{18,2},{3,19},{19,3},{4,20},{20... | collective-permute-start | bytes 2752520 | tf_op jit(solution)/shard_map/ppermute | solution.py:238
  349.1 33.2 %collective-permute-start.27 = (f32[20480]{0:T(1024)S(1)}, f32[20480]{0:T(1024)S(1)}, u32[]{:S(2)}, u32[]{:S(2)}) collective-permute-start(f32[20480]{0:T(1024)S(1)} %add.303), channel_id=1, source_target_pairs={{0,8},{8,0},{1,9},{9,1},{2,10},{10,2},{3,11},{11,3},{4,12},{12,4},... | collective-permute-start | bytes 245768 | tf_op jit(solution)/shard_map/ppermute | solution.py:238
  387.3 12.9 %collective-permute-start.29 = (bf16[128,2048]{1,0:T(8,128)(2,1)}, bf16[128,2048]{1,0:T(8,128)(2,1)S(1)}, u32[]{:S(2)}, u32[]{:S(2)}) collective-permute-start(bf16[128,2048]{1,0:T(8,128)(2,1)} %slice_bitcast_fusion.2), channel_id=1, source_target_pairs={{0,8},{8,0},{1,9},{9,1},{2,10},{10,2},{3,11},{11,3},{4,12},{12,4},... | collective-permute-start | bytes 1572872 | tf_op jit(solution)/shard_map/ppermute | solution.py:238
  390.3 9.8 %collective-permute-start.28 = (bf16[256,896]{1,0:T(8,128)(2,1)}, bf16[256,896]{1,0:T(8,128)(2,1)}, u32[]{:S(2)}, u32[]{:S(2)}) collective-permute-start(bf16[256,896]{1,0:T(8,128)(2,1)} %slice.686), channel_id=1, source_target_pairs={{0,4},{4,0},{8,12},{12,8},{1,5},{5,1},{9,13},{13,9},{2,6},{6,2},{1... | collective-permute-start | bytes 1376264 | tf_op jit(solution)/shard_map/ppermute | solution.py:238
  391.4 7.1 %collective-permute-start.30 = (f32[20480]{0:T(1024)S(1)}, f32[20480]{0:T(1024)}, u32[]{:S(2)}, u32[]{:S(2)}) collective-permute-start(f32[20480]{0:T(1024)S(1)} %add.304), channel_id=1, source_target_pairs={{0,16},{16,0},{1,17},{17,1},{2,18},{18,2},{3,19},{19,3},{4,20},{20... | collective-permute-start | bytes 245768 | tf_op jit(solution)/shard_map/ppermute | solution.py:238
  (79 other events, 312.5 us)
Sparse Core Ops, SparseCore 0:
  58.8 58.3 all-gather.2
  128.0 53.9 all-gather.4
  215.8 69.1 reduce-scatter.2
  288.7 92.2 reduce-scatter.4

commit v5 on v4

--- a/solution.py
+++ b/solution.py
@@ -12,6 +12,8 @@
 ROT = 32
 EPS = 1e-05
 BLOCK = 128
+ROWS = 512
+CHUNK = 512
 REACH = 256
 SCALE = 1.0 / math.sqrt(HEAD_DIM)
 
@@ -106,7 +108,8 @@
 
 
 def attend_grad_kernel(
-    qkv_ref, grad_ref, lse_ref, cos_ref, a_ref, b_ref, row_ref, col_ref, out_ref, key_ref, value_ref
+    qkv_ref, grad_ref, lse_ref, cos_ref, a_ref, b_ref, row_ref, col_ref, into_ref,
+    out_ref, key_ref, value_ref,
 ):
     length, lanes = grad_ref.shape
     key_ref[...] = jnp.zeros_like(key_ref)
@@ -180,7 +183,7 @@
     )(mixed, *tables, segments[:, None, :], segments.reshape(-1, 1))
 
 
-def attention_grad(qkv, grad, lse, tables, segments):
+def attention_grad(qkv, grad, lse, tables, segments, into):
     sequences, length = segments.shape
     rows, lanes = grad.shape
     spec = attention_specs(length, lanes)
@@ -189,13 +192,128 @@
         grid=(sequences,),
         in_specs=[spec["wide"], spec["slim"], spec["lse"]]
         + [spec["table"]] * 3
-        + [spec["row"], spec["col"]],
+        + [spec["row"], spec["col"], pl.BlockSpec(memory_space=pl.ANY)],
         out_specs=spec["wide"],
-        out_shape=jax.ShapeDtypeStruct((rows, 3 * lanes), BF),
+        out_shape=jax.ShapeDtypeStruct(into.shape, BF),
+        input_output_aliases={8: 0},
         scratch_shapes=[pltpu.VMEM((length, lanes), F32)] * 2,
         compiler_params=pltpu.CompilerParams(vmem_limit_bytes=32 << 20),
         name="attend_grad",
-    )(qkv, grad, lse, *tables, segments[:, None, :], segments.reshape(-1, 1))
+    )(qkv, grad, lse, *tables, segments[:, None, :], segments.reshape(-1, 1), into)
+
+
+def gelu_slope(values):
+    scale = math.sqrt(2.0 / math.pi)
+    square = values * values
+    bent = jnp.tanh(scale * (values + 0.044715 * values * square))
+    return 0.5 * (1.0 + bent) + 0.5 * values * (1.0 - bent * bent) * scale * (
+        1.0 + 3.0 * 0.044715 * square
+    )
+
+
+def branch_kernel(acts_ref, dense_ref, down_ref, out_ref):
+    local, width = dense_ref.shape
+    for low in range(0, width, CHUNK):
+        cols = slice(low, low + CHUNK)
+        total = jnp.dot(
+            acts_ref[:, :local], dense_ref[:, cols], preferred_element_type=F32
+        ) + jnp.dot(acts_ref[:, local:], down_ref[:, cols], preferred_element_type=F32)
+        out_ref[:, cols] = total.astype(BF)
+
+
+def back_kernel(grad_ref, dense_ref, down_ref, mixed_ref, context_ref, into_ref):
+    units = down_ref.shape[0]
+    first = mixed_ref.shape[1] - units
+    grad = grad_ref[...]
+    context_ref[...] = nt(grad, dense_ref[...]).astype(BF)
+    activated_grad = nt(grad, down_ref[...])
+    slope = gelu_slope(mixed_ref[:, first:])
+    into_ref[:, :first] = jnp.zeros((into_ref.shape[0], first), BF)
+    into_ref[:, first:] = (activated_grad * slope).astype(BF)
+
+
+def norm_grad(group, groups, mine, got, hidden_in, out_grad, ln_gain):
+    rows, width = hidden_in.shape
+    span = width // groups
+
+    def kernel(group_ref, mine_ref, got_ref, hidden_ref, cot_ref, gain_ref, out_ref, sum_ref):
+        for j in range(groups):
+            cols = pl.ds(pl.multiple_of((group_ref[0] ^ j) * span, span), span)
+            sum_ref[:, j * span : (j + 1) * span] = mine_ref[:, cols].astype(F32) + got_ref[
+                :, cols
+            ].astype(F32)
+        hidden = hidden_ref[...].astype(F32)
+        centred = hidden - jnp.mean(hidden, axis=-1, keepdims=True)
+        variance = jnp.mean(centred * centred, axis=-1, keepdims=True)
+        scale = lax.rsqrt(variance + EPS)
+        unit = centred * scale
+        slope = sum_ref[...] * gain_ref[...]
+        first = jnp.mean(slope, axis=-1, keepdims=True)
+        second = jnp.mean(slope * unit, axis=-1, keepdims=True)
+        out_ref[...] = scale * (slope - first - unit * second) + cot_ref[...].astype(F32)
+
+    whole = pl.BlockSpec(memory_space=pltpu.VMEM)
+    return pl.pallas_call(
+        kernel,
+        in_specs=[pl.BlockSpec(memory_space=pltpu.SMEM)] + [whole] * 5,
+        out_specs=whole,
+        out_shape=jax.ShapeDtypeStruct((rows, width), F32),
+        scratch_shapes=[pltpu.VMEM((rows, width), F32)],
+        compiler_params=pltpu.CompilerParams(vmem_limit_bytes=24 << 20),
+        name="norm_grad",
+    )(group[None], mine, got, hidden_in, out_grad, ln_gain[None, :])
+
+
+def settle(order, pieces, local):
+    rows, cols = pieces[0].shape
+    units = cols - 3 * local
+
+    def kernel(order_ref, *refs):
+        ins, qkv_ref, up_ref = refs[:4], refs[4], refs[5]
+        for m, ref in enumerate(ins):
+            to = pl.multiple_of(order_ref[m] * units, units)
+            up_ref[:, pl.ds(to, units)] = ref[:, 3 * local :].astype(F32)
+            to = pl.multiple_of(order_ref[m] * local, local)
+            for j in range(3):
+                qkv_ref[j, :, pl.ds(to, local)] = ref[:, j * local : (j + 1) * local].astype(F32)
+
+    whole = pl.BlockSpec(memory_space=pltpu.VMEM)
+    qkv, up = pl.pallas_call(
+        kernel,
+        in_specs=[pl.BlockSpec(memory_space=pltpu.SMEM)] + [whole] * 4,
+        out_specs=[whole] * 2,
+        out_shape=[
+            jax.ShapeDtypeStruct((3, rows, 4 * local), F32),
+            jax.ShapeDtypeStruct((rows, 4 * units), F32),
+        ],
+        compiler_params=pltpu.CompilerParams(vmem_limit_bytes=24 << 20),
+        name="settle",
+    )(order, *pieces)
+    return jnp.transpose(qkv, (1, 0, 2)), up
+
+
+def by_tokens(kernel, name, rows, flops, blocked, whole, outs):
+    def cut(cols):
+        return pl.BlockSpec((ROWS, cols), lambda i: (i, 0))
+
+    def kept(array):
+        return pl.BlockSpec(array.shape, lambda i: (0, 0))
+
+    specs = [cut(a.shape[1]) if a.shape[0] == rows and cutting else kept(a)
+             for a, cutting in [(a, True) for a in blocked] + [(a, False) for a in whole]]
+    size = sum(a.size * a.dtype.itemsize for a in list(blocked) + list(whole))
+    return pl.pallas_call(
+        kernel,
+        grid=(rows // ROWS,),
+        in_specs=specs,
+        out_specs=[cut(cols) for cols in outs],
+        out_shape=[jax.ShapeDtypeStruct((rows, cols), BF) for cols in outs],
+        compiler_params=pltpu.CompilerParams(vmem_limit_bytes=48 << 20),
+        cost_estimate=pl.CostEstimate(
+            flops=flops, bytes_accessed=size + 2 * rows * sum(outs), transcendentals=0
+        ),
+        name=name,
+    )(*blocked, *whole)
 
 
 def place(order, sources, count, axis, shape):
@@ -340,63 +458,80 @@
         order = jnp.stack([quad, quad ^ 1, quad ^ 2, quad ^ 3])
         rows_in, cols_out = w_fc1.shape[0], w_fc2.shape[1]
 
+        def gather_tokens(mine, other):
+            rows = lax.all_gather(
+                jnp.stack([mine, other]), ("x", "y", "core"), axis=1, tiled=True
+            )
+            return rows.reshape(-1, width)
+
         hidden = hidden_in.astype(F32)
         mine_n = own_order(layer_norm(hidden, ln_gain, ln_bias).astype(BF), 1)
         mine_g = own_order(out_grad, 1)
         in_own = take_in(quad)
         in_first = swap_h(in_own[:rows_in])
-        in_parts = trade(take_in, in_own)
         next_n = swap_with(mine_n, "l", 1, 2)
-        in_first, in_parts, next_n = step(in_first, in_parts, next_n)
-
-        def gather_tokens(mine, other):
-            rows = lax.all_gather(
-                jnp.stack([mine, other]), ("x", "y", "core"), axis=1, tiled=True
-            )
-            return rows.reshape(-1, width)
-
+        in_send = [take_in(quad ^ m) for m in (1, 2, 3)]
+        mine_n, next_n, in_first, in_send, mine_g = step(
+            mine_n, next_n, in_first, in_send, mine_g
+        )
         normed_all = gather_tokens(mine_n, next_n)
-        in_rest = swap_h(stacked([p[:rows_in] for p in in_parts[1:]], 0))
-        out_parts = trade(take_out, take_out(quad))
+        in_parts = [in_own] + [quad_swap(piece, m) for m, piece in zip((1, 2, 3), in_send)]
+        out_own = take_out(quad)
+        out_first = swap_h(out_own)
+        out_send = [take_out(quad ^ m) for m in (1, 2, 3)]
+        in_parts, mine_g, out_own, out_first, out_send = step(
+            in_parts, mine_g, out_own, out_first, out_send
+        )
+
+        in_low = swap_h(in_parts[1][:rows_in])
         next_g = swap_with(mine_g, "l", 1, 2)
-        out_stack = stacked(out_parts, 1)
-        in_rest, out_parts, out_stack, next_g = step(in_rest, out_parts, out_stack, next_g)
+        out_1 = quad_swap(out_send[0], 1)
+        in_high = stacked([p[:rows_in] for p in in_parts[2:]], 0)
+        in_low, next_g, out_1, in_high, out_send, mine_g = step(
+            in_low, next_g, out_1, in_high, out_send, mine_g
+        )
+        in_rest = swap_h(in_high)
+        out_parts = [out_own, out_1] + [quad_swap(out_send[m - 1], m) for m in (2, 3)]
+        grad_all = gather_tokens(mine_g, next_g)
+        out_stack = stacked(out_parts[1:], 1)
+        in_rest, out_parts, out_stack = step(in_rest, out_parts, out_stack)
 
         out_rest = swap_h(out_stack)
-        in_first, in_parts, in_rest = step(in_first, in_parts, in_rest)
+        in_first, in_parts, in_low, in_rest = step(in_first, in_parts, in_low, in_rest)
         sources = [(p, (0, 0), 0, m) for m, p in enumerate(in_parts)]
         for k in range(1, groups):
             sources.append((in_first[k - 1], (0, 0), k, 0))
-            sources += [(in_rest[k - 1], ((m - 1) * rows_in, 0), k, m) for m in (1, 2, 3)]
+            sources.append((in_low[k - 1], (0, 0), k, 1))
+            sources += [(in_rest[k - 1], ((m - 2) * rows_in, 0), k, m) for m in (2, 3)]
         in_w = place(order, sources, 4 * groups, 0, (width, in_cols))
         labels_all = [p[rows_in, :seg_len].astype(jnp.int32)[None] for p in in_parts]
         ordered = in_order(labels_all, 0)
         segments = jnp.where(lb == 1, jnp.roll(ordered, 2, axis=0), ordered)
-        grad_all = gather_tokens(after(mine_g, normed_all, out_stack), next_g)
         in_b = stacked([part(b_qkv, quad, 4, 1).reshape(-1), part(b_fc1, quad, 4, 0)], 0)
         mixed = dot(normed_all, in_w, ((1,), (0,))) + in_b
         tables = rotary_tables(segments.shape[1], local)
         qkv, context, lse = attention(mixed, local, tables, segments)
         before = mixed[:, qkv_cols:]
         acts = stacked([context, gelu_tanh(before).astype(BF)], 1)
-        qkv, acts, lse, before, out_rest = step(qkv, acts, lse, before, out_rest)
+        qkv, acts, lse, mixed = step(qkv, acts, lse, mixed)
 
         def slot(values, k, axis):
             return fixed(values, k, groups, axis)
 
         out_rows = acts.shape[1]
         out_part = dot(acts, grad_all, ((0,), (0,))).astype(BF)
-        cuts = [out_rows * i // 40 for i in (0, 7, 17, 24, 32, 40)]
+        cuts = [out_rows * i // 40 for i in (0, 6, 21, 30, 40)]
         out_send = [
-            [slot(out_part, k, 1)[cuts[i] : cuts[i + 1]] for i in range(5)] for k in range(groups)
+            [slot(out_part, k, 1)[cuts[i] : cuts[i + 1]] for i in range(4)] for k in range(groups)
         ]
+        out_send, out_rest = step(out_send, out_rest)
         out_ws = []
         for low, high in ((0, local), (local, out_rows)):
             sources = [(p, (low, 0), 0, m) for m, p in enumerate(out_parts)]
             for k in range(1, groups):
-                sources += [(out_rest[k - 1], (low, m * cols_out), k, m) for m in range(4)]
+                sources.append((out_first[k - 1], (low, 0), k, 0))
+                sources += [(out_rest[k - 1], (low, (m - 1) * cols_out), k, m) for m in (1, 2, 3)]
             out_ws.append(place(order, sources, 4 * groups, 1, (high - low, width)))
-        out_send, out_ws = step(out_send, out_ws)
 
         def send_out(i):
             return [swap_with(out_send[k][i], "h", k, groups) for k in range(1, groups)]
@@ -408,36 +543,51 @@
 
         out_0 = send_out(0)
         acts, out_ws = step(acts, out_ws)
-        branch = dot(acts, stacked(out_ws, 0), ((1,), (0,))).astype(BF)
+        tokens = acts.shape[0]
+        (branch,) = by_tokens(
+            branch_kernel, "branch", tokens, 2 * tokens * out_rows * width, [acts], out_ws, [width]
+        )
         branch, out_ws, out_0, out_send = step(branch, out_ws, out_0, out_send)
         branch_sum = team_sum(branch)
         out_1 = send_out(1)
-        out_ws, qkv, lse = step(out_ws, qkv, lse)
-        context_grad = dot(grad_all, out_ws[0], ((1,), (1,))).astype(BF)
-        mixed_grad = attention_grad(qkv, context_grad, lse, tables, segments)
-        mixed_grad, out_1, out_send = step(mixed_grad, out_1, out_send)
+        out_ws, qkv, lse, mixed = step(out_ws, qkv, lse, mixed)
+
+        def back(grad_ref, mixed_ref, dense_ref, down_ref, context_ref, into_ref):
+            back_kernel(grad_ref, dense_ref, down_ref, mixed_ref, context_ref, into_ref)
+
+        context_grad, into = by_tokens(
+            back, "back", tokens, 2 * tokens * out_rows * width, [grad_all, mixed], out_ws,
+            [local, in_cols],
+        )
+        into = attention_grad(qkv, context_grad, lse, tables, segments, into)
+        into, out_1, out_send = step(into, out_1, out_send)
 
         out_2 = send_out(2)
-        mixed_grad, before = step(mixed_grad, before)
-        activated_grad = dot(after(grad_all, mixed_grad), out_ws[1], ((1,), (1,)))
-        before_grad = jax.vjp(gelu_tanh, before)[1](activated_grad)[0].astype(BF)
-        into = stacked([mixed_grad, before_grad], 1)
-        into, out_2, out_send = step(into, out_2, out_send)
-        out_3 = send_out(3)
         into, in_w = step(into, in_w)
         terms = dot(into, in_w, ((1,), (1,)))
         unit = (normed_all.astype(F32) - own_order(ln_bias, 0)) / own_order(ln_gain, 0)
         gain_sum, shift_sum = jnp.sum(terms * unit, axis=0), jnp.sum(terms, axis=0)
         terms = terms.astype(BF)
-        terms, gain_sum, shift_sum, into, out_3, out_send = step(
-            terms, gain_sum, shift_sum, into, out_3, out_send
+        terms, gain_sum, shift_sum, into, out_2, out_send = step(
+            terms, gain_sum, shift_sum, into, out_2, out_send
         )
         terms_sum = team_sum(terms)
 
-        out_4 = send_out(4)
+        out_3 = send_out(3)
+        small = [
+            own_order(gain_sum, 0),
+            own_order(shift_sum, 0),
+            jnp.sum(out_grad.astype(F32), axis=0),
+        ]
+        bias = jnp.sum(into, axis=0, dtype=F32)
+        size = in_cols
+        team = 4 * (2 * lax.axis_index("y") + lax.axis_index("core"))
+        bias = lax.dynamic_update_slice(jnp.zeros((16 * size,), F32), bias, ((team + quad) * size,))
+        total = stacked(small + [bias], 0)
+        got = swap_with(total, "l", 1, 2)
         into, normed_all = step(into, normed_all)
         in_part = dot(normed_all, into, ((0,), (0,))).astype(BF)
-        in_part, into, out_4 = step(in_part, into, out_4)
+        in_part, into, out_3, total, got = step(in_part, into, out_3, total, got)
 
         def block(k, m):
             start = k * span + (quad ^ m) * (span // 4)
@@ -455,26 +605,22 @@
                 mine = mine + piece.astype(F32)
             return mine
 
-        in_a = send_in(3, 2)
-        out_got = (out_0, out_1, out_2, out_3, out_4)
+        send_a = [blocks(k, 3, 2) for k in range(groups)]
+        send_a, out_0, out_1, out_2, out_3 = step(send_a, out_0, out_1, out_2, out_3)
+        in_a = [swap_with(send_a[k], "h", k, groups) for k in range(1, groups)]
+        out_got = step(out_0, out_1, out_2, out_3)
         out_sum = stacked([add_up(out_send[0][i], got) for i, got in enumerate(out_got)], 0)
         sent = out_sum.astype(BF)
         out_back = [quad_swap(part(sent, quad ^ m, 4, 1), m) for m in (1, 2, 3)]
         got_m = swap_with(branch_sum[1], "l", 1, 2)
-        small = [
-            own_order(gain_sum, 0),
-            own_order(shift_sum, 0),
-            jnp.sum(out_grad.astype(F32), axis=0),
-        ]
-        team = 4 * (2 * lax.axis_index("y") + lax.axis_index("core"))
-        bias = jnp.sum(into, axis=0, dtype=F32)
-        size = into.shape[1]
-        bias = lax.dynamic_update_slice(jnp.zeros((16 * size,), F32), bias, ((team + quad) * size,))
-        total = stacked(small + [bias], 0)
+        total = total + got
+        bit = 1
+        while bit < groups:
+            total = total + swap_with(total, "h", bit, groups)
+            bit *= 2
         total = total + swap_c(total)
-        total = total + swap_with(total, "y", 1, 2)
         send_b = [blocks(k, 1, 0) for k in range(groups)]
-        keep_a = blocks(0, 3, 2)
+        keep_a = send_a[0]
         in_a, out_back, out_sum, total, send_b, keep_a, got_m = step(
             in_a, out_back, out_sum, total, send_b, keep_a, got_m
         )
@@ -483,8 +629,8 @@
         keep_a, in_a = step(keep_a, in_a)
         sum_a = unstack(add_up(keep_a, in_a).astype(BF), 2, 0)
         back_3, back_2 = quad_swap(sum_a[0], 3), quad_swap(sum_a[1], 2)
+        total = total + swap_with(total, "y", 1, 2)
         total = total + swap_with(total, "x", 1, 2)
-        total = total + swap_with(total, "l", 1, 2)
         out_pieces = [part(out_sum, quad, 4, 1)] + [p.astype(F32) for p in out_back]
         dense_grad = in_order([p[:local] for p in out_pieces], 0)
         down_grad = in_order([p[local:] for p in out_pieces], 0)
@@ -498,20 +644,9 @@
         send_b, in_b = step(send_b, in_b)
         sum_b = unstack(add_up(send_b[0], in_b), 2, 0)
         back_1 = quad_swap(sum_b[0].astype(BF), 1)
-        bit = 1
-        while bit < groups:
-            total = total + swap_with(total, "h", bit, groups)
-            bit *= 2
-        back_1, got_n, total, sum_b = step(back_1, got_n, total, sum_b)
-        normed_grad = own_order(terms_sum[0].astype(F32) + got_n.astype(F32), 1)
-        hidden_grad = jax.vjp(lambda v: layer_norm(v, ln_gain, ln_bias), hidden)[1](normed_grad)[0]
-        input_grad = out_grad.astype(F32) + hidden_grad
-        pieces = [sum_b[1]] + [p.astype(F32) for p in (back_1, back_2, back_3)]
-        up_grad = in_order([p[:, qkv_cols:] for p in pieces], 1)
-        qkv_grad = jnp.stack(
-            [in_order([p[:, j * local : (j + 1) * local] for p in pieces], 1) for j in range(3)],
-            axis=1,
-        )
+        back_1, got_n, sum_b = step(back_1, got_n, sum_b)
+        input_grad = norm_grad(group, groups, terms_sum[0], got_n, hidden_in, out_grad, ln_gain)
+        qkv_grad, up_grad = settle(order, [sum_b[1], back_1, back_2, back_3], local)
         gain_grad, shift_grad, out_bias_grad = (
             total[:width], total[width : 2 * width], total[2 * width : 3 * width]
         )

time: 429 us -> 408 us (0.951)
  Pallas kernels: 20.8 us -> 47.8 us
  matrix products: 72.9 us -> 50.4 us
  other arithmetic: 48.8 us -> 33.6 us
  waiting for transfers between devices: 187 us -> 177 us
    pallas_call x0 -> x4, Pallas kernels: none -> 27 us  [the longest x2 22.5 us: by_tokens(): pl.pallas_call(kernel, grid=(rows // ROWS,), in_specs=specs, out_specs=[c...]
    dot_general x7 -> x4, matrix products: 72.9 us -> 50.4 us  [dot(): lax.dot_general(left, right, (dims, ((), ())), preferred_element_type=F32)]
    ppermute x31 -> x32, waiting for transfers between devices: 187 us -> 165 us  [swap_with(): return lax.ppermute(values, axis, [(i, i ^ mask) for i in range(size)])]
    reduce_scatter x2, waiting for transfers between devices: 0.02 us -> 9.27 us  [team_sum(): lax.psum_scatter(values.reshape(2, -1, width), ('x', 'y', 'core'), scatte...]
    select_n x7 -> x3, other arithmetic: 6.62 us -> 0.94 us  [in_order(): jnp.where(lb == 1, jnp.where(xb == 1, parts[j ^ 3], parts[j ^ 2]), jnp.wh...]
    ppermute x31 -> x32, starting transfers between devices: 40.2 us -> 43.1 us  [swap_with(): return lax.ppermute(values, axis, [(i, i ^ mask) for i in range(size)])]
    unnamed x189 -> x167, local copies, waits for them, and re-layouts: 20.8 us -> 20.1 us
  transfers between devices with their start and end apart: 35 -> 36, of which waited for: 14 -> 22; matrix products, arithmetic and copies ran while one was open for 25% -> 23% of each run, Pallas kernels for 5% -> 10%
where the time goes in v5:
time: 408 us; the launch traced here: 403 us
  waiting for transfers between devices  177 us (43%)
  matrix products  50.4 us (12%)
  Pallas kernels  47.8 us (12%)
  starting transfers between devices  43.4 us (11%)
  local copies, waits for them, and re-layouts  35.5 us (9%)
  other arithmetic  33.6 us (8%)
  between operations  15.5 us (4%)
    ppermute x32, waiting for transfers between devices, swap_with(): return lax.ppermute(values, axis, [(i, i ^ mask) for i in range(size)])  165 us
    dot_general x4, matrix products, dot(): lax.dot_general(left, right, (dims, ((), ())), preferred_element_type=F32)  50.4 us
    ppermute x32, starting transfers between devices, swap_with(): return lax.ppermute(values, axis, [(i, i ^ mask) for i in range(size)])  43.1 us
    pallas_call x2, Pallas kernels, by_tokens(): pl.pallas_call(kernel, grid=(rows // ROWS,), in_specs=specs, out_specs=[c...  22.5 us
    unnamed x167, local copies, waits for them, and re-layouts  20.1 us
    pallas_call x1, Pallas kernels, attention_grad(): pl.pallas_call(attend_grad_kernel, grid=(sequences,), in_specs=[spec['wid...  11.7 us
    reduce_scatter x2, waiting for transfers between devices, team_sum(): lax.psum_scatter(values.reshape(2, -1, width), ('x', 'y', 'core'), scatte...  9.27 us
  transfers between devices with their start and end apart: 36, of which 22 were waited for; matrix products, arithmetic and copies ran while one was open for 23% of the time, Pallas kernels for 10%

profile of v5, /device:TPU:0, one launch (start us, length us, event | category | flops | bytes accessed | tf_op | source)
XLA Modules:
  0.0 403.1 jit_solution(14599913256434552115)
XLA Ops:
  10.5 4.0 %collective-permute-start.1 = (bf16[256,896]{1,0:T(8,128)(2,1)}, bf16[256,896]{1,0:T(8,128)(2,1)S(1)}, u32[]{:S(2)}, u32[]{:S(2)}) collective-permute-start(bf16[256,896]{1,0:T(8,128)(2,1)} %pad_maximum_fusion.12), channel_id=1, source_target_pairs={{0,16},{16,0},{1,17},{17,1},{2,18},{18,2},{3,19},{19,3},{4,20},{20... | collective-permute-start | bytes 1376264 | tf_op jit(solution)/shard_map/ppermute | solution.py:356
  16.0 1.6 collective-permute-start
  20.7 14.5 %collective-permute-done.1.refs_4_ = bf16[256,896]{1,0:T(8,128)(2,1)S(1)} collective-permute-done((bf16[256,896]{1,0:T(8,128)(2,1)}, bf16[256,896]{1,0:T(8,128)(2,1)S(1)}, u32[]{:S(2)}, u32[]{:S(2)}) %collective-permute-start.1) | collective-permute-done | bytes 458784 | tf_op jit(solution)/shard_map/ppermute | solution.py:356
  35.2 2.9 collective-permute-done
  42.2 1.9 collective-permute-start.4
  46.8 22.2 %collective-permute-done.5.refs_4_ = bf16[640,256]{1,0:T(8,128)(2,1)S(1)} collective-permute-done((bf16[640,256]{1,0:T(8,128)(2,1)S(1)}, bf16[640,256]{1,0:T(8,128)(2,1)S(1)}, u32[]{:S(2)}, u32[]{:S(2)}) %collective-permute-start.5) | collective-permute-done | bytes 327712 | tf_op jit(solution)/shard_map/ppermute | solution.py:356
  69.0 2.0 collective-permute-done.4.refs_3_
  72.5 1.7 collective-permute-start.6
  76.8 4.5 %collective-permute-done.8.refs_1_ = bf16[640,256]{1,0:T(8,128)(2,1)S(1)} collective-permute-done((bf16[640,256]{1,0:T(8,128)(2,1)S(1)}, bf16[640,256]{1,0:T(8,128)(2,1)S(1)}, u32[]{:S(2)}, u32[]{:S(2)}) %collective-permute-start.8) | collective-permute-done | bytes 327712 | tf_op jit(solution)/shard_map/ppermute | solution.py:356
  81.3 10.3 %collective-permute-done.6.refs_5_ = bf16[256,896]{1,0:T(8,128)(2,1)S(1)} collective-permute-done((bf16[256,896]{1,0:T(8,128)(2,1)S(1)}, bf16[256,896]{1,0:T(8,128)(2,1)S(1)}, u32[]{:S(2)}, u32[]{:S(2)}) %collective-permute-start.6) | collective-permute-done | bytes 458784 | tf_op jit(solution)/shard_map/ppermute | solution.py:356
  92.4 2.1 pad_maximum_fusion.4
  95.5 3.4 collective-permute-start.9
  99.1 2.0 collective-permute-start.11
  101.2 1.9 fusion.22
  103.1 23.3 %collective-permute-done.10.refs_2_ = bf16[640,256]{1,0:T(8,128)(2,1)S(1)} collective-permute-done((bf16[640,256]{1,0:T(8,128)(2,1)S(1)}, bf16[640,256]{1,0:T(8,128)(2,1)S(1)}, u32[]{:S(2)}, u32[]{:S(2)}) %collective-permute-start.10) | collective-permute-done | bytes 327712 | tf_op jit(solution)/shard_map/ppermute | solution.py:356
  126.4 3.7 collective-permute-done.11.refs_3_
  131.1 5.3 %collective-permute-done.9.refs_6_ = bf16[512,896]{1,0:T(8,128)(2,1)S(1)} collective-permute-done((bf16[512,896]{1,0:T(8,128)(2,1)}, bf16[512,896]{1,0:T(8,128)(2,1)S(1)}, u32[]{:S(2)}, u32[]{:S(2)}) %collective-permute-start.9) | collective-permute-done | bytes 917536 | tf_op jit(solution)/shard_map/ppermute | solution.py:356
  146.8 1.9 copy-done.7
  148.7 12.4 %broadcast_add_fusion.mixed_ref = f32[2048,896]{1,0:T(8,128)S(1)} fusion(f32[896]{0:T(1024)S(1)} %pad_maximum_fusion.19, bf16[2048,2048]{1,0:T(8,128)(2,1)} %bitcast.97, bf16[2048,896]{1,0:T(8,128)(2,1)} %copy-done.7), kind=kOutput, calls=%fused_computation.11 | convolution fusion | flops 7518027776 | bytes 19402240 | tf_op jit(solution)/shard_map/dot_general | solution.py:360
  161.2 7.0 %attend.1 = (bf16[2048,384]{1,0:T(8,128)(2,1)S(1)}, bf16[2048,128]{1,0:T(8,128)(2,1)S(1)}, f32[4,2,512]{2,1,0:T(2,128)S(1)}) custom-call(f32[2048,896]{1,0:T(8,128)S(1)} %broadcast_add_fusion.mixed_ref, f32[512,128]{1,0:T(8,128)S(1)} %copy-done.20, f32[512,128]{1,0:T(8,128)S(1)} %copy-done.18, f32[512,128]{1,0:T(8,128)S(1)} %copy-done.16, ...), custom_call_target="tpu_custom_call" | custom-call | tf_op jit(solution)/shard_map/attend/pallas_call | solution.py:171
  169.5 1.8 pad_maximum_fusion.acts_ref
  171.3 2.1 all-gather.5.cloned.1.call-done
  173.4 8.9 %convolution_convert_fusion.1 = bf16[640,2048]{1,0:T(8,128)(2,1)S(1)} fusion(bf16[2048,640]{1,0:T(8,128)(2,1)} %pad_maximum_fusion.acts_ref, bf16[2048,2048]{1,0:T(8,128)(2,1)} %bitcast.99), kind=kOutput, calls=%fused_computation.13 | convolution fusion | flops 5370019840 | bytes 13631488 | tf_op jit(solution)/shard_map/dot_general | solution.py:360
  187.4 2.5 collective-permute-start.13
  189.8 8.8 %branch.1 = bf16[2048,2048]{1,0:T(8,128)(2,1)} custom-call(bf16[2048,640]{1,0:T(8,128)(2,1)S(1)} %copy-done.15, bf16[128,2048]{1,0:T(8,128)(2,1)S(1)} %place.4.dense_ref, bf16[512,2048]{1,0:T(8,128)(2,1)S(1)} %place.5.down_ref), custom_call_target="tpu_custom_call" | custom-call | flops 5368709120 | bytes 13631488 | tf_op jit(solution)/shard_map/branch/pallas_call | solution.py:305
  203.9 13.7 %back.1 = (bf16[2048,128]{1,0:T(8,128)(2,1)S(1)}, bf16[2048,896]{1,0:T(8,128)(2,1)}) custom-call(bf16[2048,2048]{1,0:T(8,128)(2,1)} %bitcast.100, f32[2048,896]{1,0:T(8,128)} %copy-done.3, bf16[128,2048]{1,0:T(8,128)(2,1)S(1)} %copy-done.39, bf16[512,2048]{1,0:T(8,128)(2,1)S(1)} %copy-done.23), custom_call_target="tpu_custom_call" | custom-call | flops 5368709120 | bytes 22544384 | tf_op jit(solution)/shard_map/back/pallas_call | solution.py:305
  217.7 2.0 copy-done.4
  219.8 11.7 %attend_grad.1 = bf16[2048,896]{1,0:T(8,128)(2,1)S(1)} custom-call(bf16[2048,384]{1,0:T(8,128)(2,1)S(1)} %copy-done.33, bf16[2048,128]{1,0:T(8,128)(2,1)S(1)} %get-tuple-element.212.grad_ref, f32[4,2,512]{2,1,0:T(2,128)S(1)} %get-tuple-element.213.lse_ref, f32[512,128]{1,0:T(8,128)S(1)} %copy-done.21, ...), custom_call_target="tpu_custom_call", output_to_operand_aliasing={{}: (8, {})} | custom-call | tf_op jit(solution)/shard_map/attend_grad/pallas_call | solution.py:190
  231.4 1.9 copy-done.5
  233.4 1.8 collective-permute-start.15
  235.2 16.3 %fusion.35 = (f32[2048]{0:T(1024)S(1)}, f32[2048]{0:T(1024)S(1)}, bf16[2048,2048]{1,0:T(8,128)(2,1)}) fusion(f32[2048]{0:T(1024)S(1)} %get-tuple-element.380, f32[2048]{0:T(1024)S(1)} %get-tuple-element.379, bf16[2,1024,2048]{2,1,0:T(8,128)(2,1)} %all-gather.3.cloned.1.call-done, bf16[2048,896]{1,0:T(8,128)(2,1)} %copy-done.5, ...), kind=kOutput, calls=%fused_computation.163 | convolution fusion | flops 7545548800 | bytes 24150016 | tf_op jit(solution)/shard_map/dot_general | solution.py:360
  251.8 2.6 convert_reduce_fusion
  256.1 2.9 collective-permute-start.16
  258.9 12.7 %convolution_convert_fusion = bf16[2048,896]{1,0:T(8,128)(2,1)S(1)} fusion(bf16[2048,2048]{1,0:T(8,128)(2,1)} %bitcast.98, bf16[2048,896]{1,0:T(8,128)(2,1)} %copy-done.5), kind=kOutput, calls=%fused_computation.12 | convolution fusion | flops 7518027776 | bytes 15728640 | tf_op jit(solution)/shard_map/dot_general | solution.py:360
  276.7 2.9 collective-permute-start.18
  290.4 4.1 %collective-permute-done.19 = bf16[640,256]{1,0:T(8,128)(2,1)S(1)} collective-permute-done((bf16[640,256]{1,0:T(8,128)(2,1)S(1)}, bf16[640,256]{1,0:T(8,128)(2,1)S(1)}, u32[]{:S(2)}, u32[]{:S(2)}) %collective-permute-start.19) | collective-permute-done | bytes 327712 | tf_op jit(solution)/shard_map/ppermute | solution.py:356
  294.5 27.9 %collective-permute-done.20 = bf16[640,256]{1,0:T(8,128)(2,1)S(1)} collective-permute-done((bf16[640,256]{1,0:T(8,128)(2,1)S(1)}, bf16[640,256]{1,0:T(8,128)(2,1)S(1)}, u32[]{:S(2)}, u32[]{:S(2)}) %collective-permute-start.20) | collective-permute-done | bytes 327712 | tf_op jit(solution)/shard_map/ppermute | solution.py:356
  322.4 7.6 %collective-permute-done.21 = bf16[640,256]{1,0:T(8,128)(2,1)S(1)} collective-permute-done((bf16[640,256]{1,0:T(8,128)(2,1)S(1)}, bf16[640,256]{1,0:T(8,128)(2,1)S(1)}, u32[]{:S(2)}, u32[]{:S(2)}) %collective-permute-start.21) | collective-permute-done | bytes 327712 | tf_op jit(solution)/shard_map/ppermute | solution.py:356
  333.0 2.6 collective-permute-start.27
  341.2 4.9 %collective-permute-done.29 = f32[20480]{0:T(1024)S(1)} collective-permute-done((f32[20480]{0:T(1024)S(1)}, f32[20480]{0:T(1024)S(1)}, u32[]{:S(2)}, u32[]{:S(2)}) %collective-permute-start.29) | collective-permute-done | bytes 81952 | tf_op jit(solution)/shard_map/ppermute | solution.py:356
  346.1 9.2 %reduce-scatter.5.cloned.1.call-done = bf16[2,128,2048]{2,1,0:T(8,128)(2,1)} async-done(((bf16[2,1024,2048]{2,1,0:T(8,128)(2,1)}), bf16[2,128,2048]{2,1,0:T(8,128)(2,1)}) %reduce-scatter.5.cloned.1.call-update) | async-done | bytes 1048592 | tf_op jit(solution)/shard_map/reduce_scatter | solution.py:540
  355.3 10.1 %collective-permute-done.26.refs_3_ = bf16[256,896]{1,0:T(8,128)(2,1)S(1)} collective-permute-done((bf16[256,896]{1,0:T(8,128)(2,1)}, bf16[256,896]{1,0:T(8,128)(2,1)S(1)}, u32[]{:S(2)}, u32[]{:S(2)}) %collective-permute-start.26) | collective-permute-done | bytes 458784 | tf_op jit(solution)/shard_map/ppermute | solution.py:356
  365.4 7.4 %collective-permute-done.27.refs_2_ = bf16[256,896]{1,0:T(8,128)(2,1)S(1)} collective-permute-done((bf16[256,896]{1,0:T(8,128)(2,1)S(1)}, bf16[256,896]{1,0:T(8,128)(2,1)S(1)}, u32[]{:S(2)}, u32[]{:S(2)}) %collective-permute-start.27) | collective-permute-done | bytes 458784 | tf_op jit(solution)/shard_map/ppermute | solution.py:356
  372.9 4.7 %collective-permute-done.25 = bf16[512,896]{1,0:T(8,128)(2,1)} collective-permute-done((bf16[512,896]{1,0:T(8,128)(2,1)}, bf16[512,896]{1,0:T(8,128)(2,1)}, u32[]{:S(2)}, u32[]{:S(2)}) %collective-permute-start.25) | collective-permute-done | bytes 917536 | tf_op jit(solution)/shard_map/ppermute | solution.py:356
  383.4 4.3 %collective-permute-done.30.refs_1_ = bf16[256,896]{1,0:T(8,128)(2,1)S(1)} collective-permute-done((bf16[256,896]{1,0:T(8,128)(2,1)S(1)}, bf16[256,896]{1,0:T(8,128)(2,1)S(1)}, u32[]{:S(2)}, u32[]{:S(2)}) %collective-permute-start.30) | collective-permute-done | bytes 458784 | tf_op jit(solution)/shard_map/ppermute | solution.py:356
  387.7 3.4 collective-permute-done.31.got_ref
  391.1 2.7 settle.1
  393.8 1.8 norm_grad.1
  (308 shorter events, 75.8 us)
Async XLA Ops:
  7.2 91.8 %copy-start = (f32[3,512]{1,0:T(4,128)S(1)}, f32[3,512]{1,0:T(4,128)}, u32[]{:S(2)}) copy-start(f32[3,512]{1,0:T(4,128)} %param.17) | copy-start | bytes 18436
  7.2 141.5 %all-gather.3.cloned.1.call-start = ((), (), s32[]{:S(2)}) async-start(), calls=%async_computation.2 | async-start | bytes 9437184 | tf_op jit(solution)/shard_map/all_gather | solution.py:462
  10.5 24.7 %collective-permute-start.1 = (bf16[256,896]{1,0:T(8,128)(2,1)}, bf16[256,896]{1,0:T(8,128)(2,1)S(1)}, u32[]{:S(2)}, u32[]{:S(2)}) collective-permute-start(bf16[256,896]{1,0:T(8,128)(2,1)} %pad_maximum_fusion.12), channel_id=1, source_target_pairs={{0,16},{16,0},{1,17},{17,1},{2,18},{18,2},{3,19},{19,3},{4,20},{20... | collective-permute-start | bytes 1376264 | tf_op jit(solution)/shard_map/ppermute | solution.py:356
  16.0 22.1 %collective-permute-start = (bf16[128,2048]{1,0:T(8,128)(2,1)S(1)}, bf16[128,2048]{1,0:T(8,128)(2,1)S(1)}, u32[]{:S(2)}, u32[]{:S(2)}) collective-permute-start(bf16[128,2048]{1,0:T(8,128)(2,1)S(1)} %maximum_select_fusion.1), channel_id=1, source_target_pairs={{0,8},{8,0},{1,9},{9,1},{2,10},{10,2},{3,11},{11,3},{4,12},{12,4},... | collective-permute-start | bytes 1572872 | tf_op jit(solution)/shard_map/ppermute | solution.py:356
  18.8 117.5 %copy-start.24 = (bf16[272,896]{1,0:T(8,128)(2,1)}, bf16[272,896]{1,0:T(8,128)(2,1)S(1)}, u32[]{:S(2)}) copy-start(bf16[272,896]{1,0:T(8,128)(2,1)S(1)} %get-tuple-element.172.refs_0_) | copy-start | bytes 1462276
  39.2 134.2 %all-gather.5.cloned.1.call-start = ((), (), s32[]{:S(2)}) async-start(), calls=%async_computation.3 | async-start | bytes 9437184 | tf_op jit(solution)/shard_map/all_gather | solution.py:462
  40.5 28.5 %collective-permute-start.2 = (bf16[272,896]{1,0:T(8,128)(2,1)}, bf16[272,896]{1,0:T(8,128)(2,1)S(1)}, u32[]{:S(2)}, u32[]{:S(2)}) collective-permute-start(bf16[272,896]{1,0:T(8,128)(2,1)} %get-tuple-element.153), channel_id=1, source_target_pairs={{0,4},{4,0},{8,12},{12,8},{1,5},{5,1},{9,13},{13,9},{2,6},{6,2},{1... | collective-permute-start | bytes 1462280 | tf_op jit(solution)/shard_map/ppermute | solution.py:356
  42.1 26.9 %collective-permute-start.3 = (bf16[272,896]{1,0:T(8,128)(2,1)S(1)}, bf16[272,896]{1,0:T(8,128)(2,1)S(1)}, u32[]{:S(2)}, u32[]{:S(2)}) collective-permute-start(bf16[272,896]{1,0:T(8,128)(2,1)S(1)} %copy-done.62), channel_id=1, source_target_pairs={{0,8},{4,12},{8,0},{12,4},{1,9},{5,13},{9,1},{13,5},{2,10},{6,14},... | collective-permute-start | bytes 1462280 | tf_op jit(solution)/shard_map/ppermute | solution.py:356
  42.2 28.8 %collective-permute-start.4 = (bf16[272,896]{1,0:T(8,128)(2,1)}, bf16[272,896]{1,0:T(8,128)(2,1)S(1)}, u32[]{:S(2)}, u32[]{:S(2)}) collective-permute-start(bf16[272,896]{1,0:T(8,128)(2,1)} %fusion.18), channel_id=1, source_target_pairs={{0,12},{4,8},{8,4},{12,0},{1,13},{5,9},{9,5},{13,1},{2,14},{6,10},... | collective-permute-start | bytes 1462280 | tf_op jit(solution)/shard_map/ppermute | solution.py:356
  44.1 24.8 %collective-permute-start.5 = (bf16[640,256]{1,0:T(8,128)(2,1)S(1)}, bf16[640,256]{1,0:T(8,128)(2,1)S(1)}, u32[]{:S(2)}, u32[]{:S(2)}) collective-permute-start(bf16[640,256]{1,0:T(8,128)(2,1)S(1)} %pad_maximum_fusion.13.refs_0_), channel_id=1, source_target_pairs={{0,16},{16,0},{1,17},{17,1},{2,18},{18,2},{3,19},{19,3},{4,20},{20... | collective-permute-start | bytes 983048 | tf_op jit(solution)/shard_map/ppermute | solution.py:356
  69.0 67.4 %copy-start.26 = (bf16[272,896]{1,0:T(8,128)(2,1)}, bf16[272,896]{1,0:T(8,128)(2,1)S(1)}, u32[]{:S(2)}) copy-start(bf16[272,896]{1,0:T(8,128)(2,1)S(1)} %collective-permute-done.2.refs_1_) | copy-start | bytes 1462276
  69.0 67.4 %copy-start.28 = (bf16[272,896]{1,0:T(8,128)(2,1)}, bf16[272,896]{1,0:T(8,128)(2,1)S(1)}, u32[]{:S(2)}) copy-start(bf16[272,896]{1,0:T(8,128)(2,1)S(1)} %collective-permute-done.3.refs_2_) | copy-start | bytes 1462276
  71.0 21.3 %collective-permute-start.7 = (bf16[128,2048]{1,0:T(8,128)(2,1)}, bf16[128,2048]{1,0:T(8,128)(2,1)S(1)}, u32[]{:S(2)}, u32[]{:S(2)}) collective-permute-start(bf16[128,2048]{1,0:T(8,128)(2,1)} %maximum_select_fusion.2), channel_id=1, source_target_pairs={{0,8},{8,0},{1,9},{9,1},{2,10},{10,2},{3,11},{11,3},{4,12},{12,4},... | collective-permute-start | bytes 1572872 | tf_op jit(solution)/shard_map/ppermute | solution.py:356
  72.5 19.1 %collective-permute-start.6 = (bf16[256,896]{1,0:T(8,128)(2,1)S(1)}, bf16[256,896]{1,0:T(8,128)(2,1)S(1)}, u32[]{:S(2)}, u32[]{:S(2)}) collective-permute-start(bf16[256,896]{1,0:T(8,128)(2,1)S(1)} %slice.233), channel_id=1, source_target_pairs={{0,16},{16,0},{1,17},{17,1},{2,18},{18,2},{3,19},{19,3},{4,20},{20... | collective-permute-start | bytes 1376264 | tf_op jit(solution)/shard_map/ppermute | solution.py:356
  74.2 7.1 %collective-permute-start.8 = (bf16[640,256]{1,0:T(8,128)(2,1)S(1)}, bf16[640,256]{1,0:T(8,128)(2,1)S(1)}, u32[]{:S(2)}, u32[]{:S(2)}) collective-permute-start(bf16[640,256]{1,0:T(8,128)(2,1)S(1)} %get-tuple-element.162), channel_id=1, source_target_pairs={{0,4},{4,0},{8,12},{12,8},{1,5},{5,1},{9,13},{13,9},{2,6},{6,2},{1... | collective-permute-start | bytes 983048 | tf_op jit(solution)/shard_map/ppermute | solution.py:356
  75.8 23.2 %copy-start.64 = (bf16[640,256]{1,0:T(8,128)(2,1)S(1)}, bf16[640,256]{1,0:T(8,128)(2,1)}, u32[]{:S(2)}) copy-start(bf16[640,256]{1,0:T(8,128)(2,1)} %get-tuple-element.169) | copy-start | bytes 983044
  81.3 49.8 %copy-start.9 = (bf16[640,256]{1,0:T(8,128)(2,1)}, bf16[640,256]{1,0:T(8,128)(2,1)S(1)}, u32[]{:S(2)}) copy-start(bf16[640,256]{1,0:T(8,128)(2,1)S(1)} %collective-permute-done.8.refs_1_) | copy-start | bytes 983044
  94.5 186.9 %reduce-scatter.3.cloned.1.call-start = ((), (), s32[]{:S(2)}) async-start(), calls=%async_computation.4 | async-start | bytes 9437184 | tf_op jit(solution)/shard_map/reduce_scatter | solution.py:540
  95.5 40.8 %collective-permute-start.9 = (bf16[512,896]{1,0:T(8,128)(2,1)}, bf16[512,896]{1,0:T(8,128)(2,1)S(1)}, u32[]{:S(2)}, u32[]{:S(2)}) collective-permute-start(bf16[512,896]{1,0:T(8,128)(2,1)} %pad_maximum_fusion.6), channel_id=1, source_target_pairs={{0,16},{16,0},{1,17},{17,1},{2,18},{18,2},{3,19},{19,3},{4,20},{20... | collective-permute-start | bytes 2752520 | tf_op jit(solution)/shard_map/ppermute | solution.py:356
  99.0 27.3 %collective-permute-start.10 = (bf16[640,256]{1,0:T(8,128)(2,1)S(1)}, bf16[640,256]{1,0:T(8,128)(2,1)S(1)}, u32[]{:S(2)}, u32[]{:S(2)}) collective-permute-start(bf16[640,256]{1,0:T(8,128)(2,1)S(1)} %copy-done.64), channel_id=1, source_target_pairs={{0,8},{4,12},{8,0},{12,4},{1,9},{5,13},{9,1},{13,5},{2,10},{6,14},... | collective-permute-start | bytes 983048 | tf_op jit(solution)/shard_map/ppermute | solution.py:356
  99.1 30.9 %collective-permute-start.11 = (bf16[640,256]{1,0:T(8,128)(2,1)}, bf16[640,256]{1,0:T(8,128)(2,1)S(1)}, u32[]{:S(2)}, u32[]{:S(2)}) collective-permute-start(bf16[640,256]{1,0:T(8,128)(2,1)} %pad_maximum_fusion.16), channel_id=1, source_target_pairs={{0,12},{4,8},{8,4},{12,0},{1,13},{5,9},{9,5},{13,1},{2,14},{6,10},... | collective-permute-start | bytes 983048 | tf_op jit(solution)/shard_map/ppermute | solution.py:356
  138.5 47.4 %collective-permute-start.12 = (bf16[640,768]{1,0:T(8,128)(2,1)}, bf16[640,768]{1,0:T(8,128)(2,1)S(1)}, u32[]{:S(2)}, u32[]{:S(2)}) collective-permute-start(bf16[640,768]{1,0:T(8,128)(2,1)} %pad_maximum_fusion.5), channel_id=1, source_target_pairs={{0,16},{16,0},{1,17},{17,1},{2,18},{18,2},{3,19},{19,3},{4,20},{20... | collective-permute-start | bytes 2949128 | tf_op jit(solution)/shard_map/ppermute | solution.py:356
  187.4 12.2 %collective-permute-start.13 = (bf16[96,1024]{1,0:T(8,128)(2,1)S(1)}, bf16[96,1024]{1,0:T(8,128)(2,1)S(1)}, u32[]{:S(2)}, u32[]{:S(2)}) collective-permute-start(bf16[96,1024]{1,0:T(8,128)(2,1)S(1)} %get-tuple-element.195), channel_id=1, source_target_pairs={{0,16},{16,0},{1,17},{17,1},{2,18},{18,2},{3,19},{19,3},{4,20},{20... | collective-permute-start | bytes 589832 | tf_op jit(solution)/shard_map/ppermute | solution.py:356
  200.3 155.0 %reduce-scatter.5.cloned.1.call-start = ((), (), s32[]{:S(2)}) async-start(), calls=%async_computation.5 | async-start | bytes 9437184 | tf_op jit(solution)/shard_map/reduce_scatter | solution.py:540
  201.3 16.4 %copy-start.17 = (f32[512,128]{1,0:T(8,128)S(1)}, f32[512,128]{1,0:T(8,128)}, u32[]{:S(2)}) copy-start(f32[512,128]{1,0:T(8,128)} %get-tuple-element.370.b_ref) | copy-start | bytes 786436
  201.3 16.4 %copy-start.19 = (f32[512,128]{1,0:T(8,128)S(1)}, f32[512,128]{1,0:T(8,128)}, u32[]{:S(2)}) copy-start(f32[512,128]{1,0:T(8,128)} %get-tuple-element.371.a_ref) | copy-start | bytes 786436
  201.3 16.4 %copy-start.21 = (f32[512,128]{1,0:T(8,128)S(1)}, f32[512,128]{1,0:T(8,128)}, u32[]{:S(2)}) copy-start(f32[512,128]{1,0:T(8,128)} %get-tuple-element.372.cos_ref) | copy-start | bytes 786436
  201.3 32.0 %collective-permute-start.14 = (bf16[240,1024]{1,0:T(8,128)(2,1)S(1)}, bf16[240,1024]{1,0:T(8,128)(2,1)S(1)}, u32[]{:S(2)}, u32[]{:S(2)}) collective-permute-start(bf16[240,1024]{1,0:T(8,128)(2,1)S(1)} %copy-done.61), channel_id=1, source_target_pairs={{0,16},{16,0},{1,17},{17,1},{2,18},{18,2},{3,19},{19,3},{4,20},{20... | collective-permute-start | bytes 1474568 | tf_op jit(solution)/shard_map/ppermute | solution.py:356
  233.4 18.2 %copy-start.59 = (bf16[240,1024]{1,0:T(8,128)(2,1)}, bf16[240,1024]{1,0:T(8,128)(2,1)S(1)}, u32[]{:S(2)}) copy-start(bf16[240,1024]{1,0:T(8,128)(2,1)S(1)} %collective-permute-done.14) | copy-start | bytes 1474564
  233.4 18.2 %collective-permute-start.15 = (bf16[144,1024]{1,0:T(8,128)(2,1)S(1)}, bf16[144,1024]{1,0:T(8,128)(2,1)S(1)}, u32[]{:S(2)}, u32[]{:S(2)}) collective-permute-start(bf16[144,1024]{1,0:T(8,128)(2,1)S(1)} %copy-done.65), channel_id=1, source_target_pairs={{0,16},{16,0},{1,17},{17,1},{2,18},{18,2},{3,19},{19,3},{4,20},{20... | collective-permute-start | bytes 884744 | tf_op jit(solution)/shard_map/ppermute | solution.py:356
  254.7 16.9 %collective-permute-start.17 = (f32[20480]{0:T(1024)S(1)}, f32[20480]{0:T(1024)S(1)}, u32[]{:S(2)}, u32[]{:S(2)}) collective-permute-start(f32[20480]{0:T(1024)S(1)} %pad_maximum_fusion.17), channel_id=1, source_target_pairs={{0,8},{8,0},{1,9},{9,1},{2,10},{10,2},{3,11},{11,3},{4,12},{12,4},... | collective-permute-start | bytes 245768 | tf_op jit(solution)/shard_map/ppermute | solution.py:356
  256.1 17.1 %collective-permute-start.16 = (bf16[160,1024]{1,0:T(8,128)(2,1)S(1)}, bf16[160,1024]{1,0:T(8,128)(2,1)S(1)}, u32[]{:S(2)}, u32[]{:S(2)}) collective-permute-start(bf16[160,1024]{1,0:T(8,128)(2,1)S(1)} %copy-done.63), channel_id=1, source_target_pairs={{0,16},{16,0},{1,17},{17,1},{2,18},{18,2},{3,19},{19,3},{4,20},{20... | collective-permute-start | bytes 983048 | tf_op jit(solution)/shard_map/ppermute | solution.py:356
  273.1 8.1 %collective-permute-start.22 = (f32[20480]{0:T(1024)S(1)}, f32[20480]{0:T(1024)S(1)}, u32[]{:S(2)}, u32[]{:S(2)}) collective-permute-start(f32[20480]{0:T(1024)S(1)} %add.280), channel_id=1, source_target_pairs={{0,16},{16,0},{1,17},{17,1},{2,18},{18,2},{3,19},{19,3},{4,20},{20... | collective-permute-start | bytes 245768 | tf_op jit(solution)/shard_map/ppermute | solution.py:356
  276.7 53.3 %collective-permute-start.18 = (bf16[512,896]{1,0:T(8,128)(2,1)}, bf16[512,896]{1,0:T(8,128)(2,1)}, u32[]{:S(2)}, u32[]{:S(2)}) collective-permute-start(bf16[512,896]{1,0:T(8,128)(2,1)} %pad_maximum_fusion.8), channel_id=1, source_target_pairs={{0,16},{16,0},{1,17},{17,1},{2,18},{18,2},{3,19},{19,3},{4,20},{20... | collective-permute-start | bytes 2752520 | tf_op jit(solution)/shard_map/ppermute | solution.py:356
  281.3 6.5 %collective-permute-start.23 = (f32[20480]{0:T(1024)S(1)}, f32[20480]{0:T(1024)S(1)}, u32[]{:S(2)}, u32[]{:S(2)}) collective-permute-start(f32[20480]{0:T(1024)S(1)} %add.281), channel_id=1, source_target_pairs={{0,1},{1,0},{2,3},{3,2},{4,5},{5,4},{6,7},{7,6},{8,9},{9,8},{10,11... | collective-permute-start | bytes 245768 | tf_op jit(solution)/shard_map/ppermute | solution.py:356
  282.6 47.4 %collective-permute-start.24 = (bf16[128,2048]{1,0:T(8,128)(2,1)S(1)}, bf16[128,2048]{1,0:T(8,128)(2,1)S(1)}, u32[]{:S(2)}, u32[]{:S(2)}) collective-permute-start(bf16[128,2048]{1,0:T(8,128)(2,1)S(1)} %slice_bitcast_fusion.1), channel_id=1, source_target_pairs={{0,8},{8,0},{1,9},{9,1},{2,10},{10,2},{3,11},{11,3},{4,12},{12,4},... | collective-permute-start | bytes 1572872 | tf_op jit(solution)/shard_map/ppermute | solution.py:356
  284.7 9.8 %collective-permute-start.19 = (bf16[640,256]{1,0:T(8,128)(2,1)S(1)}, bf16[640,256]{1,0:T(8,128)(2,1)S(1)}, u32[]{:S(2)}, u32[]{:S(2)}) collective-permute-start(bf16[640,256]{1,0:T(8,128)(2,1)S(1)} %get-tuple-element.321), channel_id=1, source_target_pairs={{0,4},{4,0},{8,12},{12,8},{1,5},{5,1},{9,13},{13,9},{2,6},{6,2},{1... | collective-permute-start | bytes 983048 | tf_op jit(solution)/shard_map/ppermute | solution.py:356
  286.2 36.2 %collective-permute-start.20 = (bf16[640,256]{1,0:T(8,128)(2,1)S(1)}, bf16[640,256]{1,0:T(8,128)(2,1)S(1)}, u32[]{:S(2)}, u32[]{:S(2)}) collective-permute-start(bf16[640,256]{1,0:T(8,128)(2,1)S(1)} %get-tuple-element.320), channel_id=1, source_target_pairs={{0,8},{4,12},{8,0},{12,4},{1,9},{5,13},{9,1},{13,5},{2,10},{6,14},... | collective-permute-start | bytes 983048 | tf_op jit(solution)/shard_map/ppermute | solution.py:356
  287.8 42.2 %collective-permute-start.21 = (bf16[640,256]{1,0:T(8,128)(2,1)S(1)}, bf16[640,256]{1,0:T(8,128)(2,1)S(1)}, u32[]{:S(2)}, u32[]{:S(2)}) collective-permute-start(bf16[640,256]{1,0:T(8,128)(2,1)S(1)} %get-tuple-element.319), channel_id=1, source_target_pairs={{0,12},{4,8},{8,4},{12,0},{1,13},{5,9},{9,5},{13,1},{2,14},{6,10},... | collective-permute-start | bytes 983048 | tf_op jit(solution)/shard_map/ppermute | solution.py:356
  290.4 40.4 %copy-start.46 = (bf16[512,896]{1,0:T(8,128)(2,1)S(1)}, bf16[512,896]{1,0:T(8,128)(2,1)}, u32[]{:S(2)}) copy-start(bf16[512,896]{1,0:T(8,128)(2,1)} %pad_maximum_fusion.7) | copy-start | bytes 2752516
  330.2 9.5 %collective-permute-start.28 = (f32[20480]{0:T(1024)S(1)}, f32[20480]{0:T(1024)S(1)}, u32[]{:S(2)}, u32[]{:S(2)}) collective-permute-start(f32[20480]{0:T(1024)S(1)} %add.282), channel_id=1, source_target_pairs={{0,2},{2,0},{1,3},{3,1},{4,6},{6,4},{5,7},{7,5},{8,10},{10,8},{9,1... | collective-permute-start | bytes 245768 | tf_op jit(solution)/shard_map/ppermute | solution.py:356
  333.0 32.4 %collective-permute-start.26 = (bf16[256,896]{1,0:T(8,128)(2,1)}, bf16[256,896]{1,0:T(8,128)(2,1)S(1)}, u32[]{:S(2)}, u32[]{:S(2)}) collective-permute-start(bf16[256,896]{1,0:T(8,128)(2,1)} %get-tuple-element.335), channel_id=1, source_target_pairs={{0,12},{4,8},{8,4},{12,0},{1,13},{5,9},{9,5},{13,1},{2,14},{6,10},... | collective-permute-start | bytes 1376264 | tf_op jit(solution)/shard_map/ppermute | solution.py:356
  333.0 39.8 %collective-permute-start.27 = (bf16[256,896]{1,0:T(8,128)(2,1)S(1)}, bf16[256,896]{1,0:T(8,128)(2,1)S(1)}, u32[]{:S(2)}, u32[]{:S(2)}) collective-permute-start(bf16[256,896]{1,0:T(8,128)(2,1)S(1)} %get-tuple-element.334), channel_id=1, source_target_pairs={{0,8},{4,12},{8,0},{12,4},{1,9},{5,13},{9,1},{13,5},{2,10},{6,14},... | collective-permute-start | bytes 1376264 | tf_op jit(solution)/shard_map/ppermute | solution.py:356
  335.6 41.9 %collective-permute-start.25 = (bf16[512,896]{1,0:T(8,128)(2,1)}, bf16[512,896]{1,0:T(8,128)(2,1)}, u32[]{:S(2)}, u32[]{:S(2)}) collective-permute-start(bf16[512,896]{1,0:T(8,128)(2,1)} %pad_maximum_fusion.10), channel_id=1, source_target_pairs={{0,16},{16,0},{1,17},{17,1},{2,18},{18,2},{3,19},{19,3},{4,20},{20... | collective-permute-start | bytes 2752520 | tf_op jit(solution)/shard_map/ppermute | solution.py:356
  338.2 39.4 %copy-start.45 = (bf16[512,896]{1,0:T(8,128)(2,1)S(1)}, bf16[512,896]{1,0:T(8,128)(2,1)}, u32[]{:S(2)}) copy-start(bf16[512,896]{1,0:T(8,128)(2,1)} %pad_maximum_fusion.9) | copy-start | bytes 2752516
  339.7 6.3 %collective-permute-start.29 = (f32[20480]{0:T(1024)S(1)}, f32[20480]{0:T(1024)S(1)}, u32[]{:S(2)}, u32[]{:S(2)}) collective-permute-start(f32[20480]{0:T(1024)S(1)} %add.289), channel_id=1, source_target_pairs={{0,4},{4,0},{1,5},{5,1},{2,6},{6,2},{3,7},{7,3},{8,12},{12,8},{9,1... | collective-permute-start | bytes 245768 | tf_op jit(solution)/shard_map/ppermute | solution.py:356
  379.2 8.5 %collective-permute-start.30 = (bf16[256,896]{1,0:T(8,128)(2,1)S(1)}, bf16[256,896]{1,0:T(8,128)(2,1)S(1)}, u32[]{:S(2)}, u32[]{:S(2)}) collective-permute-start(bf16[256,896]{1,0:T(8,128)(2,1)S(1)} %slice.422), channel_id=1, source_target_pairs={{0,4},{4,0},{8,12},{12,8},{1,5},{5,1},{9,13},{13,9},{2,6},{6,2},{1... | collective-permute-start | bytes 1376264 | tf_op jit(solution)/shard_map/ppermute | solution.py:356
  381.5 9.6 %collective-permute-start.31 = (bf16[128,2048]{1,0:T(8,128)(2,1)S(1)}, bf16[128,2048]{1,0:T(8,128)(2,1)S(1)}, u32[]{:S(2)}, u32[]{:S(2)}) collective-permute-start(bf16[128,2048]{1,0:T(8,128)(2,1)S(1)} %get-tuple-element.322), channel_id=1, source_target_pairs={{0,8},{8,0},{1,9},{9,1},{2,10},{10,2},{3,11},{11,3},{4,12},{12,4},... | collective-permute-start | bytes 1572872 | tf_op jit(solution)/shard_map/ppermute | solution.py:356
  (69 other events, 364.3 us)
Sparse Core Ops, SparseCore 0:
  39.3 69.5 all-gather.2
  111.4 61.9 all-gather.4
  200.4 71.2 reduce-scatter.2
  275.4 79.8 reduce-scatter.4

commit v6 on v5

--- a/solution.py
+++ b/solution.py
@@ -520,9 +520,9 @@
 
         out_rows = acts.shape[1]
         out_part = dot(acts, grad_all, ((0,), (0,))).astype(BF)
-        cuts = [out_rows * i // 40 for i in (0, 6, 21, 30, 40)]
+        cuts = [out_rows * i // 40 for i in (0, 6, 27, 40)]
         out_send = [
-            [slot(out_part, k, 1)[cuts[i] : cuts[i + 1]] for i in range(4)] for k in range(groups)
+            [slot(out_part, k, 1)[cuts[i] : cuts[i + 1]] for i in range(3)] for k in range(groups)
         ]
         out_send, out_rest = step(out_send, out_rest)
         out_ws = []
@@ -562,18 +562,53 @@
         into = attention_grad(qkv, context_grad, lse, tables, segments, into)
         into, out_1, out_send = step(into, out_1, out_send)
 
+        def add_up(mine, others):
+            mine = mine.astype(F32)
+            for piece in others:
+                mine = mine + piece.astype(F32)
+            return mine
+
+        def out_total(pieces, got):
+            total = stacked([add_up(out_send[0][i], g) for i, g in zip(pieces, got)], 0)
+            sent = total.astype(BF)
+            return part(total, quad, 4, 1), [part(sent, quad ^ m, 4, 1) for m in (1, 2, 3)]
+
         out_2 = send_out(2)
-        into, in_w = step(into, in_w)
+        low_kept, low_send = out_total((0, 1), (out_0, out_1))
+        low_kept, low_send = step(low_kept, low_send)
+        low_back = [quad_swap(piece, m) for m, piece in zip((1, 2, 3), low_send)]
+        into, normed_all = step(into, normed_all)
+        in_part = dot(normed_all, into, ((0,), (0,))).astype(BF)
+        in_part, into, out_2, low_back, low_kept = step(in_part, into, out_2, low_back, low_kept)
+
+        def block(k, m):
+            start = k * span + (quad ^ m) * (span // 4)
+            return lax.dynamic_slice_in_dim(in_part, start, span // 4, 0)
+
+        def swap_block(m):
+            return [swap_with(in_send[m][k], "h", k, groups) for k in range(1, groups)]
+
+        high_kept, high_send = out_total((2,), (out_2,))
+        in_send = [[block(k, m) for k in range(groups)] for m in range(4)]
+        in_send, high_send, high_kept = step(in_send, high_send, high_kept)
+
+        in_3 = swap_block(3)
+        high_back = [quad_swap(piece, m) for m, piece in zip((1, 2, 3), high_send)]
+        into, in_w, normed_all = step(into, in_w, normed_all)
         terms = dot(into, in_w, ((1,), (1,)))
         unit = (normed_all.astype(F32) - own_order(ln_bias, 0)) / own_order(ln_gain, 0)
         gain_sum, shift_sum = jnp.sum(terms * unit, axis=0), jnp.sum(terms, axis=0)
         terms = terms.astype(BF)
-        terms, gain_sum, shift_sum, into, out_2, out_send = step(
-            terms, gain_sum, shift_sum, into, out_2, out_send
+        terms, gain_sum, shift_sum, in_3, in_send, high_back = step(
+            terms, gain_sum, shift_sum, in_3, in_send, high_back
         )
         terms_sum = team_sum(terms)
-
-        out_3 = send_out(3)
+        branch_own, branch_next = branch_sum[0], branch_sum[1]
+
+        in_2, in_1 = swap_block(2), swap_block(1)
+        in_send[3], in_3 = step(in_send[3], in_3)
+        back_3 = quad_swap(add_up(in_send[3][0], in_3).astype(BF), 3)
+        got_m = swap_with(branch_next, "l", 1, 2)
         small = [
             own_order(gain_sum, 0),
             own_order(shift_sum, 0),
@@ -584,69 +619,37 @@
         team = 4 * (2 * lax.axis_index("y") + lax.axis_index("core"))
         bias = lax.dynamic_update_slice(jnp.zeros((16 * size,), F32), bias, ((team + quad) * size,))
         total = stacked(small + [bias], 0)
-        got = swap_with(total, "l", 1, 2)
-        into, normed_all = step(into, normed_all)
-        in_part = dot(normed_all, into, ((0,), (0,))).astype(BF)
-        in_part, into, out_3, total, got = step(in_part, into, out_3, total, got)
-
-        def block(k, m):
-            start = k * span + (quad ^ m) * (span // 4)
-            return lax.dynamic_slice_in_dim(in_part, start, span // 4, 0)
-
-        def blocks(k, *which):
-            return stacked([block(k, m) for m in which], 0)
-
-        def send_in(*which):
-            return [swap_with(blocks(k, *which), "h", k, groups) for k in range(1, groups)]
-
-        def add_up(mine, others):
-            mine = mine.astype(F32)
-            for piece in others:
-                mine = mine + piece.astype(F32)
-            return mine
-
-        send_a = [blocks(k, 3, 2) for k in range(groups)]
-        send_a, out_0, out_1, out_2, out_3 = step(send_a, out_0, out_1, out_2, out_3)
-        in_a = [swap_with(send_a[k], "h", k, groups) for k in range(1, groups)]
-        out_got = step(out_0, out_1, out_2, out_3)
-        out_sum = stacked([add_up(out_send[0][i], got) for i, got in enumerate(out_got)], 0)
-        sent = out_sum.astype(BF)
-        out_back = [quad_swap(part(sent, quad ^ m, 4, 1), m) for m in (1, 2, 3)]
-        got_m = swap_with(branch_sum[1], "l", 1, 2)
-        total = total + got
+        total = total + swap_c(total)
+        total = total + swap_with(total, "y", 1, 2)
+        in_2, in_1, back_3, got_m, total, in_send = step(
+            in_2, in_1, back_3, got_m, total, in_send
+        )
+
+        in_0 = swap_block(0)
+        in_1, in_2 = step(in_1, in_2)
+        back_1 = quad_swap(add_up(in_send[1][0], in_1).astype(BF), 1)
+        back_2 = quad_swap(add_up(in_send[2][0], in_2).astype(BF), 2)
+        total = total + swap_with(total, "x", 1, 2)
+        total = total + swap_with(total, "l", 1, 2)
+        out_pieces = [stacked([low_kept, high_kept], 0)] + [
+            stacked([low, high], 0).astype(F32) for low, high in zip(low_back, high_back)
+        ]
+        dense_grad = in_order([p[:local] for p in out_pieces], 0)
+        down_grad = in_order([p[local:] for p in out_pieces], 0)
+        branch = own_order(branch_own.astype(F32) + got_m.astype(F32), 1)
+        hidden_out = (hidden + branch + b_dense + b_fc2).astype(BF)
+        own_in = add_up(in_send[0][0], in_0)
+        own_in, back_1, back_2, total, dense_grad, down_grad, hidden_out = step(
+            own_in, back_1, back_2, total, dense_grad, down_grad, hidden_out
+        )
+
         bit = 1
         while bit < groups:
             total = total + swap_with(total, "h", bit, groups)
             bit *= 2
-        total = total + swap_c(total)
-        send_b = [blocks(k, 1, 0) for k in range(groups)]
-        keep_a = send_a[0]
-        in_a, out_back, out_sum, total, send_b, keep_a, got_m = step(
-            in_a, out_back, out_sum, total, send_b, keep_a, got_m
-        )
-
-        in_b = [swap_with(send_b[k], "h", k, groups) for k in range(1, groups)]
-        keep_a, in_a = step(keep_a, in_a)
-        sum_a = unstack(add_up(keep_a, in_a).astype(BF), 2, 0)
-        back_3, back_2 = quad_swap(sum_a[0], 3), quad_swap(sum_a[1], 2)
-        total = total + swap_with(total, "y", 1, 2)
-        total = total + swap_with(total, "x", 1, 2)
-        out_pieces = [part(out_sum, quad, 4, 1)] + [p.astype(F32) for p in out_back]
-        dense_grad = in_order([p[:local] for p in out_pieces], 0)
-        down_grad = in_order([p[local:] for p in out_pieces], 0)
-        branch = own_order(branch_sum[0].astype(F32) + got_m.astype(F32), 1)
-        hidden_out = (hidden + branch + b_dense + b_fc2).astype(BF)
-        in_b, back_3, back_2, total, dense_grad, down_grad, terms_sum, send_b, hidden_out = step(
-            in_b, back_3, back_2, total, dense_grad, down_grad, terms_sum, send_b, hidden_out
-        )
-
         got_n = swap_with(terms_sum[1], "l", 1, 2)
-        send_b, in_b = step(send_b, in_b)
-        sum_b = unstack(add_up(send_b[0], in_b), 2, 0)
-        back_1 = quad_swap(sum_b[0].astype(BF), 1)
-        back_1, got_n, sum_b = step(back_1, got_n, sum_b)
         input_grad = norm_grad(group, groups, terms_sum[0], got_n, hidden_in, out_grad, ln_gain)
-        qkv_grad, up_grad = settle(order, [sum_b[1], back_1, back_2, back_3], local)
+        qkv_grad, up_grad = settle(order, [own_in, back_1, back_2, back_3], local)
         gain_grad, shift_grad, out_bias_grad = (
             total[:width], total[width : 2 * width], total[2 * width : 3 * width]
         )

time: 408 us -> 388 us (0.951)
  waiting for transfers between devices: 177 us -> 164 us
  matrix products: 50.4 us -> 46.3 us
    reduce_scatter x2, waiting for transfers between devices: 9.27 us -> 0.01 us  [team_sum(): lax.psum_scatter(values.reshape(2, -1, width), ('x', 'y', 'core'), scatte...]
    dot_general x4, matrix products: 50.4 us -> 46.3 us  [dot(): lax.dot_general(left, right, (dims, ((), ())), preferred_element_type=F32)]
    ppermute x32 -> x36, waiting for transfers between devices: 165 us -> 162 us  [swap_with(): return lax.ppermute(values, axis, [(i, i ^ mask) for i in range(size)])]
    ppermute x32 -> x36, starting transfers between devices: 43.1 us -> 45 us  [swap_with(): return lax.ppermute(values, axis, [(i, i ^ mask) for i in range(size)])]
    unnamed x167 -> x169, local copies, waits for them, and re-layouts: 20.1 us -> 18.3 us
  transfers between devices with their start and end apart: 36 -> 40, of which waited for: 22 -> 24; matrix products, arithmetic and copies ran while one was open for 23% -> 23% of each run, Pallas kernels for 10% -> 11%
where the time goes in v6:
time: 388 us; the launch traced here: 387 us
  waiting for transfers between devices  164 us (42%)
  Pallas kernels  47.4 us (12%)
  matrix products  46.3 us (12%)
  starting transfers between devices  45.3 us (12%)
  other arithmetic  35.8 us (9%)
  local copies, waits for them, and re-layouts  32.9 us (8%)
  between operations  15 us (4%)
    ppermute x36, waiting for transfers between devices, swap_with(): return lax.ppermute(values, axis, [(i, i ^ mask) for i in range(size)])  162 us
    dot_general x4, matrix products, dot(): lax.dot_general(left, right, (dims, ((), ())), preferred_element_type=F32)  46.3 us
    ppermute x36, starting transfers between devices, swap_with(): return lax.ppermute(values, axis, [(i, i ^ mask) for i in range(size)])  45 us
    pallas_call x2, Pallas kernels, by_tokens(): pl.pallas_call(kernel, grid=(rows // ROWS,), in_specs=specs, out_specs=[c...  22.1 us
    unnamed x169, local copies, waits for them, and re-layouts  18.3 us
    pallas_call x1, Pallas kernels, attention_grad(): pl.pallas_call(attend_grad_kernel, grid=(sequences,), in_specs=[spec['wid...  11.6 us
  transfers between devices with their start and end apart: 40, of which 24 were waited for; matrix products, arithmetic and copies ran while one was open for 23% of the time, Pallas kernels for 11%

profile of v6, /device:TPU:0, one launch (start us, length us, event | category | flops | bytes accessed | tf_op | source)
XLA Modules:
  0.0 386.9 jit_solution(65991823983742660)
XLA Ops:
  7.3 2.0 constant_dynamic-slice_fusion.24
  9.4 2.0 dynamic-slice_bitcast_fusion.2
  12.2 4.0 %collective-permute-start.1 = (bf16[256,896]{1,0:T(8,128)(2,1)}, bf16[256,896]{1,0:T(8,128)(2,1)S(1)}, u32[]{:S(2)}, u32[]{:S(2)}) collective-permute-start(bf16[256,896]{1,0:T(8,128)(2,1)} %pad_maximum_fusion.9), channel_id=1, source_target_pairs={{0,16},{16,0},{1,17},{17,1},{2,18},{18,2},{3,19},{19,3},{4,20},{20... | collective-permute-start | bytes 1376264 | tf_op jit(solution)/shard_map/ppermute | solution.py:356
  22.4 14.5 %collective-permute-done.1.refs_4_ = bf16[256,896]{1,0:T(8,128)(2,1)S(1)} collective-permute-done((bf16[256,896]{1,0:T(8,128)(2,1)}, bf16[256,896]{1,0:T(8,128)(2,1)S(1)}, u32[]{:S(2)}, u32[]{:S(2)}) %collective-permute-start.1) | collective-permute-done | bytes 458784 | tf_op jit(solution)/shard_map/ppermute | solution.py:356
  36.9 3.0 collective-permute-done
  44.0 1.9 collective-permute-start.4
  48.6 22.4 %collective-permute-done.5.refs_4_ = bf16[640,256]{1,0:T(8,128)(2,1)S(1)} collective-permute-done((bf16[640,256]{1,0:T(8,128)(2,1)S(1)}, bf16[640,256]{1,0:T(8,128)(2,1)S(1)}, u32[]{:S(2)}, u32[]{:S(2)}) %collective-permute-start.5) | collective-permute-done | bytes 327712 | tf_op jit(solution)/shard_map/ppermute | solution.py:356
  71.0 2.1 collective-permute-done.4.refs_3_
  78.8 4.5 %collective-permute-done.8.refs_1_ = bf16[640,256]{1,0:T(8,128)(2,1)S(1)} collective-permute-done((bf16[640,256]{1,0:T(8,128)(2,1)S(1)}, bf16[640,256]{1,0:T(8,128)(2,1)S(1)}, u32[]{:S(2)}, u32[]{:S(2)}) %collective-permute-start.8) | collective-permute-done | bytes 327712 | tf_op jit(solution)/shard_map/ppermute | solution.py:356
  83.3 10.3 %collective-permute-done.6.refs_5_ = bf16[256,896]{1,0:T(8,128)(2,1)S(1)} collective-permute-done((bf16[256,896]{1,0:T(8,128)(2,1)S(1)}, bf16[256,896]{1,0:T(8,128)(2,1)S(1)}, u32[]{:S(2)}, u32[]{:S(2)}) %collective-permute-start.6) | collective-permute-done | bytes 458784 | tf_op jit(solution)/shard_map/ppermute | solution.py:356
  94.4 2.1 pad_maximum_fusion.4
  97.5 3.4 collective-permute-start.9
  101.1 2.0 collective-permute-start.11
  103.2 1.9 fusion.28
  105.1 23.4 %collective-permute-done.10.refs_2_ = bf16[640,256]{1,0:T(8,128)(2,1)S(1)} collective-permute-done((bf16[640,256]{1,0:T(8,128)(2,1)}, bf16[640,256]{1,0:T(8,128)(2,1)S(1)}, u32[]{:S(2)}, u32[]{:S(2)}) %collective-permute-start.10) | collective-permute-done | bytes 327712 | tf_op jit(solution)/shard_map/ppermute | solution.py:356
  128.5 3.6 collective-permute-done.11.refs_3_
  133.1 5.3 %collective-permute-done.9.refs_6_ = bf16[512,896]{1,0:T(8,128)(2,1)S(1)} collective-permute-done((bf16[512,896]{1,0:T(8,128)(2,1)}, bf16[512,896]{1,0:T(8,128)(2,1)S(1)}, u32[]{:S(2)}, u32[]{:S(2)}) %collective-permute-start.9) | collective-permute-done | bytes 917536 | tf_op jit(solution)/shard_map/ppermute | solution.py:356
  148.8 1.9 copy-done.8
  150.7 12.4 %broadcast_add_fusion.mixed_ref = f32[2048,896]{1,0:T(8,128)S(1)} fusion(f32[896]{0:T(1024)S(1)} %pad_maximum_fusion.22, bf16[2048,2048]{1,0:T(8,128)(2,1)} %bitcast.96, bf16[2048,896]{1,0:T(8,128)(2,1)} %copy-done.8), kind=kOutput, calls=%fused_computation.11 | convolution fusion | flops 7518027776 | bytes 19402240 | tf_op jit(solution)/shard_map/dot_general | solution.py:360
  163.2 7.0 %attend.1 = (bf16[2048,384]{1,0:T(8,128)(2,1)S(1)}, bf16[2048,128]{1,0:T(8,128)(2,1)S(1)}, f32[4,2,512]{2,1,0:T(2,128)S(1)}) custom-call(f32[2048,896]{1,0:T(8,128)S(1)} %broadcast_add_fusion.mixed_ref, f32[512,128]{1,0:T(8,128)S(1)} %copy-done.21, f32[512,128]{1,0:T(8,128)S(1)} %copy-done.19, f32[512,128]{1,0:T(8,128)S(1)} %copy-done.17, ...), custom_call_target="tpu_custom_call" | custom-call | tf_op jit(solution)/shard_map/attend/pallas_call | solution.py:171
  171.5 1.8 pad_maximum_fusion.acts_ref
  173.4 1.9 all-gather.5.cloned.1.call-done
  175.3 8.9 %convolution_convert_fusion.1 = bf16[640,2048]{1,0:T(8,128)(2,1)S(1)} fusion(bf16[2048,640]{1,0:T(8,128)(2,1)} %pad_maximum_fusion.acts_ref, bf16[2048,2048]{1,0:T(8,128)(2,1)} %bitcast.99), kind=kOutput, calls=%fused_computation.13 | convolution fusion | flops 5370019840 | bytes 13631488 | tf_op jit(solution)/shard_map/dot_general | solution.py:360
  188.6 2.5 collective-permute-start.13
  191.1 8.5 %branch.1 = bf16[2048,2048]{1,0:T(8,128)(2,1)} custom-call(bf16[2048,640]{1,0:T(8,128)(2,1)S(1)} %copy-done.16, bf16[128,2048]{1,0:T(8,128)(2,1)S(1)} %place.4.dense_ref, bf16[512,2048]{1,0:T(8,128)(2,1)S(1)} %place.5.down_ref), custom_call_target="tpu_custom_call" | custom-call | flops 5368709120 | bytes 13631488 | tf_op jit(solution)/shard_map/branch/pallas_call | solution.py:305
  203.5 13.6 %back.1 = (bf16[2048,128]{1,0:T(8,128)(2,1)S(1)}, bf16[2048,896]{1,0:T(8,128)(2,1)}) custom-call(bf16[2048,2048]{1,0:T(8,128)(2,1)} %bitcast.100, f32[2048,896]{1,0:T(8,128)} %copy-done.3, bf16[128,2048]{1,0:T(8,128)(2,1)S(1)} %copy-done.40, bf16[512,2048]{1,0:T(8,128)(2,1)S(1)} %copy-done.24), custom_call_target="tpu_custom_call" | custom-call | flops 5368709120 | bytes 22544384 | tf_op jit(solution)/shard_map/back/pallas_call | solution.py:305
  217.1 2.2 copy-done.4
  219.3 11.6 %attend_grad.1 = bf16[2048,896]{1,0:T(8,128)(2,1)S(1)} custom-call(bf16[2048,384]{1,0:T(8,128)(2,1)S(1)} %copy-done.34, bf16[2048,128]{1,0:T(8,128)(2,1)S(1)} %get-tuple-element.212.grad_ref, f32[4,2,512]{2,1,0:T(2,128)S(1)} %get-tuple-element.213.lse_ref, f32[512,128]{1,0:T(8,128)S(1)} %copy-done.22, ...), custom_call_target="tpu_custom_call", output_to_operand_aliasing={{}: (8, {})} | custom-call | tf_op jit(solution)/shard_map/attend_grad/pallas_call | solution.py:190
  230.9 3.2 collective-permute-done.14
  238.4 11.5 %convolution_convert_fusion = bf16[2048,896]{1,0:T(8,128)(2,1)S(1)} fusion(bf16[2048,2048]{1,0:T(8,128)(2,1)} %bitcast.97, bf16[2048,896]{1,0:T(8,128)(2,1)S(1)} %attend_grad.1), kind=kOutput, calls=%fused_computation.12 | convolution fusion | flops 7518027776 | bytes 15728640 | tf_op jit(solution)/shard_map/dot_general | solution.py:360
  249.9 2.5 collective-permute-done.17
  254.0 4.0 %collective-permute-done.15 = bf16[208,1024]{1,0:T(8,128)(2,1)S(1)} collective-permute-done((bf16[208,1024]{1,0:T(8,128)(2,1)S(1)}, bf16[208,1024]{1,0:T(8,128)(2,1)S(1)}, u32[]{:S(2)}, u32[]{:S(2)}) %collective-permute-start.15) | collective-permute-done | bytes 426016 | tf_op jit(solution)/shard_map/ppermute | solution.py:356
  261.3 3.1 collective-permute-start.21
  264.4 13.4 %fusion.46 = (f32[2048]{0:T(1024)S(1)}, f32[2048]{0:T(1024)S(1)}, bf16[2048,2048]{1,0:T(8,128)(2,1)}) fusion(f32[2048]{0:T(1024)S(1)} %get-tuple-element.388, f32[2048]{0:T(1024)S(1)} %get-tuple-element.387, bf16[2048,2048]{1,0:T(8,128)(2,1)} %bitcast.98, bf16[2048,896]{1,0:T(8,128)(2,1)S(1)} %copy-done.6, bf16[2048,896]{1,0:T(8,128)(2,1)S(1)} %copy-done.9), kind=kOutput, calls=%fused_computation.175 | convolution fusion | flops 7545548800 | bytes 24150016 | tf_op jit(solution)/shard_map/dot_general | solution.py:360
  280.6 2.6 convert_reduce_fusion
  286.4 2.8 collective-permute-start.23
  297.5 3.6 collective-permute-start.28
  301.1 1.8 pad_maximum_fusion.8
  303.6 5.8 %collective-permute-done.25.refs_3_ = bf16[256,896]{1,0:T(8,128)(2,1)S(1)} collective-permute-done((bf16[256,896]{1,0:T(8,128)(2,1)}, bf16[256,896]{1,0:T(8,128)(2,1)S(1)}, u32[]{:S(2)}, u32[]{:S(2)}) %collective-permute-start.25) | collective-permute-done | bytes 458784 | tf_op jit(solution)/shard_map/ppermute | solution.py:356
  309.3 11.4 %collective-permute-done.23 = bf16[256,896]{1,0:T(8,128)(2,1)} collective-permute-done((bf16[256,896]{1,0:T(8,128)(2,1)}, bf16[256,896]{1,0:T(8,128)(2,1)}, u32[]{:S(2)}, u32[]{:S(2)}) %collective-permute-start.23) | collective-permute-done | bytes 458784 | tf_op jit(solution)/shard_map/ppermute | solution.py:356
  320.7 9.2 %collective-permute-done.24 = bf16[256,896]{1,0:T(8,128)(2,1)} collective-permute-done((bf16[256,896]{1,0:T(8,128)(2,1)}, bf16[256,896]{1,0:T(8,128)(2,1)}, u32[]{:S(2)}, u32[]{:S(2)}) %collective-permute-start.24) | collective-permute-done | bytes 458784 | tf_op jit(solution)/shard_map/ppermute | solution.py:356
  335.3 2.3 collective-permute-start.29
  338.9 14.5 %collective-permute-done.33 = f32[20480]{0:T(1024)S(1)} collective-permute-done((f32[20480]{0:T(1024)S(1)}, f32[20480]{0:T(1024)S(1)}, u32[]{:S(2)}, u32[]{:S(2)}) %collective-permute-start.33) | collective-permute-done | bytes 81952 | tf_op jit(solution)/shard_map/ppermute | solution.py:356
  353.4 4.2 %collective-permute-done.29 = bf16[256,896]{1,0:T(8,128)(2,1)S(1)} collective-permute-done((bf16[256,896]{1,0:T(8,128)(2,1)S(1)}, bf16[256,896]{1,0:T(8,128)(2,1)S(1)}, u32[]{:S(2)}, u32[]{:S(2)}) %collective-permute-start.29) | collective-permute-done | bytes 458784 | tf_op jit(solution)/shard_map/ppermute | solution.py:356
  357.7 2.7 settle.1
  360.4 3.0 collective-permute-done.35
  367.7 10.3 %collective-permute-done.34.got_ref = bf16[128,2048]{1,0:T(8,128)(2,1)S(1)} collective-permute-done((bf16[128,2048]{1,0:T(8,128)(2,1)S(1)}, bf16[128,2048]{1,0:T(8,128)(2,1)S(1)}, u32[]{:S(2)}, u32[]{:S(2)}) %collective-permute-start.34) | collective-permute-done | bytes 524320 | tf_op jit(solution)/shard_map/ppermute | solution.py:356
  378.0 1.8 norm_grad.1
  (312 shorter events, 77.6 us)
Async XLA Ops:
  7.2 93.8 %copy-start = (f32[3,512]{1,0:T(4,128)S(1)}, f32[3,512]{1,0:T(4,128)}, u32[]{:S(2)}) copy-start(f32[3,512]{1,0:T(4,128)} %param.17) | copy-start | bytes 18436
  7.2 143.5 %all-gather.3.cloned.1.call-start = ((), (), s32[]{:S(2)}) async-start(), calls=%async_computation.2 | async-start | bytes 9437184 | tf_op jit(solution)/shard_map/all_gather | solution.py:462
  12.2 24.7 %collective-permute-start.1 = (bf16[256,896]{1,0:T(8,128)(2,1)}, bf16[256,896]{1,0:T(8,128)(2,1)S(1)}, u32[]{:S(2)}, u32[]{:S(2)}) collective-permute-start(bf16[256,896]{1,0:T(8,128)(2,1)} %pad_maximum_fusion.9), channel_id=1, source_target_pairs={{0,16},{16,0},{1,17},{17,1},{2,18},{18,2},{3,19},{19,3},{4,20},{20... | collective-permute-start | bytes 1376264 | tf_op jit(solution)/shard_map/ppermute | solution.py:356
  17.8 22.1 %collective-permute-start = (bf16[128,2048]{1,0:T(8,128)(2,1)S(1)}, bf16[128,2048]{1,0:T(8,128)(2,1)S(1)}, u32[]{:S(2)}, u32[]{:S(2)}) collective-permute-start(bf16[128,2048]{1,0:T(8,128)(2,1)S(1)} %maximum_select_fusion.1), channel_id=1, source_target_pairs={{0,8},{8,0},{1,9},{9,1},{2,10},{10,2},{3,11},{11,3},{4,12},{12,4},... | collective-permute-start | bytes 1572872 | tf_op jit(solution)/shard_map/ppermute | solution.py:356
  20.7 117.7 %copy-start.25 = (bf16[272,896]{1,0:T(8,128)(2,1)}, bf16[272,896]{1,0:T(8,128)(2,1)S(1)}, u32[]{:S(2)}) copy-start(bf16[272,896]{1,0:T(8,128)(2,1)S(1)} %get-tuple-element.174.refs_0_) | copy-start | bytes 1462276
  41.0 134.3 %all-gather.5.cloned.1.call-start = ((), (), s32[]{:S(2)}) async-start(), calls=%async_computation.3 | async-start | bytes 9437184 | tf_op jit(solution)/shard_map/all_gather | solution.py:462
  42.3 28.6 %collective-permute-start.2 = (bf16[272,896]{1,0:T(8,128)(2,1)}, bf16[272,896]{1,0:T(8,128)(2,1)S(1)}, u32[]{:S(2)}, u32[]{:S(2)}) collective-permute-start(bf16[272,896]{1,0:T(8,128)(2,1)} %get-tuple-element.155), channel_id=1, source_target_pairs={{0,4},{4,0},{8,12},{12,8},{1,5},{5,1},{9,13},{13,9},{2,6},{6,2},{1... | collective-permute-start | bytes 1462280 | tf_op jit(solution)/shard_map/ppermute | solution.py:356
  43.9 27.0 %collective-permute-start.3 = (bf16[272,896]{1,0:T(8,128)(2,1)}, bf16[272,896]{1,0:T(8,128)(2,1)S(1)}, u32[]{:S(2)}, u32[]{:S(2)}) collective-permute-start(bf16[272,896]{1,0:T(8,128)(2,1)} %get-tuple-element.156), channel_id=1, source_target_pairs={{0,8},{4,12},{8,0},{12,4},{1,9},{5,13},{9,1},{13,5},{2,10},{6,14},... | collective-permute-start | bytes 1462280 | tf_op jit(solution)/shard_map/ppermute | solution.py:356
  44.0 29.1 %collective-permute-start.4 = (bf16[272,896]{1,0:T(8,128)(2,1)}, bf16[272,896]{1,0:T(8,128)(2,1)S(1)}, u32[]{:S(2)}, u32[]{:S(2)}) collective-permute-start(bf16[272,896]{1,0:T(8,128)(2,1)} %fusion.23), channel_id=1, source_target_pairs={{0,12},{4,8},{8,4},{12,0},{1,13},{5,9},{9,5},{13,1},{2,14},{6,10},... | collective-permute-start | bytes 1462280 | tf_op jit(solution)/shard_map/ppermute | solution.py:356
  45.9 25.0 %collective-permute-start.5 = (bf16[640,256]{1,0:T(8,128)(2,1)S(1)}, bf16[640,256]{1,0:T(8,128)(2,1)S(1)}, u32[]{:S(2)}, u32[]{:S(2)}) collective-permute-start(bf16[640,256]{1,0:T(8,128)(2,1)S(1)} %pad_maximum_fusion.10.refs_0_), channel_id=1, source_target_pairs={{0,16},{16,0},{1,17},{17,1},{2,18},{18,2},{3,19},{19,3},{4,20},{20... | collective-permute-start | bytes 983048 | tf_op jit(solution)/shard_map/ppermute | solution.py:356
  70.9 67.4 %copy-start.27 = (bf16[272,896]{1,0:T(8,128)(2,1)}, bf16[272,896]{1,0:T(8,128)(2,1)S(1)}, u32[]{:S(2)}) copy-start(bf16[272,896]{1,0:T(8,128)(2,1)S(1)} %collective-permute-done.2.refs_1_) | copy-start | bytes 1462276
  70.9 67.4 %copy-start.29 = (bf16[272,896]{1,0:T(8,128)(2,1)}, bf16[272,896]{1,0:T(8,128)(2,1)S(1)}, u32[]{:S(2)}) copy-start(bf16[272,896]{1,0:T(8,128)(2,1)S(1)} %collective-permute-done.3.refs_2_) | copy-start | bytes 1462276
  73.0 21.4 %collective-permute-start.7 = (bf16[128,2048]{1,0:T(8,128)(2,1)}, bf16[128,2048]{1,0:T(8,128)(2,1)S(1)}, u32[]{:S(2)}, u32[]{:S(2)}) collective-permute-start(bf16[128,2048]{1,0:T(8,128)(2,1)} %maximum_select_fusion.2), channel_id=1, source_target_pairs={{0,8},{8,0},{1,9},{9,1},{2,10},{10,2},{3,11},{11,3},{4,12},{12,4},... | collective-permute-start | bytes 1572872 | tf_op jit(solution)/shard_map/ppermute | solution.py:356
  74.5 19.1 %collective-permute-start.6 = (bf16[256,896]{1,0:T(8,128)(2,1)S(1)}, bf16[256,896]{1,0:T(8,128)(2,1)S(1)}, u32[]{:S(2)}, u32[]{:S(2)}) collective-permute-start(bf16[256,896]{1,0:T(8,128)(2,1)S(1)} %slice.211), channel_id=1, source_target_pairs={{0,16},{16,0},{1,17},{17,1},{2,18},{18,2},{3,19},{19,3},{4,20},{20... | collective-permute-start | bytes 1376264 | tf_op jit(solution)/shard_map/ppermute | solution.py:356
  76.2 7.1 %collective-permute-start.8 = (bf16[640,256]{1,0:T(8,128)(2,1)S(1)}, bf16[640,256]{1,0:T(8,128)(2,1)S(1)}, u32[]{:S(2)}, u32[]{:S(2)}) collective-permute-start(bf16[640,256]{1,0:T(8,128)(2,1)S(1)} %get-tuple-element.164), channel_id=1, source_target_pairs={{0,4},{4,0},{8,12},{12,8},{1,5},{5,1},{9,13},{13,9},{2,6},{6,2},{1... | collective-permute-start | bytes 983048 | tf_op jit(solution)/shard_map/ppermute | solution.py:356
  83.3 56.8 %copy-start.10 = (bf16[640,256]{1,0:T(8,128)(2,1)}, bf16[640,256]{1,0:T(8,128)(2,1)S(1)}, u32[]{:S(2)}) copy-start(bf16[640,256]{1,0:T(8,128)(2,1)S(1)} %collective-permute-done.8.refs_1_) | copy-start | bytes 983044
  96.5 198.1 %reduce-scatter.3.cloned.1.call-start = ((), (), s32[]{:S(2)}) async-start(), calls=%async_computation.4 | async-start | bytes 9437184 | tf_op jit(solution)/shard_map/reduce_scatter | solution.py:540
  97.5 40.8 %collective-permute-start.9 = (bf16[512,896]{1,0:T(8,128)(2,1)}, bf16[512,896]{1,0:T(8,128)(2,1)S(1)}, u32[]{:S(2)}, u32[]{:S(2)}) collective-permute-start(bf16[512,896]{1,0:T(8,128)(2,1)} %pad_maximum_fusion.6), channel_id=1, source_target_pairs={{0,16},{16,0},{1,17},{17,1},{2,18},{18,2},{3,19},{19,3},{4,20},{20... | collective-permute-start | bytes 2752520 | tf_op jit(solution)/shard_map/ppermute | solution.py:356
  101.0 27.5 %collective-permute-start.10 = (bf16[640,256]{1,0:T(8,128)(2,1)}, bf16[640,256]{1,0:T(8,128)(2,1)S(1)}, u32[]{:S(2)}, u32[]{:S(2)}) collective-permute-start(bf16[640,256]{1,0:T(8,128)(2,1)} %get-tuple-element.171), channel_id=1, source_target_pairs={{0,8},{4,12},{8,0},{12,4},{1,9},{5,13},{9,1},{13,5},{2,10},{6,14},... | collective-permute-start | bytes 983048 | tf_op jit(solution)/shard_map/ppermute | solution.py:356
  101.1 30.9 %collective-permute-start.11 = (bf16[640,256]{1,0:T(8,128)(2,1)}, bf16[640,256]{1,0:T(8,128)(2,1)S(1)}, u32[]{:S(2)}, u32[]{:S(2)}) collective-permute-start(bf16[640,256]{1,0:T(8,128)(2,1)} %pad_maximum_fusion.13), channel_id=1, source_target_pairs={{0,12},{4,8},{8,4},{12,0},{1,13},{5,9},{9,5},{13,1},{2,14},{6,10},... | collective-permute-start | bytes 983048 | tf_op jit(solution)/shard_map/ppermute | solution.py:356
  140.5 46.6 %collective-permute-start.12 = (bf16[640,768]{1,0:T(8,128)(2,1)}, bf16[640,768]{1,0:T(8,128)(2,1)S(1)}, u32[]{:S(2)}, u32[]{:S(2)}) collective-permute-start(bf16[640,768]{1,0:T(8,128)(2,1)} %pad_maximum_fusion.5), channel_id=1, source_target_pairs={{0,16},{16,0},{1,17},{17,1},{2,18},{18,2},{3,19},{19,3},{4,20},{20... | collective-permute-start | bytes 2949128 | tf_op jit(solution)/shard_map/ppermute | solution.py:356
  188.6 12.2 %collective-permute-start.13 = (bf16[96,1024]{1,0:T(8,128)(2,1)S(1)}, bf16[96,1024]{1,0:T(8,128)(2,1)S(1)}, u32[]{:S(2)}, u32[]{:S(2)}) collective-permute-start(bf16[96,1024]{1,0:T(8,128)(2,1)S(1)} %get-tuple-element.197), channel_id=1, source_target_pairs={{0,16},{16,0},{1,17},{17,1},{2,18},{18,2},{3,19},{19,3},{4,20},{20... | collective-permute-start | bytes 589832 | tf_op jit(solution)/shard_map/ppermute | solution.py:356
  200.9 164.2 %reduce-scatter.5.cloned.1.call-start = ((), (), s32[]{:S(2)}) async-start(), calls=%async_computation.5 | async-start | bytes 9437184 | tf_op jit(solution)/shard_map/reduce_scatter | solution.py:540
  201.5 32.6 %collective-permute-start.14 = (bf16[336,1024]{1,0:T(8,128)(2,1)}, bf16[336,1024]{1,0:T(8,128)(2,1)S(1)}, u32[]{:S(2)}, u32[]{:S(2)}) collective-permute-start(bf16[336,1024]{1,0:T(8,128)(2,1)} %get-tuple-element.215), channel_id=1, source_target_pairs={{0,16},{16,0},{1,17},{17,1},{2,18},{18,2},{3,19},{19,3},{4,20},{20... | collective-permute-start | bytes 2064392 | tf_op jit(solution)/shard_map/ppermute | solution.py:356
  234.8 15.1 %collective-permute-start.16 = (bf16[432,256]{1,0:T(8,128)(2,1)S(1)}, bf16[432,256]{1,0:T(8,128)(2,1)S(1)}, u32[]{:S(2)}, u32[]{:S(2)}) collective-permute-start(bf16[432,256]{1,0:T(8,128)(2,1)S(1)} %get-tuple-element.228), channel_id=1, source_target_pairs={{0,4},{4,0},{8,12},{12,8},{1,5},{5,1},{9,13},{13,9},{2,6},{6,2},{1... | collective-permute-start | bytes 663560 | tf_op jit(solution)/shard_map/ppermute | solution.py:356
  236.3 16.1 %collective-permute-start.17 = (bf16[432,256]{1,0:T(8,128)(2,1)S(1)}, bf16[432,256]{1,0:T(8,128)(2,1)S(1)}, u32[]{:S(2)}, u32[]{:S(2)}) collective-permute-start(bf16[432,256]{1,0:T(8,128)(2,1)S(1)} %get-tuple-element.229), channel_id=1, source_target_pairs={{0,8},{4,12},{8,0},{12,4},{1,9},{5,13},{9,1},{13,5},{2,10},{6,14},... | collective-permute-start | bytes 663560 | tf_op jit(solution)/shard_map/ppermute | solution.py:356
  236.9 17.1 %collective-permute-start.18 = (bf16[432,256]{1,0:T(8,128)(2,1)S(1)}, bf16[432,256]{1,0:T(8,128)(2,1)S(1)}, u32[]{:S(2)}, u32[]{:S(2)}) collective-permute-start(bf16[432,256]{1,0:T(8,128)(2,1)S(1)} %get-tuple-element.230), channel_id=1, source_target_pairs={{0,12},{4,8},{8,4},{12,0},{1,13},{5,9},{9,5},{13,1},{2,14},{6,10},... | collective-permute-start | bytes 663560 | tf_op jit(solution)/shard_map/ppermute | solution.py:356
  238.3 19.6 %collective-permute-start.15 = (bf16[208,1024]{1,0:T(8,128)(2,1)S(1)}, bf16[208,1024]{1,0:T(8,128)(2,1)S(1)}, u32[]{:S(2)}, u32[]{:S(2)}) collective-permute-start(bf16[208,1024]{1,0:T(8,128)(2,1)S(1)} %copy-done.65), channel_id=1, source_target_pairs={{0,16},{16,0},{1,17},{17,1},{2,18},{18,2},{3,19},{19,3},{4,20},{20... | collective-permute-start | bytes 1277960 | tf_op jit(solution)/shard_map/ppermute | solution.py:356
  259.9 19.8 %collective-permute-start.19 = (bf16[256,896]{1,0:T(8,128)(2,1)S(1)}, bf16[256,896]{1,0:T(8,128)(2,1)S(1)}, u32[]{:S(2)}, u32[]{:S(2)}) collective-permute-start(bf16[256,896]{1,0:T(8,128)(2,1)S(1)} %get-tuple-element.239), channel_id=1, source_target_pairs={{0,16},{16,0},{1,17},{17,1},{2,18},{18,2},{3,19},{19,3},{4,20},{20... | collective-permute-start | bytes 1376264 | tf_op jit(solution)/shard_map/ppermute | solution.py:356
  260.6 17.3 %collective-permute-start.20 = (bf16[208,256]{1,0:T(8,128)(2,1)S(1)}, bf16[208,256]{1,0:T(8,128)(2,1)S(1)}, u32[]{:S(2)}, u32[]{:S(2)}) collective-permute-start(bf16[208,256]{1,0:T(8,128)(2,1)S(1)} %get-tuple-element.247), channel_id=1, source_target_pairs={{0,4},{4,0},{8,12},{12,8},{1,5},{5,1},{9,13},{13,9},{2,6},{6,2},{1... | collective-permute-start | bytes 319496 | tf_op jit(solution)/shard_map/ppermute | solution.py:356
  261.3 16.6 %collective-permute-start.21 = (bf16[208,256]{1,0:T(8,128)(2,1)S(1)}, bf16[208,256]{1,0:T(8,128)(2,1)S(1)}, u32[]{:S(2)}, u32[]{:S(2)}) collective-permute-start(bf16[208,256]{1,0:T(8,128)(2,1)S(1)} %get-tuple-element.248), channel_id=1, source_target_pairs={{0,8},{4,12},{8,0},{12,4},{1,9},{5,13},{9,1},{13,5},{2,10},{6,14},... | collective-permute-start | bytes 319496 | tf_op jit(solution)/shard_map/ppermute | solution.py:356
  264.4 13.5 %collective-permute-start.22 = (bf16[208,256]{1,0:T(8,128)(2,1)S(1)}, bf16[208,256]{1,0:T(8,128)(2,1)S(1)}, u32[]{:S(2)}, u32[]{:S(2)}) collective-permute-start(bf16[208,256]{1,0:T(8,128)(2,1)S(1)} %get-tuple-element.249), channel_id=1, source_target_pairs={{0,12},{4,8},{8,4},{12,0},{1,13},{5,9},{9,5},{13,1},{2,14},{6,10},... | collective-permute-start | bytes 319496 | tf_op jit(solution)/shard_map/ppermute | solution.py:356
  284.2 12.4 %collective-permute-start.27 = (f32[20480]{0:T(1024)}, f32[20480]{0:T(1024)}, u32[]{:S(2)}, u32[]{:S(2)}) collective-permute-start(f32[20480]{0:T(1024)} %pad_maximum_fusion.17), channel_id=1, source_target_pairs={{0,1},{1,0},{2,3},{3,2},{4,5},{5,4},{6,7},{7,6},{8,9},{9,8},{10,11... | collective-permute-start | bytes 245768 | tf_op jit(solution)/shard_map/ppermute | solution.py:356
  285.1 24.2 %collective-permute-start.25 = (bf16[256,896]{1,0:T(8,128)(2,1)}, bf16[256,896]{1,0:T(8,128)(2,1)S(1)}, u32[]{:S(2)}, u32[]{:S(2)}) collective-permute-start(bf16[256,896]{1,0:T(8,128)(2,1)} %add_convert_fusion.2), channel_id=1, source_target_pairs={{0,12},{4,8},{8,4},{12,0},{1,13},{5,9},{9,5},{13,1},{2,14},{6,10},... | collective-permute-start | bytes 1376264 | tf_op jit(solution)/shard_map/ppermute | solution.py:356
  286.4 34.3 %collective-permute-start.23 = (bf16[256,896]{1,0:T(8,128)(2,1)}, bf16[256,896]{1,0:T(8,128)(2,1)}, u32[]{:S(2)}, u32[]{:S(2)}) collective-permute-start(bf16[256,896]{1,0:T(8,128)(2,1)} %get-tuple-element.250), channel_id=1, source_target_pairs={{0,16},{16,0},{1,17},{17,1},{2,18},{18,2},{3,19},{19,3},{4,20},{20... | collective-permute-start | bytes 1376264 | tf_op jit(solution)/shard_map/ppermute | solution.py:356
  289.2 40.7 %collective-permute-start.24 = (bf16[256,896]{1,0:T(8,128)(2,1)}, bf16[256,896]{1,0:T(8,128)(2,1)}, u32[]{:S(2)}, u32[]{:S(2)}) collective-permute-start(bf16[256,896]{1,0:T(8,128)(2,1)} %get-tuple-element.251), channel_id=1, source_target_pairs={{0,16},{16,0},{1,17},{17,1},{2,18},{18,2},{3,19},{19,3},{4,20},{20... | collective-permute-start | bytes 1376264 | tf_op jit(solution)/shard_map/ppermute | solution.py:356
  292.4 38.2 %copy-start.50 = (bf16[256,896]{1,0:T(8,128)(2,1)S(1)}, bf16[256,896]{1,0:T(8,128)(2,1)}, u32[]{:S(2)}) copy-start(bf16[256,896]{1,0:T(8,128)(2,1)} %get-tuple-element.269) | copy-start | bytes 1376260
  294.7 37.6 %copy-start.47 = (bf16[2,128,2048]{2,1,0:T(8,128)(2,1)S(1)}, bf16[2,128,2048]{2,1,0:T(8,128)(2,1)}, u32[]{:S(2)}) copy-start(bf16[2,128,2048]{2,1,0:T(8,128)(2,1)} %reduce-scatter.3.cloned.1.call-done) | copy-start | bytes 3145732
  295.9 36.5 %copy-start.49 = (bf16[256,896]{1,0:T(8,128)(2,1)S(1)}, bf16[256,896]{1,0:T(8,128)(2,1)}, u32[]{:S(2)}) copy-start(bf16[256,896]{1,0:T(8,128)(2,1)} %get-tuple-element.265) | copy-start | bytes 1376260
  295.9 34.0 %collective-permute-start.26 = (bf16[128,2048]{1,0:T(8,128)(2,1)S(1)}, bf16[128,2048]{1,0:T(8,128)(2,1)S(1)}, u32[]{:S(2)}, u32[]{:S(2)}) collective-permute-start(bf16[128,2048]{1,0:T(8,128)(2,1)S(1)} %slice_bitcast_fusion.3), channel_id=1, source_target_pairs={{0,8},{8,0},{1,9},{9,1},{2,10},{10,2},{3,11},{11,3},{4,12},{12,4},... | collective-permute-start | bytes 1572872 | tf_op jit(solution)/shard_map/ppermute | solution.py:356
  297.5 6.0 %collective-permute-start.28 = (f32[20480]{0:T(1024)S(1)}, f32[20480]{0:T(1024)S(1)}, u32[]{:S(2)}, u32[]{:S(2)}) collective-permute-start(f32[20480]{0:T(1024)S(1)} %fusion.44), channel_id=1, source_target_pairs={{0,2},{2,0},{1,3},{3,1},{4,6},{6,4},{5,7},{7,5},{8,10},{10,8},{9,1... | collective-permute-start | bytes 245768 | tf_op jit(solution)/shard_map/ppermute | solution.py:356
  329.9 7.7 %collective-permute-start.32 = (f32[20480]{0:T(1024)S(1)}, f32[20480]{0:T(1024)S(1)}, u32[]{:S(2)}, u32[]{:S(2)}) collective-permute-start(f32[20480]{0:T(1024)S(1)} %add.293), channel_id=1, source_target_pairs={{0,4},{4,0},{1,5},{5,1},{2,6},{6,2},{3,7},{7,3},{8,12},{12,8},{9,1... | collective-permute-start | bytes 245768 | tf_op jit(solution)/shard_map/ppermute | solution.py:356
  331.8 25.9 %collective-permute-start.31 = (bf16[256,896]{1,0:T(8,128)(2,1)S(1)}, bf16[256,896]{1,0:T(8,128)(2,1)S(1)}, u32[]{:S(2)}, u32[]{:S(2)}) collective-permute-start(bf16[256,896]{1,0:T(8,128)(2,1)S(1)} %add_convert_fusion), channel_id=1, source_target_pairs={{0,8},{4,12},{8,0},{12,4},{1,9},{5,13},{9,1},{13,5},{2,10},{6,14},... | collective-permute-start | bytes 1376264 | tf_op jit(solution)/shard_map/ppermute | solution.py:356
  333.7 24.0 %collective-permute-start.30 = (bf16[256,896]{1,0:T(8,128)(2,1)S(1)}, bf16[256,896]{1,0:T(8,128)(2,1)S(1)}, u32[]{:S(2)}, u32[]{:S(2)}) collective-permute-start(bf16[256,896]{1,0:T(8,128)(2,1)S(1)} %add_convert_fusion.1), channel_id=1, source_target_pairs={{0,4},{4,0},{8,12},{12,8},{1,5},{5,1},{9,13},{13,9},{2,6},{6,2},{1... | collective-permute-start | bytes 1376264 | tf_op jit(solution)/shard_map/ppermute | solution.py:356
  335.3 22.2 %collective-permute-start.29 = (bf16[256,896]{1,0:T(8,128)(2,1)S(1)}, bf16[256,896]{1,0:T(8,128)(2,1)S(1)}, u32[]{:S(2)}, u32[]{:S(2)}) collective-permute-start(bf16[256,896]{1,0:T(8,128)(2,1)S(1)} %copy-done.62), channel_id=1, source_target_pairs={{0,16},{16,0},{1,17},{17,1},{2,18},{18,2},{3,19},{19,3},{4,20},{20... | collective-permute-start | bytes 1376264 | tf_op jit(solution)/shard_map/ppermute | solution.py:356
  337.7 15.7 %collective-permute-start.33 = (f32[20480]{0:T(1024)S(1)}, f32[20480]{0:T(1024)S(1)}, u32[]{:S(2)}, u32[]{:S(2)}) collective-permute-start(f32[20480]{0:T(1024)S(1)} %add.297), channel_id=1, source_target_pairs={{0,8},{8,0},{1,9},{9,1},{2,10},{10,2},{3,11},{11,3},{4,12},{12,4},... | collective-permute-start | bytes 245768 | tf_op jit(solution)/shard_map/ppermute | solution.py:356
  357.7 5.8 %collective-permute-start.35 = (f32[20480]{0:T(1024)S(1)}, f32[20480]{0:T(1024)}, u32[]{:S(2)}, u32[]{:S(2)}) collective-permute-start(f32[20480]{0:T(1024)S(1)} %add.298), channel_id=1, source_target_pairs={{0,16},{16,0},{1,17},{17,1},{2,18},{18,2},{3,19},{19,3},{4,20},{20... | collective-permute-start | bytes 245768 | tf_op jit(solution)/shard_map/ppermute | solution.py:356
  366.4 11.6 %collective-permute-start.34 = (bf16[128,2048]{1,0:T(8,128)(2,1)S(1)}, bf16[128,2048]{1,0:T(8,128)(2,1)S(1)}, u32[]{:S(2)}, u32[]{:S(2)}) collective-permute-start(bf16[128,2048]{1,0:T(8,128)(2,1)S(1)} %get-tuple-element.321), channel_id=1, source_target_pairs={{0,8},{8,0},{1,9},{9,1},{2,10},{10,2},{3,11},{11,3},{4,12},{12,4},... | collective-permute-start | bytes 1572872 | tf_op jit(solution)/shard_map/ppermute | solution.py:356
  (74 other events, 581.2 us)
Sparse Core Ops, SparseCore 0:
  41.1 68.2 all-gather.2
  111.8 63.3 all-gather.4
  201.0 81.6 reduce-scatter.2
  286.4 76.4 reduce-scatter.4

commit v7 on v6

--- a/solution.py
+++ b/solution.py
@@ -467,20 +467,18 @@
         hidden = hidden_in.astype(F32)
         mine_n = own_order(layer_norm(hidden, ln_gain, ln_bias).astype(BF), 1)
         mine_g = own_order(out_grad, 1)
+        next_n = swap_with(mine_n, "l", 1, 2)
         in_own = take_in(quad)
+        in_send = [take_in(quad ^ m) for m in (1, 2, 3)]
+        mine_n, next_n, in_own, in_send, mine_g = step(mine_n, next_n, in_own, in_send, mine_g)
+        normed_all = gather_tokens(mine_n, next_n)
         in_first = swap_h(in_own[:rows_in])
-        next_n = swap_with(mine_n, "l", 1, 2)
-        in_send = [take_in(quad ^ m) for m in (1, 2, 3)]
-        mine_n, next_n, in_first, in_send, mine_g = step(
-            mine_n, next_n, in_first, in_send, mine_g
-        )
-        normed_all = gather_tokens(mine_n, next_n)
         in_parts = [in_own] + [quad_swap(piece, m) for m, piece in zip((1, 2, 3), in_send)]
         out_own = take_out(quad)
         out_first = swap_h(out_own)
         out_send = [take_out(quad ^ m) for m in (1, 2, 3)]
-        in_parts, mine_g, out_own, out_first, out_send = step(
-            in_parts, mine_g, out_own, out_first, out_send
+        in_parts, in_first, mine_g, out_own, out_first, out_send = step(
+            in_parts, in_first, mine_g, out_own, out_first, out_send
         )
 
         in_low = swap_h(in_parts[1][:rows_in])

time: 388 us -> 387 us (level)
  waiting for transfers between devices: 164 us -> 172 us
  local copies, waits for them, and re-layouts: 32.9 us -> 28.8 us
    ppermute x36, waiting for transfers between devices: 162 us -> 171 us  [swap_with(): return lax.ppermute(values, axis, [(i, i ^ mask) for i in range(size)])]
    select_n x5, other arithmetic: 4.55 us -> 0.43 us  [in_order(): jnp.where(lb == 1, jnp.where(xb == 1, parts[j ^ 3], parts[j ^ 2]), jnp.wh...]
    unnamed x169 -> x135, local copies, waits for them, and re-layouts: 18.3 us -> 18.1 us
  transfers between devices with their start and end apart: 40 -> 40, of which waited for: 24 -> 25; matrix products, arithmetic and copies ran while one was open for 23% -> 21% of each run, Pallas kernels for 11% -> 11%
where the time goes in v7:
time: 387 us; the launch traced here: 386 us
  waiting for transfers between devices  172 us (44%)
  Pallas kernels  47.4 us (12%)
  matrix products  46.7 us (12%)
  starting transfers between devices  43.2 us (11%)
  other arithmetic  33.5 us (9%)
  local copies, waits for them, and re-layouts  28.8 us (7%)
  between operations  14.9 us (4%)
    ppermute x36, waiting for transfers between devices, swap_with(): return lax.ppermute(values, axis, [(i, i ^ mask) for i in range(size)])  171 us
    dot_general x4, matrix products, dot(): lax.dot_general(left, right, (dims, ((), ())), preferred_element_type=F32)  46.7 us
    ppermute x36, starting transfers between devices, swap_with(): return lax.ppermute(values, axis, [(i, i ^ mask) for i in range(size)])  42.8 us
    pallas_call x2, Pallas kernels, by_tokens(): pl.pallas_call(kernel, grid=(rows // ROWS,), in_specs=specs, out_specs=[c...  22.1 us
    unnamed x135, local copies, waits for them, and re-layouts  18.1 us
    pallas_call x1, Pallas kernels, attention_grad(): pl.pallas_call(attend_grad_kernel, grid=(sequences,), in_specs=[spec['wid...  11.7 us
  transfers between devices with their start and end apart: 40, of which 25 were waited for; matrix products, arithmetic and copies ran while one was open for 21% of the time, Pallas kernels for 11%

profile of v7, /device:TPU:0, one launch (start us, length us, event | category | flops | bytes accessed | tf_op | source)
XLA Modules:
  0.0 386.0 jit_solution(16528109719690381220)
XLA Ops:
  13.0 3.1 collective-permute-start
  20.4 7.7 %collective-permute-done = bf16[128,2048]{1,0:T(8,128)(2,1)} collective-permute-done((bf16[128,2048]{1,0:T(8,128)(2,1)S(1)}, bf16[128,2048]{1,0:T(8,128)(2,1)}, u32[]{:S(2)}, u32[]{:S(2)}) %collective-permute-start) | collective-permute-done | bytes 524320 | tf_op jit(solution)/shard_map/ppermute | solution.py:356
  28.1 2.1 pad_maximum_fusion.3
  30.5 2.8 collective-permute-start.4
  38.6 31.6 %collective-permute-done.5.refs_4_ = bf16[640,256]{1,0:T(8,128)(2,1)S(1)} collective-permute-done((bf16[640,256]{1,0:T(8,128)(2,1)S(1)}, bf16[640,256]{1,0:T(8,128)(2,1)S(1)}, u32[]{:S(2)}, u32[]{:S(2)}) %collective-permute-start.5) | collective-permute-done | bytes 327712 | tf_op jit(solution)/shard_map/ppermute | solution.py:356
  70.2 2.4 collective-permute-done.3.refs_3_
  72.7 3.0 collective-permute-start.6
  78.3 13.7 %collective-permute-done.8.refs_1_ = bf16[640,256]{1,0:T(8,128)(2,1)S(1)} collective-permute-done((bf16[640,256]{1,0:T(8,128)(2,1)S(1)}, bf16[640,256]{1,0:T(8,128)(2,1)S(1)}, u32[]{:S(2)}, u32[]{:S(2)}) %collective-permute-start.8) | collective-permute-done | bytes 327712 | tf_op jit(solution)/shard_map/ppermute | solution.py:356
  96.0 2.5 collective-permute-start.9
  99.4 2.2 collective-permute-start.11
  101.6 1.9 fusion.28
  103.5 22.9 %collective-permute-done.10.refs_2_ = bf16[640,256]{1,0:T(8,128)(2,1)S(1)} collective-permute-done((bf16[640,256]{1,0:T(8,128)(2,1)}, bf16[640,256]{1,0:T(8,128)(2,1)S(1)}, u32[]{:S(2)}, u32[]{:S(2)}) %collective-permute-start.10) | collective-permute-done | bytes 327712 | tf_op jit(solution)/shard_map/ppermute | solution.py:356
  126.4 3.6 collective-permute-done.11.refs_3_
  131.0 6.9 %collective-permute-done.9.refs_6_ = bf16[512,896]{1,0:T(8,128)(2,1)S(1)} collective-permute-done((bf16[512,896]{1,0:T(8,128)(2,1)}, bf16[512,896]{1,0:T(8,128)(2,1)S(1)}, u32[]{:S(2)}, u32[]{:S(2)}) %collective-permute-start.9) | collective-permute-done | bytes 917536 | tf_op jit(solution)/shard_map/ppermute | solution.py:356
  146.9 1.9 copy-done.8
  148.9 12.6 %broadcast_add_fusion.mixed_ref = f32[2048,896]{1,0:T(8,128)S(1)} fusion(f32[896]{0:T(1024)S(1)} %pad_maximum_fusion.21, bf16[2048,2048]{1,0:T(8,128)(2,1)} %bitcast.96, bf16[2048,896]{1,0:T(8,128)(2,1)} %copy-done.8), kind=kOutput, calls=%fused_computation.11 | convolution fusion | flops 7518027776 | bytes 19402240 | tf_op jit(solution)/shard_map/dot_general | solution.py:360
  161.5 7.0 %attend.1 = (bf16[2048,384]{1,0:T(8,128)(2,1)S(1)}, bf16[2048,128]{1,0:T(8,128)(2,1)S(1)}, f32[4,2,512]{2,1,0:T(2,128)S(1)}) custom-call(f32[2048,896]{1,0:T(8,128)S(1)} %broadcast_add_fusion.mixed_ref, f32[512,128]{1,0:T(8,128)S(1)} %copy-done.20, f32[512,128]{1,0:T(8,128)S(1)} %copy-done.18, f32[512,128]{1,0:T(8,128)S(1)} %copy-done.17, ...), custom_call_target="tpu_custom_call" | custom-call | tf_op jit(solution)/shard_map/attend/pallas_call | solution.py:171
  169.8 1.7 pad_maximum_fusion.acts_ref
  171.6 8.9 %convolution_convert_fusion.1 = bf16[640,2048]{1,0:T(8,128)(2,1)S(1)} fusion(bf16[2048,640]{1,0:T(8,128)(2,1)} %pad_maximum_fusion.acts_ref, bf16[2048,2048]{1,0:T(8,128)(2,1)} %bitcast.99), kind=kOutput, calls=%fused_computation.13 | convolution fusion | flops 5370019840 | bytes 13631488 | tf_op jit(solution)/shard_map/dot_general | solution.py:360
  185.9 2.0 collective-permute-start.13
  187.9 8.6 %branch.1 = bf16[2048,2048]{1,0:T(8,128)(2,1)} custom-call(bf16[2048,640]{1,0:T(8,128)(2,1)S(1)} %copy-done.16, bf16[128,2048]{1,0:T(8,128)(2,1)S(1)} %place.4.dense_ref, bf16[512,2048]{1,0:T(8,128)(2,1)S(1)} %place.5.down_ref), custom_call_target="tpu_custom_call" | custom-call | flops 5368709120 | bytes 13631488 | tf_op jit(solution)/shard_map/branch/pallas_call | solution.py:305
  201.2 13.5 %back.1 = (bf16[2048,128]{1,0:T(8,128)(2,1)S(1)}, bf16[2048,896]{1,0:T(8,128)(2,1)}) custom-call(bf16[2048,2048]{1,0:T(8,128)(2,1)} %bitcast.100, f32[2048,896]{1,0:T(8,128)} %copy-done.3, bf16[128,2048]{1,0:T(8,128)(2,1)S(1)} %copy-done.37, bf16[512,2048]{1,0:T(8,128)(2,1)S(1)} %copy-done.23), custom_call_target="tpu_custom_call" | custom-call | flops 5368709120 | bytes 22544384 | tf_op jit(solution)/shard_map/back/pallas_call | solution.py:305
  214.7 2.1 copy-done.4
  216.8 11.7 %attend_grad.1 = bf16[2048,896]{1,0:T(8,128)(2,1)S(1)} custom-call(bf16[2048,384]{1,0:T(8,128)(2,1)S(1)} %copy-done.31, bf16[2048,128]{1,0:T(8,128)(2,1)S(1)} %get-tuple-element.214.grad_ref, f32[4,2,512]{2,1,0:T(2,128)S(1)} %get-tuple-element.215.lse_ref, f32[512,128]{1,0:T(8,128)S(1)} %copy-done.21, ...), custom_call_target="tpu_custom_call", output_to_operand_aliasing={{}: (8, {})} | custom-call | tf_op jit(solution)/shard_map/attend_grad/pallas_call | solution.py:190
  228.5 2.5 collective-permute-done.14
  231.7 2.3 collective-permute-start.16
  236.0 11.5 %convolution_convert_fusion = bf16[2048,896]{1,0:T(8,128)(2,1)S(1)} fusion(bf16[2048,2048]{1,0:T(8,128)(2,1)} %bitcast.97, bf16[2048,896]{1,0:T(8,128)(2,1)S(1)} %attend_grad.1), kind=kOutput, calls=%fused_computation.12 | convolution fusion | flops 7518027776 | bytes 15728640 | tf_op jit(solution)/shard_map/dot_general | solution.py:360
  247.5 1.8 collective-permute-done.17
  249.3 2.4 collective-permute-done.18
  251.7 5.1 %collective-permute-done.15 = bf16[208,1024]{1,0:T(8,128)(2,1)S(1)} collective-permute-done((bf16[208,1024]{1,0:T(8,128)(2,1)S(1)}, bf16[208,1024]{1,0:T(8,128)(2,1)S(1)}, u32[]{:S(2)}, u32[]{:S(2)}) %collective-permute-start.15) | collective-permute-done | bytes 426016 | tf_op jit(solution)/shard_map/ppermute | solution.py:356
  258.7 1.7 collective-permute-start.20
  260.4 1.9 collective-permute-start.21
  262.3 13.8 %fusion.46 = (f32[2048]{0:T(1024)S(1)}, f32[2048]{0:T(1024)S(1)}, bf16[2048,2048]{1,0:T(8,128)(2,1)}) fusion(f32[2048]{0:T(1024)S(1)} %get-tuple-element.390, f32[2048]{0:T(1024)S(1)} %get-tuple-element.389, bf16[2048,2048]{1,0:T(8,128)(2,1)} %bitcast.98, bf16[2048,896]{1,0:T(8,128)(2,1)S(1)} %copy-done.6, bf16[2048,896]{1,0:T(8,128)(2,1)S(1)} %copy-done.9), kind=kOutput, calls=%fused_computation.174 | convolution fusion | flops 7545548800 | bytes 24150016 | tf_op jit(solution)/shard_map/dot_general | solution.py:360
  276.1 2.7 collective-permute-done.19
  279.7 2.6 convert_reduce_fusion
  284.5 3.3 collective-permute-start.23
  291.0 1.9 collective-permute-start.26
  296.3 2.0 collective-permute-done.28
  298.3 9.5 %collective-permute-done.25.refs_3_ = bf16[256,896]{1,0:T(8,128)(2,1)S(1)} collective-permute-done((bf16[256,896]{1,0:T(8,128)(2,1)}, bf16[256,896]{1,0:T(8,128)(2,1)S(1)}, u32[]{:S(2)}, u32[]{:S(2)}) %collective-permute-start.25) | collective-permute-done | bytes 458784 | tf_op jit(solution)/shard_map/ppermute | solution.py:356
  307.9 11.4 %collective-permute-done.23 = bf16[256,896]{1,0:T(8,128)(2,1)} collective-permute-done((bf16[256,896]{1,0:T(8,128)(2,1)}, bf16[256,896]{1,0:T(8,128)(2,1)}, u32[]{:S(2)}, u32[]{:S(2)}) %collective-permute-start.23) | collective-permute-done | bytes 458784 | tf_op jit(solution)/shard_map/ppermute | solution.py:356
  319.3 9.4 %collective-permute-done.24 = bf16[256,896]{1,0:T(8,128)(2,1)} collective-permute-done((bf16[256,896]{1,0:T(8,128)(2,1)}, bf16[256,896]{1,0:T(8,128)(2,1)}, u32[]{:S(2)}, u32[]{:S(2)}) %collective-permute-start.24) | collective-permute-done | bytes 458784 | tf_op jit(solution)/shard_map/ppermute | solution.py:356
  333.6 3.0 collective-permute-start.29
  337.8 14.4 %collective-permute-done.33 = f32[20480]{0:T(1024)S(1)} collective-permute-done((f32[20480]{0:T(1024)S(1)}, f32[20480]{0:T(1024)S(1)}, u32[]{:S(2)}, u32[]{:S(2)}) %collective-permute-start.33) | collective-permute-done | bytes 81952 | tf_op jit(solution)/shard_map/ppermute | solution.py:356
  352.2 4.2 %collective-permute-done.29 = bf16[256,896]{1,0:T(8,128)(2,1)S(1)} collective-permute-done((bf16[256,896]{1,0:T(8,128)(2,1)S(1)}, bf16[256,896]{1,0:T(8,128)(2,1)S(1)}, u32[]{:S(2)}, u32[]{:S(2)}) %collective-permute-start.29) | collective-permute-done | bytes 458784 | tf_op jit(solution)/shard_map/ppermute | solution.py:356
  356.7 2.7 settle.1
  359.4 3.0 collective-permute-done.35
  366.6 10.5 %collective-permute-done.34.got_ref = bf16[128,2048]{1,0:T(8,128)(2,1)S(1)} collective-permute-done((bf16[128,2048]{1,0:T(8,128)(2,1)S(1)}, bf16[128,2048]{1,0:T(8,128)(2,1)S(1)}, u32[]{:S(2)}, u32[]{:S(2)}) %collective-permute-start.34) | collective-permute-done | bytes 524320 | tf_op jit(solution)/shard_map/ppermute | solution.py:356
  377.1 1.8 norm_grad.1
  (278 shorter events, 69.5 us)
Async XLA Ops:
  7.2 91.3 %copy-start = (f32[3,512]{1,0:T(4,128)S(1)}, f32[3,512]{1,0:T(4,128)}, u32[]{:S(2)}) copy-start(f32[3,512]{1,0:T(4,128)} %param.17) | copy-start | bytes 18436
  7.2 141.6 %all-gather.3.cloned.1.call-start = ((), (), s32[]{:S(2)}) async-start(), calls=%async_computation.2 | async-start | bytes 9437184 | tf_op jit(solution)/shard_map/all_gather | solution.py:462
  13.0 15.1 %collective-permute-start = (bf16[128,2048]{1,0:T(8,128)(2,1)S(1)}, bf16[128,2048]{1,0:T(8,128)(2,1)}, u32[]{:S(2)}, u32[]{:S(2)}) collective-permute-start(bf16[128,2048]{1,0:T(8,128)(2,1)S(1)} %maximum_select_fusion.1), channel_id=1, source_target_pairs={{0,8},{8,0},{1,9},{9,1},{2,10},{10,2},{3,11},{11,3},{4,12},{12,4},... | collective-permute-start | bytes 1572872 | tf_op jit(solution)/shard_map/ppermute | solution.py:356
  30.3 141.3 %all-gather.5.cloned.1.call-start = ((), (), s32[]{:S(2)}) async-start(), calls=%async_computation.3 | async-start | bytes 9437184 | tf_op jit(solution)/shard_map/all_gather | solution.py:462
  30.5 39.7 %collective-permute-start.4 = (bf16[256,896]{1,0:T(8,128)(2,1)S(1)}, bf16[256,896]{1,0:T(8,128)(2,1)S(1)}, u32[]{:S(2)}, u32[]{:S(2)}) collective-permute-start(bf16[256,896]{1,0:T(8,128)(2,1)S(1)} %slice.214), channel_id=1, source_target_pairs={{0,16},{16,0},{1,17},{17,1},{2,18},{18,2},{3,19},{19,3},{4,20},{20... | collective-permute-start | bytes 1376264 | tf_op jit(solution)/shard_map/ppermute | solution.py:356
  33.3 36.9 %collective-permute-start.1 = (bf16[272,896]{1,0:T(8,128)(2,1)}, bf16[272,896]{1,0:T(8,128)(2,1)S(1)}, u32[]{:S(2)}, u32[]{:S(2)}) collective-permute-start(bf16[272,896]{1,0:T(8,128)(2,1)} %get-tuple-element.156), channel_id=1, source_target_pairs={{0,4},{4,0},{8,12},{12,8},{1,5},{5,1},{9,13},{13,9},{2,6},{6,2},{1... | collective-permute-start | bytes 1462280 | tf_op jit(solution)/shard_map/ppermute | solution.py:356
  34.8 35.4 %collective-permute-start.2 = (bf16[272,896]{1,0:T(8,128)(2,1)}, bf16[272,896]{1,0:T(8,128)(2,1)S(1)}, u32[]{:S(2)}, u32[]{:S(2)}) collective-permute-start(bf16[272,896]{1,0:T(8,128)(2,1)} %fusion.23), channel_id=1, source_target_pairs={{0,8},{4,12},{8,0},{12,4},{1,9},{5,13},{9,1},{13,5},{2,10},{6,14},... | collective-permute-start | bytes 1462280 | tf_op jit(solution)/shard_map/ppermute | solution.py:356
  36.3 36.2 %collective-permute-start.3 = (bf16[272,896]{1,0:T(8,128)(2,1)}, bf16[272,896]{1,0:T(8,128)(2,1)S(1)}, u32[]{:S(2)}, u32[]{:S(2)}) collective-permute-start(bf16[272,896]{1,0:T(8,128)(2,1)} %get-tuple-element.158), channel_id=1, source_target_pairs={{0,12},{4,8},{8,4},{12,0},{1,13},{5,9},{9,5},{13,1},{2,14},{6,10},... | collective-permute-start | bytes 1462280 | tf_op jit(solution)/shard_map/ppermute | solution.py:356
  36.8 57.1 %copy-start.45 = (bf16[128,2048]{1,0:T(8,128)(2,1)S(1)}, bf16[128,2048]{1,0:T(8,128)(2,1)}, u32[]{:S(2)}) copy-start(bf16[128,2048]{1,0:T(8,128)(2,1)} %maximum_select_fusion.2) | copy-start | bytes 1572868
  36.8 33.3 %collective-permute-start.5 = (bf16[640,256]{1,0:T(8,128)(2,1)S(1)}, bf16[640,256]{1,0:T(8,128)(2,1)S(1)}, u32[]{:S(2)}, u32[]{:S(2)}) collective-permute-start(bf16[640,256]{1,0:T(8,128)(2,1)S(1)} %pad_maximum_fusion.9.refs_0_), channel_id=1, source_target_pairs={{0,16},{16,0},{1,17},{17,1},{2,18},{18,2},{3,19},{19,3},{4,20},{20... | collective-permute-start | bytes 983048 | tf_op jit(solution)/shard_map/ppermute | solution.py:356
  70.2 67.7 %copy-start.24 = (bf16[272,896]{1,0:T(8,128)(2,1)}, bf16[272,896]{1,0:T(8,128)(2,1)S(1)}, u32[]{:S(2)}) copy-start(bf16[272,896]{1,0:T(8,128)(2,1)S(1)} %collective-permute-done.1.refs_1_) | copy-start | bytes 1462276
  70.2 67.7 %copy-start.26 = (bf16[272,896]{1,0:T(8,128)(2,1)}, bf16[272,896]{1,0:T(8,128)(2,1)S(1)}, u32[]{:S(2)}) copy-start(bf16[272,896]{1,0:T(8,128)(2,1)S(1)} %collective-permute-done.2.refs_2_) | copy-start | bytes 1462276
  72.6 65.4 %copy-start.28 = (bf16[272,896]{1,0:T(8,128)(2,1)}, bf16[272,896]{1,0:T(8,128)(2,1)S(1)}, u32[]{:S(2)}) copy-start(bf16[272,896]{1,0:T(8,128)(2,1)S(1)} %collective-permute-done.3.refs_3_) | copy-start | bytes 1462276
  72.6 21.4 %collective-permute-start.7 = (bf16[128,2048]{1,0:T(8,128)(2,1)}, bf16[128,2048]{1,0:T(8,128)(2,1)S(1)}, u32[]{:S(2)}, u32[]{:S(2)}) collective-permute-start(bf16[128,2048]{1,0:T(8,128)(2,1)} %maximum_select_fusion.2), channel_id=1, source_target_pairs={{0,8},{8,0},{1,9},{9,1},{2,10},{10,2},{3,11},{11,3},{4,12},{12,4},... | collective-permute-start | bytes 1572872 | tf_op jit(solution)/shard_map/ppermute | solution.py:356
  72.7 19.4 %collective-permute-start.6 = (bf16[256,896]{1,0:T(8,128)(2,1)S(1)}, bf16[256,896]{1,0:T(8,128)(2,1)S(1)}, u32[]{:S(2)}, u32[]{:S(2)}) collective-permute-start(bf16[256,896]{1,0:T(8,128)(2,1)S(1)} %slice.215), channel_id=1, source_target_pairs={{0,16},{16,0},{1,17},{17,1},{2,18},{18,2},{3,19},{19,3},{4,20},{20... | collective-permute-start | bytes 1376264 | tf_op jit(solution)/shard_map/ppermute | solution.py:356
  75.8 16.2 %collective-permute-start.8 = (bf16[640,256]{1,0:T(8,128)(2,1)S(1)}, bf16[640,256]{1,0:T(8,128)(2,1)S(1)}, u32[]{:S(2)}, u32[]{:S(2)}) collective-permute-start(bf16[640,256]{1,0:T(8,128)(2,1)S(1)} %get-tuple-element.166), channel_id=1, source_target_pairs={{0,4},{4,0},{8,12},{12,8},{1,5},{5,1},{9,13},{13,9},{2,6},{6,2},{1... | collective-permute-start | bytes 983048 | tf_op jit(solution)/shard_map/ppermute | solution.py:356
  92.0 47.0 %copy-start.10 = (bf16[640,256]{1,0:T(8,128)(2,1)}, bf16[640,256]{1,0:T(8,128)(2,1)S(1)}, u32[]{:S(2)}) copy-start(bf16[640,256]{1,0:T(8,128)(2,1)S(1)} %collective-permute-done.8.refs_1_) | copy-start | bytes 983044
  95.0 194.8 %reduce-scatter.3.cloned.1.call-start = ((), (), s32[]{:S(2)}) async-start(), calls=%async_computation.4 | async-start | bytes 9437184 | tf_op jit(solution)/shard_map/reduce_scatter | solution.py:538
  96.0 41.9 %collective-permute-start.9 = (bf16[512,896]{1,0:T(8,128)(2,1)}, bf16[512,896]{1,0:T(8,128)(2,1)S(1)}, u32[]{:S(2)}, u32[]{:S(2)}) collective-permute-start(bf16[512,896]{1,0:T(8,128)(2,1)} %pad_maximum_fusion.6), channel_id=1, source_target_pairs={{0,16},{16,0},{1,17},{17,1},{2,18},{18,2},{3,19},{19,3},{4,20},{20... | collective-permute-start | bytes 2752520 | tf_op jit(solution)/shard_map/ppermute | solution.py:356
  98.5 27.9 %collective-permute-start.10 = (bf16[640,256]{1,0:T(8,128)(2,1)}, bf16[640,256]{1,0:T(8,128)(2,1)S(1)}, u32[]{:S(2)}, u32[]{:S(2)}) collective-permute-start(bf16[640,256]{1,0:T(8,128)(2,1)} %get-tuple-element.173), channel_id=1, source_target_pairs={{0,8},{4,12},{8,0},{12,4},{1,9},{5,13},{9,1},{13,5},{2,10},{6,14},... | collective-permute-start | bytes 983048 | tf_op jit(solution)/shard_map/ppermute | solution.py:356
  99.4 30.6 %collective-permute-start.11 = (bf16[640,256]{1,0:T(8,128)(2,1)}, bf16[640,256]{1,0:T(8,128)(2,1)S(1)}, u32[]{:S(2)}, u32[]{:S(2)}) collective-permute-start(bf16[640,256]{1,0:T(8,128)(2,1)} %pad_maximum_fusion.12), channel_id=1, source_target_pairs={{0,12},{4,8},{8,4},{12,0},{1,13},{5,9},{9,5},{13,1},{2,14},{6,10},... | collective-permute-start | bytes 983048 | tf_op jit(solution)/shard_map/ppermute | solution.py:356
  139.4 45.0 %collective-permute-start.12 = (bf16[640,768]{1,0:T(8,128)(2,1)}, bf16[640,768]{1,0:T(8,128)(2,1)S(1)}, u32[]{:S(2)}, u32[]{:S(2)}) collective-permute-start(bf16[640,768]{1,0:T(8,128)(2,1)} %pad_maximum_fusion.5), channel_id=1, source_target_pairs={{0,16},{16,0},{1,17},{17,1},{2,18},{18,2},{3,19},{19,3},{4,20},{20... | collective-permute-start | bytes 2949128 | tf_op jit(solution)/shard_map/ppermute | solution.py:356
  185.9 12.0 %collective-permute-start.13 = (bf16[96,1024]{1,0:T(8,128)(2,1)S(1)}, bf16[96,1024]{1,0:T(8,128)(2,1)S(1)}, u32[]{:S(2)}, u32[]{:S(2)}) collective-permute-start(bf16[96,1024]{1,0:T(8,128)(2,1)S(1)} %get-tuple-element.199), channel_id=1, source_target_pairs={{0,16},{16,0},{1,17},{17,1},{2,18},{18,2},{3,19},{19,3},{4,20},{20... | collective-permute-start | bytes 589832 | tf_op jit(solution)/shard_map/ppermute | solution.py:356
  198.6 165.4 %reduce-scatter.5.cloned.1.call-start = ((), (), s32[]{:S(2)}) async-start(), calls=%async_computation.5 | async-start | bytes 9437184 | tf_op jit(solution)/shard_map/reduce_scatter | solution.py:538
  199.3 31.8 %collective-permute-start.14 = (bf16[336,1024]{1,0:T(8,128)(2,1)}, bf16[336,1024]{1,0:T(8,128)(2,1)S(1)}, u32[]{:S(2)}, u32[]{:S(2)}) collective-permute-start(bf16[336,1024]{1,0:T(8,128)(2,1)} %get-tuple-element.217), channel_id=1, source_target_pairs={{0,16},{16,0},{1,17},{17,1},{2,18},{18,2},{3,19},{19,3},{4,20},{20... | collective-permute-start | bytes 2064392 | tf_op jit(solution)/shard_map/ppermute | solution.py:356
  231.7 15.8 %collective-permute-start.16 = (bf16[432,256]{1,0:T(8,128)(2,1)S(1)}, bf16[432,256]{1,0:T(8,128)(2,1)S(1)}, u32[]{:S(2)}, u32[]{:S(2)}) collective-permute-start(bf16[432,256]{1,0:T(8,128)(2,1)S(1)} %get-tuple-element.230), channel_id=1, source_target_pairs={{0,4},{4,0},{8,12},{12,8},{1,5},{5,1},{9,13},{13,9},{2,6},{6,2},{1... | collective-permute-start | bytes 663560 | tf_op jit(solution)/shard_map/ppermute | solution.py:356
  234.0 15.3 %collective-permute-start.17 = (bf16[432,256]{1,0:T(8,128)(2,1)S(1)}, bf16[432,256]{1,0:T(8,128)(2,1)S(1)}, u32[]{:S(2)}, u32[]{:S(2)}) collective-permute-start(bf16[432,256]{1,0:T(8,128)(2,1)S(1)} %get-tuple-element.231), channel_id=1, source_target_pairs={{0,8},{4,12},{8,0},{12,4},{1,9},{5,13},{9,1},{13,5},{2,10},{6,14},... | collective-permute-start | bytes 663560 | tf_op jit(solution)/shard_map/ppermute | solution.py:356
  234.0 17.7 %collective-permute-start.18 = (bf16[432,256]{1,0:T(8,128)(2,1)S(1)}, bf16[432,256]{1,0:T(8,128)(2,1)S(1)}, u32[]{:S(2)}, u32[]{:S(2)}) collective-permute-start(bf16[432,256]{1,0:T(8,128)(2,1)S(1)} %get-tuple-element.232), channel_id=1, source_target_pairs={{0,12},{4,8},{8,4},{12,0},{1,13},{5,9},{9,5},{13,1},{2,14},{6,10},... | collective-permute-start | bytes 663560 | tf_op jit(solution)/shard_map/ppermute | solution.py:356
  235.5 21.3 %collective-permute-start.15 = (bf16[208,1024]{1,0:T(8,128)(2,1)S(1)}, bf16[208,1024]{1,0:T(8,128)(2,1)S(1)}, u32[]{:S(2)}, u32[]{:S(2)}) collective-permute-start(bf16[208,1024]{1,0:T(8,128)(2,1)S(1)} %copy-done.56), channel_id=1, source_target_pairs={{0,16},{16,0},{1,17},{17,1},{2,18},{18,2},{3,19},{19,3},{4,20},{20... | collective-permute-start | bytes 1277960 | tf_op jit(solution)/shard_map/ppermute | solution.py:356
  258.7 20.1 %collective-permute-start.19 = (bf16[256,896]{1,0:T(8,128)(2,1)S(1)}, bf16[256,896]{1,0:T(8,128)(2,1)S(1)}, u32[]{:S(2)}, u32[]{:S(2)}) collective-permute-start(bf16[256,896]{1,0:T(8,128)(2,1)S(1)} %get-tuple-element.241), channel_id=1, source_target_pairs={{0,16},{16,0},{1,17},{17,1},{2,18},{18,2},{3,19},{19,3},{4,20},{20... | collective-permute-start | bytes 1376264 | tf_op jit(solution)/shard_map/ppermute | solution.py:356
  258.7 17.4 %collective-permute-start.20 = (bf16[208,256]{1,0:T(8,128)(2,1)S(1)}, bf16[208,256]{1,0:T(8,128)(2,1)S(1)}, u32[]{:S(2)}, u32[]{:S(2)}) collective-permute-start(bf16[208,256]{1,0:T(8,128)(2,1)S(1)} %get-tuple-element.249), channel_id=1, source_target_pairs={{0,4},{4,0},{8,12},{12,8},{1,5},{5,1},{9,13},{13,9},{2,6},{6,2},{1... | collective-permute-start | bytes 319496 | tf_op jit(solution)/shard_map/ppermute | solution.py:356
  260.4 15.8 %collective-permute-start.21 = (bf16[208,256]{1,0:T(8,128)(2,1)S(1)}, bf16[208,256]{1,0:T(8,128)(2,1)S(1)}, u32[]{:S(2)}, u32[]{:S(2)}) collective-permute-start(bf16[208,256]{1,0:T(8,128)(2,1)S(1)} %get-tuple-element.250), channel_id=1, source_target_pairs={{0,8},{4,12},{8,0},{12,4},{1,9},{5,13},{9,1},{13,5},{2,10},{6,14},... | collective-permute-start | bytes 319496 | tf_op jit(solution)/shard_map/ppermute | solution.py:356
  262.2 13.9 %collective-permute-start.22 = (bf16[208,256]{1,0:T(8,128)(2,1)S(1)}, bf16[208,256]{1,0:T(8,128)(2,1)S(1)}, u32[]{:S(2)}, u32[]{:S(2)}) collective-permute-start(bf16[208,256]{1,0:T(8,128)(2,1)S(1)} %get-tuple-element.251), channel_id=1, source_target_pairs={{0,12},{4,8},{8,4},{12,0},{1,13},{5,9},{9,5},{13,1},{2,14},{6,10},... | collective-permute-start | bytes 319496 | tf_op jit(solution)/shard_map/ppermute | solution.py:356
  282.7 10.2 %collective-permute-start.27 = (f32[20480]{0:T(1024)S(1)}, f32[20480]{0:T(1024)}, u32[]{:S(2)}, u32[]{:S(2)}) collective-permute-start(f32[20480]{0:T(1024)S(1)} %pad_maximum_fusion.16), channel_id=1, source_target_pairs={{0,1},{1,0},{2,3},{3,2},{4,5},{5,4},{6,7},{7,6},{8,9},{9,8},{10,11... | collective-permute-start | bytes 245768 | tf_op jit(solution)/shard_map/ppermute | solution.py:356
  283.7 24.2 %collective-permute-start.25 = (bf16[256,896]{1,0:T(8,128)(2,1)}, bf16[256,896]{1,0:T(8,128)(2,1)S(1)}, u32[]{:S(2)}, u32[]{:S(2)}) collective-permute-start(bf16[256,896]{1,0:T(8,128)(2,1)} %add_convert_fusion.2), channel_id=1, source_target_pairs={{0,12},{4,8},{8,4},{12,0},{1,13},{5,9},{9,5},{13,1},{2,14},{6,10},... | collective-permute-start | bytes 1376264 | tf_op jit(solution)/shard_map/ppermute | solution.py:356
  284.5 34.7 %collective-permute-start.23 = (bf16[256,896]{1,0:T(8,128)(2,1)}, bf16[256,896]{1,0:T(8,128)(2,1)}, u32[]{:S(2)}, u32[]{:S(2)}) collective-permute-start(bf16[256,896]{1,0:T(8,128)(2,1)} %get-tuple-element.252), channel_id=1, source_target_pairs={{0,16},{16,0},{1,17},{17,1},{2,18},{18,2},{3,19},{19,3},{4,20},{20... | collective-permute-start | bytes 1376264 | tf_op jit(solution)/shard_map/ppermute | solution.py:356
  287.9 40.8 %collective-permute-start.24 = (bf16[256,896]{1,0:T(8,128)(2,1)}, bf16[256,896]{1,0:T(8,128)(2,1)}, u32[]{:S(2)}, u32[]{:S(2)}) collective-permute-start(bf16[256,896]{1,0:T(8,128)(2,1)} %get-tuple-element.253), channel_id=1, source_target_pairs={{0,16},{16,0},{1,17},{17,1},{2,18},{18,2},{3,19},{19,3},{4,20},{20... | collective-permute-start | bytes 1376264 | tf_op jit(solution)/shard_map/ppermute | solution.py:356
  288.3 40.8 %copy-start.48 = (bf16[256,896]{1,0:T(8,128)(2,1)S(1)}, bf16[256,896]{1,0:T(8,128)(2,1)}, u32[]{:S(2)}) copy-start(bf16[256,896]{1,0:T(8,128)(2,1)} %get-tuple-element.271) | copy-start | bytes 1376260
  289.8 41.1 %copy-start.44 = (bf16[2,128,2048]{2,1,0:T(8,128)(2,1)S(1)}, bf16[2,128,2048]{2,1,0:T(8,128)(2,1)}, u32[]{:S(2)}) copy-start(bf16[2,128,2048]{2,1,0:T(8,128)(2,1)} %reduce-scatter.3.cloned.1.call-done) | copy-start | bytes 3145732
  291.0 37.8 %collective-permute-start.26 = (bf16[128,2048]{1,0:T(8,128)(2,1)S(1)}, bf16[128,2048]{1,0:T(8,128)(2,1)S(1)}, u32[]{:S(2)}, u32[]{:S(2)}) collective-permute-start(bf16[128,2048]{1,0:T(8,128)(2,1)S(1)} %slice_bitcast_fusion.3), channel_id=1, source_target_pairs={{0,8},{8,0},{1,9},{9,1},{2,10},{10,2},{3,11},{11,3},{4,12},{12,4},... | collective-permute-start | bytes 1572872 | tf_op jit(solution)/shard_map/ppermute | solution.py:356
  293.8 4.5 %collective-permute-start.28 = (f32[20480]{0:T(1024)S(1)}, f32[20480]{0:T(1024)S(1)}, u32[]{:S(2)}, u32[]{:S(2)}) collective-permute-start(f32[20480]{0:T(1024)S(1)} %fusion.44), channel_id=1, source_target_pairs={{0,2},{2,0},{1,3},{3,1},{4,6},{6,4},{5,7},{7,5},{8,10},{10,8},{9,1... | collective-permute-start | bytes 245768 | tf_op jit(solution)/shard_map/ppermute | solution.py:356
  328.8 7.8 %collective-permute-start.32 = (f32[20480]{0:T(1024)S(1)}, f32[20480]{0:T(1024)S(1)}, u32[]{:S(2)}, u32[]{:S(2)}) collective-permute-start(f32[20480]{0:T(1024)S(1)} %add.293), channel_id=1, source_target_pairs={{0,4},{4,0},{1,5},{5,1},{2,6},{6,2},{3,7},{7,3},{8,12},{12,8},{9,1... | collective-permute-start | bytes 245768 | tf_op jit(solution)/shard_map/ppermute | solution.py:356
  330.3 26.2 %collective-permute-start.31 = (bf16[256,896]{1,0:T(8,128)(2,1)S(1)}, bf16[256,896]{1,0:T(8,128)(2,1)S(1)}, u32[]{:S(2)}, u32[]{:S(2)}) collective-permute-start(bf16[256,896]{1,0:T(8,128)(2,1)S(1)} %add_convert_fusion), channel_id=1, source_target_pairs={{0,8},{4,12},{8,0},{12,4},{1,9},{5,13},{9,1},{13,5},{2,10},{6,14},... | collective-permute-start | bytes 1376264 | tf_op jit(solution)/shard_map/ppermute | solution.py:356
  332.3 24.3 %collective-permute-start.30 = (bf16[256,896]{1,0:T(8,128)(2,1)S(1)}, bf16[256,896]{1,0:T(8,128)(2,1)S(1)}, u32[]{:S(2)}, u32[]{:S(2)}) collective-permute-start(bf16[256,896]{1,0:T(8,128)(2,1)S(1)} %add_convert_fusion.1), channel_id=1, source_target_pairs={{0,4},{4,0},{8,12},{12,8},{1,5},{5,1},{9,13},{13,9},{2,6},{6,2},{1... | collective-permute-start | bytes 1376264 | tf_op jit(solution)/shard_map/ppermute | solution.py:356
  333.6 22.9 %collective-permute-start.29 = (bf16[256,896]{1,0:T(8,128)(2,1)S(1)}, bf16[256,896]{1,0:T(8,128)(2,1)S(1)}, u32[]{:S(2)}, u32[]{:S(2)}) collective-permute-start(bf16[256,896]{1,0:T(8,128)(2,1)S(1)} %copy-done.53), channel_id=1, source_target_pairs={{0,16},{16,0},{1,17},{17,1},{2,18},{18,2},{3,19},{19,3},{4,20},{20... | collective-permute-start | bytes 1376264 | tf_op jit(solution)/shard_map/ppermute | solution.py:356
  336.6 15.6 %collective-permute-start.33 = (f32[20480]{0:T(1024)S(1)}, f32[20480]{0:T(1024)S(1)}, u32[]{:S(2)}, u32[]{:S(2)}) collective-permute-start(f32[20480]{0:T(1024)S(1)} %add.297), channel_id=1, source_target_pairs={{0,8},{8,0},{1,9},{9,1},{2,10},{10,2},{3,11},{11,3},{4,12},{12,4},... | collective-permute-start | bytes 245768 | tf_op jit(solution)/shard_map/ppermute | solution.py:356
  356.6 5.8 %collective-permute-start.35 = (f32[20480]{0:T(1024)S(1)}, f32[20480]{0:T(1024)}, u32[]{:S(2)}, u32[]{:S(2)}) collective-permute-start(f32[20480]{0:T(1024)S(1)} %add.298), channel_id=1, source_target_pairs={{0,16},{16,0},{1,17},{17,1},{2,18},{18,2},{3,19},{19,3},{4,20},{20... | collective-permute-start | bytes 245768 | tf_op jit(solution)/shard_map/ppermute | solution.py:356
  365.3 11.8 %collective-permute-start.34 = (bf16[128,2048]{1,0:T(8,128)(2,1)S(1)}, bf16[128,2048]{1,0:T(8,128)(2,1)S(1)}, u32[]{:S(2)}, u32[]{:S(2)}) collective-permute-start(bf16[128,2048]{1,0:T(8,128)(2,1)S(1)} %get-tuple-element.323), channel_id=1, source_target_pairs={{0,8},{8,0},{1,9},{9,1},{2,10},{10,2},{3,11},{11,3},{4,12},{12,4},... | collective-permute-start | bytes 1572872 | tf_op jit(solution)/shard_map/ppermute | solution.py:356
  (57 other events, 587.3 us)
Sparse Core Ops, SparseCore 0:
  30.4 74.5 all-gather.2
  107.4 61.8 all-gather.4
  198.7 81.0 reduce-scatter.2
  283.5 74.9 reduce-scatter.4

commit v8 on v7

--- a/solution.py
+++ b/solution.py
@@ -574,10 +574,12 @@
         out_2 = send_out(2)
         low_kept, low_send = out_total((0, 1), (out_0, out_1))
         low_kept, low_send = step(low_kept, low_send)
-        low_back = [quad_swap(piece, m) for m, piece in zip((1, 2, 3), low_send)]
+        low_back = [quad_swap(piece, m) for m, piece in zip((2, 3), low_send[1:])]
         into, normed_all = step(into, normed_all)
         in_part = dot(normed_all, into, ((0,), (0,))).astype(BF)
-        in_part, into, out_2, low_back, low_kept = step(in_part, into, out_2, low_back, low_kept)
+        in_part, into, out_2, low_back, low_kept, low_send = step(
+            in_part, into, out_2, low_back, low_kept, low_send
+        )
 
         def block(k, m):
             start = k * span + (quad ^ m) * (span // 4)
@@ -588,18 +590,20 @@
 
         high_kept, high_send = out_total((2,), (out_2,))
         in_send = [[block(k, m) for k in range(groups)] for m in range(4)]
-        in_send, high_send, high_kept = step(in_send, high_send, high_kept)
+        in_send, high_send, high_kept, low_send = step(in_send, high_send, high_kept, low_send)
 
         in_3 = swap_block(3)
         high_back = [quad_swap(piece, m) for m, piece in zip((1, 2, 3), high_send)]
+        low_1 = quad_swap(low_send[0], 1)
         into, in_w, normed_all = step(into, in_w, normed_all)
         terms = dot(into, in_w, ((1,), (1,)))
         unit = (normed_all.astype(F32) - own_order(ln_bias, 0)) / own_order(ln_gain, 0)
         gain_sum, shift_sum = jnp.sum(terms * unit, axis=0), jnp.sum(terms, axis=0)
         terms = terms.astype(BF)
-        terms, gain_sum, shift_sum, in_3, in_send, high_back = step(
-            terms, gain_sum, shift_sum, in_3, in_send, high_back
-        )
+        terms, gain_sum, shift_sum, in_3, in_send, high_back, low_1 = step(
+            terms, gain_sum, shift_sum, in_3, in_send, high_back, low_1
+        )
+        low_back = [low_1] + low_back
         terms_sum = team_sum(terms)
         branch_own, branch_next = branch_sum[0], branch_sum[1]
 

time: 387 us -> 384 us (level)
  transfers between devices with their start and end apart: 40 -> 40, of which waited for: 25 -> 25; matrix products, arithmetic and copies ran while one was open for 21% -> 22% of each run, Pallas kernels for 11% -> 12%
where the time goes in v8:
time: 384 us; the launch traced here: 383 us
  waiting for transfers between devices  171 us (45%)
  Pallas kernels  47.4 us (12%)
  matrix products  46.3 us (12%)
  starting transfers between devices  41.3 us (11%)
  other arithmetic  33.5 us (9%)
  local copies, waits for them, and re-layouts  29 us (8%)
  between operations  14.9 us (4%)
    ppermute x36, waiting for transfers between devices, swap_with(): return lax.ppermute(values, axis, [(i, i ^ mask) for i in range(size)])  171 us
    dot_general x4, matrix products, dot(): lax.dot_general(left, right, (dims, ((), ())), preferred_element_type=F32)  46.3 us
    ppermute x36, starting transfers between devices, swap_with(): return lax.ppermute(values, axis, [(i, i ^ mask) for i in range(size)])  40.9 us
    pallas_call x2, Pallas kernels, by_tokens(): pl.pallas_call(kernel, grid=(rows // ROWS,), in_specs=specs, out_specs=[c...  22.1 us
    unnamed x135, local copies, waits for them, and re-layouts  18.1 us
    pallas_call x1, Pallas kernels, attention_grad(): pl.pallas_call(attend_grad_kernel, grid=(sequences,), in_specs=[spec['wid...  11.7 us
  transfers between devices with their start and end apart: 40, of which 25 were waited for; matrix products, arithmetic and copies ran while one was open for 22% of the time, Pallas kernels for 12%

profile of v8, /device:TPU:0, one launch (start us, length us, event | category | flops | bytes accessed | tf_op | source)
XLA Modules:
  0.0 383.5 jit_solution(1360690789365570548)
XLA Ops:
  13.0 3.1 collective-permute-start
  20.4 7.7 %collective-permute-done = bf16[128,2048]{1,0:T(8,128)(2,1)} collective-permute-done((bf16[128,2048]{1,0:T(8,128)(2,1)S(1)}, bf16[128,2048]{1,0:T(8,128)(2,1)}, u32[]{:S(2)}, u32[]{:S(2)}) %collective-permute-start) | collective-permute-done | bytes 524320 | tf_op jit(solution)/shard_map/ppermute | solution.py:356
  28.1 2.1 pad_maximum_fusion.3
  30.5 2.8 collective-permute-start.4
  38.6 31.6 %collective-permute-done.5.refs_4_ = bf16[640,256]{1,0:T(8,128)(2,1)S(1)} collective-permute-done((bf16[640,256]{1,0:T(8,128)(2,1)S(1)}, bf16[640,256]{1,0:T(8,128)(2,1)S(1)}, u32[]{:S(2)}, u32[]{:S(2)}) %collective-permute-start.5) | collective-permute-done | bytes 327712 | tf_op jit(solution)/shard_map/ppermute | solution.py:356
  70.2 2.4 collective-permute-done.3.refs_3_
  72.7 3.0 collective-permute-start.6
  78.3 13.7 %collective-permute-done.8.refs_1_ = bf16[640,256]{1,0:T(8,128)(2,1)S(1)} collective-permute-done((bf16[640,256]{1,0:T(8,128)(2,1)S(1)}, bf16[640,256]{1,0:T(8,128)(2,1)S(1)}, u32[]{:S(2)}, u32[]{:S(2)}) %collective-permute-start.8) | collective-permute-done | bytes 327712 | tf_op jit(solution)/shard_map/ppermute | solution.py:356
  96.0 2.5 collective-permute-start.9
  99.4 2.2 collective-permute-start.11
  101.6 1.9 fusion.28
  103.5 22.9 %collective-permute-done.10.refs_2_ = bf16[640,256]{1,0:T(8,128)(2,1)S(1)} collective-permute-done((bf16[640,256]{1,0:T(8,128)(2,1)}, bf16[640,256]{1,0:T(8,128)(2,1)S(1)}, u32[]{:S(2)}, u32[]{:S(2)}) %collective-permute-start.10) | collective-permute-done | bytes 327712 | tf_op jit(solution)/shard_map/ppermute | solution.py:356
  126.4 3.6 collective-permute-done.11.refs_3_
  131.0 6.9 %collective-permute-done.9.refs_6_ = bf16[512,896]{1,0:T(8,128)(2,1)S(1)} collective-permute-done((bf16[512,896]{1,0:T(8,128)(2,1)}, bf16[512,896]{1,0:T(8,128)(2,1)S(1)}, u32[]{:S(2)}, u32[]{:S(2)}) %collective-permute-start.9) | collective-permute-done | bytes 917536 | tf_op jit(solution)/shard_map/ppermute | solution.py:356
  146.9 1.9 copy-done.8
  148.9 12.6 %broadcast_add_fusion.mixed_ref = f32[2048,896]{1,0:T(8,128)S(1)} fusion(f32[896]{0:T(1024)S(1)} %pad_maximum_fusion.21, bf16[2048,2048]{1,0:T(8,128)(2,1)} %bitcast.96, bf16[2048,896]{1,0:T(8,128)(2,1)} %copy-done.8), kind=kOutput, calls=%fused_computation.11 | convolution fusion | flops 7518027776 | bytes 19402240 | tf_op jit(solution)/shard_map/dot_general | solution.py:360
  161.5 7.0 %attend.1 = (bf16[2048,384]{1,0:T(8,128)(2,1)S(1)}, bf16[2048,128]{1,0:T(8,128)(2,1)S(1)}, f32[4,2,512]{2,1,0:T(2,128)S(1)}) custom-call(f32[2048,896]{1,0:T(8,128)S(1)} %broadcast_add_fusion.mixed_ref, f32[512,128]{1,0:T(8,128)S(1)} %copy-done.20, f32[512,128]{1,0:T(8,128)S(1)} %copy-done.18, f32[512,128]{1,0:T(8,128)S(1)} %copy-done.17, ...), custom_call_target="tpu_custom_call" | custom-call | tf_op jit(solution)/shard_map/attend/pallas_call | solution.py:171
  169.8 1.7 pad_maximum_fusion.acts_ref
  171.6 8.9 %convolution_convert_fusion.1 = bf16[640,2048]{1,0:T(8,128)(2,1)S(1)} fusion(bf16[2048,640]{1,0:T(8,128)(2,1)} %pad_maximum_fusion.acts_ref, bf16[2048,2048]{1,0:T(8,128)(2,1)} %bitcast.99), kind=kOutput, calls=%fused_computation.13 | convolution fusion | flops 5370019840 | bytes 13631488 | tf_op jit(solution)/shard_map/dot_general | solution.py:360
  185.9 2.0 collective-permute-start.13
  187.9 8.6 %branch.1 = bf16[2048,2048]{1,0:T(8,128)(2,1)} custom-call(bf16[2048,640]{1,0:T(8,128)(2,1)S(1)} %copy-done.16, bf16[128,2048]{1,0:T(8,128)(2,1)S(1)} %place.4.dense_ref, bf16[512,2048]{1,0:T(8,128)(2,1)S(1)} %place.5.down_ref), custom_call_target="tpu_custom_call" | custom-call | flops 5368709120 | bytes 13631488 | tf_op jit(solution)/shard_map/branch/pallas_call | solution.py:305
  201.2 13.5 %back.1 = (bf16[2048,128]{1,0:T(8,128)(2,1)S(1)}, bf16[2048,896]{1,0:T(8,128)(2,1)}) custom-call(bf16[2048,2048]{1,0:T(8,128)(2,1)} %bitcast.100, f32[2048,896]{1,0:T(8,128)} %copy-done.3, bf16[128,2048]{1,0:T(8,128)(2,1)S(1)} %copy-done.37, bf16[512,2048]{1,0:T(8,128)(2,1)S(1)} %copy-done.23), custom_call_target="tpu_custom_call" | custom-call | flops 5368709120 | bytes 22544384 | tf_op jit(solution)/shard_map/back/pallas_call | solution.py:305
  214.7 2.1 copy-done.4
  216.8 11.7 %attend_grad.1 = bf16[2048,896]{1,0:T(8,128)(2,1)S(1)} custom-call(bf16[2048,384]{1,0:T(8,128)(2,1)S(1)} %copy-done.31, bf16[2048,128]{1,0:T(8,128)(2,1)S(1)} %get-tuple-element.216.grad_ref, f32[4,2,512]{2,1,0:T(2,128)S(1)} %get-tuple-element.217.lse_ref, f32[512,128]{1,0:T(8,128)S(1)} %copy-done.21, ...), custom_call_target="tpu_custom_call", output_to_operand_aliasing={{}: (8, {})} | custom-call | tf_op jit(solution)/shard_map/attend_grad/pallas_call | solution.py:190
  228.5 2.5 collective-permute-done.14
  231.8 3.7 collective-permute-start.17
  235.5 11.5 %convolution_convert_fusion = bf16[2048,896]{1,0:T(8,128)(2,1)S(1)} fusion(bf16[2048,2048]{1,0:T(8,128)(2,1)} %bitcast.97, bf16[2048,896]{1,0:T(8,128)(2,1)S(1)} %attend_grad.1), kind=kOutput, calls=%fused_computation.12 | convolution fusion | flops 7518027776 | bytes 15728640 | tf_op jit(solution)/shard_map/dot_general | solution.py:360
  247.0 6.1 %collective-permute-done.17 = bf16[432,256]{1,0:T(8,128)(2,1)S(1)} collective-permute-done((bf16[432,256]{1,0:T(8,128)(2,1)S(1)}, bf16[432,256]{1,0:T(8,128)(2,1)S(1)}, u32[]{:S(2)}, u32[]{:S(2)}) %collective-permute-start.17) | collective-permute-done | bytes 221216 | tf_op jit(solution)/shard_map/ppermute | solution.py:356
  253.0 3.7 collective-permute-done.15
  258.6 2.0 collective-permute-start.19
  260.6 1.8 collective-permute-start.20
  262.6 13.4 %fusion.46 = (f32[2048]{0:T(1024)S(1)}, f32[2048]{0:T(1024)S(1)}, bf16[2048,2048]{1,0:T(8,128)(2,1)}) fusion(f32[2048]{0:T(1024)S(1)} %get-tuple-element.394, f32[2048]{0:T(1024)S(1)} %get-tuple-element.393, bf16[2048,2048]{1,0:T(8,128)(2,1)} %bitcast.98, bf16[2048,896]{1,0:T(8,128)(2,1)S(1)} %copy-done.6, bf16[2048,896]{1,0:T(8,128)(2,1)S(1)} %copy-done.9), kind=kOutput, calls=%fused_computation.174 | convolution fusion | flops 7545548800 | bytes 24150016 | tf_op jit(solution)/shard_map/dot_general | solution.py:360
  276.3 2.7 collective-permute-done.18
  279.9 2.7 convert_reduce_fusion
  284.8 2.0 collective-permute-start.24
  290.1 1.9 collective-permute-start.26
  293.8 3.6 collective-permute-done.28
  297.4 9.6 %collective-permute-done.25.refs_3_ = bf16[256,896]{1,0:T(8,128)(2,1)S(1)} collective-permute-done((bf16[256,896]{1,0:T(8,128)(2,1)}, bf16[256,896]{1,0:T(8,128)(2,1)S(1)}, u32[]{:S(2)}, u32[]{:S(2)}) %collective-permute-start.25) | collective-permute-done | bytes 458784 | tf_op jit(solution)/shard_map/ppermute | solution.py:356
  307.1 11.1 %collective-permute-done.23 = bf16[256,896]{1,0:T(8,128)(2,1)} collective-permute-done((bf16[256,896]{1,0:T(8,128)(2,1)}, bf16[256,896]{1,0:T(8,128)(2,1)}, u32[]{:S(2)}, u32[]{:S(2)}) %collective-permute-start.23) | collective-permute-done | bytes 458784 | tf_op jit(solution)/shard_map/ppermute | solution.py:356
  318.2 9.4 %collective-permute-done.24 = bf16[256,896]{1,0:T(8,128)(2,1)} collective-permute-done((bf16[256,896]{1,0:T(8,128)(2,1)}, bf16[256,896]{1,0:T(8,128)(2,1)}, u32[]{:S(2)}, u32[]{:S(2)}) %collective-permute-start.24) | collective-permute-done | bytes 458784 | tf_op jit(solution)/shard_map/ppermute | solution.py:356
  327.7 1.6 collective-permute-start.32
  333.0 2.4 collective-permute-start.29
  337.3 14.8 %collective-permute-done.33 = f32[20480]{0:T(1024)S(1)} collective-permute-done((f32[20480]{0:T(1024)S(1)}, f32[20480]{0:T(1024)S(1)}, u32[]{:S(2)}, u32[]{:S(2)}) %collective-permute-start.33) | collective-permute-done | bytes 81952 | tf_op jit(solution)/shard_map/ppermute | solution.py:356
  352.1 3.2 collective-permute-done.29
  356.0 2.7 settle.1
  358.7 2.8 collective-permute-done.35
  365.8 8.8 %collective-permute-done.34.got_ref = bf16[128,2048]{1,0:T(8,128)(2,1)S(1)} collective-permute-done((bf16[128,2048]{1,0:T(8,128)(2,1)S(1)}, bf16[128,2048]{1,0:T(8,128)(2,1)S(1)}, u32[]{:S(2)}, u32[]{:S(2)}) %collective-permute-start.34) | collective-permute-done | bytes 524320 | tf_op jit(solution)/shard_map/ppermute | solution.py:356
  374.6 1.8 norm_grad.1
  (278 shorter events, 66.5 us)
Async XLA Ops:
  7.2 91.3 %copy-start = (f32[3,512]{1,0:T(4,128)S(1)}, f32[3,512]{1,0:T(4,128)}, u32[]{:S(2)}) copy-start(f32[3,512]{1,0:T(4,128)} %param.17) | copy-start | bytes 18436
  7.2 141.6 %all-gather.3.cloned.1.call-start = ((), (), s32[]{:S(2)}) async-start(), calls=%async_computation.2 | async-start | bytes 9437184 | tf_op jit(solution)/shard_map/all_gather | solution.py:462
  13.0 15.1 %collective-permute-start = (bf16[128,2048]{1,0:T(8,128)(2,1)S(1)}, bf16[128,2048]{1,0:T(8,128)(2,1)}, u32[]{:S(2)}, u32[]{:S(2)}) collective-permute-start(bf16[128,2048]{1,0:T(8,128)(2,1)S(1)} %maximum_select_fusion.1), channel_id=1, source_target_pairs={{0,8},{8,0},{1,9},{9,1},{2,10},{10,2},{3,11},{11,3},{4,12},{12,4},... | collective-permute-start | bytes 1572872 | tf_op jit(solution)/shard_map/ppermute | solution.py:356
  30.3 141.3 %all-gather.5.cloned.1.call-start = ((), (), s32[]{:S(2)}) async-start(), calls=%async_computation.3 | async-start | bytes 9437184 | tf_op jit(solution)/shard_map/all_gather | solution.py:462
  30.5 39.7 %collective-permute-start.4 = (bf16[256,896]{1,0:T(8,128)(2,1)S(1)}, bf16[256,896]{1,0:T(8,128)(2,1)S(1)}, u32[]{:S(2)}, u32[]{:S(2)}) collective-permute-start(bf16[256,896]{1,0:T(8,128)(2,1)S(1)} %slice.214), channel_id=1, source_target_pairs={{0,16},{16,0},{1,17},{17,1},{2,18},{18,2},{3,19},{19,3},{4,20},{20... | collective-permute-start | bytes 1376264 | tf_op jit(solution)/shard_map/ppermute | solution.py:356
  33.3 36.9 %collective-permute-start.1 = (bf16[272,896]{1,0:T(8,128)(2,1)}, bf16[272,896]{1,0:T(8,128)(2,1)S(1)}, u32[]{:S(2)}, u32[]{:S(2)}) collective-permute-start(bf16[272,896]{1,0:T(8,128)(2,1)} %get-tuple-element.158), channel_id=1, source_target_pairs={{0,4},{4,0},{8,12},{12,8},{1,5},{5,1},{9,13},{13,9},{2,6},{6,2},{1... | collective-permute-start | bytes 1462280 | tf_op jit(solution)/shard_map/ppermute | solution.py:356
  34.8 35.4 %collective-permute-start.2 = (bf16[272,896]{1,0:T(8,128)(2,1)}, bf16[272,896]{1,0:T(8,128)(2,1)S(1)}, u32[]{:S(2)}, u32[]{:S(2)}) collective-permute-start(bf16[272,896]{1,0:T(8,128)(2,1)} %fusion.23), channel_id=1, source_target_pairs={{0,8},{4,12},{8,0},{12,4},{1,9},{5,13},{9,1},{13,5},{2,10},{6,14},... | collective-permute-start | bytes 1462280 | tf_op jit(solution)/shard_map/ppermute | solution.py:356
  36.3 36.2 %collective-permute-start.3 = (bf16[272,896]{1,0:T(8,128)(2,1)}, bf16[272,896]{1,0:T(8,128)(2,1)S(1)}, u32[]{:S(2)}, u32[]{:S(2)}) collective-permute-start(bf16[272,896]{1,0:T(8,128)(2,1)} %get-tuple-element.160), channel_id=1, source_target_pairs={{0,12},{4,8},{8,4},{12,0},{1,13},{5,9},{9,5},{13,1},{2,14},{6,10},... | collective-permute-start | bytes 1462280 | tf_op jit(solution)/shard_map/ppermute | solution.py:356
  36.8 57.1 %copy-start.45 = (bf16[128,2048]{1,0:T(8,128)(2,1)S(1)}, bf16[128,2048]{1,0:T(8,128)(2,1)}, u32[]{:S(2)}) copy-start(bf16[128,2048]{1,0:T(8,128)(2,1)} %maximum_select_fusion.2) | copy-start | bytes 1572868
  36.8 33.3 %collective-permute-start.5 = (bf16[640,256]{1,0:T(8,128)(2,1)S(1)}, bf16[640,256]{1,0:T(8,128)(2,1)S(1)}, u32[]{:S(2)}, u32[]{:S(2)}) collective-permute-start(bf16[640,256]{1,0:T(8,128)(2,1)S(1)} %pad_maximum_fusion.9.refs_0_), channel_id=1, source_target_pairs={{0,16},{16,0},{1,17},{17,1},{2,18},{18,2},{3,19},{19,3},{4,20},{20... | collective-permute-start | bytes 983048 | tf_op jit(solution)/shard_map/ppermute | solution.py:356
  70.2 67.7 %copy-start.24 = (bf16[272,896]{1,0:T(8,128)(2,1)}, bf16[272,896]{1,0:T(8,128)(2,1)S(1)}, u32[]{:S(2)}) copy-start(bf16[272,896]{1,0:T(8,128)(2,1)S(1)} %collective-permute-done.1.refs_1_) | copy-start | bytes 1462276
  70.2 67.7 %copy-start.26 = (bf16[272,896]{1,0:T(8,128)(2,1)}, bf16[272,896]{1,0:T(8,128)(2,1)S(1)}, u32[]{:S(2)}) copy-start(bf16[272,896]{1,0:T(8,128)(2,1)S(1)} %collective-permute-done.2.refs_2_) | copy-start | bytes 1462276
  72.6 65.4 %copy-start.28 = (bf16[272,896]{1,0:T(8,128)(2,1)}, bf16[272,896]{1,0:T(8,128)(2,1)S(1)}, u32[]{:S(2)}) copy-start(bf16[272,896]{1,0:T(8,128)(2,1)S(1)} %collective-permute-done.3.refs_3_) | copy-start | bytes 1462276
  72.6 21.4 %collective-permute-start.7 = (bf16[128,2048]{1,0:T(8,128)(2,1)}, bf16[128,2048]{1,0:T(8,128)(2,1)S(1)}, u32[]{:S(2)}, u32[]{:S(2)}) collective-permute-start(bf16[128,2048]{1,0:T(8,128)(2,1)} %maximum_select_fusion.2), channel_id=1, source_target_pairs={{0,8},{8,0},{1,9},{9,1},{2,10},{10,2},{3,11},{11,3},{4,12},{12,4},... | collective-permute-start | bytes 1572872 | tf_op jit(solution)/shard_map/ppermute | solution.py:356
  72.7 19.4 %collective-permute-start.6 = (bf16[256,896]{1,0:T(8,128)(2,1)S(1)}, bf16[256,896]{1,0:T(8,128)(2,1)S(1)}, u32[]{:S(2)}, u32[]{:S(2)}) collective-permute-start(bf16[256,896]{1,0:T(8,128)(2,1)S(1)} %slice.215), channel_id=1, source_target_pairs={{0,16},{16,0},{1,17},{17,1},{2,18},{18,2},{3,19},{19,3},{4,20},{20... | collective-permute-start | bytes 1376264 | tf_op jit(solution)/shard_map/ppermute | solution.py:356
  75.8 16.2 %collective-permute-start.8 = (bf16[640,256]{1,0:T(8,128)(2,1)S(1)}, bf16[640,256]{1,0:T(8,128)(2,1)S(1)}, u32[]{:S(2)}, u32[]{:S(2)}) collective-permute-start(bf16[640,256]{1,0:T(8,128)(2,1)S(1)} %get-tuple-element.168), channel_id=1, source_target_pairs={{0,4},{4,0},{8,12},{12,8},{1,5},{5,1},{9,13},{13,9},{2,6},{6,2},{1... | collective-permute-start | bytes 983048 | tf_op jit(solution)/shard_map/ppermute | solution.py:356
  92.0 47.0 %copy-start.10 = (bf16[640,256]{1,0:T(8,128)(2,1)}, bf16[640,256]{1,0:T(8,128)(2,1)S(1)}, u32[]{:S(2)}) copy-start(bf16[640,256]{1,0:T(8,128)(2,1)S(1)} %collective-permute-done.8.refs_1_) | copy-start | bytes 983044
  95.0 193.7 %reduce-scatter.3.cloned.1.call-start = ((), (), s32[]{:S(2)}) async-start(), calls=%async_computation.4 | async-start | bytes 9437184 | tf_op jit(solution)/shard_map/reduce_scatter | solution.py:538
  96.0 41.9 %collective-permute-start.9 = (bf16[512,896]{1,0:T(8,128)(2,1)}, bf16[512,896]{1,0:T(8,128)(2,1)S(1)}, u32[]{:S(2)}, u32[]{:S(2)}) collective-permute-start(bf16[512,896]{1,0:T(8,128)(2,1)} %pad_maximum_fusion.6), channel_id=1, source_target_pairs={{0,16},{16,0},{1,17},{17,1},{2,18},{18,2},{3,19},{19,3},{4,20},{20... | collective-permute-start | bytes 2752520 | tf_op jit(solution)/shard_map/ppermute | solution.py:356
  98.5 27.9 %collective-permute-start.10 = (bf16[640,256]{1,0:T(8,128)(2,1)}, bf16[640,256]{1,0:T(8,128)(2,1)S(1)}, u32[]{:S(2)}, u32[]{:S(2)}) collective-permute-start(bf16[640,256]{1,0:T(8,128)(2,1)} %get-tuple-element.175), channel_id=1, source_target_pairs={{0,8},{4,12},{8,0},{12,4},{1,9},{5,13},{9,1},{13,5},{2,10},{6,14},... | collective-permute-start | bytes 983048 | tf_op jit(solution)/shard_map/ppermute | solution.py:356
  99.4 30.6 %collective-permute-start.11 = (bf16[640,256]{1,0:T(8,128)(2,1)}, bf16[640,256]{1,0:T(8,128)(2,1)S(1)}, u32[]{:S(2)}, u32[]{:S(2)}) collective-permute-start(bf16[640,256]{1,0:T(8,128)(2,1)} %pad_maximum_fusion.12), channel_id=1, source_target_pairs={{0,12},{4,8},{8,4},{12,0},{1,13},{5,9},{9,5},{13,1},{2,14},{6,10},... | collective-permute-start | bytes 983048 | tf_op jit(solution)/shard_map/ppermute | solution.py:356
  139.4 45.0 %collective-permute-start.12 = (bf16[640,768]{1,0:T(8,128)(2,1)}, bf16[640,768]{1,0:T(8,128)(2,1)S(1)}, u32[]{:S(2)}, u32[]{:S(2)}) collective-permute-start(bf16[640,768]{1,0:T(8,128)(2,1)} %pad_maximum_fusion.5), channel_id=1, source_target_pairs={{0,16},{16,0},{1,17},{17,1},{2,18},{18,2},{3,19},{19,3},{4,20},{20... | collective-permute-start | bytes 2949128 | tf_op jit(solution)/shard_map/ppermute | solution.py:356
  185.9 12.0 %collective-permute-start.13 = (bf16[96,1024]{1,0:T(8,128)(2,1)S(1)}, bf16[96,1024]{1,0:T(8,128)(2,1)S(1)}, u32[]{:S(2)}, u32[]{:S(2)}) collective-permute-start(bf16[96,1024]{1,0:T(8,128)(2,1)S(1)} %get-tuple-element.201), channel_id=1, source_target_pairs={{0,16},{16,0},{1,17},{17,1},{2,18},{18,2},{3,19},{19,3},{4,20},{20... | collective-permute-start | bytes 589832 | tf_op jit(solution)/shard_map/ppermute | solution.py:356
  198.6 164.6 %reduce-scatter.5.cloned.1.call-start = ((), (), s32[]{:S(2)}) async-start(), calls=%async_computation.5 | async-start | bytes 9437184 | tf_op jit(solution)/shard_map/reduce_scatter | solution.py:538
  199.3 31.8 %collective-permute-start.14 = (bf16[336,1024]{1,0:T(8,128)(2,1)}, bf16[336,1024]{1,0:T(8,128)(2,1)S(1)}, u32[]{:S(2)}, u32[]{:S(2)}) collective-permute-start(bf16[336,1024]{1,0:T(8,128)(2,1)} %get-tuple-element.219), channel_id=1, source_target_pairs={{0,16},{16,0},{1,17},{17,1},{2,18},{18,2},{3,19},{19,3},{4,20},{20... | collective-permute-start | bytes 2064392 | tf_op jit(solution)/shard_map/ppermute | solution.py:356
  231.7 15.3 %collective-permute-start.16 = (bf16[432,256]{1,0:T(8,128)(2,1)S(1)}, bf16[432,256]{1,0:T(8,128)(2,1)S(1)}, u32[]{:S(2)}, u32[]{:S(2)}) collective-permute-start(bf16[432,256]{1,0:T(8,128)(2,1)S(1)} %get-tuple-element.232), channel_id=1, source_target_pairs={{0,8},{4,12},{8,0},{12,4},{1,9},{5,13},{9,1},{13,5},{2,10},{6,14},... | collective-permute-start | bytes 663560 | tf_op jit(solution)/shard_map/ppermute | solution.py:356
  231.8 21.3 %collective-permute-start.17 = (bf16[432,256]{1,0:T(8,128)(2,1)S(1)}, bf16[432,256]{1,0:T(8,128)(2,1)S(1)}, u32[]{:S(2)}, u32[]{:S(2)}) collective-permute-start(bf16[432,256]{1,0:T(8,128)(2,1)S(1)} %get-tuple-element.233), channel_id=1, source_target_pairs={{0,12},{4,8},{8,4},{12,0},{1,13},{5,9},{9,5},{13,1},{2,14},{6,10},... | collective-permute-start | bytes 663560 | tf_op jit(solution)/shard_map/ppermute | solution.py:356
  235.5 21.3 %collective-permute-start.15 = (bf16[208,1024]{1,0:T(8,128)(2,1)S(1)}, bf16[208,1024]{1,0:T(8,128)(2,1)S(1)}, u32[]{:S(2)}, u32[]{:S(2)}) collective-permute-start(bf16[208,1024]{1,0:T(8,128)(2,1)S(1)} %copy-done.56), channel_id=1, source_target_pairs={{0,16},{16,0},{1,17},{17,1},{2,18},{18,2},{3,19},{19,3},{4,20},{20... | collective-permute-start | bytes 1277960 | tf_op jit(solution)/shard_map/ppermute | solution.py:356
  258.6 20.4 %collective-permute-start.18 = (bf16[256,896]{1,0:T(8,128)(2,1)S(1)}, bf16[256,896]{1,0:T(8,128)(2,1)S(1)}, u32[]{:S(2)}, u32[]{:S(2)}) collective-permute-start(bf16[256,896]{1,0:T(8,128)(2,1)S(1)} %get-tuple-element.244), channel_id=1, source_target_pairs={{0,16},{16,0},{1,17},{17,1},{2,18},{18,2},{3,19},{19,3},{4,20},{20... | collective-permute-start | bytes 1376264 | tf_op jit(solution)/shard_map/ppermute | solution.py:356
  258.6 17.7 %collective-permute-start.22 = (bf16[432,256]{1,0:T(8,128)(2,1)S(1)}, bf16[432,256]{1,0:T(8,128)(2,1)S(1)}, u32[]{:S(2)}, u32[]{:S(2)}) collective-permute-start(bf16[432,256]{1,0:T(8,128)(2,1)S(1)} %get-tuple-element.255), channel_id=1, source_target_pairs={{0,4},{4,0},{8,12},{12,8},{1,5},{5,1},{9,13},{13,9},{2,6},{6,2},{1... | collective-permute-start | bytes 663560 | tf_op jit(solution)/shard_map/ppermute | solution.py:356
  258.6 17.7 %collective-permute-start.19 = (bf16[208,256]{1,0:T(8,128)(2,1)S(1)}, bf16[208,256]{1,0:T(8,128)(2,1)S(1)}, u32[]{:S(2)}, u32[]{:S(2)}) collective-permute-start(bf16[208,256]{1,0:T(8,128)(2,1)S(1)} %get-tuple-element.252), channel_id=1, source_target_pairs={{0,4},{4,0},{8,12},{12,8},{1,5},{5,1},{9,13},{13,9},{2,6},{6,2},{1... | collective-permute-start | bytes 319496 | tf_op jit(solution)/shard_map/ppermute | solution.py:356
  260.6 15.7 %collective-permute-start.20 = (bf16[208,256]{1,0:T(8,128)(2,1)S(1)}, bf16[208,256]{1,0:T(8,128)(2,1)S(1)}, u32[]{:S(2)}, u32[]{:S(2)}) collective-permute-start(bf16[208,256]{1,0:T(8,128)(2,1)S(1)} %get-tuple-element.253), channel_id=1, source_target_pairs={{0,8},{4,12},{8,0},{12,4},{1,9},{5,13},{9,1},{13,5},{2,10},{6,14},... | collective-permute-start | bytes 319496 | tf_op jit(solution)/shard_map/ppermute | solution.py:356
  262.5 13.8 %collective-permute-start.21 = (bf16[208,256]{1,0:T(8,128)(2,1)S(1)}, bf16[208,256]{1,0:T(8,128)(2,1)S(1)}, u32[]{:S(2)}, u32[]{:S(2)}) collective-permute-start(bf16[208,256]{1,0:T(8,128)(2,1)S(1)} %get-tuple-element.254), channel_id=1, source_target_pairs={{0,12},{4,8},{8,4},{12,0},{1,13},{5,9},{9,5},{13,1},{2,14},{6,10},... | collective-permute-start | bytes 319496 | tf_op jit(solution)/shard_map/ppermute | solution.py:356
  282.9 9.1 %collective-permute-start.27 = (f32[20480]{0:T(1024)S(1)}, f32[20480]{0:T(1024)}, u32[]{:S(2)}, u32[]{:S(2)}) collective-permute-start(f32[20480]{0:T(1024)S(1)} %pad_maximum_fusion.16), channel_id=1, source_target_pairs={{0,1},{1,0},{2,3},{3,2},{4,5},{5,4},{6,7},{7,6},{8,9},{9,8},{10,11... | collective-permute-start | bytes 245768 | tf_op jit(solution)/shard_map/ppermute | solution.py:356
  283.9 23.2 %collective-permute-start.25 = (bf16[256,896]{1,0:T(8,128)(2,1)}, bf16[256,896]{1,0:T(8,128)(2,1)S(1)}, u32[]{:S(2)}, u32[]{:S(2)}) collective-permute-start(bf16[256,896]{1,0:T(8,128)(2,1)} %add_convert_fusion.2), channel_id=1, source_target_pairs={{0,12},{4,8},{8,4},{12,0},{1,13},{5,9},{9,5},{13,1},{2,14},{6,10},... | collective-permute-start | bytes 1376264 | tf_op jit(solution)/shard_map/ppermute | solution.py:356
  283.9 34.3 %collective-permute-start.23 = (bf16[256,896]{1,0:T(8,128)(2,1)}, bf16[256,896]{1,0:T(8,128)(2,1)}, u32[]{:S(2)}, u32[]{:S(2)}) collective-permute-start(bf16[256,896]{1,0:T(8,128)(2,1)} %get-tuple-element.256), channel_id=1, source_target_pairs={{0,16},{16,0},{1,17},{17,1},{2,18},{18,2},{3,19},{19,3},{4,20},{20... | collective-permute-start | bytes 1376264 | tf_op jit(solution)/shard_map/ppermute | solution.py:356
  284.8 42.9 %collective-permute-start.24 = (bf16[256,896]{1,0:T(8,128)(2,1)}, bf16[256,896]{1,0:T(8,128)(2,1)}, u32[]{:S(2)}, u32[]{:S(2)}) collective-permute-start(bf16[256,896]{1,0:T(8,128)(2,1)} %get-tuple-element.257), channel_id=1, source_target_pairs={{0,16},{16,0},{1,17},{17,1},{2,18},{18,2},{3,19},{19,3},{4,20},{20... | collective-permute-start | bytes 1376264 | tf_op jit(solution)/shard_map/ppermute | solution.py:356
  290.1 37.7 %collective-permute-start.26 = (bf16[128,2048]{1,0:T(8,128)(2,1)S(1)}, bf16[128,2048]{1,0:T(8,128)(2,1)S(1)}, u32[]{:S(2)}, u32[]{:S(2)}) collective-permute-start(bf16[128,2048]{1,0:T(8,128)(2,1)S(1)} %slice_bitcast_fusion.3), channel_id=1, source_target_pairs={{0,8},{8,0},{1,9},{9,1},{2,10},{10,2},{3,11},{11,3},{4,12},{12,4},... | collective-permute-start | bytes 1572872 | tf_op jit(solution)/shard_map/ppermute | solution.py:356
  292.9 4.5 %collective-permute-start.28 = (f32[20480]{0:T(1024)S(1)}, f32[20480]{0:T(1024)S(1)}, u32[]{:S(2)}, u32[]{:S(2)}) collective-permute-start(f32[20480]{0:T(1024)S(1)} %fusion.44), channel_id=1, source_target_pairs={{0,2},{2,0},{1,3},{3,1},{4,6},{6,4},{5,7},{7,5},{8,10},{10,8},{9,1... | collective-permute-start | bytes 245768 | tf_op jit(solution)/shard_map/ppermute | solution.py:356
  293.8 42.4 %copy-start.62 = (f32[2048]{0:T(1024)S(1)}, f32[2048]{0:T(1024)}, u32[]{:S(2)}) copy-start(f32[2048]{0:T(1024)} %param.23) | copy-start | bytes 24580
  293.8 42.4 %copy-start.63 = (f32[2048]{0:T(1024)S(1)}, f32[2048]{0:T(1024)}, u32[]{:S(2)}) copy-start(f32[2048]{0:T(1024)} %param.19) | copy-start | bytes 24580
  327.7 7.7 %collective-permute-start.32 = (f32[20480]{0:T(1024)S(1)}, f32[20480]{0:T(1024)S(1)}, u32[]{:S(2)}, u32[]{:S(2)}) collective-permute-start(f32[20480]{0:T(1024)S(1)} %add.293), channel_id=1, source_target_pairs={{0,4},{4,0},{1,5},{5,1},{2,6},{6,2},{3,7},{7,3},{8,12},{12,8},{9,1... | collective-permute-start | bytes 245768 | tf_op jit(solution)/shard_map/ppermute | solution.py:356
  330.5 24.9 %collective-permute-start.31 = (bf16[256,896]{1,0:T(8,128)(2,1)S(1)}, bf16[256,896]{1,0:T(8,128)(2,1)S(1)}, u32[]{:S(2)}, u32[]{:S(2)}) collective-permute-start(bf16[256,896]{1,0:T(8,128)(2,1)S(1)} %add_convert_fusion), channel_id=1, source_target_pairs={{0,8},{4,12},{8,0},{12,4},{1,9},{5,13},{9,1},{13,5},{2,10},{6,14},... | collective-permute-start | bytes 1376264 | tf_op jit(solution)/shard_map/ppermute | solution.py:356
  332.1 23.4 %collective-permute-start.30 = (bf16[256,896]{1,0:T(8,128)(2,1)S(1)}, bf16[256,896]{1,0:T(8,128)(2,1)S(1)}, u32[]{:S(2)}, u32[]{:S(2)}) collective-permute-start(bf16[256,896]{1,0:T(8,128)(2,1)S(1)} %add_convert_fusion.1), channel_id=1, source_target_pairs={{0,4},{4,0},{8,12},{12,8},{1,5},{5,1},{9,13},{13,9},{2,6},{6,2},{1... | collective-permute-start | bytes 1376264 | tf_op jit(solution)/shard_map/ppermute | solution.py:356
  333.0 22.4 %collective-permute-start.29 = (bf16[256,896]{1,0:T(8,128)(2,1)S(1)}, bf16[256,896]{1,0:T(8,128)(2,1)S(1)}, u32[]{:S(2)}, u32[]{:S(2)}) collective-permute-start(bf16[256,896]{1,0:T(8,128)(2,1)S(1)} %copy-done.53), channel_id=1, source_target_pairs={{0,16},{16,0},{1,17},{17,1},{2,18},{18,2},{3,19},{19,3},{4,20},{20... | collective-permute-start | bytes 1376264 | tf_op jit(solution)/shard_map/ppermute | solution.py:356
  335.4 16.7 %collective-permute-start.33 = (f32[20480]{0:T(1024)S(1)}, f32[20480]{0:T(1024)S(1)}, u32[]{:S(2)}, u32[]{:S(2)}) collective-permute-start(f32[20480]{0:T(1024)S(1)} %add.297), channel_id=1, source_target_pairs={{0,8},{8,0},{1,9},{9,1},{2,10},{10,2},{3,11},{11,3},{4,12},{12,4},... | collective-permute-start | bytes 245768 | tf_op jit(solution)/shard_map/ppermute | solution.py:356
  355.5 6.1 %collective-permute-start.35 = (f32[20480]{0:T(1024)S(1)}, f32[20480]{0:T(1024)}, u32[]{:S(2)}, u32[]{:S(2)}) collective-permute-start(f32[20480]{0:T(1024)S(1)} %add.298), channel_id=1, source_target_pairs={{0,16},{16,0},{1,17},{17,1},{2,18},{18,2},{3,19},{19,3},{4,20},{20... | collective-permute-start | bytes 245768 | tf_op jit(solution)/shard_map/ppermute | solution.py:356
  364.5 10.1 %collective-permute-start.34 = (bf16[128,2048]{1,0:T(8,128)(2,1)S(1)}, bf16[128,2048]{1,0:T(8,128)(2,1)S(1)}, u32[]{:S(2)}, u32[]{:S(2)}) collective-permute-start(bf16[128,2048]{1,0:T(8,128)(2,1)S(1)} %get-tuple-element.327), channel_id=1, source_target_pairs={{0,8},{8,0},{1,9},{9,1},{2,10},{10,2},{3,11},{11,3},{4,12},{12,4},... | collective-permute-start | bytes 1572872 | tf_op jit(solution)/shard_map/ppermute | solution.py:356
  (57 other events, 590.7 us)
Sparse Core Ops, SparseCore 0:
  30.4 74.5 all-gather.2
  107.4 61.8 all-gather.4
  198.7 83.0 reduce-scatter.2
  285.5 73.9 reduce-scatter.4
